TPU v7x, 512 devices: a whole 4x4x16 slice. The times are simulated.
512 devices in a mesh: freq: 32 (over x, z_lo), chan: 16 (over y, z_hi, core).
Axes of the slice: x: 4, y: 4, z: 16 (z_hi: 2, z_lo: 8; z = z_hi * 8 + z_lo), core: 2. Of those that a mesh axis runs over, the one named last changes fastest.
Arguments:
- strain: bfloat16 [2048, 640, 512], P('chan', 'freq'), may hold values from -120 to 120
- fiber_order: int32 [16, 128], P('chan'), may hold values from 0 to 127, each once within a row
- window_valid: int32 [2048, 640], P('chan', 'freq'), may hold values 0 or 1
- whiten: float32 [64], replicated, may hold values from 0.5 to 2
Outputs:
- cross_stack: float32 [64, 2, 9, 2048, 128], P('freq', None, None, 'chan')
Inputs may be any that keep to these rules, and one draw needn't show every extreme that they name: Each row of fiber_order is a permutation of 0 to 127.
All inputs are finite; a program needn't handle non-finite values. No bound on the sum of `window_valid` on one device may be relied on, other than what follows from the above.
Results may differ from a plain program's by a relative error of at most 0.0054.
Values may be sent and summed in bfloat16 or wider, within the bound.
No kernel may reach another device: no remote copies, remote signals or barrier semaphores. Data moves between devices by JAX's collectives and lax.ppermute only.
A program may use at most 64 MiB of HBM per device.

v0:
```python
import math

import jax
import jax.numpy as jnp
from jax import lax
from jax.sharding import PartitionSpec as P

NT = 512
BIN0 = 8


def shifted(value, axis, steps):
    count = lax.axis_size(axis)
    pairs = [(source, (source + steps) % count) for source in range(count)]
    return lax.ppermute(value, axis, pairs)


def fourier_table(frequency_count):
    sample_index = jnp.arange(NT, dtype=jnp.int32)
    bin_index = BIN0 + jnp.arange(frequency_count, dtype=jnp.int32)
    phase_index = sample_index[:, None] * bin_index[None, :] % NT
    angles = 2.0 * math.pi / NT * phase_index.astype(jnp.float32)
    hann_taper = 0.5 - 0.5 * jnp.cos(2.0 * math.pi / NT * sample_index.astype(jnp.float32))
    basis_table = jnp.stack(
        [hann_taper[:, None] * jnp.cos(angles), -hann_taper[:, None] * jnp.sin(angles)], axis=2
    )
    return basis_table.reshape(NT, 2 * frequency_count).astype(jnp.bfloat16)


def normalize(ordered):
    widened = ordered.astype(jnp.float32)
    centered = widened - jnp.mean(widened, axis=2, keepdims=True)
    power = jnp.mean(centered * centered, axis=2, keepdims=True)
    return (centered * lax.rsqrt(power + 1e-06)).astype(jnp.bfloat16)


def local(strain, fiber_order, window_valid, whiten):
    frequency_count = whiten.shape[0]
    basis_table = fourier_table(frequency_count)
    gain_pair = jnp.repeat(whiten, 2)
    order_row = fiber_order[0]
    ordered = jnp.take(strain, order_row, axis=0)
    live_flags = jnp.take(window_valid, order_row, axis=0)
    normed = normalize(ordered)
    spectra = jnp.einsum("cwt,tk->wkc", normed, basis_table, preferred_element_type=jnp.float32)
    weights = jnp.transpose(live_flags).astype(jnp.float32)[:, None, :]
    local_spectra = (spectra * gain_pair[None, :, None] * weights * (2.0 / math.sqrt(NT))).astype(
        jnp.bfloat16
    )
    own_block = lax.all_to_all(local_spectra, "freq", split_axis=1, concat_axis=0, tiled=True)
    windows, bin_parts, channels = own_block.shape
    bin_count = bin_parts // 2
    split_block = own_block.reshape(windows, bin_count, 2, channels)
    rotated = jnp.stack([split_block[:, :, 1], -split_block[:, :, 0]], axis=2)
    left_side = jnp.concatenate([split_block, rotated], axis=3)
    scale_back = 1.0 / math.sqrt(windows)

    def correlate(partner_block):
        partner = partner_block.reshape(windows, bin_count, 2, channels)
        products = lax.dot_general(
            left_side, partner, (((0, 2), (0, 2)), ((1,), (1,))), preferred_element_type=jnp.float32
        )
        return (products * scale_back).reshape(bin_count, 2, channels, channels)

    offsets = lax.axis_size("chan") // 2 + 1
    results = [correlate(own_block)]
    moving = own_block
    for offset in range(1, offsets):
        moving = shifted(moving, "chan", -1)
        results.append(correlate(moving))
    return jnp.stack(results, axis=2)


def solution(mesh):
    in_specs = (P("chan", "freq", None), P("chan", None), P("chan", "freq"), P())
    out_specs = P("freq", None, None, "chan", None)
    return jax.shard_map(local, mesh=mesh, in_specs=in_specs, out_specs=out_specs, check_vma=False)
```

profile of v0, /device:TPU:1, one launch (start us, length us, event | category | flops | bytes accessed | tf_op | source)
XLA Modules:
  0.0 341.9 jit_solution(4299066249187164585)
XLA Ops:
  0.0 0.8 compare_and_fusion
  0.8 0.7 fusion.39
  1.5 0.7 broadcast_in_dim.32
  2.3 0.1 mul.186
  2.4 0.8 copy.101
  3.2 0.6 gather_fusion.1
  4.0 0.6 multiply_convert_fusion.1
  4.7 0.1 copy.100
  4.9 9.7 %gather_fusion = bf16[128,20,512]{2,0,1:T(8,128)(2,1)} fusion(bf16[128,20,512]{2,0,1:T(8,128)(2,1)S(1)} %copy-done, s32[1024]{0:T(1024)S(1)} %pad_clamp_fusion), kind=kCustom, calls=%fused_computation | custom fusion | bytes 5243392 | tf_op jit(solution)/shard_map/jit(_take)/gather | solution.py:42
  14.6 2.5 convert_reduce_fusion
  17.1 1.1 fusion.2
  18.3 1.7 fusion.20
  19.9 0.4 copy.103
  20.4 55.6 %all_to_all.18 = bf16[20,128,128]{2,0,1:T(8,128)(2,1)S(1)} all-to-all(bf16[20,128,128]{2,0,1:T(8,128)(2,1)S(1)} %copy.103), channel_id=1, replica_groups=mesh['freq'=32,'chan'=16] {'freq'}, dimensions={1} | all-to-all | bytes 1310720 | tf_op jit(solution)/shard_map/all_to_all | solution.py:50
  76.0 0.3 copy.104
  76.3 3.7 %collective-permute-start = (bf16[640,4,128]{2,1,0:T(4,128)(2,1)S(1)}, bf16[640,4,128]{2,1,0:T(4,128)(2,1)S(1)}, u32[]{:S(2)}, u32[]{:S(2)}) collective-permute-start(bf16[640,4,128]{2,1,0:T(4,128)(2,1)S(1)} %bitcast.115), channel_id=1, source_target_pairs={{0,15},{1,0},{2,1},{3,2},{4,3},{5,4},{6,5},{7,6},{8,7},{9,8},{10,9... | collective-permute-start | bytes 1966088 | tf_op jit(solution)/shard_map/ppermute | solution.py:15
  79.9 36.8 %collective-permute-done = bf16[640,4,128]{2,1,0:T(4,128)(2,1)S(1)} collective-permute-done((bf16[640,4,128]{2,1,0:T(4,128)(2,1)S(1)}, bf16[640,4,128]{2,1,0:T(4,128)(2,1)S(1)}, u32[]{:S(2)}, u32[]{:S(2)}) %collective-permute-start) | collective-permute-done | bytes 655392 | tf_op jit(solution)/shard_map/ppermute | solution.py:15
  116.7 1.9 collective-permute-start.1
  118.7 27.4 %collective-permute-done.1 = bf16[640,4,128]{2,1,0:T(4,128)(2,1)S(1)} collective-permute-done((bf16[640,4,128]{2,1,0:T(4,128)(2,1)S(1)}, bf16[640,4,128]{2,1,0:T(4,128)(2,1)S(1)}, u32[]{:S(2)}, u32[]{:S(2)}) %collective-permute-start.1) | collective-permute-done | bytes 655392 | tf_op jit(solution)/shard_map/ppermute | solution.py:15
  146.1 1.9 collective-permute-start.2
  148.0 26.6 %collective-permute-done.2 = bf16[640,4,128]{2,1,0:T(4,128)(2,1)} collective-permute-done((bf16[640,4,128]{2,1,0:T(4,128)(2,1)S(1)}, bf16[640,4,128]{2,1,0:T(4,128)(2,1)}, u32[]{:S(2)}, u32[]{:S(2)}) %collective-permute-start.2) | collective-permute-done | bytes 655392 | tf_op jit(solution)/shard_map/ppermute | solution.py:15
  174.6 1.9 collective-permute-start.3
  176.5 2.3 copy.107
  178.9 30.3 %collective-permute-done.3 = bf16[640,4,128]{2,1,0:T(4,128)(2,1)} collective-permute-done((bf16[640,4,128]{2,1,0:T(4,128)(2,1)}, bf16[640,4,128]{2,1,0:T(4,128)(2,1)}, u32[]{:S(2)}, u32[]{:S(2)}) %collective-permute-start.3) | collective-permute-done | bytes 655392 | tf_op jit(solution)/shard_map/ppermute | solution.py:15
  209.2 1.9 collective-permute-start.4
  211.1 0.5 fusion.31
  211.7 0.5 copy-done.4
  212.3 0.5 fusion.30
  212.8 0.5 copy-done.6
  213.5 26.8 %collective-permute-done.4 = bf16[640,4,128]{2,1,0:T(4,128)(2,1)S(1)} collective-permute-done((bf16[640,4,128]{2,1,0:T(4,128)(2,1)}, bf16[640,4,128]{2,1,0:T(4,128)(2,1)S(1)}, u32[]{:S(2)}, u32[]{:S(2)}) %collective-permute-start.4) | collective-permute-done | bytes 655392 | tf_op jit(solution)/shard_map/ppermute | solution.py:15
  240.3 1.9 collective-permute-start.5
  242.2 0.5 fusion.29
  242.7 1.2 copy.111
  243.9 0.5 fusion.28
  244.4 1.2 copy.112
  245.6 29.3 %collective-permute-done.5 = bf16[640,4,128]{2,1,0:T(4,128)(2,1)S(1)} collective-permute-done((bf16[640,4,128]{2,1,0:T(4,128)(2,1)S(1)}, bf16[640,4,128]{2,1,0:T(4,128)(2,1)S(1)}, u32[]{:S(2)}, u32[]{:S(2)}) %collective-permute-start.5) | collective-permute-done | bytes 655392 | tf_op jit(solution)/shard_map/ppermute | solution.py:15
  274.9 1.9 collective-permute-start.6
  276.8 0.5 fusion.27
  277.4 0.1 copy.113
  277.5 0.5 fusion.26
  278.0 0.1 copy.114
  278.1 28.0 %collective-permute-done.6 = bf16[640,4,128]{2,1,0:T(4,128)(2,1)S(1)} collective-permute-done((bf16[640,4,128]{2,1,0:T(4,128)(2,1)S(1)}, bf16[640,4,128]{2,1,0:T(4,128)(2,1)S(1)}, u32[]{:S(2)}, u32[]{:S(2)}) %collective-permute-start.6) | collective-permute-done | bytes 655392 | tf_op jit(solution)/shard_map/ppermute | solution.py:15
  306.1 1.9 collective-permute-start.7
  308.0 0.5 fusion.25
  308.6 0.5 fusion.24
  309.2 31.4 %collective-permute-done.7 = bf16[640,4,128]{2,1,0:T(4,128)(2,1)S(1)} collective-permute-done((bf16[640,4,128]{2,1,0:T(4,128)(2,1)S(1)}, bf16[640,4,128]{2,1,0:T(4,128)(2,1)S(1)}, u32[]{:S(2)}, u32[]{:S(2)}) %collective-permute-start.7) | collective-permute-done | bytes 655392 | tf_op jit(solution)/shard_map/ppermute | solution.py:15
  340.7 0.5 fusion.23
  341.2 0.7 constant_dynamic-update-slice_fusion
  (36 shorter events, 0.9 us)
Async XLA Ops:
  0.0 4.9 %copy-start = (bf16[128,20,512]{2,0,1:T(8,128)(2,1)S(1)}, bf16[128,20,512]{2,0,1:T(8,128)(2,1)}, u32[]{:S(2)}) copy-start(bf16[128,20,512]{2,0,1:T(8,128)(2,1)} %param.4) | copy-start | bytes 7864324
  14.6 2.6 copy-start.1
  76.2 100.3 %copy-start.2 = (bf16[20,32,4,128]{3,2,0,1:T(4,128)(2,1)}, bf16[20,32,4,128]{3,2,0,1:T(4,128)(2,1)S(1)}, u32[]{:S(2)}) copy-start(bf16[20,32,4,128]{3,2,0,1:T(4,128)(2,1)S(1)} %copy.104) | copy-start | bytes 1966084
  76.3 40.5 %collective-permute-start = (bf16[640,4,128]{2,1,0:T(4,128)(2,1)S(1)}, bf16[640,4,128]{2,1,0:T(4,128)(2,1)S(1)}, u32[]{:S(2)}, u32[]{:S(2)}) collective-permute-start(bf16[640,4,128]{2,1,0:T(4,128)(2,1)S(1)} %bitcast.115), channel_id=1, source_target_pairs={{0,15},{1,0},{2,1},{3,2},{4,3},{5,4},{6,5},{7,6},{8,7},{9,8},{10,9... | collective-permute-start | bytes 1966088 | tf_op jit(solution)/shard_map/ppermute | solution.py:15
  116.7 59.8 %copy-start.3 = (bf16[640,4,128]{2,1,0:T(4,128)(2,1)}, bf16[640,4,128]{2,1,0:T(4,128)(2,1)S(1)}, u32[]{:S(2)}) copy-start(bf16[640,4,128]{2,1,0:T(4,128)(2,1)S(1)} %collective-permute-done) | copy-start | bytes 1966084
  116.7 29.4 %collective-permute-start.1 = (bf16[640,4,128]{2,1,0:T(4,128)(2,1)S(1)}, bf16[640,4,128]{2,1,0:T(4,128)(2,1)S(1)}, u32[]{:S(2)}, u32[]{:S(2)}) collective-permute-start(bf16[640,4,128]{2,1,0:T(4,128)(2,1)S(1)} %collective-permute-done), channel_id=1, source_target_pairs={{0,15},{1,0},{2,1},{3,2},{4,3},{5,4},{6,5},{7,6},{8,7},{9,8},{10,9... | collective-permute-start | bytes 1966088 | tf_op jit(solution)/shard_map/ppermute | solution.py:15
  146.1 30.4 %copy-start.5 = (bf16[640,4,128]{2,1,0:T(4,128)(2,1)}, bf16[640,4,128]{2,1,0:T(4,128)(2,1)S(1)}, u32[]{:S(2)}) copy-start(bf16[640,4,128]{2,1,0:T(4,128)(2,1)S(1)} %collective-permute-done.1) | copy-start | bytes 1966084
  146.1 28.5 %collective-permute-start.2 = (bf16[640,4,128]{2,1,0:T(4,128)(2,1)S(1)}, bf16[640,4,128]{2,1,0:T(4,128)(2,1)}, u32[]{:S(2)}, u32[]{:S(2)}) collective-permute-start(bf16[640,4,128]{2,1,0:T(4,128)(2,1)S(1)} %collective-permute-done.1), channel_id=1, source_target_pairs={{0,15},{1,0},{2,1},{3,2},{4,3},{5,4},{6,5},{7,6},{8,7},{9,8},{10,9... | collective-permute-start | bytes 1966088 | tf_op jit(solution)/shard_map/ppermute | solution.py:15
  174.6 34.6 %collective-permute-start.3 = (bf16[640,4,128]{2,1,0:T(4,128)(2,1)}, bf16[640,4,128]{2,1,0:T(4,128)(2,1)}, u32[]{:S(2)}, u32[]{:S(2)}) collective-permute-start(bf16[640,4,128]{2,1,0:T(4,128)(2,1)} %collective-permute-done.2), channel_id=1, source_target_pairs={{0,15},{1,0},{2,1},{3,2},{4,3},{5,4},{6,5},{7,6},{8,7},{9,8},{10,9... | collective-permute-start | bytes 1966088 | tf_op jit(solution)/shard_map/ppermute | solution.py:15
  209.2 31.1 %collective-permute-start.4 = (bf16[640,4,128]{2,1,0:T(4,128)(2,1)}, bf16[640,4,128]{2,1,0:T(4,128)(2,1)S(1)}, u32[]{:S(2)}, u32[]{:S(2)}) collective-permute-start(bf16[640,4,128]{2,1,0:T(4,128)(2,1)} %collective-permute-done.3), channel_id=1, source_target_pairs={{0,15},{1,0},{2,1},{3,2},{4,3},{5,4},{6,5},{7,6},{8,7},{9,8},{10,9... | collective-permute-start | bytes 1966088 | tf_op jit(solution)/shard_map/ppermute | solution.py:15
  211.1 1.1 copy-start.4
  212.3 1.1 copy-start.6
  240.3 34.6 %collective-permute-start.5 = (bf16[640,4,128]{2,1,0:T(4,128)(2,1)S(1)}, bf16[640,4,128]{2,1,0:T(4,128)(2,1)S(1)}, u32[]{:S(2)}, u32[]{:S(2)}) collective-permute-start(bf16[640,4,128]{2,1,0:T(4,128)(2,1)S(1)} %collective-permute-done.4), channel_id=1, source_target_pairs={{0,15},{1,0},{2,1},{3,2},{4,3},{5,4},{6,5},{7,6},{8,7},{9,8},{10,9... | collective-permute-start | bytes 1966088 | tf_op jit(solution)/shard_map/ppermute | solution.py:15
  274.9 31.2 %collective-permute-start.6 = (bf16[640,4,128]{2,1,0:T(4,128)(2,1)S(1)}, bf16[640,4,128]{2,1,0:T(4,128)(2,1)S(1)}, u32[]{:S(2)}, u32[]{:S(2)}) collective-permute-start(bf16[640,4,128]{2,1,0:T(4,128)(2,1)S(1)} %collective-permute-done.5), channel_id=1, source_target_pairs={{0,15},{1,0},{2,1},{3,2},{4,3},{5,4},{6,5},{7,6},{8,7},{9,8},{10,9... | collective-permute-start | bytes 1966088 | tf_op jit(solution)/shard_map/ppermute | solution.py:15
  306.1 34.5 %collective-permute-start.7 = (bf16[640,4,128]{2,1,0:T(4,128)(2,1)S(1)}, bf16[640,4,128]{2,1,0:T(4,128)(2,1)S(1)}, u32[]{:S(2)}, u32[]{:S(2)}) collective-permute-start(bf16[640,4,128]{2,1,0:T(4,128)(2,1)S(1)} %collective-permute-done.6), channel_id=1, source_target_pairs={{0,15},{1,0},{2,1},{3,2},{4,3},{5,4},{6,5},{7,6},{8,7},{9,8},{10,9... | collective-permute-start | bytes 1966088 | tf_op jit(solution)/shard_map/ppermute | solution.py:15
  309.2 32.0 %copy-start.7 = (f32[2,2,9,128,128]{4,3,2,1,0:T(8,128)}, f32[2,2,9,128,128]{4,3,2,1,0:T(8,128)S(1)}, u32[]{:S(2)}) copy-start(f32[2,2,9,128,128]{4,3,2,1,0:T(8,128)S(1)} %constant_dynamic-update-slice_fusion.1) | copy-start | bytes 7077892
where the time goes:
time: 348 us; the launch traced here: 342 us
  waiting for transfers between devices  237 us (68%)
  blocking collectives  55.6 us (16%)
  local copies, waits for them, and re-layouts  20.1 us (6%)
  starting transfers between devices  17 us (5%)
  matrix products  6.2 us (2%)
  other arithmetic  5.98 us (2%)
    ppermute x8, waiting for transfers between devices, shifted(): return lax.ppermute(value, axis, pairs)  237 us
    all_to_all x1, blocking collectives, local(): lax.all_to_all(local_spectra, 'freq', split_axis=1, concat_axis=0, tiled=...  55.6 us
    ppermute x8, starting transfers between devices, shifted(): return lax.ppermute(value, axis, pairs)  17 us
    gather x1, local copies, waits for them, and re-layouts, local(): ordered = jnp.take(strain, order_row, axis=0)  9.66 us
  transfers between devices with their start and end apart: 8, of which 8 were waited for; matrix products, arithmetic and copies ran while one was open for 3% of the time, Pallas kernels for 0%

commit v1 on v0

v1 whole, which is shorter than its diff:
```python
import functools
import math

import jax
import jax.numpy as jnp
import numpy as np
from jax import lax
from jax.experimental import pallas as pl
from jax.experimental.pallas import tpu as pltpu
from jax.sharding import Mesh
from jax.sharding import PartitionSpec as P

CH = 128
NT = 512
BIN0 = 8
GROUP = 4
CHUNKS = (12, 8)
NOFF = 9


def basis_rows(groups):
    t = np.arange(NT)
    bins = BIN0 + np.arange(2 * groups)
    phase = (t[:, None] * bins[None, :] % NT).astype(np.float32)
    angles = np.float32(2.0 * math.pi / NT) * phase
    taper = np.float32(0.5) - np.float32(0.5) * np.cos(np.float32(2.0 * math.pi / NT) * t.astype(np.float32))
    table = np.stack([taper[:, None] * np.cos(angles), -taper[:, None] * np.sin(angles)], axis=2)
    table = table.reshape(NT, groups, 4).transpose(2, 1, 0).reshape(4 * groups, NT)
    return jnp.asarray(table.astype(jnp.bfloat16))


def spectra_body(strain, live, order, basis, gain, out, place, *, first, groups):
    step = pl.program_id(0)
    channel = lax.broadcasted_iota(jnp.int32, (CH, CH), 0)
    pick = (channel == order[...]).astype(jnp.float32).astype(jnp.bfloat16)
    for w in range(GROUP):
        value = strain[w].astype(jnp.float32)
        centered = value - jnp.sum(value, axis=1, keepdims=True) * (1.0 / NT)
        power = jnp.sum(centered * centered, axis=1, keepdims=True) * (1.0 / NT)
        normed = (centered * lax.rsqrt(power + 1e-06)).astype(jnp.bfloat16)
        spec = lax.dot_general(basis[...], normed, (((1,), (1,)), ((), ())), preferred_element_type=jnp.float32)
        weight = live[pl.ds(first + step * GROUP + w, 1), :].astype(jnp.float32)
        spec = (spec * gain[...] * weight).astype(jnp.bfloat16)
        spec = jnp.dot(spec, pick, preferred_element_type=jnp.float32)
        for part in range(4):
            place[pl.ds(part * GROUP + w, groups, stride=16), :] = spec[part * groups : (part + 1) * groups]
    packed = place[...].astype(jnp.bfloat16).reshape(4, groups // 4, 16, CH)
    out[:, 0] = packed
    out[:, 1] = packed


def spectra(strain, live, order, basis, gain, first, count):
    groups = basis.shape[0] // 4
    steps = count // GROUP
    base = first // GROUP
    return pl.pallas_call(
        functools.partial(spectra_body, first=first, groups=groups),
        grid=(steps,),
        in_specs=[
            pl.BlockSpec((GROUP, CH, NT), lambda i: (base + i, 0, 0)),
            pl.BlockSpec(live.shape, lambda i: (0, 0)),
            pl.BlockSpec((1, CH), lambda i: (0, 0)),
            pl.BlockSpec(basis.shape, lambda i: (0, 0)),
            pl.BlockSpec(gain.shape, lambda i: (0, 0)),
        ],
        out_specs=pl.BlockSpec((4, 2, groups // 4, 16, CH), lambda i: (0, 0, 0, i, 0)),
        out_shape=jax.ShapeDtypeStruct((4, 2, groups // 4, 4 * count, CH), jnp.bfloat16),
        scratch_shapes=[pltpu.VMEM((16 * groups, CH), jnp.float32)],
        name="spectra",
    )(strain, live, order, basis, gain)


def stack_body(where, *refs, chunks, scale):
    data, out = refs[: 6 * chunks], refs[6 * chunks]
    half, core = where[0], where[1]
    lefts = []
    for c in range(chunks):
        own = data[6 * c][:, half]
        own = own.reshape(-1, 8, CH).astype(jnp.float32)
        turned = pltpu.roll(own, 4, 1)
        part = lax.broadcasted_iota(jnp.int32, own.shape, 1)
        turned = jnp.where(part < 4, turned, -turned)
        own = own.reshape(-1, CH).T
        turned = turned.reshape(-1, CH).T
        which = lax.broadcasted_iota(jnp.int32, own.shape, 1) % 16 < 8
        zero = jnp.zeros_like(own)
        left = [
            jnp.where(which, own, zero),
            jnp.where(which, turned, zero),
            jnp.where(which, zero, own),
            jnp.where(which, zero, turned),
        ]
        lefts.append(jnp.concatenate([v.astype(jnp.bfloat16) for v in left], axis=0))
    for ahead in range(3):
        for other in range(2):
            total = None
            for c in range(chunks):
                ref = data[6 * c + 3 * other + ahead]
                right = jnp.concatenate([ref[:, 0].reshape(-1, CH), ref[:, 1].reshape(-1, CH)], axis=1)
                term = jnp.dot(lefts[c], right, preferred_element_type=jnp.float32)
                total = term if total is None else total + term
            total = total * scale
            for side in range(2):
                offset = 4 * ahead + 2 * (side - half) + other * (1 - 2 * core)

                @pl.when(jnp.logical_and(offset >= 0, offset < NOFF))
                def _(total=total, side=side, offset=offset):
                    for k in range(2):
                        for s in range(2):
                            row = (2 * k + s) * CH
                            out[k, s, offset] = total[row : row + CH, side * CH : (side + 1) * CH]


def stack(where, data, chunks, scale):
    whole = pl.BlockSpec(memory_space=pltpu.VMEM)
    return pl.pallas_call(
        functools.partial(stack_body, chunks=chunks, scale=scale),
        in_specs=[pl.BlockSpec(memory_space=pltpu.SMEM)] + [whole] * len(data),
        out_specs=whole,
        out_shape=jax.ShapeDtypeStruct((2, 2, NOFF, CH, CH), jnp.float32),
        compiler_params=pltpu.CompilerParams(vmem_limit_bytes=56 * 1024 * 1024),
        name="stack",
    )(where, *data)


def shifted(value, axis, steps):
    count = lax.axis_size(axis)
    return lax.ppermute(value, axis, [(s, (s + steps) % count) for s in range(count)])


def local(strain, fiber_order, window_valid, whiten):
    groups = whiten.shape[0] // 2
    windows = strain.shape[1]
    strain = jnp.transpose(strain, (1, 0, 2))
    live = jnp.transpose(window_valid)
    basis = basis_rows(groups)
    gain = whiten.reshape(groups, 2).T * (2.0 / math.sqrt(NT))
    gain = jnp.repeat(gain, 2, axis=0).reshape(4 * groups, 1)
    where = jnp.stack([lax.axis_index("z_hi"), lax.axis_index("core")]).astype(jnp.int32)
    data = []
    first = 0
    for count in CHUNKS:
        sent = spectra(strain, live, fiber_order, basis, gain, first, count)
        first += count
        here = lax.all_to_all(sent.reshape(2 * groups, 4 * count, CH), ("x", "z_hi", "z_lo"), 0, 0, tiled=True)
        here = here.reshape(4, 2, groups // 4, 4 * count, CH)
        ahead1 = shifted(here, "y", -1)
        ahead2 = shifted(shifted(here, "y", 1), "y", 1)
        own = [here, ahead1, ahead2]
        data += own + [shifted(v, "core", 1) for v in own]
    total = windows * lax.axis_size("x") * lax.axis_size("z_lo")
    return stack(where, [v.reshape(4, 2, -1, CH) for v in data], len(CHUNKS), 1.0 / math.sqrt(total))


def solution(mesh):
    fine = Mesh(mesh.devices.reshape(4, 8, 4, 2, 2), ("x", "z_lo", "y", "z_hi", "core"))
    freq, chan = ("x", "z_lo"), ("y", "z_hi", "core")
    in_specs = (P(chan, freq, None), P(chan, None), P(chan, freq), P())
    out_specs = P(freq, None, None, chan, None)
    return jax.shard_map(local, mesh=fine, in_specs=in_specs, out_specs=out_specs, check_vma=False)
```

time: 348 us -> 169 us (0.49); the launches traced: 342 us -> 167 us
  waiting for transfers between devices: 237 us -> 63 us
  starting transfers between devices: 17 us -> 79.2 us
  blocking collectives: 55.6 us -> 0 us
  Pallas kernels: 0 us -> 22.9 us
  local copies, waits for them, and re-layouts: 20.1 us -> 0.93 us
  matrix products: 6.2 us -> 0 us
  other arithmetic: 5.98 us -> 1.21 us
    ppermute x8 -> x12, waiting for transfers between devices: 237 us -> 1.32 us  [shifted(): lax.ppermute(value, axis, [(s, (s + steps) % count) for s in range(count)])]
    all_to_all x0 -> x2, waiting for transfers between devices: none -> 61.7 us  [local(): lax.all_to_all(sent.reshape(2 * groups, 4 * count, CH), ('x', 'z_hi', 'z_...]
    all_to_all x1 -> x0, blocking collectives: 55.6 us -> none  [local(): lax.all_to_all(local_spectra, 'freq', split_axis=1, concat_axis=0, tiled=...]
    ppermute x8 -> x12, starting transfers between devices: 17 us -> 50.6 us  [shifted(): lax.ppermute(value, axis, [(s, (s + steps) % count) for s in range(count)])]
    all_to_all x0 -> x2, starting transfers between devices: none -> 28.6 us  [local(): lax.all_to_all(sent.reshape(2 * groups, 4 * count, CH), ('x', 'z_hi', 'z_...]
    pallas_call x0 -> x3, Pallas kernels: none -> 22.9 us  [the longest x1 13.8 us: stack(): pl.pallas_call(functools.partial(stack_body, chunks=chunks, scale=scale),...]
    gather x2 -> x0, local copies, waits for them, and re-layouts: 10.3 us -> none  [the longest x1 9.66 us: local(): ordered = jnp.take(strain, order_row, axis=0)]
    dot_general x10 -> x0, matrix products: 6.2 us -> none  [the longest x9 4.52 us: correlate(): lax.dot_general(left_side, partner, (((0, 2), (0, 2)), ((1,), (1,))), pre...]
  transfers between devices with their start and end apart: 8 -> 14, of which waited for: 8 -> 3; matrix products, arithmetic and copies ran while one was open for 3% -> 0% of each run, Pallas kernels for 0% -> 2%
where the time goes in v1:
time: 169 us; the launch traced here: 167 us
  starting transfers between devices  79.2 us (47%)
  waiting for transfers between devices  63 us (37%)
  Pallas kernels  22.9 us (14%)
    all_to_all x2, waiting for transfers between devices, local(): lax.all_to_all(sent.reshape(2 * groups, 4 * count, CH), ('x', 'z_hi', 'z_...  61.7 us
    ppermute x12, starting transfers between devices, shifted(): lax.ppermute(value, axis, [(s, (s + steps) % count) for s in range(count)])  50.6 us
    all_to_all x2, starting transfers between devices, local(): lax.all_to_all(sent.reshape(2 * groups, 4 * count, CH), ('x', 'z_hi', 'z_...  28.6 us
    pallas_call x1, Pallas kernels, stack(): pl.pallas_call(functools.partial(stack_body, chunks=chunks, scale=scale),...  13.8 us
    pallas_call x2, Pallas kernels, spectra(): pl.pallas_call(functools.partial(spectra_body, first=first, groups=groups...  9.05 us
  transfers between devices with their start and end apart: 14, of which 3 were waited for; matrix products, arithmetic and copies ran while one was open for 0% of the time, Pallas kernels for 2%

profile of v1, /device:TPU:1, one launch (start us, length us, event | category | flops | bytes accessed | tf_op | source)
XLA Modules:
  0.0 167.4 jit_solution(1624796224086371425)
XLA Ops:
  0.0 0.7 broadcast_multiply_fusion
  0.7 0.1 mul.14
  0.8 0.1 copy.9
  0.8 0.7 reshape_reshape.12.gain
  1.6 5.1 %spectra.2 = bf16[4,2,8,48,128]{4,3,2,1,0:T(8,128)(2,1)} custom-call(bf16[20,128,512]{2,1,0:T(8,128)(2,1)} %bitcast.21, s32[20,128]{1,0:T(8,128)} %bitcast.37, s32[1,128]{1,0:T(1,128)} %order.3, bf16[128,512]{1,0:T(8,128)(2,1)} %constant.10.clone.basis, f32[128,1]{1,0:T(8,128)} %reshape_reshape.12.gain), custom_call_target="tpu_custom_call" | custom-call | tf_op jit(solution)/shard_map/spectra/pallas_call | solution.py:56
  6.7 19.1 %all-to-all-start = ((bf16[64,48,128]{2,1,0:T(8,128)(2,1)}), bf16[64,48,128]{2,1,0:T(8,128)(2,1)S(1)}, u32[]{:S(2)}, u32[]{:S(2)}) async-start(bf16[64,48,128]{2,1,0:T(8,128)(2,1)} %bitcast.27), calls=%async_computation | async-start | bytes 1572864 | tf_op jit(solution)/shard_map/all_to_all | solution.py:145
  25.8 4.0 %spectra.3 = bf16[4,2,8,32,128]{4,3,2,1,0:T(8,128)(2,1)} custom-call(bf16[20,128,512]{2,1,0:T(8,128)(2,1)} %bitcast.22, s32[20,128]{1,0:T(8,128)} %bitcast.38, s32[1,128]{1,0:T(1,128)} %order.3, bf16[128,512]{1,0:T(8,128)(2,1)} %constant.10.clone.basis, f32[128,1]{1,0:T(8,128)} %reshape_reshape.12.gain), custom_call_target="tpu_custom_call" | custom-call | tf_op jit(solution)/shard_map/spectra/pallas_call | solution.py:56
  29.8 35.8 %all-to-all-done = bf16[64,48,128]{2,1,0:T(8,128)(2,1)S(1)} async-done(((bf16[64,48,128]{2,1,0:T(8,128)(2,1)}), bf16[64,48,128]{2,1,0:T(8,128)(2,1)S(1)}, u32[]{:S(2)}, u32[]{:S(2)}) %all-to-all-start) | async-done | bytes 786464 | tf_op jit(solution)/shard_map/all_to_all | solution.py:145
  65.6 0.0 copy-start
  65.6 9.4 %all-to-all-start.1 = ((bf16[64,32,128]{2,1,0:T(8,128)(2,1)}), bf16[64,32,128]{2,1,0:T(8,128)(2,1)S(1)}, u32[]{:S(2)}, u32[]{:S(2)}) async-start(bf16[64,32,128]{2,1,0:T(8,128)(2,1)} %bitcast.32), calls=%async_computation.1 | async-start | bytes 1048576 | tf_op jit(solution)/shard_map/all_to_all | solution.py:145
  75.0 3.2 %collective-permute-start.1 = (bf16[4,2,8,48,128]{4,3,2,1,0:T(8,128)(2,1)S(1)}, bf16[4,2,8,48,128]{4,3,2,1,0:T(8,128)(2,1)}, u32[]{:S(2)}, u32[]{:S(2)}) collective-permute-start(bf16[4,2,8,48,128]{4,3,2,1,0:T(8,128)(2,1)S(1)} %bitcast.23), channel_id=1, source_target_pairs={{0,4},{4,8},{8,12},{12,0},{1,5},{5,9},{9,13},{13,1},{2,6},{6,10},{... | collective-permute-start | bytes 2359304 | tf_op jit(solution)/shard_map/ppermute | solution.py:128
  78.2 25.9 %all-to-all-done.1 = bf16[64,32,128]{2,1,0:T(8,128)(2,1)S(1)} async-done(((bf16[64,32,128]{2,1,0:T(8,128)(2,1)}), bf16[64,32,128]{2,1,0:T(8,128)(2,1)S(1)}, u32[]{:S(2)}, u32[]{:S(2)}) %all-to-all-start.1) | async-done | bytes 524320 | tf_op jit(solution)/shard_map/all_to_all | solution.py:145
  104.1 0.0 copy-start.1
  104.1 3.2 %collective-permute-start.7 = (bf16[4,2,8,32,128]{4,3,2,1,0:T(8,128)(2,1)S(1)}, bf16[4,2,8,32,128]{4,3,2,1,0:T(8,128)(2,1)S(1)}, u32[]{:S(2)}, u32[]{:S(2)}) collective-permute-start(bf16[4,2,8,32,128]{4,3,2,1,0:T(8,128)(2,1)S(1)} %bitcast.28), channel_id=1, source_target_pairs={{0,4},{4,8},{8,12},{12,0},{1,5},{5,9},{9,13},{13,1},{2,6},{6,10},{... | collective-permute-start | bytes 1572872 | tf_op jit(solution)/shard_map/ppermute | solution.py:128
  107.3 3.4 %collective-permute-start = (bf16[4,2,8,48,128]{4,3,2,1,0:T(8,128)(2,1)S(1)}, bf16[4,2,8,48,128]{4,3,2,1,0:T(8,128)(2,1)S(1)}, u32[]{:S(2)}, u32[]{:S(2)}) collective-permute-start(bf16[4,2,8,48,128]{4,3,2,1,0:T(8,128)(2,1)S(1)} %bitcast.24), channel_id=1, source_target_pairs={{0,12},{4,0},{8,4},{12,8},{1,13},{5,1},{9,5},{13,9},{2,14},{6,2},{... | collective-permute-start | bytes 2359304 | tf_op jit(solution)/shard_map/ppermute | solution.py:128
  110.7 0.0 collective-permute-done.1
  110.7 1.9 %collective-permute-start.2 = (bf16[4,2,8,48,128]{4,3,2,1,0:T(8,128)(2,1)}, bf16[4,2,8,48,128]{4,3,2,1,0:T(8,128)(2,1)S(1)}, u32[]{:S(2)}, u32[]{:S(2)}) collective-permute-start(bf16[4,2,8,48,128]{4,3,2,1,0:T(8,128)(2,1)} %collective-permute-done.1), channel_id=1, source_target_pairs={{0,4},{4,8},{8,12},{12,0},{1,5},{5,9},{9,13},{13,1},{2,6},{6,10},{... | collective-permute-start | bytes 2359304 | tf_op jit(solution)/shard_map/ppermute | solution.py:128
  112.6 6.3 %collective-permute-start.9 = (bf16[4,2,8,32,128]{4,3,2,1,0:T(8,128)(2,1)S(1)}, bf16[4,2,8,32,128]{4,3,2,1,0:T(8,128)(2,1)S(1)}, u32[]{:S(2)}, u32[]{:S(2)}) collective-permute-start(bf16[4,2,8,32,128]{4,3,2,1,0:T(8,128)(2,1)S(1)} %bitcast.29), channel_id=1, source_target_pairs={{0,1},{1,0},{2,3},{3,2},{4,5},{5,4},{6,7},{7,6},{8,9},{9,8},{10,11... | collective-permute-start | bytes 1572872 | tf_op jit(solution)/shard_map/ppermute | solution.py:128
  118.9 4.5 %collective-permute-start.6 = (bf16[4,2,8,32,128]{4,3,2,1,0:T(8,128)(2,1)S(1)}, bf16[4,2,8,32,128]{4,3,2,1,0:T(8,128)(2,1)}, u32[]{:S(2)}, u32[]{:S(2)}) collective-permute-start(bf16[4,2,8,32,128]{4,3,2,1,0:T(8,128)(2,1)S(1)} %bitcast.30), channel_id=1, source_target_pairs={{0,12},{4,0},{8,4},{12,8},{1,13},{5,1},{9,5},{13,9},{2,14},{6,2},{... | collective-permute-start | bytes 1572872 | tf_op jit(solution)/shard_map/ppermute | solution.py:128
  123.5 0.0 collective-permute-done.7
  123.5 1.9 %collective-permute-start.8 = (bf16[4,2,8,32,128]{4,3,2,1,0:T(8,128)(2,1)S(1)}, bf16[4,2,8,32,128]{4,3,2,1,0:T(8,128)(2,1)}, u32[]{:S(2)}, u32[]{:S(2)}) collective-permute-start(bf16[4,2,8,32,128]{4,3,2,1,0:T(8,128)(2,1)S(1)} %collective-permute-done.7), channel_id=1, source_target_pairs={{0,4},{4,8},{8,12},{12,0},{1,5},{5,9},{9,13},{13,1},{2,6},{6,10},{... | collective-permute-start | bytes 1572872 | tf_op jit(solution)/shard_map/ppermute | solution.py:128
  125.4 0.0 collective-permute-done.9
  125.4 0.0 copy-start.4
  125.4 4.4 %collective-permute-start.3 = (bf16[4,2,8,48,128]{4,3,2,1,0:T(8,128)(2,1)S(1)}, bf16[4,2,8,48,128]{4,3,2,1,0:T(8,128)(2,1)}, u32[]{:S(2)}, u32[]{:S(2)}) collective-permute-start(bf16[4,2,8,48,128]{4,3,2,1,0:T(8,128)(2,1)S(1)} %bitcast.25), channel_id=1, source_target_pairs={{0,1},{1,0},{2,3},{3,2},{4,5},{5,4},{6,7},{7,6},{8,9},{9,8},{10,11... | collective-permute-start | bytes 2359304 | tf_op jit(solution)/shard_map/ppermute | solution.py:128
  129.8 0.0 collective-permute-done
  129.9 0.0 copy-start.2
  129.9 5.6 %collective-permute-start.4 = (bf16[4,2,8,48,128]{4,3,2,1,0:T(8,128)(2,1)S(1)}, bf16[4,2,8,48,128]{4,3,2,1,0:T(8,128)(2,1)}, u32[]{:S(2)}, u32[]{:S(2)}) collective-permute-start(bf16[4,2,8,48,128]{4,3,2,1,0:T(8,128)(2,1)S(1)} %collective-permute-done), channel_id=1, source_target_pairs={{0,1},{1,0},{2,3},{3,2},{4,5},{5,4},{6,7},{7,6},{8,9},{9,8},{10,11... | collective-permute-start | bytes 2359304 | tf_op jit(solution)/shard_map/ppermute | solution.py:128
  135.4 0.0 collective-permute-done.2
  135.5 0.0 copy-start.3
  135.5 8.9 %collective-permute-start.5 = (bf16[4,2,8,48,128]{4,3,2,1,0:T(8,128)(2,1)S(1)}, bf16[4,2,8,48,128]{4,3,2,1,0:T(8,128)(2,1)}, u32[]{:S(2)}, u32[]{:S(2)}) collective-permute-start(bf16[4,2,8,48,128]{4,3,2,1,0:T(8,128)(2,1)S(1)} %collective-permute-done.2), channel_id=1, source_target_pairs={{0,1},{1,0},{2,3},{3,2},{4,5},{5,4},{6,7},{7,6},{8,9},{9,8},{10,11... | collective-permute-start | bytes 2359304 | tf_op jit(solution)/shard_map/ppermute | solution.py:128
  144.4 0.0 collective-permute-done.6
  144.4 1.9 %collective-permute-start.10 = (bf16[4,2,8,32,128]{4,3,2,1,0:T(8,128)(2,1)}, bf16[4,2,8,32,128]{4,3,2,1,0:T(8,128)(2,1)}, u32[]{:S(2)}, u32[]{:S(2)}) collective-permute-start(bf16[4,2,8,32,128]{4,3,2,1,0:T(8,128)(2,1)} %collective-permute-done.6), channel_id=1, source_target_pairs={{0,1},{1,0},{2,3},{3,2},{4,5},{5,4},{6,7},{7,6},{8,9},{9,8},{10,11... | collective-permute-start | bytes 1572872 | tf_op jit(solution)/shard_map/ppermute | solution.py:128
  146.3 0.0 collective-permute-done.8
  146.3 5.4 %collective-permute-start.11 = (bf16[4,2,8,32,128]{4,3,2,1,0:T(8,128)(2,1)}, bf16[4,2,8,32,128]{4,3,2,1,0:T(8,128)(2,1)}, u32[]{:S(2)}, u32[]{:S(2)}) collective-permute-start(bf16[4,2,8,32,128]{4,3,2,1,0:T(8,128)(2,1)} %collective-permute-done.8), channel_id=1, source_target_pairs={{0,1},{1,0},{2,3},{3,2},{4,5},{5,4},{6,7},{7,6},{8,9},{9,8},{10,11... | collective-permute-start | bytes 1572872 | tf_op jit(solution)/shard_map/ppermute | solution.py:128
  151.7 0.6 pad_add_fusion.where
  152.3 0.0 collective-permute-done.10
  152.3 1.3 collective-permute-done.11
  153.6 0.0 collective-permute-done.3
  153.6 0.0 collective-permute-done.4
  153.6 0.0 collective-permute-done.5
  153.6 0.0 copy-done
  153.6 0.0 copy-done.1
  153.6 0.0 copy-done.4
  153.6 0.0 copy-done.2
  153.6 0.0 copy-done.3
  153.6 13.8 %stack.13 = f32[2,2,9,128,128]{4,3,2,1,0:T(8,128)} custom-call(s32[2]{0:T(128)} %pad_add_fusion.where, bf16[4,2,384,128]{3,2,1,0:T(8,128)(2,1)} %bitcast.26, bf16[4,2,384,128]{3,2,1,0:T(8,128)(2,1)} %bitcast.33, bf16[4,2,384,128]{3,2,1,0:T(8,128)(2,1)} %bitcast.34, bf16[4,2,384,128]{3,2,1,0:T(8,128)(2,1)} %bitcast.10.refs_3_, ...), custom_call_target="tpu_custom_call" | custom-call | tf_op jit(solution)/shard_map/stack/pallas_call | solution.py:116
  (1 shorter events, 0.0 us)
Async XLA Ops:
  6.7 58.9 %all-to-all-start = ((bf16[64,48,128]{2,1,0:T(8,128)(2,1)}), bf16[64,48,128]{2,1,0:T(8,128)(2,1)S(1)}, u32[]{:S(2)}, u32[]{:S(2)}) async-start(bf16[64,48,128]{2,1,0:T(8,128)(2,1)} %bitcast.27), calls=%async_computation | async-start | bytes 1572864 | tf_op jit(solution)/shard_map/all_to_all | solution.py:145
  65.6 88.0 %copy-start = (bf16[64,48,128]{2,1,0:T(8,128)(2,1)}, bf16[64,48,128]{2,1,0:T(8,128)(2,1)S(1)}, u32[]{:S(2)}) copy-start(bf16[64,48,128]{2,1,0:T(8,128)(2,1)S(1)} %all-to-all-done) | copy-start | bytes 2359300
  65.6 38.5 %all-to-all-start.1 = ((bf16[64,32,128]{2,1,0:T(8,128)(2,1)}), bf16[64,32,128]{2,1,0:T(8,128)(2,1)S(1)}, u32[]{:S(2)}, u32[]{:S(2)}) async-start(bf16[64,32,128]{2,1,0:T(8,128)(2,1)} %bitcast.32), calls=%async_computation.1 | async-start | bytes 1048576 | tf_op jit(solution)/shard_map/all_to_all | solution.py:145
  75.0 35.7 %collective-permute-start.1 = (bf16[4,2,8,48,128]{4,3,2,1,0:T(8,128)(2,1)S(1)}, bf16[4,2,8,48,128]{4,3,2,1,0:T(8,128)(2,1)}, u32[]{:S(2)}, u32[]{:S(2)}) collective-permute-start(bf16[4,2,8,48,128]{4,3,2,1,0:T(8,128)(2,1)S(1)} %bitcast.23), channel_id=1, source_target_pairs={{0,4},{4,8},{8,12},{12,0},{1,5},{5,9},{9,13},{13,1},{2,6},{6,10},{... | collective-permute-start | bytes 2359304 | tf_op jit(solution)/shard_map/ppermute | solution.py:128
  104.1 49.5 %copy-start.1 = (bf16[64,32,128]{2,1,0:T(8,128)(2,1)}, bf16[64,32,128]{2,1,0:T(8,128)(2,1)S(1)}, u32[]{:S(2)}) copy-start(bf16[64,32,128]{2,1,0:T(8,128)(2,1)S(1)} %all-to-all-done.1) | copy-start | bytes 1572868
  104.1 19.3 %collective-permute-start.7 = (bf16[4,2,8,32,128]{4,3,2,1,0:T(8,128)(2,1)S(1)}, bf16[4,2,8,32,128]{4,3,2,1,0:T(8,128)(2,1)S(1)}, u32[]{:S(2)}, u32[]{:S(2)}) collective-permute-start(bf16[4,2,8,32,128]{4,3,2,1,0:T(8,128)(2,1)S(1)} %bitcast.28), channel_id=1, source_target_pairs={{0,4},{4,8},{8,12},{12,0},{1,5},{5,9},{9,13},{13,1},{2,6},{6,10},{... | collective-permute-start | bytes 1572872 | tf_op jit(solution)/shard_map/ppermute | solution.py:128
  107.3 22.5 %collective-permute-start = (bf16[4,2,8,48,128]{4,3,2,1,0:T(8,128)(2,1)S(1)}, bf16[4,2,8,48,128]{4,3,2,1,0:T(8,128)(2,1)S(1)}, u32[]{:S(2)}, u32[]{:S(2)}) collective-permute-start(bf16[4,2,8,48,128]{4,3,2,1,0:T(8,128)(2,1)S(1)} %bitcast.24), channel_id=1, source_target_pairs={{0,12},{4,0},{8,4},{12,8},{1,13},{5,1},{9,5},{13,9},{2,14},{6,2},{... | collective-permute-start | bytes 2359304 | tf_op jit(solution)/shard_map/ppermute | solution.py:128
  110.7 24.8 %collective-permute-start.2 = (bf16[4,2,8,48,128]{4,3,2,1,0:T(8,128)(2,1)}, bf16[4,2,8,48,128]{4,3,2,1,0:T(8,128)(2,1)S(1)}, u32[]{:S(2)}, u32[]{:S(2)}) collective-permute-start(bf16[4,2,8,48,128]{4,3,2,1,0:T(8,128)(2,1)} %collective-permute-done.1), channel_id=1, source_target_pairs={{0,4},{4,8},{8,12},{12,0},{1,5},{5,9},{9,13},{13,1},{2,6},{6,10},{... | collective-permute-start | bytes 2359304 | tf_op jit(solution)/shard_map/ppermute | solution.py:128
  112.6 12.8 %collective-permute-start.9 = (bf16[4,2,8,32,128]{4,3,2,1,0:T(8,128)(2,1)S(1)}, bf16[4,2,8,32,128]{4,3,2,1,0:T(8,128)(2,1)S(1)}, u32[]{:S(2)}, u32[]{:S(2)}) collective-permute-start(bf16[4,2,8,32,128]{4,3,2,1,0:T(8,128)(2,1)S(1)} %bitcast.29), channel_id=1, source_target_pairs={{0,1},{1,0},{2,3},{3,2},{4,5},{5,4},{6,7},{7,6},{8,9},{9,8},{10,11... | collective-permute-start | bytes 1572872 | tf_op jit(solution)/shard_map/ppermute | solution.py:128
  118.9 25.5 %collective-permute-start.6 = (bf16[4,2,8,32,128]{4,3,2,1,0:T(8,128)(2,1)S(1)}, bf16[4,2,8,32,128]{4,3,2,1,0:T(8,128)(2,1)}, u32[]{:S(2)}, u32[]{:S(2)}) collective-permute-start(bf16[4,2,8,32,128]{4,3,2,1,0:T(8,128)(2,1)S(1)} %bitcast.30), channel_id=1, source_target_pairs={{0,12},{4,0},{8,4},{12,8},{1,13},{5,1},{9,5},{13,9},{2,14},{6,2},{... | collective-permute-start | bytes 1572872 | tf_op jit(solution)/shard_map/ppermute | solution.py:128
  123.5 22.9 %collective-permute-start.8 = (bf16[4,2,8,32,128]{4,3,2,1,0:T(8,128)(2,1)S(1)}, bf16[4,2,8,32,128]{4,3,2,1,0:T(8,128)(2,1)}, u32[]{:S(2)}, u32[]{:S(2)}) collective-permute-start(bf16[4,2,8,32,128]{4,3,2,1,0:T(8,128)(2,1)S(1)} %collective-permute-done.7), channel_id=1, source_target_pairs={{0,4},{4,8},{8,12},{12,0},{1,5},{5,9},{9,13},{13,1},{2,6},{6,10},{... | collective-permute-start | bytes 1572872 | tf_op jit(solution)/shard_map/ppermute | solution.py:128
  125.4 28.2 %copy-start.4 = (bf16[4,2,8,32,128]{4,3,2,1,0:T(8,128)(2,1)}, bf16[4,2,8,32,128]{4,3,2,1,0:T(8,128)(2,1)S(1)}, u32[]{:S(2)}) copy-start(bf16[4,2,8,32,128]{4,3,2,1,0:T(8,128)(2,1)S(1)} %collective-permute-done.9) | copy-start | bytes 1572868
  125.4 28.2 %collective-permute-start.3 = (bf16[4,2,8,48,128]{4,3,2,1,0:T(8,128)(2,1)S(1)}, bf16[4,2,8,48,128]{4,3,2,1,0:T(8,128)(2,1)}, u32[]{:S(2)}, u32[]{:S(2)}) collective-permute-start(bf16[4,2,8,48,128]{4,3,2,1,0:T(8,128)(2,1)S(1)} %bitcast.25), channel_id=1, source_target_pairs={{0,1},{1,0},{2,3},{3,2},{4,5},{5,4},{6,7},{7,6},{8,9},{9,8},{10,11... | collective-permute-start | bytes 2359304 | tf_op jit(solution)/shard_map/ppermute | solution.py:128
  129.9 23.8 %copy-start.2 = (bf16[4,2,8,48,128]{4,3,2,1,0:T(8,128)(2,1)}, bf16[4,2,8,48,128]{4,3,2,1,0:T(8,128)(2,1)S(1)}, u32[]{:S(2)}) copy-start(bf16[4,2,8,48,128]{4,3,2,1,0:T(8,128)(2,1)S(1)} %collective-permute-done) | copy-start | bytes 2359300
  129.9 23.7 %collective-permute-start.4 = (bf16[4,2,8,48,128]{4,3,2,1,0:T(8,128)(2,1)S(1)}, bf16[4,2,8,48,128]{4,3,2,1,0:T(8,128)(2,1)}, u32[]{:S(2)}, u32[]{:S(2)}) collective-permute-start(bf16[4,2,8,48,128]{4,3,2,1,0:T(8,128)(2,1)S(1)} %collective-permute-done), channel_id=1, source_target_pairs={{0,1},{1,0},{2,3},{3,2},{4,5},{5,4},{6,7},{7,6},{8,9},{9,8},{10,11... | collective-permute-start | bytes 2359304 | tf_op jit(solution)/shard_map/ppermute | solution.py:128
  135.5 18.2 %copy-start.3 = (bf16[4,2,8,48,128]{4,3,2,1,0:T(8,128)(2,1)}, bf16[4,2,8,48,128]{4,3,2,1,0:T(8,128)(2,1)S(1)}, u32[]{:S(2)}) copy-start(bf16[4,2,8,48,128]{4,3,2,1,0:T(8,128)(2,1)S(1)} %collective-permute-done.2) | copy-start | bytes 2359300
  135.5 18.1 %collective-permute-start.5 = (bf16[4,2,8,48,128]{4,3,2,1,0:T(8,128)(2,1)S(1)}, bf16[4,2,8,48,128]{4,3,2,1,0:T(8,128)(2,1)}, u32[]{:S(2)}, u32[]{:S(2)}) collective-permute-start(bf16[4,2,8,48,128]{4,3,2,1,0:T(8,128)(2,1)S(1)} %collective-permute-done.2), channel_id=1, source_target_pairs={{0,1},{1,0},{2,3},{3,2},{4,5},{5,4},{6,7},{7,6},{8,9},{9,8},{10,11... | collective-permute-start | bytes 2359304 | tf_op jit(solution)/shard_map/ppermute | solution.py:128
  144.4 7.9 %collective-permute-start.10 = (bf16[4,2,8,32,128]{4,3,2,1,0:T(8,128)(2,1)}, bf16[4,2,8,32,128]{4,3,2,1,0:T(8,128)(2,1)}, u32[]{:S(2)}, u32[]{:S(2)}) collective-permute-start(bf16[4,2,8,32,128]{4,3,2,1,0:T(8,128)(2,1)} %collective-permute-done.6), channel_id=1, source_target_pairs={{0,1},{1,0},{2,3},{3,2},{4,5},{5,4},{6,7},{7,6},{8,9},{9,8},{10,11... | collective-permute-start | bytes 1572872 | tf_op jit(solution)/shard_map/ppermute | solution.py:128
  146.3 7.2 %collective-permute-start.11 = (bf16[4,2,8,32,128]{4,3,2,1,0:T(8,128)(2,1)}, bf16[4,2,8,32,128]{4,3,2,1,0:T(8,128)(2,1)}, u32[]{:S(2)}, u32[]{:S(2)}) collective-permute-start(bf16[4,2,8,32,128]{4,3,2,1,0:T(8,128)(2,1)} %collective-permute-done.8), channel_id=1, source_target_pairs={{0,1},{1,0},{2,3},{3,2},{4,5},{5,4},{6,7},{7,6},{8,9},{9,8},{10,11... | collective-permute-start | bytes 1572872 | tf_op jit(solution)/shard_map/ppermute | solution.py:128

commit v2 on v1

v2 whole, which is shorter than its diff:
```python
import functools
import math

import jax
import jax.numpy as jnp
import numpy as np
from jax import lax
from jax.experimental import pallas as pl
from jax.experimental.pallas import tpu as pltpu
from jax.sharding import Mesh
from jax.sharding import PartitionSpec as P

CH = 128
NT = 512
BIN0 = 8
GROUP = 2
CHUNKS = (14, 6)
NOFF = 9
VMEM = pltpu.CompilerParams(vmem_limit_bytes=48 * 1024 * 1024)


def basis_rows(groups):
    t = np.arange(NT)
    bins = BIN0 + np.arange(2 * groups)
    phase = (t[:, None] * bins[None, :] % NT).astype(np.float32)
    angles = np.float32(2.0 * math.pi / NT) * phase
    taper = np.float32(0.5) - np.float32(0.5) * np.cos(np.float32(2.0 * math.pi / NT) * t.astype(np.float32))
    table = np.stack([taper[:, None] * np.cos(angles), -taper[:, None] * np.sin(angles)], axis=2)
    table = table.reshape(NT, groups, 4).transpose(2, 1, 0).reshape(4 * groups, NT)
    return jnp.asarray(table.astype(jnp.bfloat16))


def spectra_body(strain, live, order, basis, whiten, out, place, *, first, groups, rows):
    step = pl.program_id(0)
    channel = lax.broadcasted_iota(jnp.int32, (CH, CH), 0)
    pick = (channel == order[...]).astype(jnp.float32).astype(jnp.bfloat16)
    shape = (4 * groups, 2 * groups)
    row = lax.broadcasted_iota(jnp.int32, shape, 0)
    column = lax.broadcasted_iota(jnp.int32, shape, 1)
    spread = jnp.where(column == 2 * (row % groups) + row // (2 * groups), whiten[...], 0.0)
    gain = jnp.sum(spread, axis=1, keepdims=True) * (2.0 / math.sqrt(NT))
    for w in range(GROUP):
        at = step * GROUP + w
        value = strain[w].astype(jnp.float32)
        centered = value - jnp.sum(value, axis=1, keepdims=True) * (1.0 / NT)
        power = jnp.sum(centered * centered, axis=1, keepdims=True) * (1.0 / NT)
        normed = (centered * lax.rsqrt(power + 1e-06)).astype(jnp.bfloat16)
        spec = lax.dot_general(basis[...], normed, (((1,), (1,)), ((), ())), preferred_element_type=jnp.float32)
        weight = live[pl.ds(first + at, 1), :].astype(jnp.float32)
        spec = (spec * gain * weight).astype(jnp.bfloat16)
        spec = jnp.dot(spec, pick, preferred_element_type=jnp.float32)
        for part in range(4):
            place[pl.ds(at * 4 + part, groups, stride=rows), :] = spec[part * groups : (part + 1) * groups]

    @pl.when(step == pl.num_programs(0) - 1)
    def _():
        for x in range(4):
            size = groups * rows // 4
            packed = place[x * size : (x + 1) * size].astype(jnp.bfloat16)
            out[x, 0] = packed
            out[x, 1] = packed


def spectra(strain, live, order, basis, whiten, first, count):
    groups = basis.shape[0] // 4
    base = first // GROUP
    rows = 4 * count
    shape = (4, 2, groups * rows // 4, CH)
    whole = lambda v: pl.BlockSpec(v.shape, lambda i: (0,) * v.ndim)
    return pl.pallas_call(
        functools.partial(spectra_body, first=first, groups=groups, rows=rows),
        grid=(count // GROUP,),
        in_specs=[
            pl.BlockSpec((GROUP, CH, NT), lambda i: (base + i, 0, 0)),
            whole(live),
            whole(order),
            whole(basis),
            whole(whiten),
        ],
        out_specs=pl.BlockSpec(shape, lambda i: (0, 0, 0, 0)),
        out_shape=jax.ShapeDtypeStruct(shape, jnp.bfloat16),
        scratch_shapes=[pltpu.VMEM((groups * rows, CH), jnp.float32)],
        compiler_params=VMEM,
        name="spectra",
    )(strain, live, order, basis, whiten)


def left_body(where, data, out):
    own = data[:, where[0]]
    own = own.reshape(-1, CH).astype(jnp.float32)
    own = own.reshape(-1, 8, CH)
    part = lax.broadcasted_iota(jnp.int32, own.shape, 1)
    turned = jnp.where(part % 2 == 0, pltpu.roll(own, 7, 1), -pltpu.roll(own, 1, 1))
    own = own.reshape(-1, CH).T
    turned = turned.reshape(-1, CH).T
    first = lax.broadcasted_iota(jnp.int32, own.shape, 1) % 4 < 2
    zero = jnp.zeros_like(own)
    out[0 * CH : 1 * CH] = jnp.where(first, own, zero).astype(jnp.bfloat16)
    out[1 * CH : 2 * CH] = jnp.where(first, turned, zero).astype(jnp.bfloat16)
    out[2 * CH : 3 * CH] = jnp.where(first, zero, own).astype(jnp.bfloat16)
    out[3 * CH : 4 * CH] = jnp.where(first, zero, turned).astype(jnp.bfloat16)


def left_of(where, data):
    whole = pl.BlockSpec(memory_space=pltpu.VMEM)
    return pl.pallas_call(
        left_body,
        in_specs=[pl.BlockSpec(memory_space=pltpu.SMEM), whole],
        out_specs=whole,
        out_shape=jax.ShapeDtypeStruct((4 * CH, data.shape[0] * data.shape[2]), jnp.bfloat16),
        compiler_params=VMEM,
        name="left",
    )(where, data)


def product(left, ref):
    right = jnp.concatenate([ref[:, 0].reshape(-1, CH), ref[:, 1].reshape(-1, CH)], axis=1)
    return jnp.dot(left[...], right, preferred_element_type=jnp.float32)


def early_body(left, *refs):
    data, out = refs[:-1], refs[-1]
    for i, ref in enumerate(data):
        out[i] = product(left, ref)


def early(left, data):
    whole = pl.BlockSpec(memory_space=pltpu.VMEM)
    return pl.pallas_call(
        early_body,
        in_specs=[whole] * (1 + len(data)),
        out_specs=whole,
        out_shape=jax.ShapeDtypeStruct((len(data), 4 * CH, 2 * CH), jnp.float32),
        compiler_params=VMEM,
        name="early",
    )(left, *data)


def late_body(where, left, begun, one, two, *refs, ahead, scale):
    out, stage, done = refs[-3:]
    half, core = where[0], where[1]
    jobs = []
    for other, ref in enumerate((one, two)):
        total = (begun[other] + product(left, ref)) * scale
        for side in range(2):
            spot = 2 * other + side
            for part in range(4):
                row = part * CH
                stage[spot, part // 2, part % 2] = total[row : row + CH, side * CH : (side + 1) * CH]
            offset = 4 * ahead + 2 * (side - half) + other * (1 - 2 * core)
            valid = jnp.logical_and(offset >= 0, offset < NOFF)
            target = jnp.clip(offset, 0, NOFF - 1)
            copy = pltpu.make_async_copy(stage.at[spot], out.at[:, :, target], done.at[spot])
            jobs.append((valid, copy))
            pl.when(valid)(copy.start)
    for valid, copy in jobs:
        pl.when(valid)(copy.wait)


def late(where, left, begun, one, two, filled, ahead, scale):
    whole = pl.BlockSpec(memory_space=pltpu.VMEM)
    somewhere = pl.BlockSpec(memory_space=pl.ANY)
    extra = [] if filled is None else [filled]
    return pl.pallas_call(
        functools.partial(late_body, ahead=ahead, scale=scale),
        grid=(1,),
        in_specs=[
            pl.BlockSpec(memory_space=pltpu.SMEM),
            whole,
            pl.BlockSpec((2, 4 * CH, 2 * CH), lambda i: (ahead, 0, 0)),
            whole,
            whole,
        ]
        + [somewhere] * len(extra),
        out_specs=somewhere,
        out_shape=jax.ShapeDtypeStruct((2, 2, NOFF, CH, CH), jnp.float32),
        input_output_aliases={5: 0} if extra else {},
        scratch_shapes=[pltpu.VMEM((4, 2, 2, CH, CH), jnp.float32), pltpu.SemaphoreType.DMA((4,))],
        compiler_params=VMEM,
        name="late",
    )(where, left, begun, one, two, *extra)


def shifted(value, axis, steps):
    count = lax.axis_size(axis)
    return lax.ppermute(value, axis, [(s, (s + steps) % count) for s in range(count)])


def upper(value, steps):
    count = lax.axis_size("y")
    pairs = [(2 * y + 1, 2 * ((y + steps) % count) + 1) for y in range(count)]
    return lax.ppermute(value, ("y", "z_hi"), pairs)


def neighbours(here):
    ahead1 = shifted(here, "y", -1)
    ahead2 = jnp.stack([shifted(shifted(here[:, 0], "y", 1), "y", 1), upper(here[:, 1], 2)], axis=1)
    own = [here, ahead1, ahead2]
    return [w for v in own for w in (v, shifted(v, "core", 1))]


def local(strain, fiber_order, window_valid, whiten):
    groups = whiten.shape[0] // 2
    windows = strain.shape[1]
    strain = jnp.transpose(strain, (1, 0, 2))
    live = jnp.transpose(window_valid)
    basis = basis_rows(groups)
    where = jnp.stack([lax.axis_index("z_hi"), lax.axis_index("core")]).astype(jnp.int32)
    scale = 1.0 / math.sqrt(windows * lax.axis_size("x") * lax.axis_size("z_lo"))

    def made(first, count):
        sent = spectra(strain, live, fiber_order, basis, whiten.reshape(1, -1), first, count)
        return sent.reshape(2 * groups, 4 * count, CH)

    def spread(sent):
        here = lax.all_to_all(sent, ("x", "z_hi", "z_lo"), 0, 0, tiled=True)
        return here.reshape(4, 2, -1, CH)

    first, second = spread(made(0, CHUNKS[0])), made(*CHUNKS)
    first, second = lax.optimization_barrier((first, second))
    head = neighbours(first)
    tail = spread(second)
    tail, *head = lax.optimization_barrier((tail, *head))
    rest = neighbours(tail)
    begun = early(left_of(where, head[0]), head)
    left = left_of(where, tail)
    filled = None
    for ahead in range(3):
        one, two = rest[2 * ahead : 2 * ahead + 2]
        filled = late(where, left, begun, one, two, filled, ahead, scale)
    return filled


def solution(mesh):
    fine = Mesh(mesh.devices.reshape(4, 8, 4, 2, 2), ("x", "z_lo", "y", "z_hi", "core"))
    freq, chan = ("x", "z_lo"), ("y", "z_hi", "core")
    in_specs = (P(chan, freq, None), P(chan, None), P(chan, freq), P())
    out_specs = P(freq, None, None, chan, None)
    return jax.shard_map(local, mesh=fine, in_specs=in_specs, out_specs=out_specs, check_vma=False)
```

time: 169 us -> 164 us (0.970)
  local copies, waits for them, and re-layouts: 0.93 us -> 12 us
  starting transfers between devices: 79.2 us -> 69.9 us
  waiting for transfers between devices: 63 us -> 55.2 us
    all_to_all x2, waiting for transfers between devices: 61.7 us -> 42.4 us  [spread(): here = lax.all_to_all(sent, ('x', 'z_hi', 'z_lo'), 0, 0, tiled=True)]
    unnamed x10 -> x34, local copies, waits for them, and re-layouts: 0.02 us -> 11.9 us
    ppermute x12, waiting for transfers between devices: 1.32 us -> 12.8 us  [shifted(): lax.ppermute(value, axis, [(s, (s + steps) % count) for s in range(count)])]
    ppermute x12, starting transfers between devices: 50.6 us -> 40 us  [shifted(): lax.ppermute(value, axis, [(s, (s + steps) % count) for s in range(count)])]
    pallas_call x1 -> x6, Pallas kernels: 13.8 us -> 16.2 us  [the longest x3 7.82 us: late(): pl.pallas_call(functools.partial(late_body, ahead=ahead, scale=scale), gr...]
    pallas_call x2, Pallas kernels: 9.05 us -> 7.24 us  [spectra(): pl.pallas_call(functools.partial(spectra_body, first=first, groups=groups...]
  transfers between devices with their start and end apart: 14 -> 16, of which waited for: 3 -> 5; matrix products, arithmetic and copies ran while one was open for 0% -> 0% of each run, Pallas kernels for 2% -> 10%
where the time goes in v2:
time: 164 us; the launch traced here: 161 us
  starting transfers between devices  69.9 us (43%)
  waiting for transfers between devices  55.2 us (34%)
  Pallas kernels  23.4 us (14%)
  local copies, waits for them, and re-layouts  12 us (7%)
    all_to_all x2, waiting for transfers between devices, spread(): here = lax.all_to_all(sent, ('x', 'z_hi', 'z_lo'), 0, 0, tiled=True)  42.4 us
    ppermute x12, starting transfers between devices, shifted(): lax.ppermute(value, axis, [(s, (s + steps) % count) for s in range(count)])  40 us
    all_to_all x2, starting transfers between devices, spread(): here = lax.all_to_all(sent, ('x', 'z_hi', 'z_lo'), 0, 0, tiled=True)  28.5 us
    ppermute x12, waiting for transfers between devices, shifted(): lax.ppermute(value, axis, [(s, (s + steps) % count) for s in range(count)])  12.8 us
    unnamed x34, local copies, waits for them, and re-layouts  11.9 us
    pallas_call x3, Pallas kernels, late(): pl.pallas_call(functools.partial(late_body, ahead=ahead, scale=scale), gr...  7.82 us
    pallas_call x2, Pallas kernels, spectra(): pl.pallas_call(functools.partial(spectra_body, first=first, groups=groups...  7.24 us
    pallas_call x1, Pallas kernels, early(): pl.pallas_call(early_body, in_specs=[whole] * (1 + len(data)), out_specs=...  6.65 us
  transfers between devices with their start and end apart: 16, of which 5 were waited for; matrix products, arithmetic and copies ran while one was open for 0% of the time, Pallas kernels for 10%

profile of v2, /device:TPU:1, one launch (start us, length us, event | category | flops | bytes accessed | tf_op | source)
XLA Modules:
  0.0 161.0 jit_solution(9480662515355588824)
XLA Ops:
  0.0 1.7 %copy-done.2 = bf16[128,20,512]{2,0,1:T(8,128)(2,1)S(1)} copy-done((bf16[128,20,512]{2,0,1:T(8,128)(2,1)S(1)}, bf16[128,20,512]{2,0,1:T(8,128)(2,1)}, u32[]{:S(2)}) %copy-start.2) | copy-done | bytes 2621464
  1.7 0.9 copy-done.9
  2.6 0.7 copy-done.11
  3.4 0.7 copy-done.13
  4.0 0.7 copy-done.15
  4.7 5.1 %spectra.2 = bf16[4,2,448,128]{3,2,1,0:T(8,128)(2,1)S(1)} custom-call(bf16[20,128,512]{2,1,0:T(8,128)(2,1)S(1)} %bitcast.26, s32[20,128]{1,0:T(8,128)S(1)} %bitcast.35, s32[1,128]{1,0:T(1,128)S(1)} %copy-done.13, bf16[128,512]{1,0:T(8,128)(2,1)S(1)} %copy-done.9, f32[1,64]{1,0:T(1,128)S(1)} %bitcast.37), custom_call_target="tpu_custom_call" | custom-call | tf_op jit(solution)/shard_map/spectra/pallas_call | solution.py:70
  9.7 0.0 copy-start.5
  9.8 0.9 copy-done.5
  10.7 19.1 %all-to-all-start = ((bf16[64,56,128]{2,1,0:T(8,128)(2,1)}), bf16[64,56,128]{2,1,0:T(8,128)(2,1)S(1)}, u32[]{:S(2)}, u32[]{:S(2)}) async-start(bf16[64,56,128]{2,1,0:T(8,128)(2,1)} %bitcast.33), calls=%async_computation | async-start | bytes 1835008 | tf_op jit(solution)/shard_map/all_to_all | solution.py:216
  29.8 0.0 copy-start.10
  29.8 0.9 copy-done.10
  30.7 0.7 copy-done.16
  31.4 2.2 %spectra.3 = bf16[4,2,192,128]{3,2,1,0:T(8,128)(2,1)S(1)} custom-call(bf16[20,128,512]{2,1,0:T(8,128)(2,1)S(1)} %bitcast.27, s32[20,128]{1,0:T(8,128)S(1)} %bitcast.36, s32[1,128]{1,0:T(1,128)S(1)} %copy-done.14, bf16[128,512]{1,0:T(8,128)(2,1)S(1)} %copy-done.10, f32[1,64]{1,0:T(1,128)S(1)} %bitcast.38), custom_call_target="tpu_custom_call" | custom-call | tf_op jit(solution)/shard_map/spectra/pallas_call | solution.py:70
  33.6 0.7 copy-done.6
  34.3 41.0 %all-to-all-done = bf16[64,56,128]{2,1,0:T(8,128)(2,1)S(1)} async-done(((bf16[64,56,128]{2,1,0:T(8,128)(2,1)}), bf16[64,56,128]{2,1,0:T(8,128)(2,1)S(1)}, u32[]{:S(2)}, u32[]{:S(2)}) %all-to-all-start) | async-done | bytes 917536 | tf_op jit(solution)/shard_map/all_to_all | solution.py:216
  75.3 0.1 slice_bitcast_fusion.1
  75.3 3.2 %collective-permute-start.3 = (bf16[4,448,128]{2,1,0:T(8,128)(2,1)S(1)}, bf16[4,448,128]{2,1,0:T(8,128)(2,1)}, u32[]{:S(2)}, u32[]{:S(2)}) collective-permute-start(bf16[4,448,128]{2,1,0:T(8,128)(2,1)S(1)} %get-tuple-element.23), channel_id=1, source_target_pairs={{0,4},{4,8},{8,12},{12,0},{1,5},{5,9},{9,13},{13,1},{2,6},{6,10},{... | collective-permute-start | bytes 1376264 | tf_op jit(solution)/shard_map/ppermute | solution.py:186
  78.5 3.4 %collective-permute-start.1 = (bf16[4,2,448,128]{3,2,1,0:T(8,128)(2,1)S(1)}, bf16[4,2,448,128]{3,2,1,0:T(8,128)(2,1)S(1)}, u32[]{:S(2)}, u32[]{:S(2)}) collective-permute-start(bf16[4,2,448,128]{3,2,1,0:T(8,128)(2,1)S(1)} %bitcast.22), channel_id=1, source_target_pairs={{0,12},{4,0},{8,4},{12,8},{1,13},{5,1},{9,5},{13,9},{2,14},{6,2},{... | collective-permute-start | bytes 2752520 | tf_op jit(solution)/shard_map/ppermute | solution.py:186
  81.9 9.4 %all-to-all-start.1 = ((bf16[64,24,128]{2,1,0:T(8,128)(2,1)}), bf16[64,24,128]{2,1,0:T(8,128)(2,1)S(1)}, u32[]{:S(2)}, u32[]{:S(2)}) async-start(bf16[64,24,128]{2,1,0:T(8,128)(2,1)} %bitcast.34), calls=%async_computation.1 | async-start | bytes 786432 | tf_op jit(solution)/shard_map/all_to_all | solution.py:216
  91.3 0.7 collective-permute-start.5
  92.0 0.0 collective-permute-done.3
  92.0 1.9 %collective-permute-start.4 = (bf16[4,448,128]{2,1,0:T(8,128)(2,1)}, bf16[4,448,128]{2,1,0:T(8,128)(2,1)S(1)}, u32[]{:S(2)}, u32[]{:S(2)}) collective-permute-start(bf16[4,448,128]{2,1,0:T(8,128)(2,1)} %collective-permute-done.3), channel_id=1, source_target_pairs={{0,4},{4,8},{8,12},{12,0},{1,5},{5,9},{9,13},{13,1},{2,6},{6,10},{... | collective-permute-start | bytes 1376264 | tf_op jit(solution)/shard_map/ppermute | solution.py:186
  93.9 3.9 %collective-permute-start = (bf16[4,2,448,128]{3,2,1,0:T(8,128)(2,1)S(1)}, bf16[4,2,448,128]{3,2,1,0:T(8,128)(2,1)S(1)}, u32[]{:S(2)}, u32[]{:S(2)}) collective-permute-start(bf16[4,2,448,128]{3,2,1,0:T(8,128)(2,1)S(1)} %bitcast.23), channel_id=1, source_target_pairs={{0,1},{1,0},{2,3},{3,2},{4,5},{5,4},{6,7},{7,6},{8,9},{9,8},{10,11... | collective-permute-start | bytes 2752520 | tf_op jit(solution)/shard_map/ppermute | solution.py:186
  97.8 7.9 %collective-permute-done.4 = bf16[4,448,128]{2,1,0:T(8,128)(2,1)S(1)} collective-permute-done((bf16[4,448,128]{2,1,0:T(8,128)(2,1)}, bf16[4,448,128]{2,1,0:T(8,128)(2,1)S(1)}, u32[]{:S(2)}, u32[]{:S(2)}) %collective-permute-start.4) | collective-permute-done | bytes 458784 | tf_op jit(solution)/shard_map/ppermute | solution.py:186
  105.7 0.1 pad_maximum_fusion.refs_4_
  105.8 4.5 %collective-permute-start.6 = (bf16[4,2,448,128]{3,2,1,0:T(8,128)(2,1)S(1)}, bf16[4,2,448,128]{3,2,1,0:T(8,128)(2,1)}, u32[]{:S(2)}, u32[]{:S(2)}) collective-permute-start(bf16[4,2,448,128]{3,2,1,0:T(8,128)(2,1)S(1)} %pad_maximum_fusion.refs_4_), channel_id=1, source_target_pairs={{0,1},{1,0},{2,3},{3,2},{4,5},{5,4},{6,7},{7,6},{8,9},{9,8},{10,11... | collective-permute-start | bytes 2752520 | tf_op jit(solution)/shard_map/ppermute | solution.py:186
  110.3 1.9 %collective-permute-start.2 = (bf16[4,2,448,128]{3,2,1,0:T(8,128)(2,1)S(1)}, bf16[4,2,448,128]{3,2,1,0:T(8,128)(2,1)}, u32[]{:S(2)}, u32[]{:S(2)}) collective-permute-start(bf16[4,2,448,128]{3,2,1,0:T(8,128)(2,1)S(1)} %collective-permute-done.1.refs_2_), channel_id=1, source_target_pairs={{0,1},{1,0},{2,3},{3,2},{4,5},{5,4},{6,7},{7,6},{8,9},{9,8},{10,11... | collective-permute-start | bytes 2752520 | tf_op jit(solution)/shard_map/ppermute | solution.py:186
  112.2 0.9 copy-done.7
  113.1 1.4 all-to-all-done.1
  114.6 0.2 collective-permute-done.2.refs_3_
  114.8 3.0 %collective-permute-start.11 = (bf16[4,2,192,128]{3,2,1,0:T(8,128)(2,1)S(1)}, bf16[4,2,192,128]{3,2,1,0:T(8,128)(2,1)}, u32[]{:S(2)}, u32[]{:S(2)}) collective-permute-start(bf16[4,2,192,128]{3,2,1,0:T(8,128)(2,1)S(1)} %bitcast.28), channel_id=1, source_target_pairs={{0,12},{4,0},{8,4},{12,8},{1,13},{5,1},{9,5},{13,9},{2,14},{6,2},{... | collective-permute-start | bytes 1179656 | tf_op jit(solution)/shard_map/ppermute | solution.py:186
  117.8 2.2 %collective-permute-start.7 = (bf16[4,192,128]{2,1,0:T(8,128)(2,1)S(1)}, bf16[4,192,128]{2,1,0:T(8,128)(2,1)S(1)}, u32[]{:S(2)}, u32[]{:S(2)}) collective-permute-start(bf16[4,192,128]{2,1,0:T(8,128)(2,1)S(1)} %get-tuple-element.25), channel_id=1, source_target_pairs={{0,4},{4,8},{8,12},{12,0},{1,5},{5,9},{9,13},{13,1},{2,6},{6,10},{... | collective-permute-start | bytes 589832 | tf_op jit(solution)/shard_map/ppermute | solution.py:186
  120.1 0.7 collective-permute-start.9
  120.8 4.7 %collective-permute-done.7 = bf16[4,192,128]{2,1,0:T(8,128)(2,1)S(1)} collective-permute-done((bf16[4,192,128]{2,1,0:T(8,128)(2,1)S(1)}, bf16[4,192,128]{2,1,0:T(8,128)(2,1)S(1)}, u32[]{:S(2)}, u32[]{:S(2)}) %collective-permute-start.7) | collective-permute-done | bytes 196640 | tf_op jit(solution)/shard_map/ppermute | solution.py:186
  125.5 1.9 %collective-permute-start.8 = (bf16[4,192,128]{2,1,0:T(8,128)(2,1)S(1)}, bf16[4,192,128]{2,1,0:T(8,128)(2,1)S(1)}, u32[]{:S(2)}, u32[]{:S(2)}) collective-permute-start(bf16[4,192,128]{2,1,0:T(8,128)(2,1)S(1)} %collective-permute-done.7), channel_id=1, source_target_pairs={{0,4},{4,8},{8,12},{12,0},{1,5},{5,9},{9,13},{13,1},{2,6},{6,10},{... | collective-permute-start | bytes 589832 | tf_op jit(solution)/shard_map/ppermute | solution.py:186
  127.4 7.3 %collective-permute-start.13 = (bf16[4,2,192,128]{3,2,1,0:T(8,128)(2,1)S(1)}, bf16[4,2,192,128]{3,2,1,0:T(8,128)(2,1)}, u32[]{:S(2)}, u32[]{:S(2)}) collective-permute-start(bf16[4,2,192,128]{3,2,1,0:T(8,128)(2,1)S(1)} %bitcast.30), channel_id=1, source_target_pairs={{0,1},{1,0},{2,3},{3,2},{4,5},{5,4},{6,7},{7,6},{8,9},{9,8},{10,11... | collective-permute-start | bytes 1179656 | tf_op jit(solution)/shard_map/ppermute | solution.py:186
  134.7 1.9 %collective-permute-start.12 = (bf16[4,2,192,128]{3,2,1,0:T(8,128)(2,1)}, bf16[4,2,192,128]{3,2,1,0:T(8,128)(2,1)}, u32[]{:S(2)}, u32[]{:S(2)}) collective-permute-start(bf16[4,2,192,128]{3,2,1,0:T(8,128)(2,1)} %collective-permute-done.11.one), channel_id=1, source_target_pairs={{0,1},{1,0},{2,3},{3,2},{4,5},{5,4},{6,7},{7,6},{8,9},{9,8},{10,11... | collective-permute-start | bytes 1179656 | tf_op jit(solution)/shard_map/ppermute | solution.py:186
  136.7 4.9 %collective-permute-start.10 = (bf16[4,2,192,128]{3,2,1,0:T(8,128)(2,1)S(1)}, bf16[4,2,192,128]{3,2,1,0:T(8,128)(2,1)}, u32[]{:S(2)}, u32[]{:S(2)}) collective-permute-start(bf16[4,2,192,128]{3,2,1,0:T(8,128)(2,1)S(1)} %pad_maximum_fusion.1.one), channel_id=1, source_target_pairs={{0,1},{1,0},{2,3},{3,2},{4,5},{5,4},{6,7},{7,6},{8,9},{9,8},{10,11... | collective-permute-start | bytes 1179656 | tf_op jit(solution)/shard_map/ppermute | solution.py:186
  141.6 0.1 pad_add_fusion.where
  141.7 0.7 left.2
  142.4 1.0 left.3
  143.4 0.0 copy-start.4
  143.4 1.2 copy-done.4
  144.6 6.6 %early.1.begun = f32[6,512,256]{2,1,0:T(8,128)} custom-call(bf16[512,1792]{1,0:T(8,128)(2,1)} %copy-done.4, bf16[4,2,448,128]{3,2,1,0:T(8,128)(2,1)S(1)} %bitcast.25, bf16[4,2,448,128]{3,2,1,0:T(8,128)(2,1)S(1)} %copy-done.8, bf16[4,2,448,128]{3,2,1,0:T(8,128)(2,1)S(1)} %collective-permute-done.1.refs_2_, ...), custom_call_target="tpu_custom_call" | custom-call | tf_op jit(solution)/shard_map/early/pallas_call | solution.py:129
  151.3 1.9 %copy-done = f32[6,512,256]{2,1,0:T(8,128)S(1)} copy-done((f32[6,512,256]{2,1,0:T(8,128)S(1)}, f32[6,512,256]{2,1,0:T(8,128)}, u32[]{:S(2)}) %copy-start) | copy-done | bytes 3145752
  153.2 2.7 %late.3.refs_0_ = f32[2,2,9,128,128]{4,3,2,1,0:T(8,128)} custom-call(s32[2]{0:T(128)S(1)} %pad_add_fusion.where, bf16[512,768]{1,0:T(8,128)(2,1)S(1)} %left.2, f32[6,512,256]{2,1,0:T(8,128)S(1)} %copy-done, bf16[4,2,192,128]{3,2,1,0:T(8,128)(2,1)S(1)} %bitcast.32, bf16[4,2,192,128]{3,2,1,0:T(8,128)(2,1)} %collective-permute-done.13.two), custom_call_target="tpu_custom_call" | custom-call | tf_op jit(solution)/shard_map/late/pallas_call | solution.py:164
  155.9 2.7 %late.4.refs_0_ = f32[2,2,9,128,128]{4,3,2,1,0:T(8,128)} custom-call(s32[2]{0:T(128)S(1)} %pad_add_fusion.where, bf16[512,768]{1,0:T(8,128)(2,1)S(1)} %left.2, f32[6,512,256]{2,1,0:T(8,128)S(1)} %copy-done.1, bf16[4,2,192,128]{3,2,1,0:T(8,128)(2,1)} %collective-permute-done.11.one, ...), custom_call_target="tpu_custom_call", output_to_operand_aliasing={{}: (5, {})} | custom-call | tf_op jit(solution)/shard_map/late/pallas_call | solution.py:164
  158.6 2.4 %late.5 = f32[2,2,9,128,128]{4,3,2,1,0:T(8,128)} custom-call(s32[2]{0:T(128)S(1)} %pad_add_fusion.where, bf16[512,768]{1,0:T(8,128)(2,1)S(1)} %left.2, f32[6,512,256]{2,1,0:T(8,128)S(1)} %copy-done.1, bf16[4,2,192,128]{3,2,1,0:T(8,128)(2,1)S(1)} %pad_maximum_fusion.1.one, ...), custom_call_target="tpu_custom_call", output_to_operand_aliasing={{}: (5, {})} | custom-call | tf_op jit(solution)/shard_map/late/pallas_call | solution.py:164
  (31 shorter events, 0.1 us)
Async XLA Ops:
  0.0 1.7 %copy-start.2 = (bf16[128,20,512]{2,0,1:T(8,128)(2,1)S(1)}, bf16[128,20,512]{2,0,1:T(8,128)(2,1)}, u32[]{:S(2)}) copy-start(bf16[128,20,512]{2,0,1:T(8,128)(2,1)} %param.5) | copy-start | bytes 7864324
  1.7 0.9 copy-start.9
  2.6 0.7 copy-start.11
  3.4 0.7 copy-start.13
  4.0 0.7 copy-start.15
  4.7 25.1 %copy-start.3 = (bf16[128,20,512]{2,0,1:T(8,128)(2,1)S(1)}, bf16[128,20,512]{2,0,1:T(8,128)(2,1)}, u32[]{:S(2)}) copy-start(bf16[128,20,512]{2,0,1:T(8,128)(2,1)} %param.5) | copy-start | bytes 7864324
  4.7 25.1 %copy-start.12 = (s32[128,20]{0,1:T(8,128)S(1)}, s32[128,20]{0,1:T(8,128)}, u32[]{:S(2)}) copy-start(s32[128,20]{0,1:T(8,128)} %param.7) | copy-start | bytes 30724
  4.7 25.1 %copy-start.14 = (s32[1,128]{1,0:T(1,128)S(1)}, s32[1,128]{1,0:T(1,128)}, u32[]{:S(2)}) copy-start(s32[1,128]{1,0:T(1,128)} %order.3) | copy-start | bytes 1540
  9.7 0.9 copy-start.5
  10.7 64.6 %all-to-all-start = ((bf16[64,56,128]{2,1,0:T(8,128)(2,1)}), bf16[64,56,128]{2,1,0:T(8,128)(2,1)S(1)}, u32[]{:S(2)}, u32[]{:S(2)}) async-start(bf16[64,56,128]{2,1,0:T(8,128)(2,1)} %bitcast.33), calls=%async_computation | async-start | bytes 1835008 | tf_op jit(solution)/shard_map/all_to_all | solution.py:216
  29.8 0.9 copy-start.10
  30.7 0.7 copy-start.16
  33.6 0.7 copy-start.6
  75.3 16.7 %collective-permute-start.3 = (bf16[4,448,128]{2,1,0:T(8,128)(2,1)S(1)}, bf16[4,448,128]{2,1,0:T(8,128)(2,1)}, u32[]{:S(2)}, u32[]{:S(2)}) collective-permute-start(bf16[4,448,128]{2,1,0:T(8,128)(2,1)S(1)} %get-tuple-element.23), channel_id=1, source_target_pairs={{0,4},{4,8},{8,12},{12,0},{1,5},{5,9},{9,13},{13,1},{2,6},{6,10},{... | collective-permute-start | bytes 1376264 | tf_op jit(solution)/shard_map/ppermute | solution.py:186
  78.5 31.7 %collective-permute-start.1 = (bf16[4,2,448,128]{3,2,1,0:T(8,128)(2,1)S(1)}, bf16[4,2,448,128]{3,2,1,0:T(8,128)(2,1)S(1)}, u32[]{:S(2)}, u32[]{:S(2)}) collective-permute-start(bf16[4,2,448,128]{3,2,1,0:T(8,128)(2,1)S(1)} %bitcast.22), channel_id=1, source_target_pairs={{0,12},{4,0},{8,4},{12,8},{1,13},{5,1},{9,5},{13,9},{2,14},{6,2},{... | collective-permute-start | bytes 2752520 | tf_op jit(solution)/shard_map/ppermute | solution.py:186
  81.9 32.6 %all-to-all-start.1 = ((bf16[64,24,128]{2,1,0:T(8,128)(2,1)}), bf16[64,24,128]{2,1,0:T(8,128)(2,1)S(1)}, u32[]{:S(2)}, u32[]{:S(2)}) async-start(bf16[64,24,128]{2,1,0:T(8,128)(2,1)} %bitcast.34), calls=%async_computation.1 | async-start | bytes 786432 | tf_op jit(solution)/shard_map/all_to_all | solution.py:216
  91.3 6.5 %collective-permute-start.5 = (bf16[4,448,128]{2,1,0:T(8,128)(2,1)S(1)}, bf16[4,448,128]{2,1,0:T(8,128)(2,1)S(1)}, u32[]{:S(2)}, u32[]{:S(2)}) collective-permute-start(bf16[4,448,128]{2,1,0:T(8,128)(2,1)S(1)} %get-tuple-element.24), channel_id=1, source_target_pairs={{2,10},{6,14},{10,2},{14,6},{3,11},{7,15},{11,3},{15,7},{18,26},{2... | collective-permute-start | bytes 1376264 | tf_op jit(solution)/shard_map/ppermute | solution.py:192
  92.0 13.7 %collective-permute-start.4 = (bf16[4,448,128]{2,1,0:T(8,128)(2,1)}, bf16[4,448,128]{2,1,0:T(8,128)(2,1)S(1)}, u32[]{:S(2)}, u32[]{:S(2)}) collective-permute-start(bf16[4,448,128]{2,1,0:T(8,128)(2,1)} %collective-permute-done.3), channel_id=1, source_target_pairs={{0,4},{4,8},{8,12},{12,0},{1,5},{5,9},{9,13},{13,1},{2,6},{6,10},{... | collective-permute-start | bytes 1376264 | tf_op jit(solution)/shard_map/ppermute | solution.py:186
  93.9 18.3 %collective-permute-start = (bf16[4,2,448,128]{3,2,1,0:T(8,128)(2,1)S(1)}, bf16[4,2,448,128]{3,2,1,0:T(8,128)(2,1)S(1)}, u32[]{:S(2)}, u32[]{:S(2)}) collective-permute-start(bf16[4,2,448,128]{3,2,1,0:T(8,128)(2,1)S(1)} %bitcast.23), channel_id=1, source_target_pairs={{0,1},{1,0},{2,3},{3,2},{4,5},{5,4},{6,7},{7,6},{8,9},{9,8},{10,11... | collective-permute-start | bytes 2752520 | tf_op jit(solution)/shard_map/ppermute | solution.py:186
  105.8 8.8 %collective-permute-start.6 = (bf16[4,2,448,128]{3,2,1,0:T(8,128)(2,1)S(1)}, bf16[4,2,448,128]{3,2,1,0:T(8,128)(2,1)}, u32[]{:S(2)}, u32[]{:S(2)}) collective-permute-start(bf16[4,2,448,128]{3,2,1,0:T(8,128)(2,1)S(1)} %pad_maximum_fusion.refs_4_), channel_id=1, source_target_pairs={{0,1},{1,0},{2,3},{3,2},{4,5},{5,4},{6,7},{7,6},{8,9},{9,8},{10,11... | collective-permute-start | bytes 2752520 | tf_op jit(solution)/shard_map/ppermute | solution.py:186
  110.3 4.5 %collective-permute-start.2 = (bf16[4,2,448,128]{3,2,1,0:T(8,128)(2,1)S(1)}, bf16[4,2,448,128]{3,2,1,0:T(8,128)(2,1)}, u32[]{:S(2)}, u32[]{:S(2)}) collective-permute-start(bf16[4,2,448,128]{3,2,1,0:T(8,128)(2,1)S(1)} %collective-permute-done.1.refs_2_), channel_id=1, source_target_pairs={{0,1},{1,0},{2,3},{3,2},{4,5},{5,4},{6,7},{7,6},{8,9},{9,8},{10,11... | collective-permute-start | bytes 2752520 | tf_op jit(solution)/shard_map/ppermute | solution.py:186
  112.2 0.9 copy-start.7
  114.8 19.9 %collective-permute-start.11 = (bf16[4,2,192,128]{3,2,1,0:T(8,128)(2,1)S(1)}, bf16[4,2,192,128]{3,2,1,0:T(8,128)(2,1)}, u32[]{:S(2)}, u32[]{:S(2)}) collective-permute-start(bf16[4,2,192,128]{3,2,1,0:T(8,128)(2,1)S(1)} %bitcast.28), channel_id=1, source_target_pairs={{0,12},{4,0},{8,4},{12,8},{1,13},{5,1},{9,5},{13,9},{2,14},{6,2},{... | collective-permute-start | bytes 1179656 | tf_op jit(solution)/shard_map/ppermute | solution.py:186
  117.8 7.6 %collective-permute-start.7 = (bf16[4,192,128]{2,1,0:T(8,128)(2,1)S(1)}, bf16[4,192,128]{2,1,0:T(8,128)(2,1)S(1)}, u32[]{:S(2)}, u32[]{:S(2)}) collective-permute-start(bf16[4,192,128]{2,1,0:T(8,128)(2,1)S(1)} %get-tuple-element.25), channel_id=1, source_target_pairs={{0,4},{4,8},{8,12},{12,0},{1,5},{5,9},{9,13},{13,1},{2,6},{6,10},{... | collective-permute-start | bytes 589832 | tf_op jit(solution)/shard_map/ppermute | solution.py:186
  120.1 16.5 %collective-permute-start.9 = (bf16[4,192,128]{2,1,0:T(8,128)(2,1)S(1)}, bf16[4,192,128]{2,1,0:T(8,128)(2,1)S(1)}, u32[]{:S(2)}, u32[]{:S(2)}) collective-permute-start(bf16[4,192,128]{2,1,0:T(8,128)(2,1)S(1)} %get-tuple-element.26), channel_id=1, source_target_pairs={{2,10},{6,14},{10,2},{14,6},{3,11},{7,15},{11,3},{15,7},{18,26},{2... | collective-permute-start | bytes 589832 | tf_op jit(solution)/shard_map/ppermute | solution.py:192
  125.5 11.2 %collective-permute-start.8 = (bf16[4,192,128]{2,1,0:T(8,128)(2,1)S(1)}, bf16[4,192,128]{2,1,0:T(8,128)(2,1)S(1)}, u32[]{:S(2)}, u32[]{:S(2)}) collective-permute-start(bf16[4,192,128]{2,1,0:T(8,128)(2,1)S(1)} %collective-permute-done.7), channel_id=1, source_target_pairs={{0,4},{4,8},{8,12},{12,0},{1,5},{5,9},{9,13},{13,1},{2,6},{6,10},{... | collective-permute-start | bytes 589832 | tf_op jit(solution)/shard_map/ppermute | solution.py:186
  127.4 23.9 %collective-permute-start.13 = (bf16[4,2,192,128]{3,2,1,0:T(8,128)(2,1)S(1)}, bf16[4,2,192,128]{3,2,1,0:T(8,128)(2,1)}, u32[]{:S(2)}, u32[]{:S(2)}) collective-permute-start(bf16[4,2,192,128]{3,2,1,0:T(8,128)(2,1)S(1)} %bitcast.30), channel_id=1, source_target_pairs={{0,1},{1,0},{2,3},{3,2},{4,5},{5,4},{6,7},{7,6},{8,9},{9,8},{10,11... | collective-permute-start | bytes 1179656 | tf_op jit(solution)/shard_map/ppermute | solution.py:186
  134.7 21.2 %collective-permute-start.12 = (bf16[4,2,192,128]{3,2,1,0:T(8,128)(2,1)}, bf16[4,2,192,128]{3,2,1,0:T(8,128)(2,1)}, u32[]{:S(2)}, u32[]{:S(2)}) collective-permute-start(bf16[4,2,192,128]{3,2,1,0:T(8,128)(2,1)} %collective-permute-done.11.one), channel_id=1, source_target_pairs={{0,1},{1,0},{2,3},{3,2},{4,5},{5,4},{6,7},{7,6},{8,9},{9,8},{10,11... | collective-permute-start | bytes 1179656 | tf_op jit(solution)/shard_map/ppermute | solution.py:186
  136.7 21.9 %collective-permute-start.10 = (bf16[4,2,192,128]{3,2,1,0:T(8,128)(2,1)S(1)}, bf16[4,2,192,128]{3,2,1,0:T(8,128)(2,1)}, u32[]{:S(2)}, u32[]{:S(2)}) collective-permute-start(bf16[4,2,192,128]{3,2,1,0:T(8,128)(2,1)S(1)} %pad_maximum_fusion.1.one), channel_id=1, source_target_pairs={{0,1},{1,0},{2,3},{3,2},{4,5},{5,4},{6,7},{7,6},{8,9},{9,8},{10,11... | collective-permute-start | bytes 1179656 | tf_op jit(solution)/shard_map/ppermute | solution.py:186
  141.6 3.1 %copy-start.8 = (bf16[4,2,448,128]{3,2,1,0:T(8,128)(2,1)S(1)}, bf16[4,2,448,128]{3,2,1,0:T(8,128)(2,1)}, u32[]{:S(2)}) copy-start(bf16[4,2,448,128]{3,2,1,0:T(8,128)(2,1)} %copy-done.7) | copy-start | bytes 2752516
  143.4 1.2 copy-start.4
  151.3 1.9 %copy-start = (f32[6,512,256]{2,1,0:T(8,128)S(1)}, f32[6,512,256]{2,1,0:T(8,128)}, u32[]{:S(2)}) copy-start(f32[6,512,256]{2,1,0:T(8,128)} %early.1.begun) | copy-start | bytes 9437188
  153.2 2.7 %copy-start.1 = (f32[6,512,256]{2,1,0:T(8,128)S(1)}, f32[6,512,256]{2,1,0:T(8,128)}, u32[]{:S(2)}) copy-start(f32[6,512,256]{2,1,0:T(8,128)} %early.1.begun) | copy-start | bytes 9437188

commit v3 on v2

--- a/solution.py
+++ b/solution.py
@@ -16,7 +16,10 @@
 GROUP = 2
 CHUNKS = (14, 6)
 NOFF = 9
-VMEM = pltpu.CompilerParams(vmem_limit_bytes=48 * 1024 * 1024)
+
+
+def grant(mib):
+    return pltpu.CompilerParams(vmem_limit_bytes=mib * 1024 * 1024)
 
 
 def basis_rows(groups):
@@ -80,7 +83,6 @@
         out_specs=pl.BlockSpec(shape, lambda i: (0, 0, 0, 0)),
         out_shape=jax.ShapeDtypeStruct(shape, jnp.bfloat16),
         scratch_shapes=[pltpu.VMEM((groups * rows, CH), jnp.float32)],
-        compiler_params=VMEM,
         name="spectra",
     )(strain, live, order, basis, whiten)
 
@@ -108,7 +110,7 @@
         in_specs=[pl.BlockSpec(memory_space=pltpu.SMEM), whole],
         out_specs=whole,
         out_shape=jax.ShapeDtypeStruct((4 * CH, data.shape[0] * data.shape[2]), jnp.bfloat16),
-        compiler_params=VMEM,
+        compiler_params=grant(12),
         name="left",
     )(where, data)
 
@@ -119,19 +121,19 @@
 
 
 def early_body(left, *refs):
-    data, out = refs[:-1], refs[-1]
-    for i, ref in enumerate(data):
-        out[i] = product(left, ref)
+    for i in range(6):
+        refs[6 + i // 2][i % 2] = product(left, refs[i])
 
 
 def early(left, data):
     whole = pl.BlockSpec(memory_space=pltpu.VMEM)
     return pl.pallas_call(
         early_body,
-        in_specs=[whole] * (1 + len(data)),
-        out_specs=whole,
-        out_shape=jax.ShapeDtypeStruct((len(data), 4 * CH, 2 * CH), jnp.float32),
-        compiler_params=VMEM,
+        in_specs=[whole] * 7,
+        out_specs=[whole] * 3,
+        out_shape=[jax.ShapeDtypeStruct((2, 4 * CH, 2 * CH), jnp.float32)] * 3,
+        cost_estimate=pl.CostEstimate(flops=7 * 10**9, transcendentals=0, bytes_accessed=12 * 10**6),
+        compiler_params=grant(24),
         name="early",
     )(left, *data)
 
@@ -163,11 +165,10 @@
     extra = [] if filled is None else [filled]
     return pl.pallas_call(
         functools.partial(late_body, ahead=ahead, scale=scale),
-        grid=(1,),
         in_specs=[
             pl.BlockSpec(memory_space=pltpu.SMEM),
             whole,
-            pl.BlockSpec((2, 4 * CH, 2 * CH), lambda i: (ahead, 0, 0)),
+            whole,
             whole,
             whole,
         ]
@@ -176,7 +177,8 @@
         out_shape=jax.ShapeDtypeStruct((2, 2, NOFF, CH, CH), jnp.float32),
         input_output_aliases={5: 0} if extra else {},
         scratch_shapes=[pltpu.VMEM((4, 2, 2, CH, CH), jnp.float32), pltpu.SemaphoreType.DMA((4,))],
-        compiler_params=VMEM,
+        cost_estimate=pl.CostEstimate(flops=2 * 10**9, transcendentals=0, bytes_accessed=4 * 10**6),
+        compiler_params=grant(16),
         name="late",
     )(where, left, begun, one, two, *extra)
 
@@ -192,10 +194,16 @@
     return lax.ppermute(value, ("y", "z_hi"), pairs)
 
 
-def neighbours(here):
+def fetched(here, direct):
     ahead1 = shifted(here, "y", -1)
-    ahead2 = jnp.stack([shifted(shifted(here[:, 0], "y", 1), "y", 1), upper(here[:, 1], 2)], axis=1)
-    own = [here, ahead1, ahead2]
+    if direct:
+        low = shifted(here[:, 0], "y", 2)
+    else:
+        low = shifted(shifted(here[:, 0], "y", 1), "y", 1)
+    return [here, ahead1, jnp.stack([low, upper(here[:, 1], 2)], axis=1)]
+
+
+def both(own):
     return [w for v in own for w in (v, shifted(v, "core", 1))]
 
 
@@ -218,16 +226,19 @@
 
     first, second = spread(made(0, CHUNKS[0])), made(*CHUNKS)
     first, second = lax.optimization_barrier((first, second))
-    head = neighbours(first)
+    head = both(fetched(first, False))
     tail = spread(second)
     tail, *head = lax.optimization_barrier((tail, *head))
-    rest = neighbours(tail)
+    rest = fetched(tail, True)
+    crossed = shifted(tail, "core", 1)
     begun = early(left_of(where, head[0]), head)
     left = left_of(where, tail)
+    *rest, crossed, left, begun = lax.optimization_barrier((*rest[1:], crossed, left, begun))
+    rest = [tail, crossed, *both(rest)]
     filled = None
     for ahead in range(3):
         one, two = rest[2 * ahead : 2 * ahead + 2]
-        filled = late(where, left, begun, one, two, filled, ahead, scale)
+        filled = late(where, left, begun[ahead], one, two, filled, ahead, scale)
     return filled
 
 

time: 164 us -> 151 us (0.921)
  the two profiles are of different devices: /device:TPU:1 before, /device:TPU:271 now
where the time goes in v3:
time: 151 us; the launch traced here: 150 us
  starting transfers between devices  67.9 us (45%)
  waiting for transfers between devices  57.4 us (38%)
  Pallas kernels  24.5 us (16%)
    all_to_all x2, waiting for transfers between devices, spread(): here = lax.all_to_all(sent, ('x', 'z_hi', 'z_lo'), 0, 0, tiled=True)  35.9 us
    ppermute x11, starting transfers between devices, shifted(): lax.ppermute(value, axis, [(s, (s + steps) % count) for s in range(count)])  30.7 us
    all_to_all x2, starting transfers between devices, spread(): here = lax.all_to_all(sent, ('x', 'z_hi', 'z_lo'), 0, 0, tiled=True)  29.4 us
    pallas_call x2, Pallas kernels, spectra(): pl.pallas_call(functools.partial(spectra_body, first=first, groups=groups...  11.9 us
    ppermute x11, waiting for transfers between devices, shifted(): lax.ppermute(value, axis, [(s, (s + steps) % count) for s in range(count)])  11.6 us
    ppermute x2, waiting for transfers between devices, upper(): return lax.ppermute(value, ('y', 'z_hi'), pairs)  9.92 us
    ppermute x2, starting transfers between devices, upper(): return lax.ppermute(value, ('y', 'z_hi'), pairs)  7.77 us
    pallas_call x3, Pallas kernels, late(): pl.pallas_call(functools.partial(late_body, ahead=ahead, scale=scale), in...  6.11 us
  transfers between devices with their start and end apart: 15, of which 7 were waited for; matrix products, arithmetic and copies ran while one was open for 0% of the time, Pallas kernels for 10%

profile of v3, /device:TPU:271, one launch (start us, length us, event | category | flops | bytes accessed | tf_op | source)
XLA Modules:
  0.0 150.3 jit_solution(17087626033060455552)
XLA Ops:
  0.0 7.7 %spectra.2 = bf16[4,2,448,128]{3,2,1,0:T(8,128)(2,1)} custom-call(bf16[20,128,512]{2,1,0:T(8,128)(2,1)} %bitcast.31, s32[20,128]{1,0:T(8,128)} %bitcast.39, s32[1,128]{1,0:T(1,128)} %order.3, bf16[128,512]{1,0:T(8,128)(2,1)} %constant.8.clone.basis, f32[1,64]{1,0:T(1,128)} %bitcast.41), custom_call_target="tpu_custom_call" | custom-call | tf_op jit(solution)/shard_map/spectra/pallas_call | solution.py:73
  7.7 14.7 %all-to-all-start = ((bf16[64,56,128]{2,1,0:T(8,128)(2,1)}), bf16[64,56,128]{2,1,0:T(8,128)(2,1)S(1)}, u32[]{:S(2)}, u32[]{:S(2)}) async-start(bf16[64,56,128]{2,1,0:T(8,128)(2,1)} %bitcast.33), calls=%async_computation | async-start | bytes 1835008 | tf_op jit(solution)/shard_map/all_to_all | solution.py:224
  22.4 4.2 %spectra.3 = bf16[4,2,192,128]{3,2,1,0:T(8,128)(2,1)} custom-call(bf16[20,128,512]{2,1,0:T(8,128)(2,1)} %bitcast.32, s32[20,128]{1,0:T(8,128)} %bitcast.40, s32[1,128]{1,0:T(1,128)} %order.3, bf16[128,512]{1,0:T(8,128)(2,1)} %constant.8.clone.basis, f32[1,64]{1,0:T(1,128)} %bitcast.42), custom_call_target="tpu_custom_call" | custom-call | tf_op jit(solution)/shard_map/spectra/pallas_call | solution.py:73
  26.6 35.9 %all-to-all-done = bf16[64,56,128]{2,1,0:T(8,128)(2,1)S(1)} async-done(((bf16[64,56,128]{2,1,0:T(8,128)(2,1)}), bf16[64,56,128]{2,1,0:T(8,128)(2,1)S(1)}, u32[]{:S(2)}, u32[]{:S(2)}) %all-to-all-start) | async-done | bytes 917536 | tf_op jit(solution)/shard_map/all_to_all | solution.py:224
  62.5 0.1 slice_bitcast_fusion.1
  62.5 3.2 %collective-permute-start.3 = (bf16[4,448,128]{2,1,0:T(8,128)(2,1)S(1)}, bf16[4,448,128]{2,1,0:T(8,128)(2,1)}, u32[]{:S(2)}, u32[]{:S(2)}) collective-permute-start(bf16[4,448,128]{2,1,0:T(8,128)(2,1)S(1)} %get-tuple-element.43), channel_id=1, source_target_pairs={{0,4},{4,8},{8,12},{12,0},{1,5},{5,9},{9,13},{13,1},{2,6},{6,10},{... | collective-permute-start | bytes 1376264 | tf_op jit(solution)/shard_map/ppermute | solution.py:188
  65.7 2.1 %collective-permute-start.1 = (bf16[4,2,448,128]{3,2,1,0:T(8,128)(2,1)S(1)}, bf16[4,2,448,128]{3,2,1,0:T(8,128)(2,1)S(1)}, u32[]{:S(2)}, u32[]{:S(2)}) collective-permute-start(bf16[4,2,448,128]{3,2,1,0:T(8,128)(2,1)S(1)} %bitcast.22), channel_id=1, source_target_pairs={{0,12},{4,0},{8,4},{12,8},{1,13},{5,1},{9,5},{13,9},{2,14},{6,2},{... | collective-permute-start | bytes 2752520 | tf_op jit(solution)/shard_map/ppermute | solution.py:188
  67.8 14.8 %all-to-all-start.1 = ((bf16[64,24,128]{2,1,0:T(8,128)(2,1)}), bf16[64,24,128]{2,1,0:T(8,128)(2,1)S(1)}, u32[]{:S(2)}, u32[]{:S(2)}) async-start(bf16[64,24,128]{2,1,0:T(8,128)(2,1)} %bitcast.34), calls=%async_computation.1 | async-start | bytes 786432 | tf_op jit(solution)/shard_map/all_to_all | solution.py:224
  82.6 3.9 %collective-permute-start.5 = (bf16[4,448,128]{2,1,0:T(8,128)(2,1)S(1)}, bf16[4,448,128]{2,1,0:T(8,128)(2,1)S(1)}, u32[]{:S(2)}, u32[]{:S(2)}) collective-permute-start(bf16[4,448,128]{2,1,0:T(8,128)(2,1)S(1)} %get-tuple-element.44), channel_id=1, source_target_pairs={{2,10},{6,14},{10,2},{14,6},{3,11},{7,15},{11,3},{15,7},{18,26},{2... | collective-permute-start | bytes 1376264 | tf_op jit(solution)/shard_map/ppermute | solution.py:194
  86.5 0.0 collective-permute-done.3
  86.6 2.5 %collective-permute-start.4 = (bf16[4,448,128]{2,1,0:T(8,128)(2,1)}, bf16[4,448,128]{2,1,0:T(8,128)(2,1)S(1)}, u32[]{:S(2)}, u32[]{:S(2)}) collective-permute-start(bf16[4,448,128]{2,1,0:T(8,128)(2,1)} %collective-permute-done.3), channel_id=1, source_target_pairs={{0,4},{4,8},{8,12},{12,0},{1,5},{5,9},{9,13},{13,1},{2,6},{6,10},{... | collective-permute-start | bytes 1376264 | tf_op jit(solution)/shard_map/ppermute | solution.py:188
  89.1 4.4 %collective-permute-start = (bf16[4,2,448,128]{3,2,1,0:T(8,128)(2,1)S(1)}, bf16[4,2,448,128]{3,2,1,0:T(8,128)(2,1)}, u32[]{:S(2)}, u32[]{:S(2)}) collective-permute-start(bf16[4,2,448,128]{3,2,1,0:T(8,128)(2,1)S(1)} %bitcast.23), channel_id=1, source_target_pairs={{0,1},{1,0},{2,3},{3,2},{4,5},{5,4},{6,7},{7,6},{8,9},{9,8},{10,11... | collective-permute-start | bytes 2752520 | tf_op jit(solution)/shard_map/ppermute | solution.py:188
  93.5 5.7 %collective-permute-done.5 = bf16[4,448,128]{2,1,0:T(8,128)(2,1)S(1)} collective-permute-done((bf16[4,448,128]{2,1,0:T(8,128)(2,1)S(1)}, bf16[4,448,128]{2,1,0:T(8,128)(2,1)S(1)}, u32[]{:S(2)}, u32[]{:S(2)}) %collective-permute-start.5) | collective-permute-done | bytes 458784 | tf_op jit(solution)/shard_map/ppermute | solution.py:194
  99.2 8.3 %collective-permute-done.4 = bf16[4,448,128]{2,1,0:T(8,128)(2,1)S(1)} collective-permute-done((bf16[4,448,128]{2,1,0:T(8,128)(2,1)}, bf16[4,448,128]{2,1,0:T(8,128)(2,1)S(1)}, u32[]{:S(2)}, u32[]{:S(2)}) %collective-permute-start.4) | collective-permute-done | bytes 458784 | tf_op jit(solution)/shard_map/ppermute | solution.py:188
  107.5 0.1 pad_maximum_fusion.refs_4_
  107.6 3.4 %collective-permute-start.6 = (bf16[4,2,448,128]{3,2,1,0:T(8,128)(2,1)S(1)}, bf16[4,2,448,128]{3,2,1,0:T(8,128)(2,1)}, u32[]{:S(2)}, u32[]{:S(2)}) collective-permute-start(bf16[4,2,448,128]{3,2,1,0:T(8,128)(2,1)S(1)} %pad_maximum_fusion.refs_4_), channel_id=1, source_target_pairs={{0,1},{1,0},{2,3},{3,2},{4,5},{5,4},{6,7},{7,6},{8,9},{9,8},{10,11... | collective-permute-start | bytes 2752520 | tf_op jit(solution)/shard_map/ppermute | solution.py:188
  110.9 0.0 collective-permute-done.1.refs_2_
  111.0 1.9 %collective-permute-start.2 = (bf16[4,2,448,128]{3,2,1,0:T(8,128)(2,1)S(1)}, bf16[4,2,448,128]{3,2,1,0:T(8,128)(2,1)}, u32[]{:S(2)}, u32[]{:S(2)}) collective-permute-start(bf16[4,2,448,128]{3,2,1,0:T(8,128)(2,1)S(1)} %collective-permute-done.1.refs_2_), channel_id=1, source_target_pairs={{0,1},{1,0},{2,3},{3,2},{4,5},{5,4},{6,7},{7,6},{8,9},{9,8},{10,11... | collective-permute-start | bytes 2752520 | tf_op jit(solution)/shard_map/ppermute | solution.py:188
  112.9 0.1 pad_add_fusion.where
  113.0 0.0 collective-permute-done.refs_1_
  113.0 0.0 all-to-all-done.1
  113.0 0.2 collective-permute-done.6.refs_5_
  113.2 2.3 %collective-permute-done.2.refs_3_ = bf16[4,2,448,128]{3,2,1,0:T(8,128)(2,1)} collective-permute-done((bf16[4,2,448,128]{3,2,1,0:T(8,128)(2,1)S(1)}, bf16[4,2,448,128]{3,2,1,0:T(8,128)(2,1)}, u32[]{:S(2)}, u32[]{:S(2)}) %collective-permute-start.2) | collective-permute-done | bytes 917536 | tf_op jit(solution)/shard_map/ppermute | solution.py:188
  115.5 2.0 %collective-permute-start.10 = (bf16[4,2,192,128]{3,2,1,0:T(8,128)(2,1)S(1)}, bf16[4,2,192,128]{3,2,1,0:T(8,128)(2,1)S(1)}, u32[]{:S(2)}, u32[]{:S(2)}) collective-permute-start(bf16[4,2,192,128]{3,2,1,0:T(8,128)(2,1)S(1)} %bitcast.27), channel_id=1, source_target_pairs={{0,1},{1,0},{2,3},{3,2},{4,5},{5,4},{6,7},{7,6},{8,9},{9,8},{10,11... | collective-permute-start | bytes 1179656 | tf_op jit(solution)/shard_map/ppermute | solution.py:188
  117.5 3.2 %collective-permute-start.7 = (bf16[4,2,192,128]{3,2,1,0:T(8,128)(2,1)S(1)}, bf16[4,2,192,128]{3,2,1,0:T(8,128)(2,1)S(1)}, u32[]{:S(2)}, u32[]{:S(2)}) collective-permute-start(bf16[4,2,192,128]{3,2,1,0:T(8,128)(2,1)S(1)} %bitcast.28), channel_id=1, source_target_pairs={{0,12},{4,0},{8,4},{12,8},{1,13},{5,1},{9,5},{13,9},{2,14},{6,2},{... | collective-permute-start | bytes 1179656 | tf_op jit(solution)/shard_map/ppermute | solution.py:188
  120.7 2.9 %collective-permute-start.8 = (bf16[4,192,128]{2,1,0:T(8,128)(2,1)S(1)}, bf16[4,192,128]{2,1,0:T(8,128)(2,1)S(1)}, u32[]{:S(2)}, u32[]{:S(2)}) collective-permute-start(bf16[4,192,128]{2,1,0:T(8,128)(2,1)S(1)} %get-tuple-element.45), channel_id=1, source_target_pairs={{0,8},{4,12},{8,0},{12,4},{1,9},{5,13},{9,1},{13,5},{2,10},{6,14},... | collective-permute-start | bytes 589832 | tf_op jit(solution)/shard_map/ppermute | solution.py:188
  123.7 3.9 %collective-permute-start.9 = (bf16[4,192,128]{2,1,0:T(8,128)(2,1)S(1)}, bf16[4,192,128]{2,1,0:T(8,128)(2,1)S(1)}, u32[]{:S(2)}, u32[]{:S(2)}) collective-permute-start(bf16[4,192,128]{2,1,0:T(8,128)(2,1)S(1)} %get-tuple-element.46), channel_id=1, source_target_pairs={{2,10},{6,14},{10,2},{14,6},{3,11},{7,15},{11,3},{15,7},{18,26},{2... | collective-permute-start | bytes 589832 | tf_op jit(solution)/shard_map/ppermute | solution.py:194
  127.5 1.0 left.3
  128.5 4.7 %early.1 = (f32[2,512,256]{2,1,0:T(8,128)S(1)}, f32[2,512,256]{2,1,0:T(8,128)S(1)}, f32[2,512,256]{2,1,0:T(8,128)S(1)}) custom-call(bf16[512,1792]{1,0:T(8,128)(2,1)S(1)} %left.3, bf16[4,2,448,128]{3,2,1,0:T(8,128)(2,1)S(1)} %bitcast.25, bf16[4,2,448,128]{3,2,1,0:T(8,128)(2,1)} %collective-permute-done.refs_1_, ...), custom_call_target="tpu_custom_call" | custom-call | flops 7000000000 | bytes 12000000 | tf_op jit(solution)/shard_map/early/pallas_call | solution.py:130
  133.3 0.7 left.2
  134.0 0.8 collective-permute-done.8
  134.8 4.2 %collective-permute-done.9 = bf16[4,192,128]{2,1,0:T(8,128)(2,1)S(1)} collective-permute-done((bf16[4,192,128]{2,1,0:T(8,128)(2,1)S(1)}, bf16[4,192,128]{2,1,0:T(8,128)(2,1)S(1)}, u32[]{:S(2)}, u32[]{:S(2)}) %collective-permute-start.9) | collective-permute-done | bytes 196640 | tf_op jit(solution)/shard_map/ppermute | solution.py:194
  139.1 0.0 collective-permute-done.10.two
  139.1 0.0 collective-permute-done.7.one
  139.1 3.1 %collective-permute-start.12 = (bf16[4,2,192,128]{3,2,1,0:T(8,128)(2,1)S(1)}, bf16[4,2,192,128]{3,2,1,0:T(8,128)(2,1)S(1)}, u32[]{:S(2)}, u32[]{:S(2)}) collective-permute-start(bf16[4,2,192,128]{3,2,1,0:T(8,128)(2,1)S(1)} %collective-permute-done.7.one), channel_id=1, source_target_pairs={{0,1},{1,0},{2,3},{3,2},{4,5},{5,4},{6,7},{7,6},{8,9},{9,8},{10,11... | collective-permute-start | bytes 1179656 | tf_op jit(solution)/shard_map/ppermute | solution.py:188
  142.2 1.9 %collective-permute-start.11 = (bf16[4,2,192,128]{3,2,1,0:T(8,128)(2,1)S(1)}, bf16[4,2,192,128]{3,2,1,0:T(8,128)(2,1)S(1)}, u32[]{:S(2)}, u32[]{:S(2)}) collective-permute-start(bf16[4,2,192,128]{3,2,1,0:T(8,128)(2,1)S(1)} %pad_maximum_fusion.1.one), channel_id=1, source_target_pairs={{0,1},{1,0},{2,3},{3,2},{4,5},{5,4},{6,7},{7,6},{8,9},{9,8},{10,11... | collective-permute-start | bytes 1179656 | tf_op jit(solution)/shard_map/ppermute | solution.py:188
  144.2 1.9 %late.3.refs_0_ = f32[2,2,9,128,128]{4,3,2,1,0:T(8,128)} custom-call(s32[2]{0:T(128)S(1)} %pad_add_fusion.where, bf16[512,768]{1,0:T(8,128)(2,1)S(1)} %left.2, f32[2,512,256]{2,1,0:T(8,128)S(1)} %get-tuple-element.41.begun, bf16[4,2,192,128]{3,2,1,0:T(8,128)(2,1)S(1)} %bitcast.30, bf16[4,2,192,128]{3,2,1,0:T(8,128)(2,1)S(1)} %collective-permute-done.10.two), custom_call_target="tpu_custom_call" | custom-call | flops 2000000000 | bytes 4000000 | tf_op jit(solution)/shard_map/late/pallas_call | solution.py:166
  146.0 0.0 collective-permute-done.12.two
  146.0 2.1 %late.4.refs_0_ = f32[2,2,9,128,128]{4,3,2,1,0:T(8,128)} custom-call(s32[2]{0:T(128)S(1)} %pad_add_fusion.where, bf16[512,768]{1,0:T(8,128)(2,1)S(1)} %left.2, f32[2,512,256]{2,1,0:T(8,128)S(1)} %get-tuple-element.39.begun, bf16[4,2,192,128]{3,2,1,0:T(8,128)(2,1)S(1)} %collective-permute-done.7.one, ...), custom_call_target="tpu_custom_call", output_to_operand_aliasing={{}: (5, {})} | custom-call | flops 2000000000 | bytes 4000000 | tf_op jit(solution)/shard_map/late/pallas_call | solution.py:166
  148.2 0.0 collective-permute-done.11.two
  148.2 2.1 %late.5 = f32[2,2,9,128,128]{4,3,2,1,0:T(8,128)} custom-call(s32[2]{0:T(128)S(1)} %pad_add_fusion.where, bf16[512,768]{1,0:T(8,128)(2,1)S(1)} %left.2, f32[2,512,256]{2,1,0:T(8,128)S(1)} %get-tuple-element.37.begun, bf16[4,2,192,128]{3,2,1,0:T(8,128)(2,1)S(1)} %pad_maximum_fusion.1.one, ...), custom_call_target="tpu_custom_call", output_to_operand_aliasing={{}: (5, {})} | custom-call | flops 2000000000 | bytes 4000000 | tf_op jit(solution)/shard_map/late/pallas_call | solution.py:166
  (2 shorter events, 0.1 us)
Async XLA Ops:
  7.7 54.7 %all-to-all-start = ((bf16[64,56,128]{2,1,0:T(8,128)(2,1)}), bf16[64,56,128]{2,1,0:T(8,128)(2,1)S(1)}, u32[]{:S(2)}, u32[]{:S(2)}) async-start(bf16[64,56,128]{2,1,0:T(8,128)(2,1)} %bitcast.33), calls=%async_computation | async-start | bytes 1835008 | tf_op jit(solution)/shard_map/all_to_all | solution.py:224
  62.5 24.0 %collective-permute-start.3 = (bf16[4,448,128]{2,1,0:T(8,128)(2,1)S(1)}, bf16[4,448,128]{2,1,0:T(8,128)(2,1)}, u32[]{:S(2)}, u32[]{:S(2)}) collective-permute-start(bf16[4,448,128]{2,1,0:T(8,128)(2,1)S(1)} %get-tuple-element.43), channel_id=1, source_target_pairs={{0,4},{4,8},{8,12},{12,0},{1,5},{5,9},{9,13},{13,1},{2,6},{6,10},{... | collective-permute-start | bytes 1376264 | tf_op jit(solution)/shard_map/ppermute | solution.py:188
  65.7 45.2 %collective-permute-start.1 = (bf16[4,2,448,128]{3,2,1,0:T(8,128)(2,1)S(1)}, bf16[4,2,448,128]{3,2,1,0:T(8,128)(2,1)S(1)}, u32[]{:S(2)}, u32[]{:S(2)}) collective-permute-start(bf16[4,2,448,128]{3,2,1,0:T(8,128)(2,1)S(1)} %bitcast.22), channel_id=1, source_target_pairs={{0,12},{4,0},{8,4},{12,8},{1,13},{5,1},{9,5},{13,9},{2,14},{6,2},{... | collective-permute-start | bytes 2752520 | tf_op jit(solution)/shard_map/ppermute | solution.py:188
  67.8 45.1 %all-to-all-start.1 = ((bf16[64,24,128]{2,1,0:T(8,128)(2,1)}), bf16[64,24,128]{2,1,0:T(8,128)(2,1)S(1)}, u32[]{:S(2)}, u32[]{:S(2)}) async-start(bf16[64,24,128]{2,1,0:T(8,128)(2,1)} %bitcast.34), calls=%async_computation.1 | async-start | bytes 786432 | tf_op jit(solution)/shard_map/all_to_all | solution.py:224
  82.6 16.6 %collective-permute-start.5 = (bf16[4,448,128]{2,1,0:T(8,128)(2,1)S(1)}, bf16[4,448,128]{2,1,0:T(8,128)(2,1)S(1)}, u32[]{:S(2)}, u32[]{:S(2)}) collective-permute-start(bf16[4,448,128]{2,1,0:T(8,128)(2,1)S(1)} %get-tuple-element.44), channel_id=1, source_target_pairs={{2,10},{6,14},{10,2},{14,6},{3,11},{7,15},{11,3},{15,7},{18,26},{2... | collective-permute-start | bytes 1376264 | tf_op jit(solution)/shard_map/ppermute | solution.py:194
  86.6 20.9 %collective-permute-start.4 = (bf16[4,448,128]{2,1,0:T(8,128)(2,1)}, bf16[4,448,128]{2,1,0:T(8,128)(2,1)S(1)}, u32[]{:S(2)}, u32[]{:S(2)}) collective-permute-start(bf16[4,448,128]{2,1,0:T(8,128)(2,1)} %collective-permute-done.3), channel_id=1, source_target_pairs={{0,4},{4,8},{8,12},{12,0},{1,5},{5,9},{9,13},{13,1},{2,6},{6,10},{... | collective-permute-start | bytes 1376264 | tf_op jit(solution)/shard_map/ppermute | solution.py:188
  89.1 23.9 %collective-permute-start = (bf16[4,2,448,128]{3,2,1,0:T(8,128)(2,1)S(1)}, bf16[4,2,448,128]{3,2,1,0:T(8,128)(2,1)}, u32[]{:S(2)}, u32[]{:S(2)}) collective-permute-start(bf16[4,2,448,128]{3,2,1,0:T(8,128)(2,1)S(1)} %bitcast.23), channel_id=1, source_target_pairs={{0,1},{1,0},{2,3},{3,2},{4,5},{5,4},{6,7},{7,6},{8,9},{9,8},{10,11... | collective-permute-start | bytes 2752520 | tf_op jit(solution)/shard_map/ppermute | solution.py:188
  107.6 5.6 %collective-permute-start.6 = (bf16[4,2,448,128]{3,2,1,0:T(8,128)(2,1)S(1)}, bf16[4,2,448,128]{3,2,1,0:T(8,128)(2,1)}, u32[]{:S(2)}, u32[]{:S(2)}) collective-permute-start(bf16[4,2,448,128]{3,2,1,0:T(8,128)(2,1)S(1)} %pad_maximum_fusion.refs_4_), channel_id=1, source_target_pairs={{0,1},{1,0},{2,3},{3,2},{4,5},{5,4},{6,7},{7,6},{8,9},{9,8},{10,11... | collective-permute-start | bytes 2752520 | tf_op jit(solution)/shard_map/ppermute | solution.py:188
  111.0 4.5 %collective-permute-start.2 = (bf16[4,2,448,128]{3,2,1,0:T(8,128)(2,1)S(1)}, bf16[4,2,448,128]{3,2,1,0:T(8,128)(2,1)}, u32[]{:S(2)}, u32[]{:S(2)}) collective-permute-start(bf16[4,2,448,128]{3,2,1,0:T(8,128)(2,1)S(1)} %collective-permute-done.1.refs_2_), channel_id=1, source_target_pairs={{0,1},{1,0},{2,3},{3,2},{4,5},{5,4},{6,7},{7,6},{8,9},{9,8},{10,11... | collective-permute-start | bytes 2752520 | tf_op jit(solution)/shard_map/ppermute | solution.py:188
  115.5 23.6 %collective-permute-start.10 = (bf16[4,2,192,128]{3,2,1,0:T(8,128)(2,1)S(1)}, bf16[4,2,192,128]{3,2,1,0:T(8,128)(2,1)S(1)}, u32[]{:S(2)}, u32[]{:S(2)}) collective-permute-start(bf16[4,2,192,128]{3,2,1,0:T(8,128)(2,1)S(1)} %bitcast.27), channel_id=1, source_target_pairs={{0,1},{1,0},{2,3},{3,2},{4,5},{5,4},{6,7},{7,6},{8,9},{9,8},{10,11... | collective-permute-start | bytes 1179656 | tf_op jit(solution)/shard_map/ppermute | solution.py:188
  117.5 21.6 %collective-permute-start.7 = (bf16[4,2,192,128]{3,2,1,0:T(8,128)(2,1)S(1)}, bf16[4,2,192,128]{3,2,1,0:T(8,128)(2,1)S(1)}, u32[]{:S(2)}, u32[]{:S(2)}) collective-permute-start(bf16[4,2,192,128]{3,2,1,0:T(8,128)(2,1)S(1)} %bitcast.28), channel_id=1, source_target_pairs={{0,12},{4,0},{8,4},{12,8},{1,13},{5,1},{9,5},{13,9},{2,14},{6,2},{... | collective-permute-start | bytes 1179656 | tf_op jit(solution)/shard_map/ppermute | solution.py:188
  120.7 14.1 %collective-permute-start.8 = (bf16[4,192,128]{2,1,0:T(8,128)(2,1)S(1)}, bf16[4,192,128]{2,1,0:T(8,128)(2,1)S(1)}, u32[]{:S(2)}, u32[]{:S(2)}) collective-permute-start(bf16[4,192,128]{2,1,0:T(8,128)(2,1)S(1)} %get-tuple-element.45), channel_id=1, source_target_pairs={{0,8},{4,12},{8,0},{12,4},{1,9},{5,13},{9,1},{13,5},{2,10},{6,14},... | collective-permute-start | bytes 589832 | tf_op jit(solution)/shard_map/ppermute | solution.py:188
  123.7 15.4 %collective-permute-start.9 = (bf16[4,192,128]{2,1,0:T(8,128)(2,1)S(1)}, bf16[4,192,128]{2,1,0:T(8,128)(2,1)S(1)}, u32[]{:S(2)}, u32[]{:S(2)}) collective-permute-start(bf16[4,192,128]{2,1,0:T(8,128)(2,1)S(1)} %get-tuple-element.46), channel_id=1, source_target_pairs={{2,10},{6,14},{10,2},{14,6},{3,11},{7,15},{11,3},{15,7},{18,26},{2... | collective-permute-start | bytes 589832 | tf_op jit(solution)/shard_map/ppermute | solution.py:194
  139.1 6.9 %collective-permute-start.12 = (bf16[4,2,192,128]{3,2,1,0:T(8,128)(2,1)S(1)}, bf16[4,2,192,128]{3,2,1,0:T(8,128)(2,1)S(1)}, u32[]{:S(2)}, u32[]{:S(2)}) collective-permute-start(bf16[4,2,192,128]{3,2,1,0:T(8,128)(2,1)S(1)} %collective-permute-done.7.one), channel_id=1, source_target_pairs={{0,1},{1,0},{2,3},{3,2},{4,5},{5,4},{6,7},{7,6},{8,9},{9,8},{10,11... | collective-permute-start | bytes 1179656 | tf_op jit(solution)/shard_map/ppermute | solution.py:188
  142.2 5.9 %collective-permute-start.11 = (bf16[4,2,192,128]{3,2,1,0:T(8,128)(2,1)S(1)}, bf16[4,2,192,128]{3,2,1,0:T(8,128)(2,1)S(1)}, u32[]{:S(2)}, u32[]{:S(2)}) collective-permute-start(bf16[4,2,192,128]{3,2,1,0:T(8,128)(2,1)S(1)} %pad_maximum_fusion.1.one), channel_id=1, source_target_pairs={{0,1},{1,0},{2,3},{3,2},{4,5},{5,4},{6,7},{7,6},{8,9},{9,8},{10,11... | collective-permute-start | bytes 1179656 | tf_op jit(solution)/shard_map/ppermute | solution.py:188

commit v4 on v3

--- a/solution.py
+++ b/solution.py
@@ -33,8 +33,15 @@
     return jnp.asarray(table.astype(jnp.bfloat16))
 
 
-def spectra_body(strain, live, order, basis, whiten, out, place, *, first, groups, rows):
-    step = pl.program_id(0)
+def spectra_body(strain, live, order, basis, whiten, out, held, place, loaded, *, first, count, groups):
+    rows = 4 * count
+
+    def load(i):
+        part = pl.ds(first + i * GROUP, GROUP)
+        return pltpu.make_async_copy(strain.at[part], held.at[pl.ds(i * GROUP, GROUP)], loaded.at[i])
+
+    for i in range(count // GROUP):
+        load(i).start()
     channel = lax.broadcasted_iota(jnp.int32, (CH, CH), 0)
     pick = (channel == order[...]).astype(jnp.float32).astype(jnp.bfloat16)
     shape = (4 * groups, 2 * groups)
@@ -42,47 +49,40 @@
     column = lax.broadcasted_iota(jnp.int32, shape, 1)
     spread = jnp.where(column == 2 * (row % groups) + row // (2 * groups), whiten[...], 0.0)
     gain = jnp.sum(spread, axis=1, keepdims=True) * (2.0 / math.sqrt(NT))
-    for w in range(GROUP):
-        at = step * GROUP + w
-        value = strain[w].astype(jnp.float32)
-        centered = value - jnp.sum(value, axis=1, keepdims=True) * (1.0 / NT)
-        power = jnp.sum(centered * centered, axis=1, keepdims=True) * (1.0 / NT)
-        normed = (centered * lax.rsqrt(power + 1e-06)).astype(jnp.bfloat16)
-        spec = lax.dot_general(basis[...], normed, (((1,), (1,)), ((), ())), preferred_element_type=jnp.float32)
-        weight = live[pl.ds(first + at, 1), :].astype(jnp.float32)
-        spec = (spec * gain * weight).astype(jnp.bfloat16)
-        spec = jnp.dot(spec, pick, preferred_element_type=jnp.float32)
-        for part in range(4):
-            place[pl.ds(at * 4 + part, groups, stride=rows), :] = spec[part * groups : (part + 1) * groups]
-
-    @pl.when(step == pl.num_programs(0) - 1)
-    def _():
-        for x in range(4):
-            size = groups * rows // 4
-            packed = place[x * size : (x + 1) * size].astype(jnp.bfloat16)
-            out[x, 0] = packed
-            out[x, 1] = packed
+    for i in range(count // GROUP):
+        load(i).wait()
+        for at in range(i * GROUP, (i + 1) * GROUP):
+            value = held[at].astype(jnp.float32)
+            centered = value - jnp.sum(value, axis=1, keepdims=True) * (1.0 / NT)
+            power = jnp.sum(centered * centered, axis=1, keepdims=True) * (1.0 / NT)
+            normed = (centered * lax.rsqrt(power + 1e-06)).astype(jnp.bfloat16)
+            spec = lax.dot_general(basis[...], normed, (((1,), (1,)), ((), ())), preferred_element_type=jnp.float32)
+            weight = live[first + at : first + at + 1, :].astype(jnp.float32)
+            spec = (spec * gain * weight).astype(jnp.bfloat16)
+            spec = jnp.dot(spec, pick, preferred_element_type=jnp.float32)
+            for part in range(4):
+                place[pl.ds(at * 4 + part, groups, stride=rows), :] = spec[part * groups : (part + 1) * groups]
+    for x in range(4):
+        size = groups * rows // 4
+        packed = place[x * size : (x + 1) * size].astype(jnp.bfloat16)
+        out[x, 0] = packed
+        out[x, 1] = packed
 
 
 def spectra(strain, live, order, basis, whiten, first, count):
     groups = basis.shape[0] // 4
-    base = first // GROUP
     rows = 4 * count
-    shape = (4, 2, groups * rows // 4, CH)
-    whole = lambda v: pl.BlockSpec(v.shape, lambda i: (0,) * v.ndim)
-    return pl.pallas_call(
-        functools.partial(spectra_body, first=first, groups=groups, rows=rows),
-        grid=(count // GROUP,),
-        in_specs=[
-            pl.BlockSpec((GROUP, CH, NT), lambda i: (base + i, 0, 0)),
-            whole(live),
-            whole(order),
-            whole(basis),
-            whole(whiten),
+    whole = pl.BlockSpec(memory_space=pltpu.VMEM)
+    return pl.pallas_call(
+        functools.partial(spectra_body, first=first, count=count, groups=groups),
+        in_specs=[pl.BlockSpec(memory_space=pl.ANY)] + [whole] * 4,
+        out_specs=whole,
+        out_shape=jax.ShapeDtypeStruct((4, 2, groups * rows // 4, CH), jnp.bfloat16),
+        scratch_shapes=[
+            pltpu.VMEM((count, CH, NT), jnp.bfloat16),
+            pltpu.VMEM((groups * rows, CH), jnp.float32),
+            pltpu.SemaphoreType.DMA((count // GROUP,)),
         ],
-        out_specs=pl.BlockSpec(shape, lambda i: (0, 0, 0, 0)),
-        out_shape=jax.ShapeDtypeStruct(shape, jnp.bfloat16),
-        scratch_shapes=[pltpu.VMEM((groups * rows, CH), jnp.float32)],
         name="spectra",
     )(strain, live, order, basis, whiten)
 
@@ -188,19 +188,8 @@
     return lax.ppermute(value, axis, [(s, (s + steps) % count) for s in range(count)])
 
 
-def upper(value, steps):
-    count = lax.axis_size("y")
-    pairs = [(2 * y + 1, 2 * ((y + steps) % count) + 1) for y in range(count)]
-    return lax.ppermute(value, ("y", "z_hi"), pairs)
-
-
-def fetched(here, direct):
-    ahead1 = shifted(here, "y", -1)
-    if direct:
-        low = shifted(here[:, 0], "y", 2)
-    else:
-        low = shifted(shifted(here[:, 0], "y", 1), "y", 1)
-    return [here, ahead1, jnp.stack([low, upper(here[:, 1], 2)], axis=1)]
+def fetched(here):
+    return [here, shifted(here, "y", -1), shifted(here, "y", 2)]
 
 
 def both(own):
@@ -226,10 +215,10 @@
 
     first, second = spread(made(0, CHUNKS[0])), made(*CHUNKS)
     first, second = lax.optimization_barrier((first, second))
-    head = both(fetched(first, False))
+    head = both(fetched(first))
     tail = spread(second)
     tail, *head = lax.optimization_barrier((tail, *head))
-    rest = fetched(tail, True)
+    rest = fetched(tail)
     crossed = shifted(tail, "core", 1)
     begun = early(left_of(where, head[0]), head)
     left = left_of(where, tail)

time: 151 us -> 159 us (1.053)
  the two profiles are of different devices: /device:TPU:271 before, /device:TPU:1 now
where the time goes in v4:
time: 159 us; the launch traced here: 157 us
  starting transfers between devices  80.6 us (51%)
  waiting for transfers between devices  50.6 us (32%)
  Pallas kernels  25.2 us (16%)
    ppermute x10, starting transfers between devices, shifted(): lax.ppermute(value, axis, [(s, (s + steps) % count) for s in range(count)])  52.1 us
    all_to_all x2, waiting for transfers between devices, spread(): here = lax.all_to_all(sent, ('x', 'z_hi', 'z_lo'), 0, 0, tiled=True)  40.7 us
    all_to_all x2, starting transfers between devices, spread(): here = lax.all_to_all(sent, ('x', 'z_hi', 'z_lo'), 0, 0, tiled=True)  28.5 us
    pallas_call x2, Pallas kernels, spectra(): pl.pallas_call(functools.partial(spectra_body, first=first, count=count,...  12.6 us
    ppermute x10, waiting for transfers between devices, shifted(): lax.ppermute(value, axis, [(s, (s + steps) % count) for s in range(count)])  9.97 us
    pallas_call x3, Pallas kernels, late(): pl.pallas_call(functools.partial(late_body, ahead=ahead, scale=scale), in...  6.09 us
    pallas_call x1, Pallas kernels, early(): pl.pallas_call(early_body, in_specs=[whole] * 7, out_specs=[whole] * 3, o...  4.74 us
  transfers between devices with their start and end apart: 12, of which 5 were waited for; matrix products, arithmetic and copies ran while one was open for 0% of the time, Pallas kernels for 10%

profile of v4, /device:TPU:1, one launch (start us, length us, event | category | flops | bytes accessed | tf_op | source)
XLA Modules:
  0.0 156.7 jit_solution(18306426433378034096)
XLA Ops:
  0.0 7.8 %spectra.2 = bf16[4,2,448,128]{3,2,1,0:T(8,128)(2,1)} custom-call(bf16[20,128,512]{2,1,0:T(8,128)(2,1)} %bitcast.19, s32[20,128]{1,0:T(8,128)} %bitcast.23, s32[1,128]{1,0:T(1,128)} %order.3, bf16[128,512]{1,0:T(8,128)(2,1)} %constant.8.clone.basis, f32[1,64]{1,0:T(1,128)} %bitcast.25), custom_call_target="tpu_custom_call" | custom-call | tf_op jit(solution)/shard_map/spectra/pallas_call | solution.py:76
  7.8 19.1 %all-to-all-start = ((bf16[64,56,128]{2,1,0:T(8,128)(2,1)}), bf16[64,56,128]{2,1,0:T(8,128)(2,1)S(1)}, u32[]{:S(2)}, u32[]{:S(2)}) async-start(bf16[64,56,128]{2,1,0:T(8,128)(2,1)} %bitcast.21), calls=%async_computation | async-start | bytes 1835008 | tf_op jit(solution)/shard_map/all_to_all | solution.py:213
  26.9 4.8 %spectra.3 = bf16[4,2,192,128]{3,2,1,0:T(8,128)(2,1)} custom-call(bf16[20,128,512]{2,1,0:T(8,128)(2,1)} %bitcast.20, s32[20,128]{1,0:T(8,128)} %bitcast.24, s32[1,128]{1,0:T(1,128)} %order.3, bf16[128,512]{1,0:T(8,128)(2,1)} %constant.8.clone.basis, f32[1,64]{1,0:T(1,128)} %bitcast.26), custom_call_target="tpu_custom_call" | custom-call | tf_op jit(solution)/shard_map/spectra/pallas_call | solution.py:76
  31.7 40.7 %all-to-all-done = bf16[64,56,128]{2,1,0:T(8,128)(2,1)S(1)} async-done(((bf16[64,56,128]{2,1,0:T(8,128)(2,1)}), bf16[64,56,128]{2,1,0:T(8,128)(2,1)S(1)}, u32[]{:S(2)}, u32[]{:S(2)}) %all-to-all-start) | async-done | bytes 917536 | tf_op jit(solution)/shard_map/all_to_all | solution.py:213
  72.4 4.6 %collective-permute-start.1 = (bf16[4,2,448,128]{3,2,1,0:T(8,128)(2,1)S(1)}, bf16[4,2,448,128]{3,2,1,0:T(8,128)(2,1)S(1)}, u32[]{:S(2)}, u32[]{:S(2)}) collective-permute-start(bf16[4,2,448,128]{3,2,1,0:T(8,128)(2,1)S(1)} %bitcast.9), channel_id=1, source_target_pairs={{0,12},{4,0},{8,4},{12,8},{1,13},{5,1},{9,5},{13,9},{2,14},{6,2},{... | collective-permute-start | bytes 2752520 | tf_op jit(solution)/shard_map/ppermute | solution.py:188
  77.0 2.3 %collective-permute-start.3 = (bf16[4,2,448,128]{3,2,1,0:T(8,128)(2,1)S(1)}, bf16[4,2,448,128]{3,2,1,0:T(8,128)(2,1)S(1)}, u32[]{:S(2)}, u32[]{:S(2)}) collective-permute-start(bf16[4,2,448,128]{3,2,1,0:T(8,128)(2,1)S(1)} %bitcast.10), channel_id=1, source_target_pairs={{0,8},{4,12},{8,0},{12,4},{1,9},{5,13},{9,1},{13,5},{2,10},{6,14},... | collective-permute-start | bytes 2752520 | tf_op jit(solution)/shard_map/ppermute | solution.py:188
  79.3 9.4 %all-to-all-start.1 = ((bf16[64,24,128]{2,1,0:T(8,128)(2,1)}), bf16[64,24,128]{2,1,0:T(8,128)(2,1)S(1)}, u32[]{:S(2)}, u32[]{:S(2)}) async-start(bf16[64,24,128]{2,1,0:T(8,128)(2,1)} %bitcast.22), calls=%async_computation.1 | async-start | bytes 786432 | tf_op jit(solution)/shard_map/all_to_all | solution.py:213
  88.7 3.6 %collective-permute-start = (bf16[4,2,448,128]{3,2,1,0:T(8,128)(2,1)S(1)}, bf16[4,2,448,128]{3,2,1,0:T(8,128)(2,1)}, u32[]{:S(2)}, u32[]{:S(2)}) collective-permute-start(bf16[4,2,448,128]{3,2,1,0:T(8,128)(2,1)S(1)} %bitcast.11), channel_id=1, source_target_pairs={{0,1},{1,0},{2,3},{3,2},{4,5},{5,4},{6,7},{7,6},{8,9},{9,8},{10,11... | collective-permute-start | bytes 2752520 | tf_op jit(solution)/shard_map/ppermute | solution.py:188
  92.3 1.5 collective-permute-done.1.refs_2_
  93.8 25.4 %collective-permute-start.2 = (bf16[4,2,448,128]{3,2,1,0:T(8,128)(2,1)S(1)}, bf16[4,2,448,128]{3,2,1,0:T(8,128)(2,1)}, u32[]{:S(2)}, u32[]{:S(2)}) collective-permute-start(bf16[4,2,448,128]{3,2,1,0:T(8,128)(2,1)S(1)} %collective-permute-done.1.refs_2_), channel_id=1, source_target_pairs={{0,1},{1,0},{2,3},{3,2},{4,5},{5,4},{6,7},{7,6},{8,9},{9,8},{10,11... | collective-permute-start | bytes 2752520 | tf_op jit(solution)/shard_map/ppermute | solution.py:188
  119.2 0.0 collective-permute-done.3.refs_4_
  119.2 1.9 %collective-permute-start.4 = (bf16[4,2,448,128]{3,2,1,0:T(8,128)(2,1)S(1)}, bf16[4,2,448,128]{3,2,1,0:T(8,128)(2,1)}, u32[]{:S(2)}, u32[]{:S(2)}) collective-permute-start(bf16[4,2,448,128]{3,2,1,0:T(8,128)(2,1)S(1)} %collective-permute-done.3.refs_4_), channel_id=1, source_target_pairs={{0,1},{1,0},{2,3},{3,2},{4,5},{5,4},{6,7},{7,6},{8,9},{9,8},{10,11... | collective-permute-start | bytes 2752520 | tf_op jit(solution)/shard_map/ppermute | solution.py:188
  121.1 0.1 pad_add_fusion.where
  121.2 0.0 collective-permute-done.refs_1_
  121.2 0.0 all-to-all-done.1
  121.2 0.2 collective-permute-done.2.refs_3_
  121.4 2.3 %collective-permute-done.4.refs_5_ = bf16[4,2,448,128]{3,2,1,0:T(8,128)(2,1)} collective-permute-done((bf16[4,2,448,128]{3,2,1,0:T(8,128)(2,1)S(1)}, bf16[4,2,448,128]{3,2,1,0:T(8,128)(2,1)}, u32[]{:S(2)}, u32[]{:S(2)}) %collective-permute-start.4) | collective-permute-done | bytes 917536 | tf_op jit(solution)/shard_map/ppermute | solution.py:188
  123.7 5.3 %collective-permute-start.5 = (bf16[4,2,192,128]{3,2,1,0:T(8,128)(2,1)S(1)}, bf16[4,2,192,128]{3,2,1,0:T(8,128)(2,1)S(1)}, u32[]{:S(2)}, u32[]{:S(2)}) collective-permute-start(bf16[4,2,192,128]{3,2,1,0:T(8,128)(2,1)S(1)} %bitcast.14), channel_id=1, source_target_pairs={{0,12},{4,0},{8,4},{12,8},{1,13},{5,1},{9,5},{13,9},{2,14},{6,2},{... | collective-permute-start | bytes 1179656 | tf_op jit(solution)/shard_map/ppermute | solution.py:188
  129.0 1.9 %collective-permute-start.6 = (bf16[4,2,192,128]{3,2,1,0:T(8,128)(2,1)S(1)}, bf16[4,2,192,128]{3,2,1,0:T(8,128)(2,1)S(1)}, u32[]{:S(2)}, u32[]{:S(2)}) collective-permute-start(bf16[4,2,192,128]{3,2,1,0:T(8,128)(2,1)S(1)} %bitcast.15), channel_id=1, source_target_pairs={{0,8},{4,12},{8,0},{12,4},{1,9},{5,13},{9,1},{13,5},{2,10},{6,14},... | collective-permute-start | bytes 1179656 | tf_op jit(solution)/shard_map/ppermute | solution.py:188
  130.9 2.3 %collective-permute-start.7 = (bf16[4,2,192,128]{3,2,1,0:T(8,128)(2,1)S(1)}, bf16[4,2,192,128]{3,2,1,0:T(8,128)(2,1)S(1)}, u32[]{:S(2)}, u32[]{:S(2)}) collective-permute-start(bf16[4,2,192,128]{3,2,1,0:T(8,128)(2,1)S(1)} %bitcast.16), channel_id=1, source_target_pairs={{0,1},{1,0},{2,3},{3,2},{4,5},{5,4},{6,7},{7,6},{8,9},{9,8},{10,11... | collective-permute-start | bytes 1179656 | tf_op jit(solution)/shard_map/ppermute | solution.py:188
  133.3 0.7 left.2
  134.0 1.0 left.3
  135.0 4.7 %early.1 = (f32[2,512,256]{2,1,0:T(8,128)S(1)}, f32[2,512,256]{2,1,0:T(8,128)S(1)}, f32[2,512,256]{2,1,0:T(8,128)S(1)}) custom-call(bf16[512,1792]{1,0:T(8,128)(2,1)S(1)} %left.3, bf16[4,2,448,128]{3,2,1,0:T(8,128)(2,1)S(1)} %bitcast.13, bf16[4,2,448,128]{3,2,1,0:T(8,128)(2,1)} %collective-permute-done.refs_1_, ...), custom_call_target="tpu_custom_call" | custom-call | flops 7000000000 | bytes 12000000 | tf_op jit(solution)/shard_map/early/pallas_call | solution.py:130
  139.7 6.0 %collective-permute-done.5.one = bf16[4,2,192,128]{3,2,1,0:T(8,128)(2,1)S(1)} collective-permute-done((bf16[4,2,192,128]{3,2,1,0:T(8,128)(2,1)S(1)}, bf16[4,2,192,128]{3,2,1,0:T(8,128)(2,1)S(1)}, u32[]{:S(2)}, u32[]{:S(2)}) %collective-permute-start.5) | collective-permute-done | bytes 393248 | tf_op jit(solution)/shard_map/ppermute | solution.py:188
  145.8 0.0 collective-permute-done.6.one
  145.8 0.0 collective-permute-done.7.two
  145.8 2.9 %collective-permute-start.9 = (bf16[4,2,192,128]{3,2,1,0:T(8,128)(2,1)S(1)}, bf16[4,2,192,128]{3,2,1,0:T(8,128)(2,1)S(1)}, u32[]{:S(2)}, u32[]{:S(2)}) collective-permute-start(bf16[4,2,192,128]{3,2,1,0:T(8,128)(2,1)S(1)} %collective-permute-done.5.one), channel_id=1, source_target_pairs={{0,1},{1,0},{2,3},{3,2},{4,5},{5,4},{6,7},{7,6},{8,9},{9,8},{10,11... | collective-permute-start | bytes 1179656 | tf_op jit(solution)/shard_map/ppermute | solution.py:188
  148.6 1.9 %collective-permute-start.8 = (bf16[4,2,192,128]{3,2,1,0:T(8,128)(2,1)S(1)}, bf16[4,2,192,128]{3,2,1,0:T(8,128)(2,1)S(1)}, u32[]{:S(2)}, u32[]{:S(2)}) collective-permute-start(bf16[4,2,192,128]{3,2,1,0:T(8,128)(2,1)S(1)} %collective-permute-done.6.one), channel_id=1, source_target_pairs={{0,1},{1,0},{2,3},{3,2},{4,5},{5,4},{6,7},{7,6},{8,9},{9,8},{10,11... | collective-permute-start | bytes 1179656 | tf_op jit(solution)/shard_map/ppermute | solution.py:188
  150.6 2.0 %late.3.refs_0_ = f32[2,2,9,128,128]{4,3,2,1,0:T(8,128)} custom-call(s32[2]{0:T(128)S(1)} %pad_add_fusion.where, bf16[512,768]{1,0:T(8,128)(2,1)S(1)} %left.2, f32[2,512,256]{2,1,0:T(8,128)S(1)} %get-tuple-element.41.begun, bf16[4,2,192,128]{3,2,1,0:T(8,128)(2,1)S(1)} %bitcast.18, bf16[4,2,192,128]{3,2,1,0:T(8,128)(2,1)S(1)} %collective-permute-done.7.two), custom_call_target="tpu_custom_call" | custom-call | flops 2000000000 | bytes 4000000 | tf_op jit(solution)/shard_map/late/pallas_call | solution.py:166
  152.6 0.0 collective-permute-done.9.two
  152.6 2.1 %late.4.refs_0_ = f32[2,2,9,128,128]{4,3,2,1,0:T(8,128)} custom-call(s32[2]{0:T(128)S(1)} %pad_add_fusion.where, bf16[512,768]{1,0:T(8,128)(2,1)S(1)} %left.2, f32[2,512,256]{2,1,0:T(8,128)S(1)} %get-tuple-element.39.begun, bf16[4,2,192,128]{3,2,1,0:T(8,128)(2,1)S(1)} %collective-permute-done.5.one, ...), custom_call_target="tpu_custom_call", output_to_operand_aliasing={{}: (5, {})} | custom-call | flops 2000000000 | bytes 4000000 | tf_op jit(solution)/shard_map/late/pallas_call | solution.py:166
  154.7 0.0 collective-permute-done.8.two
  154.7 1.9 %late.5 = f32[2,2,9,128,128]{4,3,2,1,0:T(8,128)} custom-call(s32[2]{0:T(128)S(1)} %pad_add_fusion.where, bf16[512,768]{1,0:T(8,128)(2,1)S(1)} %left.2, f32[2,512,256]{2,1,0:T(8,128)S(1)} %get-tuple-element.37.begun, bf16[4,2,192,128]{3,2,1,0:T(8,128)(2,1)S(1)} %collective-permute-done.6.one, ...), custom_call_target="tpu_custom_call", output_to_operand_aliasing={{}: (5, {})} | custom-call | flops 2000000000 | bytes 4000000 | tf_op jit(solution)/shard_map/late/pallas_call | solution.py:166
Async XLA Ops:
  7.8 64.6 %all-to-all-start = ((bf16[64,56,128]{2,1,0:T(8,128)(2,1)}), bf16[64,56,128]{2,1,0:T(8,128)(2,1)S(1)}, u32[]{:S(2)}, u32[]{:S(2)}) async-start(bf16[64,56,128]{2,1,0:T(8,128)(2,1)} %bitcast.21), calls=%async_computation | async-start | bytes 1835008 | tf_op jit(solution)/shard_map/all_to_all | solution.py:213
  72.4 21.4 %collective-permute-start.1 = (bf16[4,2,448,128]{3,2,1,0:T(8,128)(2,1)S(1)}, bf16[4,2,448,128]{3,2,1,0:T(8,128)(2,1)S(1)}, u32[]{:S(2)}, u32[]{:S(2)}) collective-permute-start(bf16[4,2,448,128]{3,2,1,0:T(8,128)(2,1)S(1)} %bitcast.9), channel_id=1, source_target_pairs={{0,12},{4,0},{8,4},{12,8},{1,13},{5,1},{9,5},{13,9},{2,14},{6,2},{... | collective-permute-start | bytes 2752520 | tf_op jit(solution)/shard_map/ppermute | solution.py:188
  77.0 42.1 %collective-permute-start.3 = (bf16[4,2,448,128]{3,2,1,0:T(8,128)(2,1)S(1)}, bf16[4,2,448,128]{3,2,1,0:T(8,128)(2,1)S(1)}, u32[]{:S(2)}, u32[]{:S(2)}) collective-permute-start(bf16[4,2,448,128]{3,2,1,0:T(8,128)(2,1)S(1)} %bitcast.10), channel_id=1, source_target_pairs={{0,8},{4,12},{8,0},{12,4},{1,9},{5,13},{9,1},{13,5},{2,10},{6,14},... | collective-permute-start | bytes 2752520 | tf_op jit(solution)/shard_map/ppermute | solution.py:188
  79.3 41.9 %all-to-all-start.1 = ((bf16[64,24,128]{2,1,0:T(8,128)(2,1)}), bf16[64,24,128]{2,1,0:T(8,128)(2,1)S(1)}, u32[]{:S(2)}, u32[]{:S(2)}) async-start(bf16[64,24,128]{2,1,0:T(8,128)(2,1)} %bitcast.22), calls=%async_computation.1 | async-start | bytes 786432 | tf_op jit(solution)/shard_map/all_to_all | solution.py:213
  88.7 32.5 %collective-permute-start = (bf16[4,2,448,128]{3,2,1,0:T(8,128)(2,1)S(1)}, bf16[4,2,448,128]{3,2,1,0:T(8,128)(2,1)}, u32[]{:S(2)}, u32[]{:S(2)}) collective-permute-start(bf16[4,2,448,128]{3,2,1,0:T(8,128)(2,1)S(1)} %bitcast.11), channel_id=1, source_target_pairs={{0,1},{1,0},{2,3},{3,2},{4,5},{5,4},{6,7},{7,6},{8,9},{9,8},{10,11... | collective-permute-start | bytes 2752520 | tf_op jit(solution)/shard_map/ppermute | solution.py:188
  93.8 27.6 %collective-permute-start.2 = (bf16[4,2,448,128]{3,2,1,0:T(8,128)(2,1)S(1)}, bf16[4,2,448,128]{3,2,1,0:T(8,128)(2,1)}, u32[]{:S(2)}, u32[]{:S(2)}) collective-permute-start(bf16[4,2,448,128]{3,2,1,0:T(8,128)(2,1)S(1)} %collective-permute-done.1.refs_2_), channel_id=1, source_target_pairs={{0,1},{1,0},{2,3},{3,2},{4,5},{5,4},{6,7},{7,6},{8,9},{9,8},{10,11... | collective-permute-start | bytes 2752520 | tf_op jit(solution)/shard_map/ppermute | solution.py:188
  119.2 4.5 %collective-permute-start.4 = (bf16[4,2,448,128]{3,2,1,0:T(8,128)(2,1)S(1)}, bf16[4,2,448,128]{3,2,1,0:T(8,128)(2,1)}, u32[]{:S(2)}, u32[]{:S(2)}) collective-permute-start(bf16[4,2,448,128]{3,2,1,0:T(8,128)(2,1)S(1)} %collective-permute-done.3.refs_4_), channel_id=1, source_target_pairs={{0,1},{1,0},{2,3},{3,2},{4,5},{5,4},{6,7},{7,6},{8,9},{9,8},{10,11... | collective-permute-start | bytes 2752520 | tf_op jit(solution)/shard_map/ppermute | solution.py:188
  123.7 22.1 %collective-permute-start.5 = (bf16[4,2,192,128]{3,2,1,0:T(8,128)(2,1)S(1)}, bf16[4,2,192,128]{3,2,1,0:T(8,128)(2,1)S(1)}, u32[]{:S(2)}, u32[]{:S(2)}) collective-permute-start(bf16[4,2,192,128]{3,2,1,0:T(8,128)(2,1)S(1)} %bitcast.14), channel_id=1, source_target_pairs={{0,12},{4,0},{8,4},{12,8},{1,13},{5,1},{9,5},{13,9},{2,14},{6,2},{... | collective-permute-start | bytes 1179656 | tf_op jit(solution)/shard_map/ppermute | solution.py:188
  129.0 16.8 %collective-permute-start.6 = (bf16[4,2,192,128]{3,2,1,0:T(8,128)(2,1)S(1)}, bf16[4,2,192,128]{3,2,1,0:T(8,128)(2,1)S(1)}, u32[]{:S(2)}, u32[]{:S(2)}) collective-permute-start(bf16[4,2,192,128]{3,2,1,0:T(8,128)(2,1)S(1)} %bitcast.15), channel_id=1, source_target_pairs={{0,8},{4,12},{8,0},{12,4},{1,9},{5,13},{9,1},{13,5},{2,10},{6,14},... | collective-permute-start | bytes 1179656 | tf_op jit(solution)/shard_map/ppermute | solution.py:188
  130.9 14.9 %collective-permute-start.7 = (bf16[4,2,192,128]{3,2,1,0:T(8,128)(2,1)S(1)}, bf16[4,2,192,128]{3,2,1,0:T(8,128)(2,1)S(1)}, u32[]{:S(2)}, u32[]{:S(2)}) collective-permute-start(bf16[4,2,192,128]{3,2,1,0:T(8,128)(2,1)S(1)} %bitcast.16), channel_id=1, source_target_pairs={{0,1},{1,0},{2,3},{3,2},{4,5},{5,4},{6,7},{7,6},{8,9},{9,8},{10,11... | collective-permute-start | bytes 1179656 | tf_op jit(solution)/shard_map/ppermute | solution.py:188
  145.8 6.8 %collective-permute-start.9 = (bf16[4,2,192,128]{3,2,1,0:T(8,128)(2,1)S(1)}, bf16[4,2,192,128]{3,2,1,0:T(8,128)(2,1)S(1)}, u32[]{:S(2)}, u32[]{:S(2)}) collective-permute-start(bf16[4,2,192,128]{3,2,1,0:T(8,128)(2,1)S(1)} %collective-permute-done.5.one), channel_id=1, source_target_pairs={{0,1},{1,0},{2,3},{3,2},{4,5},{5,4},{6,7},{7,6},{8,9},{9,8},{10,11... | collective-permute-start | bytes 1179656 | tf_op jit(solution)/shard_map/ppermute | solution.py:188
  148.6 6.1 %collective-permute-start.8 = (bf16[4,2,192,128]{3,2,1,0:T(8,128)(2,1)S(1)}, bf16[4,2,192,128]{3,2,1,0:T(8,128)(2,1)S(1)}, u32[]{:S(2)}, u32[]{:S(2)}) collective-permute-start(bf16[4,2,192,128]{3,2,1,0:T(8,128)(2,1)S(1)} %collective-permute-done.6.one), channel_id=1, source_target_pairs={{0,1},{1,0},{2,3},{3,2},{4,5},{5,4},{6,7},{7,6},{8,9},{9,8},{10,11... | collective-permute-start | bytes 1179656 | tf_op jit(solution)/shard_map/ppermute | solution.py:188

commit v5 on v0

v5 whole, which is shorter than its diff:
```python
import functools
import math

import jax
import jax.numpy as jnp
import numpy as np
from jax import lax
from jax.experimental import pallas as pl
from jax.experimental.pallas import tpu as pltpu
from jax.sharding import Mesh
from jax.sharding import PartitionSpec as P

CH = 128
NT = 512
BIN0 = 8
NOFF = 9
PIECES = (0, 1, 5, 9)


def grant(mib):
    return pltpu.CompilerParams(vmem_limit_bytes=mib * 1024 * 1024)


def slot_bins(bins):
    return lambda slot: bins // 4 * (slot // (bins // 4)) + 2 * (slot % (bins // 8)) + slot // (bins // 8) % 2


def basis_rows(bins):
    t = np.arange(NT)
    kept = BIN0 + slot_bins(bins)(np.arange(bins))
    phase = (t[:, None] * kept[None, :] % NT).astype(np.float32)
    angles = np.float32(2.0 * math.pi / NT) * phase
    taper = np.float32(0.5) - np.float32(0.5) * np.cos(np.float32(2.0 * math.pi / NT) * t.astype(np.float32))
    table = np.concatenate([taper[:, None] * np.cos(angles), -taper[:, None] * np.sin(angles)], axis=1)
    return jnp.asarray(table.T.astype(jnp.bfloat16))


def spectra_body(strain, live, order, basis, whiten, out, held, place, loaded, *, parts):
    windows = strain.shape[0]
    bins = basis.shape[0] // 2
    rows = 2 * windows
    size = windows // parts

    def load(i):
        part = pl.ds(i * size, size)
        return pltpu.make_async_copy(strain.at[part], held.at[part], loaded.at[i])

    for i in range(parts):
        load(i).start()
    channel = lax.broadcasted_iota(jnp.int32, (CH, CH), 0)
    pick = (channel == order[...]).astype(jnp.float32).astype(jnp.bfloat16)
    row = lax.broadcasted_iota(jnp.int32, (2 * bins, bins), 0)
    column = lax.broadcasted_iota(jnp.int32, (2 * bins, bins), 1)
    spread = jnp.where(column == slot_bins(bins)(row % bins), whiten[...], 0.0)
    gain = jnp.sum(spread, axis=1, keepdims=True) * (2.0 / math.sqrt(NT))
    for i in range(parts):
        load(i).wait()
        for at in range(i * size, (i + 1) * size):
            value = held[at].astype(jnp.float32)
            centered = value - jnp.sum(value, axis=1, keepdims=True) * (1.0 / NT)
            power = jnp.sum(centered * centered, axis=1, keepdims=True) * (1.0 / NT)
            normed = (centered * lax.rsqrt(power + 1e-06)).astype(jnp.bfloat16)
            spec = lax.dot_general(basis[...], normed, (((1,), (1,)), ((), ())), preferred_element_type=jnp.float32)
            weight = live[at : at + 1, :].astype(jnp.float32)
            spec = (spec * gain * weight).astype(jnp.bfloat16)
            spec = jnp.dot(spec, pick, preferred_element_type=jnp.float32)
            for s in range(2):
                place[pl.ds(2 * at + s, bins, stride=rows), :] = spec[s * bins : (s + 1) * bins]
    for x in range(4):
        part = slice(x * bins * rows // 4, (x + 1) * bins * rows // 4)
        out[part] = place[part].astype(jnp.bfloat16)


def spectra(strain, live, order, basis, whiten):
    windows = strain.shape[0]
    total = basis.shape[0] * windows
    parts = 4 if windows % 4 == 0 else 1
    whole = pl.BlockSpec(memory_space=pltpu.VMEM)
    return pl.pallas_call(
        functools.partial(spectra_body, parts=parts),
        in_specs=[pl.BlockSpec(memory_space=pl.ANY)] + [whole] * 4,
        out_specs=whole,
        out_shape=jax.ShapeDtypeStruct((total, CH), jnp.bfloat16),
        scratch_shapes=[
            pltpu.VMEM((windows, CH, NT), jnp.bfloat16),
            pltpu.VMEM((total, CH), jnp.float32),
            pltpu.SemaphoreType.DMA((parts,)),
        ],
        name="spectra",
    )(strain, live, order, basis, whiten)


def left_body(where, data, left, piece, *, scale):
    half = where[0]
    for i, side in enumerate((half, 1 - half)):
        block = data[:, side].reshape(-1, CH)
        own = block.astype(jnp.float32).reshape(-1, 8, CH)
        part = lax.broadcasted_iota(jnp.int32, own.shape, 1)
        turned = jnp.where(part % 2 == 0, pltpu.roll(own, 7, 1), -pltpu.roll(own, 1, 1))
        own = own.reshape(-1, CH).T.astype(jnp.bfloat16)
        turned = turned.reshape(-1, CH).T.astype(jnp.bfloat16)
        left[(2 * i) * CH : (2 * i + 1) * CH] = own
        left[(2 * i + 1) * CH : (2 * i + 2) * CH] = turned
        if i == 1:
            for s, value in enumerate((own, turned)):
                total = jnp.dot(value, block, preferred_element_type=jnp.float32)
                piece[0, s] = (total * scale).astype(jnp.bfloat16)


def left_of(where, data, scale):
    whole = pl.BlockSpec(memory_space=pltpu.VMEM)
    return pl.pallas_call(
        functools.partial(left_body, scale=scale),
        in_specs=[pl.BlockSpec(memory_space=pltpu.SMEM), whole],
        out_specs=[whole, whole],
        out_shape=[
            jax.ShapeDtypeStruct((4 * CH, data.shape[0] * data.shape[2]), jnp.bfloat16),
            jax.ShapeDtypeStruct((1, 2, CH, CH), jnp.bfloat16),
        ],
        compiler_params=grant(12),
        name="left",
    )(where, data)


def product_body(where, left, *refs, aheads, scale, begun):
    count = 2 * len(aheads)
    data = refs[:count]
    outs = refs[count + begun :]
    if begun == 2:
        out, later, kept, sent, kept_done, sent_done = outs
        now = None
    else:
        out, now, later, kept, sent, kept_done, sent_done = outs
    half, core = where[0], where[1]
    jobs = []
    for i, ahead in enumerate(aheads):
        for other in range(2):
            ref = data[2 * i + other]
            right = jnp.concatenate([ref[:, 0].reshape(-1, CH), ref[:, 1].reshape(-1, CH)], axis=1)
            total = jnp.dot(left[...], right, preferred_element_type=jnp.float32) * scale
            for side in range(2):
                spot = (2 * i + other) * 2 + side
                columns = slice(side * CH, (side + 1) * CH)
                turn = 4 * ahead + other * (1 - 2 * core)
                for s in range(2):
                    kept[spot, s] = total[s * CH : (s + 1) * CH, columns]
                    sent[spot, s] = total[(2 + s) * CH : (3 + s) * CH, columns].astype(jnp.bfloat16)
                offset = turn + 2 * (side - half)
                target = jnp.clip(offset, 0, NOFF - 1)
                copy = pltpu.make_async_copy(kept.at[spot], out.at[half, :, target], kept_done.at[spot])
                jobs.append((jnp.logical_and(offset >= 0, offset < NOFF), copy))
                offset = turn + 2 * (side - 1 + half)
                target = jnp.clip(offset - PIECES[2], 0, PIECES[3] - PIECES[2] - 1)
                copy = pltpu.make_async_copy(sent.at[spot], later.at[target], sent_done.at[spot])
                jobs.append((jnp.logical_and(offset >= PIECES[2], offset < PIECES[3]), copy))
                if now is not None:
                    target = jnp.clip(offset - PIECES[1], 0, PIECES[2] - PIECES[1] - 1)
                    copy = pltpu.make_async_copy(sent.at[spot], now.at[target], sent_done.at[spot])
                    jobs.append((jnp.logical_and(offset >= PIECES[1], offset < PIECES[2]), copy))
                for valid, copy in jobs[-3 if now is not None else -2 :]:
                    pl.when(valid)(copy.start)
    for valid, copy in jobs:
        pl.when(valid)(copy.wait)


def products(where, left, data, begun, aheads, scale):
    whole = pl.BlockSpec(memory_space=pltpu.VMEM)
    somewhere = pl.BlockSpec(memory_space=pl.ANY)
    spots = 4 * len(aheads)
    out = jax.ShapeDtypeStruct((2, 2, NOFF, CH, CH), jnp.float32)
    piece = [jax.ShapeDtypeStruct((PIECES[i + 1] - PIECES[i], 2, CH, CH), jnp.bfloat16) for i in (1, 2)]
    outs = [out, piece[1]] if begun else [out, *piece]
    first = 2 + len(data)
    return pl.pallas_call(
        functools.partial(product_body, aheads=aheads, scale=scale, begun=len(begun)),
        in_specs=[pl.BlockSpec(memory_space=pltpu.SMEM)] + [whole] * (1 + len(data)) + [somewhere] * len(begun),
        out_specs=[somewhere] * len(outs),
        out_shape=outs,
        input_output_aliases={first + i: i for i in range(len(begun))},
        scratch_shapes=[
            pltpu.VMEM((spots, 2, CH, CH), jnp.float32),
            pltpu.VMEM((spots, 2, CH, CH), jnp.bfloat16),
            pltpu.SemaphoreType.DMA((spots,)),
            pltpu.SemaphoreType.DMA((spots,)),
        ],
        compiler_params=grant(20),
        name="products",
    )(where, left, *data, *begun)


def merge_body(where, piece, filled, out, stage, done, *, first):
    copies = []
    for i in range(piece.shape[0]):
        stage[i] = piece[i].astype(jnp.float32)
        copies.append(pltpu.make_async_copy(stage.at[i], out.at[1 - where[0], :, first + i], done.at[i]))
        copies[-1].start()
    for copy in copies:
        copy.wait()


def merged(where, piece, filled, first):
    whole = pl.BlockSpec(memory_space=pltpu.VMEM)
    somewhere = pl.BlockSpec(memory_space=pl.ANY)
    return pl.pallas_call(
        functools.partial(merge_body, first=first),
        in_specs=[pl.BlockSpec(memory_space=pltpu.SMEM), whole, somewhere],
        out_specs=somewhere,
        out_shape=jax.ShapeDtypeStruct(filled.shape, filled.dtype),
        input_output_aliases={2: 0},
        scratch_shapes=[pltpu.VMEM(piece.shape, jnp.float32), pltpu.SemaphoreType.DMA((piece.shape[0],))],
        compiler_params=grant(8),
        name="merge",
    )(where, piece, filled)


def shifted(value, axis, steps):
    count = lax.axis_size(axis)
    return lax.ppermute(value, axis, [(s, (s + steps) % count) for s in range(count)])


def local(strain, fiber_order, window_valid, whiten):
    bins = whiten.shape[0]
    windows = strain.shape[1]
    strain = jnp.transpose(strain, (1, 0, 2))
    live = jnp.transpose(window_valid)
    where = jnp.stack([lax.axis_index("z_hi"), lax.axis_index("core")]).astype(jnp.int32)
    scale = 1.0 / math.sqrt(windows * lax.axis_size("x") * lax.axis_size("z_lo"))
    sent = spectra(strain, live, fiber_order, basis_rows(bins), whiten.reshape(1, -1))
    here = lax.all_to_all(sent.reshape(bins, 2 * windows, CH), ("x", "z_hi", "z_lo"), 0, 0, tiled=True)
    here = here.reshape(4, 2, -1, CH)
    ahead1 = shifted(here, "y", -1)
    ahead2 = shifted(here, "y", 1)
    other0 = shifted(here, "core", 1)
    left, piece0 = left_of(where, here, scale)
    ahead1, left, piece0 = lax.optimization_barrier((ahead1, left, piece0))
    piece0 = shifted(piece0, "z_hi", 1)
    ahead2 = shifted(ahead2, "y", 1)
    other1 = shifted(ahead1, "core", 1)
    left, piece0 = lax.optimization_barrier((left, piece0))
    out, piece1, piece2 = products(where, left, [here, other0, ahead1, other1], [], (0, 1), scale)
    ahead2, out, piece2 = lax.optimization_barrier((ahead2, out, piece2))
    piece1 = shifted(piece1, "z_hi", 1)
    other2 = shifted(ahead2, "core", 1)
    out, piece2 = products(where, left, [ahead2, other2], [out, piece2], (2,), scale)
    piece2 = shifted(piece2, "z_hi", 1)
    for first, piece in zip(PIECES, (piece0, piece1, piece2)):
        out = merged(where, piece, out, first)
    return out


def solution(mesh):
    fine = Mesh(mesh.devices.reshape(4, 8, 4, 2, 2), ("x", "z_lo", "y", "z_hi", "core"))
    freq, chan = ("x", "z_lo"), ("y", "z_hi", "core")
    in_specs = (P(chan, freq, None), P(chan, None), P(chan, freq), P())
    out_specs = P(freq, None, None, chan, None)
    return jax.shard_map(local, mesh=fine, in_specs=in_specs, out_specs=out_specs, check_vma=False)
```

time: 348 us -> 172 us (0.49)
  the two profiles are of different devices: /device:TPU:1 before, /device:TPU:39 now
where the time goes in v5:
time: 172 us; the launch traced here: 171 us
  waiting for transfers between devices  54.5 us (32%)
  blocking collectives  54.4 us (32%)
  starting transfers between devices  41.6 us (24%)
  Pallas kernels  20.4 us (12%)
    ppermute x9, waiting for transfers between devices, shifted(): lax.ppermute(value, axis, [(s, (s + steps) % count) for s in range(count)])  54.5 us
    all_to_all x1, blocking collectives, local(): lax.all_to_all(sent.reshape(bins, 2 * windows, CH), ('x', 'z_hi', 'z_lo')...  54.4 us
    ppermute x9, starting transfers between devices, shifted(): lax.ppermute(value, axis, [(s, (s + steps) % count) for s in range(count)])  41.6 us
    pallas_call x2, Pallas kernels, products(): pl.pallas_call(functools.partial(product_body, aheads=aheads, scale=scale...  8.06 us
    pallas_call x1, Pallas kernels, spectra(): pl.pallas_call(functools.partial(spectra_body, parts=parts), in_specs=[pl...  7.19 us
    pallas_call x3, Pallas kernels, merged(): pl.pallas_call(functools.partial(merge_body, first=first), in_specs=[pl.B...  3.95 us
  transfers between devices with their start and end apart: 9, of which 5 were waited for; matrix products, arithmetic and copies ran while one was open for 0% of the time, Pallas kernels for 7%

profile of v5, /device:TPU:39, one launch (start us, length us, event | category | flops | bytes accessed | tf_op | source)
XLA Modules:
  0.0 171.1 jit_solution(8080864199476311708)
XLA Ops:
  0.0 7.2 %spectra.1 = bf16[2560,128]{1,0:T(8,128)(2,1)} custom-call(bf16[20,128,512]{2,1,0:T(8,128)(2,1)} %bitcast.12, s32[20,128]{1,0:T(8,128)} %bitcast.14, s32[1,128]{1,0:T(1,128)} %order.1, bf16[128,512]{1,0:T(8,128)(2,1)} %constant.8.clone.basis, f32[1,64]{1,0:T(1,128)} %bitcast.15), custom_call_target="tpu_custom_call" | custom-call | tf_op jit(solution)/shard_map/spectra/pallas_call | solution.py:79
  7.2 54.4 %all_to_all.5 = bf16[64,40,128]{2,1,0:T(8,128)(2,1)S(1)} all-to-all(bf16[64,40,128]{2,1,0:T(8,128)(2,1)} %bitcast.13), channel_id=1, replica_groups=mesh['x'=4,'z_lo'=8,'y'=4,'z_hi'=2,'core'=2] {'x','z_hi','z_lo'}, dimensions={0} | all-to-all | bytes 1310720 | tf_op jit(solution)/shard_map/all_to_all | solution.py:229
  61.6 4.6 %collective-permute-start = (bf16[4,2,320,128]{3,2,1,0:T(8,128)(2,1)S(1)}, bf16[4,2,320,128]{3,2,1,0:T(8,128)(2,1)S(1)}, u32[]{:S(2)}, u32[]{:S(2)}) collective-permute-start(bf16[4,2,320,128]{3,2,1,0:T(8,128)(2,1)S(1)} %bitcast.7), channel_id=1, source_target_pairs={{0,12},{4,0},{8,4},{12,8},{1,13},{5,1},{9,5},{13,9},{2,14},{6,2},{... | collective-permute-start | bytes 1966088 | tf_op jit(solution)/shard_map/ppermute | solution.py:218
  66.3 1.9 %collective-permute-start.2 = (bf16[4,2,320,128]{3,2,1,0:T(8,128)(2,1)S(1)}, bf16[4,2,320,128]{3,2,1,0:T(8,128)(2,1)S(1)}, u32[]{:S(2)}, u32[]{:S(2)}) collective-permute-start(bf16[4,2,320,128]{3,2,1,0:T(8,128)(2,1)S(1)} %bitcast.8), channel_id=1, source_target_pairs={{0,4},{4,8},{8,12},{12,0},{1,5},{5,9},{9,13},{13,1},{2,6},{6,10},{... | collective-permute-start | bytes 1966088 | tf_op jit(solution)/shard_map/ppermute | solution.py:218
  68.2 0.1 pad_add_fusion.where
  68.3 3.5 %collective-permute-start.4 = (bf16[4,2,320,128]{3,2,1,0:T(8,128)(2,1)S(1)}, bf16[4,2,320,128]{3,2,1,0:T(8,128)(2,1)S(1)}, u32[]{:S(2)}, u32[]{:S(2)}) collective-permute-start(bf16[4,2,320,128]{3,2,1,0:T(8,128)(2,1)S(1)} %bitcast.9), channel_id=1, source_target_pairs={{0,1},{1,0},{2,3},{3,2},{4,5},{5,4},{6,7},{7,6},{8,9},{9,8},{10,11... | collective-permute-start | bytes 1966088 | tf_op jit(solution)/shard_map/ppermute | solution.py:218
  71.8 1.2 left.1
  73.0 6.0 %collective-permute-done.refs_2_ = bf16[4,2,320,128]{3,2,1,0:T(8,128)(2,1)S(1)} collective-permute-done((bf16[4,2,320,128]{3,2,1,0:T(8,128)(2,1)S(1)}, bf16[4,2,320,128]{3,2,1,0:T(8,128)(2,1)S(1)}, u32[]{:S(2)}, u32[]{:S(2)}) %collective-permute-start) | collective-permute-done | bytes 655392 | tf_op jit(solution)/shard_map/ppermute | solution.py:218
  79.0 4.1 %collective-permute-start.5 = (bf16[4,2,320,128]{3,2,1,0:T(8,128)(2,1)S(1)}, bf16[4,2,320,128]{3,2,1,0:T(8,128)(2,1)S(1)}, u32[]{:S(2)}, u32[]{:S(2)}) collective-permute-start(bf16[4,2,320,128]{3,2,1,0:T(8,128)(2,1)S(1)} %collective-permute-done.refs_2_), channel_id=1, source_target_pairs={{0,1},{1,0},{2,3},{3,2},{4,5},{5,4},{6,7},{7,6},{8,9},{9,8},{10,11... | collective-permute-start | bytes 1966088 | tf_op jit(solution)/shard_map/ppermute | solution.py:218
  83.1 0.9 collective-permute-done.2
  84.0 1.9 %collective-permute-start.3 = (bf16[4,2,320,128]{3,2,1,0:T(8,128)(2,1)S(1)}, bf16[4,2,320,128]{3,2,1,0:T(8,128)(2,1)S(1)}, u32[]{:S(2)}, u32[]{:S(2)}) collective-permute-start(bf16[4,2,320,128]{3,2,1,0:T(8,128)(2,1)S(1)} %collective-permute-done.2), channel_id=1, source_target_pairs={{0,4},{4,8},{8,12},{12,0},{1,5},{5,9},{9,13},{13,1},{2,6},{6,10},{... | collective-permute-start | bytes 1966088 | tf_op jit(solution)/shard_map/ppermute | solution.py:218
  85.9 4.3 %collective-permute-start.1 = (bf16[1,2,128,128]{3,2,1,0:T(8,128)(2,1)S(1)}, bf16[1,2,128,128]{3,2,1,0:T(8,128)(2,1)S(1)}, u32[]{:S(2)}, u32[]{:S(2)}) collective-permute-start(bf16[1,2,128,128]{3,2,1,0:T(8,128)(2,1)S(1)} %get-tuple-element.23), channel_id=1, source_target_pairs={{0,2},{2,0},{1,3},{3,1},{4,6},{6,4},{5,7},{7,5},{8,10},{10,8},{9,1... | collective-permute-start | bytes 196616 | tf_op jit(solution)/shard_map/ppermute | solution.py:218
  90.2 9.8 %collective-permute-done.1.piece = bf16[1,2,128,128]{3,2,1,0:T(8,128)(2,1)S(1)} collective-permute-done((bf16[1,2,128,128]{3,2,1,0:T(8,128)(2,1)S(1)}, bf16[1,2,128,128]{3,2,1,0:T(8,128)(2,1)S(1)}, u32[]{:S(2)}, u32[]{:S(2)}) %collective-permute-start.1) | collective-permute-done | bytes 65568 | tf_op jit(solution)/shard_map/ppermute | solution.py:218
  100.0 0.0 collective-permute-done.4.refs_1_
  100.0 0.0 collective-permute-done.5.refs_3_
  100.0 5.0 %products.2 = (f32[2,2,9,128,128]{4,3,2,1,0:T(8,128)}, bf16[4,2,128,128]{3,2,1,0:T(8,128)(2,1)S(1)}, bf16[4,2,128,128]{3,2,1,0:T(8,128)(2,1)S(1)}) custom-call(s32[2]{0:T(128)S(1)} %pad_add_fusion.where, bf16[512,1280]{1,0:T(8,128)(2,1)S(1)} %get-tuple-element.24.left, bf16[4,2,320,128]{3,2,1,0:T(8,128)(2,1)S(1)} %bitcast.11, ...), custom_call_target="tpu_custom_call" | custom-call | tf_op jit(solution)/shard_map/products/pallas_call | solution.py:174
  105.1 0.0 collective-permute-done.3.refs_0_
  105.1 7.2 %collective-permute-start.6 = (bf16[4,2,320,128]{3,2,1,0:T(8,128)(2,1)S(1)}, bf16[4,2,320,128]{3,2,1,0:T(8,128)(2,1)S(1)}, u32[]{:S(2)}, u32[]{:S(2)}) collective-permute-start(bf16[4,2,320,128]{3,2,1,0:T(8,128)(2,1)S(1)} %collective-permute-done.3.refs_0_), channel_id=1, source_target_pairs={{0,1},{1,0},{2,3},{3,2},{4,5},{5,4},{6,7},{7,6},{8,9},{9,8},{10,11... | collective-permute-start | bytes 1966088 | tf_op jit(solution)/shard_map/ppermute | solution.py:218
  112.3 3.9 %collective-permute-start.8 = (bf16[4,2,128,128]{3,2,1,0:T(8,128)(2,1)S(1)}, bf16[4,2,128,128]{3,2,1,0:T(8,128)(2,1)S(1)}, u32[]{:S(2)}, u32[]{:S(2)}) collective-permute-start(bf16[4,2,128,128]{3,2,1,0:T(8,128)(2,1)S(1)} %get-tuple-element.32), channel_id=1, source_target_pairs={{0,2},{2,0},{1,3},{3,1},{4,6},{6,4},{5,7},{7,5},{8,10},{10,8},{9,1... | collective-permute-start | bytes 786440 | tf_op jit(solution)/shard_map/ppermute | solution.py:218
  116.2 0.0 collective-permute-done.6.refs_1_
  116.2 3.0 %products.3 = (f32[2,2,9,128,128]{4,3,2,1,0:T(8,128)}, bf16[4,2,128,128]{3,2,1,0:T(8,128)(2,1)S(1)}) custom-call(s32[2]{0:T(128)S(1)} %pad_add_fusion.where, bf16[512,1280]{1,0:T(8,128)(2,1)S(1)} %get-tuple-element.24.left, bf16[4,2,320,128]{3,2,1,0:T(8,128)(2,1)S(1)} %collective-permute-done.3.refs_0_, ...), custom_call_target="tpu_custom_call", output_to_operand_aliasing={{0}: (4, {}), {1}: (5, {})} | custom-call | tf_op jit(solution)/shard_map/products/pallas_call | solution.py:174
  119.3 10.2 %collective-permute-start.7 = (bf16[4,2,128,128]{3,2,1,0:T(8,128)(2,1)S(1)}, bf16[4,2,128,128]{3,2,1,0:T(8,128)(2,1)S(1)}, u32[]{:S(2)}, u32[]{:S(2)}) collective-permute-start(bf16[4,2,128,128]{3,2,1,0:T(8,128)(2,1)S(1)} %get-tuple-element.31), channel_id=1, source_target_pairs={{0,2},{2,0},{1,3},{3,1},{4,6},{6,4},{5,7},{7,5},{8,10},{10,8},{9,1... | collective-permute-start | bytes 786440 | tf_op jit(solution)/shard_map/ppermute | solution.py:218
  129.4 1.2 merge.3.filled
  130.6 33.5 %collective-permute-done.8.piece = bf16[4,2,128,128]{3,2,1,0:T(8,128)(2,1)S(1)} collective-permute-done((bf16[4,2,128,128]{3,2,1,0:T(8,128)(2,1)S(1)}, bf16[4,2,128,128]{3,2,1,0:T(8,128)(2,1)S(1)}, u32[]{:S(2)}, u32[]{:S(2)}) %collective-permute-start.8) | collective-permute-done | bytes 262176 | tf_op jit(solution)/shard_map/ppermute | solution.py:218
  164.2 1.4 merge.4.filled
  165.5 4.2 %collective-permute-done.7.piece = bf16[4,2,128,128]{3,2,1,0:T(8,128)(2,1)S(1)} collective-permute-done((bf16[4,2,128,128]{3,2,1,0:T(8,128)(2,1)S(1)}, bf16[4,2,128,128]{3,2,1,0:T(8,128)(2,1)S(1)}, u32[]{:S(2)}, u32[]{:S(2)}) %collective-permute-start.7) | collective-permute-done | bytes 262176 | tf_op jit(solution)/shard_map/ppermute | solution.py:218
  169.8 1.4 merge.5
Async XLA Ops:
  61.6 17.3 %collective-permute-start = (bf16[4,2,320,128]{3,2,1,0:T(8,128)(2,1)S(1)}, bf16[4,2,320,128]{3,2,1,0:T(8,128)(2,1)S(1)}, u32[]{:S(2)}, u32[]{:S(2)}) collective-permute-start(bf16[4,2,320,128]{3,2,1,0:T(8,128)(2,1)S(1)} %bitcast.7), channel_id=1, source_target_pairs={{0,12},{4,0},{8,4},{12,8},{1,13},{5,1},{9,5},{13,9},{2,14},{6,2},{... | collective-permute-start | bytes 1966088 | tf_op jit(solution)/shard_map/ppermute | solution.py:218
  66.3 17.7 %collective-permute-start.2 = (bf16[4,2,320,128]{3,2,1,0:T(8,128)(2,1)S(1)}, bf16[4,2,320,128]{3,2,1,0:T(8,128)(2,1)S(1)}, u32[]{:S(2)}, u32[]{:S(2)}) collective-permute-start(bf16[4,2,320,128]{3,2,1,0:T(8,128)(2,1)S(1)} %bitcast.8), channel_id=1, source_target_pairs={{0,4},{4,8},{8,12},{12,0},{1,5},{5,9},{9,13},{13,1},{2,6},{6,10},{... | collective-permute-start | bytes 1966088 | tf_op jit(solution)/shard_map/ppermute | solution.py:218
  68.3 31.8 %collective-permute-start.4 = (bf16[4,2,320,128]{3,2,1,0:T(8,128)(2,1)S(1)}, bf16[4,2,320,128]{3,2,1,0:T(8,128)(2,1)S(1)}, u32[]{:S(2)}, u32[]{:S(2)}) collective-permute-start(bf16[4,2,320,128]{3,2,1,0:T(8,128)(2,1)S(1)} %bitcast.9), channel_id=1, source_target_pairs={{0,1},{1,0},{2,3},{3,2},{4,5},{5,4},{6,7},{7,6},{8,9},{9,8},{10,11... | collective-permute-start | bytes 1966088 | tf_op jit(solution)/shard_map/ppermute | solution.py:218
  79.0 21.1 %collective-permute-start.5 = (bf16[4,2,320,128]{3,2,1,0:T(8,128)(2,1)S(1)}, bf16[4,2,320,128]{3,2,1,0:T(8,128)(2,1)S(1)}, u32[]{:S(2)}, u32[]{:S(2)}) collective-permute-start(bf16[4,2,320,128]{3,2,1,0:T(8,128)(2,1)S(1)} %collective-permute-done.refs_2_), channel_id=1, source_target_pairs={{0,1},{1,0},{2,3},{3,2},{4,5},{5,4},{6,7},{7,6},{8,9},{9,8},{10,11... | collective-permute-start | bytes 1966088 | tf_op jit(solution)/shard_map/ppermute | solution.py:218
  84.0 21.1 %collective-permute-start.3 = (bf16[4,2,320,128]{3,2,1,0:T(8,128)(2,1)S(1)}, bf16[4,2,320,128]{3,2,1,0:T(8,128)(2,1)S(1)}, u32[]{:S(2)}, u32[]{:S(2)}) collective-permute-start(bf16[4,2,320,128]{3,2,1,0:T(8,128)(2,1)S(1)} %collective-permute-done.2), channel_id=1, source_target_pairs={{0,4},{4,8},{8,12},{12,0},{1,5},{5,9},{9,13},{13,1},{2,6},{6,10},{... | collective-permute-start | bytes 1966088 | tf_op jit(solution)/shard_map/ppermute | solution.py:218
  85.9 14.1 %collective-permute-start.1 = (bf16[1,2,128,128]{3,2,1,0:T(8,128)(2,1)S(1)}, bf16[1,2,128,128]{3,2,1,0:T(8,128)(2,1)S(1)}, u32[]{:S(2)}, u32[]{:S(2)}) collective-permute-start(bf16[1,2,128,128]{3,2,1,0:T(8,128)(2,1)S(1)} %get-tuple-element.23), channel_id=1, source_target_pairs={{0,2},{2,0},{1,3},{3,1},{4,6},{6,4},{5,7},{7,5},{8,10},{10,8},{9,1... | collective-permute-start | bytes 196616 | tf_op jit(solution)/shard_map/ppermute | solution.py:218
  105.1 11.1 %collective-permute-start.6 = (bf16[4,2,320,128]{3,2,1,0:T(8,128)(2,1)S(1)}, bf16[4,2,320,128]{3,2,1,0:T(8,128)(2,1)S(1)}, u32[]{:S(2)}, u32[]{:S(2)}) collective-permute-start(bf16[4,2,320,128]{3,2,1,0:T(8,128)(2,1)S(1)} %collective-permute-done.3.refs_0_), channel_id=1, source_target_pairs={{0,1},{1,0},{2,3},{3,2},{4,5},{5,4},{6,7},{7,6},{8,9},{9,8},{10,11... | collective-permute-start | bytes 1966088 | tf_op jit(solution)/shard_map/ppermute | solution.py:218
  112.3 51.9 %collective-permute-start.8 = (bf16[4,2,128,128]{3,2,1,0:T(8,128)(2,1)S(1)}, bf16[4,2,128,128]{3,2,1,0:T(8,128)(2,1)S(1)}, u32[]{:S(2)}, u32[]{:S(2)}) collective-permute-start(bf16[4,2,128,128]{3,2,1,0:T(8,128)(2,1)S(1)} %get-tuple-element.32), channel_id=1, source_target_pairs={{0,2},{2,0},{1,3},{3,1},{4,6},{6,4},{5,7},{7,5},{8,10},{10,8},{9,1... | collective-permute-start | bytes 786440 | tf_op jit(solution)/shard_map/ppermute | solution.py:218
  119.3 50.5 %collective-permute-start.7 = (bf16[4,2,128,128]{3,2,1,0:T(8,128)(2,1)S(1)}, bf16[4,2,128,128]{3,2,1,0:T(8,128)(2,1)S(1)}, u32[]{:S(2)}, u32[]{:S(2)}) collective-permute-start(bf16[4,2,128,128]{3,2,1,0:T(8,128)(2,1)S(1)} %get-tuple-element.31), channel_id=1, source_target_pairs={{0,2},{2,0},{1,3},{3,1},{4,6},{6,4},{5,7},{7,5},{8,10},{10,8},{9,1... | collective-permute-start | bytes 786440 | tf_op jit(solution)/shard_map/ppermute | solution.py:218

commit v6 on v4

--- a/solution.py
+++ b/solution.py
@@ -13,8 +13,8 @@
 CH = 128
 NT = 512
 BIN0 = 8
-GROUP = 2
-CHUNKS = (14, 6)
+GROUP = 4
+CHUNKS = (12, 8)
 NOFF = 9
 
 
@@ -188,8 +188,19 @@
     return lax.ppermute(value, axis, [(s, (s + steps) % count) for s in range(count)])
 
 
-def fetched(here):
-    return [here, shifted(here, "y", -1), shifted(here, "y", 2)]
+def upper(value, steps):
+    count = lax.axis_size("y")
+    pairs = [(2 * y + 1, 2 * ((y + steps) % count) + 1) for y in range(count)]
+    return lax.ppermute(value, ("y", "z_hi"), pairs)
+
+
+def fetched(here, direct):
+    ahead1 = shifted(here, "y", -1)
+    if direct:
+        low = shifted(here[:, 0], "y", 2)
+    else:
+        low = shifted(shifted(here[:, 0], "y", 1), "y", 1)
+    return [here, ahead1, jnp.stack([low, upper(here[:, 1], 2)], axis=1)]
 
 
 def both(own):
@@ -215,18 +226,17 @@
 
     first, second = spread(made(0, CHUNKS[0])), made(*CHUNKS)
     first, second = lax.optimization_barrier((first, second))
-    head = both(fetched(first))
+    head = both(fetched(first, False))
     tail = spread(second)
     tail, *head = lax.optimization_barrier((tail, *head))
-    rest = fetched(tail)
-    crossed = shifted(tail, "core", 1)
+    rest = fetched(tail, True)
     begun = early(left_of(where, head[0]), head)
     left = left_of(where, tail)
-    *rest, crossed, left, begun = lax.optimization_barrier((*rest[1:], crossed, left, begun))
-    rest = [tail, crossed, *both(rest)]
+    ahead1, ahead2, left, *begun = lax.optimization_barrier((*rest[1:], left, *begun))
+    data = both([tail, ahead1, ahead2])
     filled = None
     for ahead in range(3):
-        one, two = rest[2 * ahead : 2 * ahead + 2]
+        one, two = data[2 * ahead : 2 * ahead + 2]
         filled = late(where, left, begun[ahead], one, two, filled, ahead, scale)
     return filled
 

time: 159 us -> 149 us (0.937)
  the two profiles are of different devices: /device:TPU:1 before, /device:TPU:287 now
where the time goes in v6:
time: 149 us
  starting transfers between devices  68.1 us (46%)
  waiting for transfers between devices  56.7 us (38%)
  Pallas kernels  23.2 us (16%)
    ppermute x11, starting transfers between devices, shifted(): lax.ppermute(value, axis, [(s, (s + steps) % count) for s in range(count)])  32.7 us
    all_to_all x2, starting transfers between devices, spread(): here = lax.all_to_all(sent, ('x', 'z_hi', 'z_lo'), 0, 0, tiled=True)  29.6 us
    all_to_all x2, waiting for transfers between devices, spread(): here = lax.all_to_all(sent, ('x', 'z_hi', 'z_lo'), 0, 0, tiled=True)  29.4 us
    ppermute x2, waiting for transfers between devices, upper(): return lax.ppermute(value, ('y', 'z_hi'), pairs)  16.7 us
    pallas_call x2, Pallas kernels, spectra(): pl.pallas_call(functools.partial(spectra_body, first=first, count=count,...  10.8 us
    ppermute x11, waiting for transfers between devices, shifted(): lax.ppermute(value, axis, [(s, (s + steps) % count) for s in range(count)])  10.6 us
    pallas_call x3, Pallas kernels, late(): pl.pallas_call(functools.partial(late_body, ahead=ahead, scale=scale), in...  6.51 us
    ppermute x2, starting transfers between devices, upper(): return lax.ppermute(value, ('y', 'z_hi'), pairs)  5.83 us
  transfers between devices with their start and end apart: 15, of which 7 were waited for; matrix products, arithmetic and copies ran while one was open for 0% of the time, Pallas kernels for 10%

profile of v6, /device:TPU:287, one launch (start us, length us, event | category | flops | bytes accessed | tf_op | source)
XLA Modules:
  0.0 148.5 jit_solution(17310407146411668434)
XLA Ops:
  0.0 5.9 %spectra.2 = bf16[4,2,384,128]{3,2,1,0:T(8,128)(2,1)} custom-call(bf16[20,128,512]{2,1,0:T(8,128)(2,1)} %bitcast.31, s32[20,128]{1,0:T(8,128)} %bitcast.39, s32[1,128]{1,0:T(1,128)} %order.3, bf16[128,512]{1,0:T(8,128)(2,1)} %constant.8.clone.basis, f32[1,64]{1,0:T(1,128)} %bitcast.41), custom_call_target="tpu_custom_call" | custom-call | tf_op jit(solution)/shard_map/spectra/pallas_call | solution.py:76
  5.9 14.7 %all-to-all-start = ((bf16[64,48,128]{2,1,0:T(8,128)(2,1)}), bf16[64,48,128]{2,1,0:T(8,128)(2,1)S(1)}, u32[]{:S(2)}, u32[]{:S(2)}) async-start(bf16[64,48,128]{2,1,0:T(8,128)(2,1)} %bitcast.33), calls=%async_computation | async-start | bytes 1572864 | tf_op jit(solution)/shard_map/all_to_all | solution.py:224
  20.5 4.9 %spectra.3 = bf16[4,2,256,128]{3,2,1,0:T(8,128)(2,1)} custom-call(bf16[20,128,512]{2,1,0:T(8,128)(2,1)} %bitcast.32, s32[20,128]{1,0:T(8,128)} %bitcast.40, s32[1,128]{1,0:T(1,128)} %order.3, bf16[128,512]{1,0:T(8,128)(2,1)} %constant.8.clone.basis, f32[1,64]{1,0:T(1,128)} %bitcast.42), custom_call_target="tpu_custom_call" | custom-call | tf_op jit(solution)/shard_map/spectra/pallas_call | solution.py:76
  25.5 29.4 %all-to-all-done = bf16[64,48,128]{2,1,0:T(8,128)(2,1)S(1)} async-done(((bf16[64,48,128]{2,1,0:T(8,128)(2,1)}), bf16[64,48,128]{2,1,0:T(8,128)(2,1)S(1)}, u32[]{:S(2)}, u32[]{:S(2)}) %all-to-all-start) | async-done | bytes 786464 | tf_op jit(solution)/shard_map/all_to_all | solution.py:224
  54.9 14.9 %all-to-all-start.1 = ((bf16[64,32,128]{2,1,0:T(8,128)(2,1)}), bf16[64,32,128]{2,1,0:T(8,128)(2,1)S(1)}, u32[]{:S(2)}, u32[]{:S(2)}) async-start(bf16[64,32,128]{2,1,0:T(8,128)(2,1)} %bitcast.34), calls=%async_computation.1 | async-start | bytes 1048576 | tf_op jit(solution)/shard_map/all_to_all | solution.py:224
  69.8 0.1 slice_bitcast_fusion.1
  69.8 1.9 %collective-permute-start.3 = (bf16[4,384,128]{2,1,0:T(8,128)(2,1)S(1)}, bf16[4,384,128]{2,1,0:T(8,128)(2,1)S(1)}, u32[]{:S(2)}, u32[]{:S(2)}) collective-permute-start(bf16[4,384,128]{2,1,0:T(8,128)(2,1)S(1)} %get-tuple-element.41), channel_id=1, source_target_pairs={{0,4},{4,8},{8,12},{12,0},{1,5},{5,9},{9,13},{13,1},{2,6},{6,10},{... | collective-permute-start | bytes 1179656 | tf_op jit(solution)/shard_map/ppermute | solution.py:188
  71.8 3.4 %collective-permute-start.1 = (bf16[4,2,384,128]{3,2,1,0:T(8,128)(2,1)S(1)}, bf16[4,2,384,128]{3,2,1,0:T(8,128)(2,1)S(1)}, u32[]{:S(2)}, u32[]{:S(2)}) collective-permute-start(bf16[4,2,384,128]{3,2,1,0:T(8,128)(2,1)S(1)} %bitcast.22), channel_id=1, source_target_pairs={{0,12},{4,0},{8,4},{12,8},{1,13},{5,1},{9,5},{13,9},{2,14},{6,2},{... | collective-permute-start | bytes 2359304 | tf_op jit(solution)/shard_map/ppermute | solution.py:188
  75.1 2.9 %collective-permute-start.5 = (bf16[4,384,128]{2,1,0:T(8,128)(2,1)S(1)}, bf16[4,384,128]{2,1,0:T(8,128)(2,1)S(1)}, u32[]{:S(2)}, u32[]{:S(2)}) collective-permute-start(bf16[4,384,128]{2,1,0:T(8,128)(2,1)S(1)} %get-tuple-element.42), channel_id=1, source_target_pairs={{2,10},{6,14},{10,2},{14,6},{3,11},{7,15},{11,3},{15,7},{18,26},{2... | collective-permute-start | bytes 1179656 | tf_op jit(solution)/shard_map/ppermute | solution.py:194
  78.0 2.9 %collective-permute-done.3 = bf16[4,384,128]{2,1,0:T(8,128)(2,1)S(1)} collective-permute-done((bf16[4,384,128]{2,1,0:T(8,128)(2,1)S(1)}, bf16[4,384,128]{2,1,0:T(8,128)(2,1)S(1)}, u32[]{:S(2)}, u32[]{:S(2)}) %collective-permute-start.3) | collective-permute-done | bytes 393248 | tf_op jit(solution)/shard_map/ppermute | solution.py:188
  81.0 3.2 %collective-permute-start.4 = (bf16[4,384,128]{2,1,0:T(8,128)(2,1)S(1)}, bf16[4,384,128]{2,1,0:T(8,128)(2,1)S(1)}, u32[]{:S(2)}, u32[]{:S(2)}) collective-permute-start(bf16[4,384,128]{2,1,0:T(8,128)(2,1)S(1)} %collective-permute-done.3), channel_id=1, source_target_pairs={{0,4},{4,8},{8,12},{12,0},{1,5},{5,9},{9,13},{13,1},{2,6},{6,10},{... | collective-permute-start | bytes 1179656 | tf_op jit(solution)/shard_map/ppermute | solution.py:188
  84.2 5.2 %collective-permute-start = (bf16[4,2,384,128]{3,2,1,0:T(8,128)(2,1)S(1)}, bf16[4,2,384,128]{3,2,1,0:T(8,128)(2,1)}, u32[]{:S(2)}, u32[]{:S(2)}) collective-permute-start(bf16[4,2,384,128]{3,2,1,0:T(8,128)(2,1)S(1)} %bitcast.23), channel_id=1, source_target_pairs={{0,1},{1,0},{2,3},{3,2},{4,5},{5,4},{6,7},{7,6},{8,9},{9,8},{10,11... | collective-permute-start | bytes 2359304 | tf_op jit(solution)/shard_map/ppermute | solution.py:188
  89.3 11.1 %collective-permute-done.5 = bf16[4,384,128]{2,1,0:T(8,128)(2,1)S(1)} collective-permute-done((bf16[4,384,128]{2,1,0:T(8,128)(2,1)S(1)}, bf16[4,384,128]{2,1,0:T(8,128)(2,1)S(1)}, u32[]{:S(2)}, u32[]{:S(2)}) %collective-permute-start.5) | collective-permute-done | bytes 393248 | tf_op jit(solution)/shard_map/ppermute | solution.py:194
  100.4 0.0 collective-permute-done.4
  100.4 0.1 pad_maximum_fusion.refs_4_
  100.5 4.6 %collective-permute-start.6 = (bf16[4,2,384,128]{3,2,1,0:T(8,128)(2,1)S(1)}, bf16[4,2,384,128]{3,2,1,0:T(8,128)(2,1)}, u32[]{:S(2)}, u32[]{:S(2)}) collective-permute-start(bf16[4,2,384,128]{3,2,1,0:T(8,128)(2,1)S(1)} %pad_maximum_fusion.refs_4_), channel_id=1, source_target_pairs={{0,1},{1,0},{2,3},{3,2},{4,5},{5,4},{6,7},{7,6},{8,9},{9,8},{10,11... | collective-permute-start | bytes 2359304 | tf_op jit(solution)/shard_map/ppermute | solution.py:188
  105.1 0.0 collective-permute-done.1.refs_2_
  105.1 1.9 %collective-permute-start.2 = (bf16[4,2,384,128]{3,2,1,0:T(8,128)(2,1)S(1)}, bf16[4,2,384,128]{3,2,1,0:T(8,128)(2,1)}, u32[]{:S(2)}, u32[]{:S(2)}) collective-permute-start(bf16[4,2,384,128]{3,2,1,0:T(8,128)(2,1)S(1)} %collective-permute-done.1.refs_2_), channel_id=1, source_target_pairs={{0,1},{1,0},{2,3},{3,2},{4,5},{5,4},{6,7},{7,6},{8,9},{9,8},{10,11... | collective-permute-start | bytes 2359304 | tf_op jit(solution)/shard_map/ppermute | solution.py:188
  107.0 0.1 pad_add_fusion.where
  107.1 0.0 collective-permute-done.refs_1_
  107.1 0.0 collective-permute-done.6.refs_5_
  107.1 2.3 %collective-permute-done.2.refs_3_ = bf16[4,2,384,128]{3,2,1,0:T(8,128)(2,1)} collective-permute-done((bf16[4,2,384,128]{3,2,1,0:T(8,128)(2,1)S(1)}, bf16[4,2,384,128]{3,2,1,0:T(8,128)(2,1)}, u32[]{:S(2)}, u32[]{:S(2)}) %collective-permute-start.2) | collective-permute-done | bytes 786464 | tf_op jit(solution)/shard_map/ppermute | solution.py:188
  109.4 0.0 all-to-all-done.1
  109.5 1.9 %collective-permute-start.7 = (bf16[4,2,256,128]{3,2,1,0:T(8,128)(2,1)S(1)}, bf16[4,2,256,128]{3,2,1,0:T(8,128)(2,1)S(1)}, u32[]{:S(2)}, u32[]{:S(2)}) collective-permute-start(bf16[4,2,256,128]{3,2,1,0:T(8,128)(2,1)S(1)} %bitcast.27), channel_id=1, source_target_pairs={{0,12},{4,0},{8,4},{12,8},{1,13},{5,1},{9,5},{13,9},{2,14},{6,2},{... | collective-permute-start | bytes 1572872 | tf_op jit(solution)/shard_map/ppermute | solution.py:188
  111.4 2.0 %collective-permute-start.12 = (bf16[4,2,256,128]{3,2,1,0:T(8,128)(2,1)S(1)}, bf16[4,2,256,128]{3,2,1,0:T(8,128)(2,1)S(1)}, u32[]{:S(2)}, u32[]{:S(2)}) collective-permute-start(bf16[4,2,256,128]{3,2,1,0:T(8,128)(2,1)S(1)} %bitcast.28), channel_id=1, source_target_pairs={{0,1},{1,0},{2,3},{3,2},{4,5},{5,4},{6,7},{7,6},{8,9},{9,8},{10,11... | collective-permute-start | bytes 1572872 | tf_op jit(solution)/shard_map/ppermute | solution.py:188
  113.4 3.8 %collective-permute-start.8 = (bf16[4,256,128]{2,1,0:T(8,128)(2,1)S(1)}, bf16[4,256,128]{2,1,0:T(8,128)(2,1)S(1)}, u32[]{:S(2)}, u32[]{:S(2)}) collective-permute-start(bf16[4,256,128]{2,1,0:T(8,128)(2,1)S(1)} %get-tuple-element.43), channel_id=1, source_target_pairs={{0,8},{4,12},{8,0},{12,4},{1,9},{5,13},{9,1},{13,5},{2,10},{6,14},... | collective-permute-start | bytes 786440 | tf_op jit(solution)/shard_map/ppermute | solution.py:188
  117.3 3.0 %collective-permute-start.9 = (bf16[4,256,128]{2,1,0:T(8,128)(2,1)S(1)}, bf16[4,256,128]{2,1,0:T(8,128)(2,1)S(1)}, u32[]{:S(2)}, u32[]{:S(2)}) collective-permute-start(bf16[4,256,128]{2,1,0:T(8,128)(2,1)S(1)} %get-tuple-element.44), channel_id=1, source_target_pairs={{2,10},{6,14},{10,2},{14,6},{3,11},{7,15},{11,3},{15,7},{18,26},{2... | collective-permute-start | bytes 786440 | tf_op jit(solution)/shard_map/ppermute | solution.py:194
  120.3 0.9 left.3
  121.2 4.2 %early.1 = (f32[2,512,256]{2,1,0:T(8,128)S(1)}, f32[2,512,256]{2,1,0:T(8,128)S(1)}, f32[2,512,256]{2,1,0:T(8,128)S(1)}) custom-call(bf16[512,1536]{1,0:T(8,128)(2,1)S(1)} %left.3, bf16[4,2,384,128]{3,2,1,0:T(8,128)(2,1)S(1)} %bitcast.25, bf16[4,2,384,128]{3,2,1,0:T(8,128)(2,1)} %collective-permute-done.refs_1_, ...), custom_call_target="tpu_custom_call" | custom-call | flops 7000000000 | bytes 12000000 | tf_op jit(solution)/shard_map/early/pallas_call | solution.py:130
  125.4 0.8 left.2
  126.2 4.9 %collective-permute-done.8 = bf16[4,256,128]{2,1,0:T(8,128)(2,1)S(1)} collective-permute-done((bf16[4,256,128]{2,1,0:T(8,128)(2,1)S(1)}, bf16[4,256,128]{2,1,0:T(8,128)(2,1)S(1)}, u32[]{:S(2)}, u32[]{:S(2)}) %collective-permute-start.8) | collective-permute-done | bytes 262176 | tf_op jit(solution)/shard_map/ppermute | solution.py:188
  131.1 5.6 %collective-permute-done.9 = bf16[4,256,128]{2,1,0:T(8,128)(2,1)S(1)} collective-permute-done((bf16[4,256,128]{2,1,0:T(8,128)(2,1)S(1)}, bf16[4,256,128]{2,1,0:T(8,128)(2,1)S(1)}, u32[]{:S(2)}, u32[]{:S(2)}) %collective-permute-start.9) | collective-permute-done | bytes 262176 | tf_op jit(solution)/shard_map/ppermute | solution.py:194
  136.7 0.1 pad_maximum_fusion.1.one
  136.8 0.4 collective-permute-done.7.one
  137.2 2.9 %collective-permute-start.11 = (bf16[4,2,256,128]{3,2,1,0:T(8,128)(2,1)S(1)}, bf16[4,2,256,128]{3,2,1,0:T(8,128)(2,1)S(1)}, u32[]{:S(2)}, u32[]{:S(2)}) collective-permute-start(bf16[4,2,256,128]{3,2,1,0:T(8,128)(2,1)S(1)} %collective-permute-done.7.one), channel_id=1, source_target_pairs={{0,1},{1,0},{2,3},{3,2},{4,5},{5,4},{6,7},{7,6},{8,9},{9,8},{10,11... | collective-permute-start | bytes 1572872 | tf_op jit(solution)/shard_map/ppermute | solution.py:188
  140.1 1.9 %collective-permute-start.10 = (bf16[4,2,256,128]{3,2,1,0:T(8,128)(2,1)S(1)}, bf16[4,2,256,128]{3,2,1,0:T(8,128)(2,1)S(1)}, u32[]{:S(2)}, u32[]{:S(2)}) collective-permute-start(bf16[4,2,256,128]{3,2,1,0:T(8,128)(2,1)S(1)} %pad_maximum_fusion.1.one), channel_id=1, source_target_pairs={{0,1},{1,0},{2,3},{3,2},{4,5},{5,4},{6,7},{7,6},{8,9},{9,8},{10,11... | collective-permute-start | bytes 1572872 | tf_op jit(solution)/shard_map/ppermute | solution.py:188
  142.0 0.0 collective-permute-done.12.two
  142.0 2.0 %late.3.refs_0_ = f32[2,2,9,128,128]{4,3,2,1,0:T(8,128)} custom-call(s32[2]{0:T(128)S(1)} %pad_add_fusion.where, bf16[512,1024]{1,0:T(8,128)(2,1)S(1)} %left.2, f32[2,512,256]{2,1,0:T(8,128)S(1)} %get-tuple-element.40.begun, bf16[4,2,256,128]{3,2,1,0:T(8,128)(2,1)S(1)} %bitcast.30, bf16[4,2,256,128]{3,2,1,0:T(8,128)(2,1)S(1)} %collective-permute-done.12.two), custom_call_target="tpu_custom_call" | custom-call | flops 2000000000 | bytes 4000000 | tf_op jit(solution)/shard_map/late/pallas_call | solution.py:166
  144.0 0.0 collective-permute-done.11.two
  144.0 2.3 %late.4.refs_0_ = f32[2,2,9,128,128]{4,3,2,1,0:T(8,128)} custom-call(s32[2]{0:T(128)S(1)} %pad_add_fusion.where, bf16[512,1024]{1,0:T(8,128)(2,1)S(1)} %left.2, f32[2,512,256]{2,1,0:T(8,128)S(1)} %get-tuple-element.38.begun, bf16[4,2,256,128]{3,2,1,0:T(8,128)(2,1)S(1)} %collective-permute-done.7.one, ...), custom_call_target="tpu_custom_call", output_to_operand_aliasing={{}: (5, {})} | custom-call | flops 2000000000 | bytes 4000000 | tf_op jit(solution)/shard_map/late/pallas_call | solution.py:166
  146.3 0.0 collective-permute-done.10.two
  146.3 2.3 %late.5 = f32[2,2,9,128,128]{4,3,2,1,0:T(8,128)} custom-call(s32[2]{0:T(128)S(1)} %pad_add_fusion.where, bf16[512,1024]{1,0:T(8,128)(2,1)S(1)} %left.2, f32[2,512,256]{2,1,0:T(8,128)S(1)} %get-tuple-element.36.begun, bf16[4,2,256,128]{3,2,1,0:T(8,128)(2,1)S(1)} %pad_maximum_fusion.1.one, ...), custom_call_target="tpu_custom_call", output_to_operand_aliasing={{}: (5, {})} | custom-call | flops 2000000000 | bytes 4000000 | tf_op jit(solution)/shard_map/late/pallas_call | solution.py:166
  (1 shorter events, 0.0 us)
Async XLA Ops:
  5.9 49.0 %all-to-all-start = ((bf16[64,48,128]{2,1,0:T(8,128)(2,1)}), bf16[64,48,128]{2,1,0:T(8,128)(2,1)S(1)}, u32[]{:S(2)}, u32[]{:S(2)}) async-start(bf16[64,48,128]{2,1,0:T(8,128)(2,1)} %bitcast.33), calls=%async_computation | async-start | bytes 1572864 | tf_op jit(solution)/shard_map/all_to_all | solution.py:224
  54.9 54.6 %all-to-all-start.1 = ((bf16[64,32,128]{2,1,0:T(8,128)(2,1)}), bf16[64,32,128]{2,1,0:T(8,128)(2,1)S(1)}, u32[]{:S(2)}, u32[]{:S(2)}) async-start(bf16[64,32,128]{2,1,0:T(8,128)(2,1)} %bitcast.34), calls=%async_computation.1 | async-start | bytes 1048576 | tf_op jit(solution)/shard_map/all_to_all | solution.py:224
  69.8 11.1 %collective-permute-start.3 = (bf16[4,384,128]{2,1,0:T(8,128)(2,1)S(1)}, bf16[4,384,128]{2,1,0:T(8,128)(2,1)S(1)}, u32[]{:S(2)}, u32[]{:S(2)}) collective-permute-start(bf16[4,384,128]{2,1,0:T(8,128)(2,1)S(1)} %get-tuple-element.41), channel_id=1, source_target_pairs={{0,4},{4,8},{8,12},{12,0},{1,5},{5,9},{9,13},{13,1},{2,6},{6,10},{... | collective-permute-start | bytes 1179656 | tf_op jit(solution)/shard_map/ppermute | solution.py:188
  71.8 33.3 %collective-permute-start.1 = (bf16[4,2,384,128]{3,2,1,0:T(8,128)(2,1)S(1)}, bf16[4,2,384,128]{3,2,1,0:T(8,128)(2,1)S(1)}, u32[]{:S(2)}, u32[]{:S(2)}) collective-permute-start(bf16[4,2,384,128]{3,2,1,0:T(8,128)(2,1)S(1)} %bitcast.22), channel_id=1, source_target_pairs={{0,12},{4,0},{8,4},{12,8},{1,13},{5,1},{9,5},{13,9},{2,14},{6,2},{... | collective-permute-start | bytes 2359304 | tf_op jit(solution)/shard_map/ppermute | solution.py:188
  75.1 25.3 %collective-permute-start.5 = (bf16[4,384,128]{2,1,0:T(8,128)(2,1)S(1)}, bf16[4,384,128]{2,1,0:T(8,128)(2,1)S(1)}, u32[]{:S(2)}, u32[]{:S(2)}) collective-permute-start(bf16[4,384,128]{2,1,0:T(8,128)(2,1)S(1)} %get-tuple-element.42), channel_id=1, source_target_pairs={{2,10},{6,14},{10,2},{14,6},{3,11},{7,15},{11,3},{15,7},{18,26},{2... | collective-permute-start | bytes 1179656 | tf_op jit(solution)/shard_map/ppermute | solution.py:194
  81.0 19.5 %collective-permute-start.4 = (bf16[4,384,128]{2,1,0:T(8,128)(2,1)S(1)}, bf16[4,384,128]{2,1,0:T(8,128)(2,1)S(1)}, u32[]{:S(2)}, u32[]{:S(2)}) collective-permute-start(bf16[4,384,128]{2,1,0:T(8,128)(2,1)S(1)} %collective-permute-done.3), channel_id=1, source_target_pairs={{0,4},{4,8},{8,12},{12,0},{1,5},{5,9},{9,13},{13,1},{2,6},{6,10},{... | collective-permute-start | bytes 1179656 | tf_op jit(solution)/shard_map/ppermute | solution.py:188
  84.2 23.0 %collective-permute-start = (bf16[4,2,384,128]{3,2,1,0:T(8,128)(2,1)S(1)}, bf16[4,2,384,128]{3,2,1,0:T(8,128)(2,1)}, u32[]{:S(2)}, u32[]{:S(2)}) collective-permute-start(bf16[4,2,384,128]{3,2,1,0:T(8,128)(2,1)S(1)} %bitcast.23), channel_id=1, source_target_pairs={{0,1},{1,0},{2,3},{3,2},{4,5},{5,4},{6,7},{7,6},{8,9},{9,8},{10,11... | collective-permute-start | bytes 2359304 | tf_op jit(solution)/shard_map/ppermute | solution.py:188
  100.5 6.6 %collective-permute-start.6 = (bf16[4,2,384,128]{3,2,1,0:T(8,128)(2,1)S(1)}, bf16[4,2,384,128]{3,2,1,0:T(8,128)(2,1)}, u32[]{:S(2)}, u32[]{:S(2)}) collective-permute-start(bf16[4,2,384,128]{3,2,1,0:T(8,128)(2,1)S(1)} %pad_maximum_fusion.refs_4_), channel_id=1, source_target_pairs={{0,1},{1,0},{2,3},{3,2},{4,5},{5,4},{6,7},{7,6},{8,9},{9,8},{10,11... | collective-permute-start | bytes 2359304 | tf_op jit(solution)/shard_map/ppermute | solution.py:188
  105.1 4.3 %collective-permute-start.2 = (bf16[4,2,384,128]{3,2,1,0:T(8,128)(2,1)S(1)}, bf16[4,2,384,128]{3,2,1,0:T(8,128)(2,1)}, u32[]{:S(2)}, u32[]{:S(2)}) collective-permute-start(bf16[4,2,384,128]{3,2,1,0:T(8,128)(2,1)S(1)} %collective-permute-done.1.refs_2_), channel_id=1, source_target_pairs={{0,1},{1,0},{2,3},{3,2},{4,5},{5,4},{6,7},{7,6},{8,9},{9,8},{10,11... | collective-permute-start | bytes 2359304 | tf_op jit(solution)/shard_map/ppermute | solution.py:188
  109.5 27.7 %collective-permute-start.7 = (bf16[4,2,256,128]{3,2,1,0:T(8,128)(2,1)S(1)}, bf16[4,2,256,128]{3,2,1,0:T(8,128)(2,1)S(1)}, u32[]{:S(2)}, u32[]{:S(2)}) collective-permute-start(bf16[4,2,256,128]{3,2,1,0:T(8,128)(2,1)S(1)} %bitcast.27), channel_id=1, source_target_pairs={{0,12},{4,0},{8,4},{12,8},{1,13},{5,1},{9,5},{13,9},{2,14},{6,2},{... | collective-permute-start | bytes 1572872 | tf_op jit(solution)/shard_map/ppermute | solution.py:188
  111.4 30.6 %collective-permute-start.12 = (bf16[4,2,256,128]{3,2,1,0:T(8,128)(2,1)S(1)}, bf16[4,2,256,128]{3,2,1,0:T(8,128)(2,1)S(1)}, u32[]{:S(2)}, u32[]{:S(2)}) collective-permute-start(bf16[4,2,256,128]{3,2,1,0:T(8,128)(2,1)S(1)} %bitcast.28), channel_id=1, source_target_pairs={{0,1},{1,0},{2,3},{3,2},{4,5},{5,4},{6,7},{7,6},{8,9},{9,8},{10,11... | collective-permute-start | bytes 1572872 | tf_op jit(solution)/shard_map/ppermute | solution.py:188
  113.4 17.7 %collective-permute-start.8 = (bf16[4,256,128]{2,1,0:T(8,128)(2,1)S(1)}, bf16[4,256,128]{2,1,0:T(8,128)(2,1)S(1)}, u32[]{:S(2)}, u32[]{:S(2)}) collective-permute-start(bf16[4,256,128]{2,1,0:T(8,128)(2,1)S(1)} %get-tuple-element.43), channel_id=1, source_target_pairs={{0,8},{4,12},{8,0},{12,4},{1,9},{5,13},{9,1},{13,5},{2,10},{6,14},... | collective-permute-start | bytes 786440 | tf_op jit(solution)/shard_map/ppermute | solution.py:188
  117.3 19.4 %collective-permute-start.9 = (bf16[4,256,128]{2,1,0:T(8,128)(2,1)S(1)}, bf16[4,256,128]{2,1,0:T(8,128)(2,1)S(1)}, u32[]{:S(2)}, u32[]{:S(2)}) collective-permute-start(bf16[4,256,128]{2,1,0:T(8,128)(2,1)S(1)} %get-tuple-element.44), channel_id=1, source_target_pairs={{2,10},{6,14},{10,2},{14,6},{3,11},{7,15},{11,3},{15,7},{18,26},{2... | collective-permute-start | bytes 786440 | tf_op jit(solution)/shard_map/ppermute | solution.py:194
  137.2 6.8 %collective-permute-start.11 = (bf16[4,2,256,128]{3,2,1,0:T(8,128)(2,1)S(1)}, bf16[4,2,256,128]{3,2,1,0:T(8,128)(2,1)S(1)}, u32[]{:S(2)}, u32[]{:S(2)}) collective-permute-start(bf16[4,2,256,128]{3,2,1,0:T(8,128)(2,1)S(1)} %collective-permute-done.7.one), channel_id=1, source_target_pairs={{0,1},{1,0},{2,3},{3,2},{4,5},{5,4},{6,7},{7,6},{8,9},{9,8},{10,11... | collective-permute-start | bytes 1572872 | tf_op jit(solution)/shard_map/ppermute | solution.py:188
  140.1 6.2 %collective-permute-start.10 = (bf16[4,2,256,128]{3,2,1,0:T(8,128)(2,1)S(1)}, bf16[4,2,256,128]{3,2,1,0:T(8,128)(2,1)S(1)}, u32[]{:S(2)}, u32[]{:S(2)}) collective-permute-start(bf16[4,2,256,128]{3,2,1,0:T(8,128)(2,1)S(1)} %pad_maximum_fusion.1.one), channel_id=1, source_target_pairs={{0,1},{1,0},{2,3},{3,2},{4,5},{5,4},{6,7},{7,6},{8,9},{9,8},{10,11... | collective-permute-start | bytes 1572872 | tf_op jit(solution)/shard_map/ppermute | solution.py:188

commit v7 on v6

--- a/solution.py
+++ b/solution.py
@@ -13,8 +13,8 @@
 CH = 128
 NT = 512
 BIN0 = 8
-GROUP = 4
-CHUNKS = (12, 8)
+GROUP = 5
+CHUNKS = (10, 10)
 NOFF = 9
 
 
@@ -194,13 +194,10 @@
     return lax.ppermute(value, ("y", "z_hi"), pairs)
 
 
-def fetched(here, direct):
+def fetched(here, held):
     ahead1 = shifted(here, "y", -1)
-    if direct:
-        low = shifted(here[:, 0], "y", 2)
-    else:
-        low = shifted(shifted(here[:, 0], "y", 1), "y", 1)
-    return [here, ahead1, jnp.stack([low, upper(here[:, 1], 2)], axis=1)]
+    low, *held = lax.optimization_barrier((shifted(here[:, 0], "y", 1), *held))
+    return [here, ahead1, jnp.stack([shifted(low, "y", 1), upper(here[:, 1], 2)], axis=1)], held
 
 
 def both(own):
@@ -226,17 +223,17 @@
 
     first, second = spread(made(0, CHUNKS[0])), made(*CHUNKS)
     first, second = lax.optimization_barrier((first, second))
-    head = both(fetched(first, False))
+    head = both(fetched(first, [])[0])
     tail = spread(second)
     tail, *head = lax.optimization_barrier((tail, *head))
-    rest = fetched(tail, True)
+    (_, ahead1, ahead2), head = fetched(tail, head)
     begun = early(left_of(where, head[0]), head)
     left = left_of(where, tail)
-    ahead1, ahead2, left, *begun = lax.optimization_barrier((*rest[1:], left, *begun))
-    data = both([tail, ahead1, ahead2])
-    filled = None
-    for ahead in range(3):
-        one, two = data[2 * ahead : 2 * ahead + 2]
+    filled = late(where, left, begun[0], tail, shifted(tail, "core", 1), None, 0, scale)
+    ahead1, ahead2, left, filled, *begun = lax.optimization_barrier((ahead1, ahead2, left, filled, *begun))
+    data = both([ahead1, ahead2])
+    for ahead in (1, 2):
+        one, two = data[2 * ahead - 2 : 2 * ahead]
         filled = late(where, left, begun[ahead], one, two, filled, ahead, scale)
     return filled
 

time: 149 us -> 142 us (0.953)
  the two profiles are of different devices: /device:TPU:287 before, /device:TPU:1 now
where the time goes in v7:
time: 142 us; the launch traced here: 140 us
  starting transfers between devices  68.9 us (49%)
  waiting for transfers between devices  47.3 us (33%)
  Pallas kernels  21 us (15%)
  local copies, waits for them, and re-layouts  2.64 us (2%)
    ppermute x12, starting transfers between devices, shifted(): lax.ppermute(value, axis, [(s, (s + steps) % count) for s in range(count)])  39.2 us
    all_to_all x2, waiting for transfers between devices, spread(): here = lax.all_to_all(sent, ('x', 'z_hi', 'z_lo'), 0, 0, tiled=True)  32.2 us
    all_to_all x2, starting transfers between devices, spread(): here = lax.all_to_all(sent, ('x', 'z_hi', 'z_lo'), 0, 0, tiled=True)  28.4 us
    ppermute x12, waiting for transfers between devices, shifted(): lax.ppermute(value, axis, [(s, (s + steps) % count) for s in range(count)])  15.1 us
    pallas_call x2, Pallas kernels, spectra(): pl.pallas_call(functools.partial(spectra_body, first=first, count=count,...  10.1 us
    pallas_call x3, Pallas kernels, late(): pl.pallas_call(functools.partial(late_body, ahead=ahead, scale=scale), in...  6.96 us
  transfers between devices with their start and end apart: 16, of which 7 were waited for; matrix products, arithmetic and copies ran while one was open for 0% of the time, Pallas kernels for 10%

profile of v7, /device:TPU:1, one launch (start us, length us, event | category | flops | bytes accessed | tf_op | source)
XLA Modules:
  0.0 140.4 jit_solution(1831364412322070243)
XLA Ops:
  0.0 5.1 %spectra.2 = bf16[4,2,320,128]{3,2,1,0:T(8,128)(2,1)} custom-call(bf16[20,128,512]{2,1,0:T(8,128)(2,1)} %bitcast.31, s32[20,128]{1,0:T(8,128)} %bitcast.39, s32[1,128]{1,0:T(1,128)} %order.3, bf16[128,512]{1,0:T(8,128)(2,1)} %constant.8.clone.basis, f32[1,64]{1,0:T(1,128)} %bitcast.41), custom_call_target="tpu_custom_call" | custom-call | tf_op jit(solution)/shard_map/spectra/pallas_call | solution.py:76
  5.1 19.1 %all-to-all-start = ((bf16[64,40,128]{2,1,0:T(8,128)(2,1)}), bf16[64,40,128]{2,1,0:T(8,128)(2,1)S(1)}, u32[]{:S(2)}, u32[]{:S(2)}) async-start(bf16[64,40,128]{2,1,0:T(8,128)(2,1)} %bitcast.34), calls=%async_computation | async-start | bytes 1310720 | tf_op jit(solution)/shard_map/all_to_all | solution.py:221
  24.2 5.0 %spectra.3 = bf16[4,2,320,128]{3,2,1,0:T(8,128)(2,1)} custom-call(bf16[20,128,512]{2,1,0:T(8,128)(2,1)} %bitcast.32, s32[20,128]{1,0:T(8,128)} %bitcast.40, s32[1,128]{1,0:T(1,128)} %order.3, bf16[128,512]{1,0:T(8,128)(2,1)} %constant.8.clone.basis, f32[1,64]{1,0:T(1,128)} %bitcast.42), custom_call_target="tpu_custom_call" | custom-call | tf_op jit(solution)/shard_map/spectra/pallas_call | solution.py:76
  29.3 29.3 %all-to-all-done = bf16[64,40,128]{2,1,0:T(8,128)(2,1)S(1)} async-done(((bf16[64,40,128]{2,1,0:T(8,128)(2,1)}), bf16[64,40,128]{2,1,0:T(8,128)(2,1)S(1)}, u32[]{:S(2)}, u32[]{:S(2)}) %all-to-all-start) | async-done | bytes 655392 | tf_op jit(solution)/shard_map/all_to_all | solution.py:221
  58.6 9.2 %all-to-all-start.1 = ((bf16[64,40,128]{2,1,0:T(8,128)(2,1)}), bf16[64,40,128]{2,1,0:T(8,128)(2,1)S(1)}, u32[]{:S(2)}, u32[]{:S(2)}) async-start(bf16[64,40,128]{2,1,0:T(8,128)(2,1)} %bitcast.33), calls=%async_computation.1 | async-start | bytes 1310720 | tf_op jit(solution)/shard_map/all_to_all | solution.py:221
  67.9 3.2 %collective-permute-start.3 = (bf16[4,320,128]{2,1,0:T(8,128)(2,1)S(1)}, bf16[4,320,128]{2,1,0:T(8,128)(2,1)S(1)}, u32[]{:S(2)}, u32[]{:S(2)}) collective-permute-start(bf16[4,320,128]{2,1,0:T(8,128)(2,1)S(1)} %get-tuple-element.57), channel_id=1, source_target_pairs={{0,4},{4,8},{8,12},{12,0},{1,5},{5,9},{9,13},{13,1},{2,6},{6,10},{... | collective-permute-start | bytes 983048 | tf_op jit(solution)/shard_map/ppermute | solution.py:188
  71.1 3.4 %collective-permute-start.1 = (bf16[4,2,320,128]{3,2,1,0:T(8,128)(2,1)S(1)}, bf16[4,2,320,128]{3,2,1,0:T(8,128)(2,1)S(1)}, u32[]{:S(2)}, u32[]{:S(2)}) collective-permute-start(bf16[4,2,320,128]{3,2,1,0:T(8,128)(2,1)S(1)} %bitcast.27), channel_id=1, source_target_pairs={{0,12},{4,0},{8,4},{12,8},{1,13},{5,1},{9,5},{13,9},{2,14},{6,2},{... | collective-permute-start | bytes 1966088 | tf_op jit(solution)/shard_map/ppermute | solution.py:188
  74.5 0.7 collective-permute-start.5
  75.2 4.0 %collective-permute-done.3 = bf16[4,320,128]{2,1,0:T(8,128)(2,1)S(1)} collective-permute-done((bf16[4,320,128]{2,1,0:T(8,128)(2,1)S(1)}, bf16[4,320,128]{2,1,0:T(8,128)(2,1)S(1)}, u32[]{:S(2)}, u32[]{:S(2)}) %collective-permute-start.3) | collective-permute-done | bytes 327712 | tf_op jit(solution)/shard_map/ppermute | solution.py:188
  79.1 1.9 %collective-permute-start.4 = (bf16[4,320,128]{2,1,0:T(8,128)(2,1)S(1)}, bf16[4,320,128]{2,1,0:T(8,128)(2,1)S(1)}, u32[]{:S(2)}, u32[]{:S(2)}) collective-permute-start(bf16[4,320,128]{2,1,0:T(8,128)(2,1)S(1)} %collective-permute-done.3), channel_id=1, source_target_pairs={{0,4},{4,8},{8,12},{12,0},{1,5},{5,9},{9,13},{13,1},{2,6},{6,10},{... | collective-permute-start | bytes 983048 | tf_op jit(solution)/shard_map/ppermute | solution.py:188
  81.1 4.2 %collective-permute-start = (bf16[4,2,320,128]{3,2,1,0:T(8,128)(2,1)S(1)}, bf16[4,2,320,128]{3,2,1,0:T(8,128)(2,1)S(1)}, u32[]{:S(2)}, u32[]{:S(2)}) collective-permute-start(bf16[4,2,320,128]{3,2,1,0:T(8,128)(2,1)S(1)} %bitcast.28), channel_id=1, source_target_pairs={{0,1},{1,0},{2,3},{3,2},{4,5},{5,4},{6,7},{7,6},{8,9},{9,8},{10,11... | collective-permute-start | bytes 1966088 | tf_op jit(solution)/shard_map/ppermute | solution.py:188
  85.3 0.0 collective-permute-done.5
  85.3 4.1 %collective-permute-done.4 = bf16[4,320,128]{2,1,0:T(8,128)(2,1)S(1)} collective-permute-done((bf16[4,320,128]{2,1,0:T(8,128)(2,1)S(1)}, bf16[4,320,128]{2,1,0:T(8,128)(2,1)S(1)}, u32[]{:S(2)}, u32[]{:S(2)}) %collective-permute-start.4) | collective-permute-done | bytes 327712 | tf_op jit(solution)/shard_map/ppermute | solution.py:188
  89.4 0.1 pad_maximum_fusion.refs_4_
  89.5 4.9 %collective-permute-start.6 = (bf16[4,2,320,128]{3,2,1,0:T(8,128)(2,1)S(1)}, bf16[4,2,320,128]{3,2,1,0:T(8,128)(2,1)S(1)}, u32[]{:S(2)}, u32[]{:S(2)}) collective-permute-start(bf16[4,2,320,128]{3,2,1,0:T(8,128)(2,1)S(1)} %pad_maximum_fusion.refs_4_), channel_id=1, source_target_pairs={{0,1},{1,0},{2,3},{3,2},{4,5},{5,4},{6,7},{7,6},{8,9},{9,8},{10,11... | collective-permute-start | bytes 1966088 | tf_op jit(solution)/shard_map/ppermute | solution.py:188
  94.3 0.0 collective-permute-done.1.refs_2_
  94.4 1.9 %collective-permute-start.2 = (bf16[4,2,320,128]{3,2,1,0:T(8,128)(2,1)S(1)}, bf16[4,2,320,128]{3,2,1,0:T(8,128)(2,1)S(1)}, u32[]{:S(2)}, u32[]{:S(2)}) collective-permute-start(bf16[4,2,320,128]{3,2,1,0:T(8,128)(2,1)S(1)} %collective-permute-done.1.refs_2_), channel_id=1, source_target_pairs={{0,1},{1,0},{2,3},{3,2},{4,5},{5,4},{6,7},{7,6},{8,9},{9,8},{10,11... | collective-permute-start | bytes 1966088 | tf_op jit(solution)/shard_map/ppermute | solution.py:188
  96.3 0.0 collective-permute-done.refs_1_
  96.3 0.0 collective-permute-done.6.refs_5_
  96.3 0.0 copy-start
  96.3 0.8 copy-done
  97.2 1.2 collective-permute-done.2.refs_3_
  98.4 0.9 copy-done.2
  99.2 2.9 %all-to-all-done.1 = bf16[64,40,128]{2,1,0:T(8,128)(2,1)S(1)} async-done(((bf16[64,40,128]{2,1,0:T(8,128)(2,1)}), bf16[64,40,128]{2,1,0:T(8,128)(2,1)S(1)}, u32[]{:S(2)}, u32[]{:S(2)}) %all-to-all-start.1) | async-done | bytes 655392 | tf_op jit(solution)/shard_map/all_to_all | solution.py:221
  102.1 0.9 slice_bitcast_fusion.1
  103.0 3.2 %collective-permute-start.8 = (bf16[4,320,128]{2,1,0:T(8,128)(2,1)}, bf16[4,320,128]{2,1,0:T(8,128)(2,1)}, u32[]{:S(2)}, u32[]{:S(2)}) collective-permute-start(bf16[4,320,128]{2,1,0:T(8,128)(2,1)} %get-tuple-element.55), channel_id=1, source_target_pairs={{0,4},{4,8},{8,12},{12,0},{1,5},{5,9},{9,13},{13,1},{2,6},{6,10},{... | collective-permute-start | bytes 983048 | tf_op jit(solution)/shard_map/ppermute | solution.py:188
  106.2 0.1 pad_add_fusion.where
  106.3 6.3 %collective-permute-start.11 = (bf16[4,2,320,128]{3,2,1,0:T(8,128)(2,1)S(1)}, bf16[4,2,320,128]{3,2,1,0:T(8,128)(2,1)S(1)}, u32[]{:S(2)}, u32[]{:S(2)}) collective-permute-start(bf16[4,2,320,128]{3,2,1,0:T(8,128)(2,1)S(1)} %bitcast.22), channel_id=1, source_target_pairs={{0,1},{1,0},{2,3},{3,2},{4,5},{5,4},{6,7},{7,6},{8,9},{9,8},{10,11... | collective-permute-start | bytes 1966088 | tf_op jit(solution)/shard_map/ppermute | solution.py:188
  112.6 3.3 %collective-permute-start.7 = (bf16[4,2,320,128]{3,2,1,0:T(8,128)(2,1)S(1)}, bf16[4,2,320,128]{3,2,1,0:T(8,128)(2,1)S(1)}, u32[]{:S(2)}, u32[]{:S(2)}) collective-permute-start(bf16[4,2,320,128]{3,2,1,0:T(8,128)(2,1)S(1)} %bitcast.23), channel_id=1, source_target_pairs={{0,12},{4,0},{8,4},{12,8},{1,13},{5,1},{9,5},{13,9},{2,14},{6,2},{... | collective-permute-start | bytes 1966088 | tf_op jit(solution)/shard_map/ppermute | solution.py:188
  115.9 0.9 left.2
  116.8 0.7 collective-permute-start.10
  117.5 0.0 collective-permute-done.8
  117.5 0.9 left.3
  118.4 2.0 %collective-permute-start.9 = (bf16[4,320,128]{2,1,0:T(8,128)(2,1)}, bf16[4,320,128]{2,1,0:T(8,128)(2,1)S(1)}, u32[]{:S(2)}, u32[]{:S(2)}) collective-permute-start(bf16[4,320,128]{2,1,0:T(8,128)(2,1)} %collective-permute-done.8), channel_id=1, source_target_pairs={{0,4},{4,8},{8,12},{12,0},{1,5},{5,9},{9,13},{13,1},{2,6},{6,10},{... | collective-permute-start | bytes 983048 | tf_op jit(solution)/shard_map/ppermute | solution.py:188
  120.4 0.0 copy-done.1
  120.4 2.2 %early.1 = (f32[2,512,256]{2,1,0:T(8,128)S(1)}, f32[2,512,256]{2,1,0:T(8,128)S(1)}, f32[2,512,256]{2,1,0:T(8,128)S(1)}) custom-call(bf16[512,1280]{1,0:T(8,128)(2,1)S(1)} %left.3, bf16[4,2,320,128]{3,2,1,0:T(8,128)(2,1)S(1)} %bitcast.30, bf16[4,2,320,128]{3,2,1,0:T(8,128)(2,1)S(1)} %collective-permute-done.refs_1_, ...), custom_call_target="tpu_custom_call" | custom-call | flops 7000000000 | bytes 12000000 | tf_op jit(solution)/shard_map/early/pallas_call | solution.py:130
  122.6 0.0 collective-permute-done.11.two
  122.6 2.3 %late.3.refs_0_ = f32[2,2,9,128,128]{4,3,2,1,0:T(8,128)} custom-call(s32[2]{0:T(128)S(1)} %pad_add_fusion.where, bf16[512,1280]{1,0:T(8,128)(2,1)S(1)} %left.2, f32[2,512,256]{2,1,0:T(8,128)S(1)} %get-tuple-element.46.begun, bf16[4,2,320,128]{3,2,1,0:T(8,128)(2,1)S(1)} %bitcast.25, bf16[4,2,320,128]{3,2,1,0:T(8,128)(2,1)S(1)} %collective-permute-done.11.two), custom_call_target="tpu_custom_call" | custom-call | flops 2000000000 | bytes 4000000 | tf_op jit(solution)/shard_map/late/pallas_call | solution.py:166
  124.9 0.0 collective-permute-done.10
  124.9 5.7 %collective-permute-done.9 = bf16[4,320,128]{2,1,0:T(8,128)(2,1)S(1)} collective-permute-done((bf16[4,320,128]{2,1,0:T(8,128)(2,1)}, bf16[4,320,128]{2,1,0:T(8,128)(2,1)S(1)}, u32[]{:S(2)}, u32[]{:S(2)}) %collective-permute-start.9) | collective-permute-done | bytes 327712 | tf_op jit(solution)/shard_map/ppermute | solution.py:188
  130.7 0.1 pad_maximum_fusion.1.one
  130.8 0.1 collective-permute-done.7.one
  130.9 2.9 %collective-permute-start.13 = (bf16[4,2,320,128]{3,2,1,0:T(8,128)(2,1)S(1)}, bf16[4,2,320,128]{3,2,1,0:T(8,128)(2,1)S(1)}, u32[]{:S(2)}, u32[]{:S(2)}) collective-permute-start(bf16[4,2,320,128]{3,2,1,0:T(8,128)(2,1)S(1)} %collective-permute-done.7.one), channel_id=1, source_target_pairs={{0,1},{1,0},{2,3},{3,2},{4,5},{5,4},{6,7},{7,6},{8,9},{9,8},{10,11... | collective-permute-start | bytes 1966088 | tf_op jit(solution)/shard_map/ppermute | solution.py:188
  133.8 1.9 %collective-permute-start.12 = (bf16[4,2,320,128]{3,2,1,0:T(8,128)(2,1)S(1)}, bf16[4,2,320,128]{3,2,1,0:T(8,128)(2,1)S(1)}, u32[]{:S(2)}, u32[]{:S(2)}) collective-permute-start(bf16[4,2,320,128]{3,2,1,0:T(8,128)(2,1)S(1)} %pad_maximum_fusion.1.one), channel_id=1, source_target_pairs={{0,1},{1,0},{2,3},{3,2},{4,5},{5,4},{6,7},{7,6},{8,9},{9,8},{10,11... | collective-permute-start | bytes 1966088 | tf_op jit(solution)/shard_map/ppermute | solution.py:188
  135.7 0.0 collective-permute-done.13.two
  135.7 2.4 %late.4.refs_0_ = f32[2,2,9,128,128]{4,3,2,1,0:T(8,128)} custom-call(s32[2]{0:T(128)S(1)} %pad_add_fusion.where, bf16[512,1280]{1,0:T(8,128)(2,1)S(1)} %left.2, f32[2,512,256]{2,1,0:T(8,128)S(1)} %get-tuple-element.52.begun, bf16[4,2,320,128]{3,2,1,0:T(8,128)(2,1)S(1)} %collective-permute-done.7.one, ...), custom_call_target="tpu_custom_call", output_to_operand_aliasing={{}: (5, {})} | custom-call | flops 2000000000 | bytes 4000000 | tf_op jit(solution)/shard_map/late/pallas_call | solution.py:166
  138.1 0.0 collective-permute-done.12.two
  138.2 2.2 %late.5 = f32[2,2,9,128,128]{4,3,2,1,0:T(8,128)} custom-call(s32[2]{0:T(128)S(1)} %pad_add_fusion.where, bf16[512,1280]{1,0:T(8,128)(2,1)S(1)} %left.2, f32[2,512,256]{2,1,0:T(8,128)S(1)} %get-tuple-element.50.begun, bf16[4,2,320,128]{3,2,1,0:T(8,128)(2,1)S(1)} %pad_maximum_fusion.1.one, ...), custom_call_target="tpu_custom_call", output_to_operand_aliasing={{}: (5, {})} | custom-call | flops 2000000000 | bytes 4000000 | tf_op jit(solution)/shard_map/late/pallas_call | solution.py:166
  (5 shorter events, 0.1 us)
Async XLA Ops:
  5.1 53.5 %all-to-all-start = ((bf16[64,40,128]{2,1,0:T(8,128)(2,1)}), bf16[64,40,128]{2,1,0:T(8,128)(2,1)S(1)}, u32[]{:S(2)}, u32[]{:S(2)}) async-start(bf16[64,40,128]{2,1,0:T(8,128)(2,1)} %bitcast.34), calls=%async_computation | async-start | bytes 1310720 | tf_op jit(solution)/shard_map/all_to_all | solution.py:221
  58.6 43.5 %all-to-all-start.1 = ((bf16[64,40,128]{2,1,0:T(8,128)(2,1)}), bf16[64,40,128]{2,1,0:T(8,128)(2,1)S(1)}, u32[]{:S(2)}, u32[]{:S(2)}) async-start(bf16[64,40,128]{2,1,0:T(8,128)(2,1)} %bitcast.33), calls=%async_computation.1 | async-start | bytes 1310720 | tf_op jit(solution)/shard_map/all_to_all | solution.py:221
  67.9 11.2 %collective-permute-start.3 = (bf16[4,320,128]{2,1,0:T(8,128)(2,1)S(1)}, bf16[4,320,128]{2,1,0:T(8,128)(2,1)S(1)}, u32[]{:S(2)}, u32[]{:S(2)}) collective-permute-start(bf16[4,320,128]{2,1,0:T(8,128)(2,1)S(1)} %get-tuple-element.57), channel_id=1, source_target_pairs={{0,4},{4,8},{8,12},{12,0},{1,5},{5,9},{9,13},{13,1},{2,6},{6,10},{... | collective-permute-start | bytes 983048 | tf_op jit(solution)/shard_map/ppermute | solution.py:188
  71.1 23.2 %collective-permute-start.1 = (bf16[4,2,320,128]{3,2,1,0:T(8,128)(2,1)S(1)}, bf16[4,2,320,128]{3,2,1,0:T(8,128)(2,1)S(1)}, u32[]{:S(2)}, u32[]{:S(2)}) collective-permute-start(bf16[4,2,320,128]{3,2,1,0:T(8,128)(2,1)S(1)} %bitcast.27), channel_id=1, source_target_pairs={{0,12},{4,0},{8,4},{12,8},{1,13},{5,1},{9,5},{13,9},{2,14},{6,2},{... | collective-permute-start | bytes 1966088 | tf_op jit(solution)/shard_map/ppermute | solution.py:188
  74.5 10.8 %collective-permute-start.5 = (bf16[4,320,128]{2,1,0:T(8,128)(2,1)S(1)}, bf16[4,320,128]{2,1,0:T(8,128)(2,1)S(1)}, u32[]{:S(2)}, u32[]{:S(2)}) collective-permute-start(bf16[4,320,128]{2,1,0:T(8,128)(2,1)S(1)} %get-tuple-element.58), channel_id=1, source_target_pairs={{2,10},{6,14},{10,2},{14,6},{3,11},{7,15},{11,3},{15,7},{18,26},{2... | collective-permute-start | bytes 983048 | tf_op jit(solution)/shard_map/ppermute | solution.py:194
  79.1 10.2 %collective-permute-start.4 = (bf16[4,320,128]{2,1,0:T(8,128)(2,1)S(1)}, bf16[4,320,128]{2,1,0:T(8,128)(2,1)S(1)}, u32[]{:S(2)}, u32[]{:S(2)}) collective-permute-start(bf16[4,320,128]{2,1,0:T(8,128)(2,1)S(1)} %collective-permute-done.3), channel_id=1, source_target_pairs={{0,4},{4,8},{8,12},{12,0},{1,5},{5,9},{9,13},{13,1},{2,6},{6,10},{... | collective-permute-start | bytes 983048 | tf_op jit(solution)/shard_map/ppermute | solution.py:188
  81.1 15.2 %collective-permute-start = (bf16[4,2,320,128]{3,2,1,0:T(8,128)(2,1)S(1)}, bf16[4,2,320,128]{3,2,1,0:T(8,128)(2,1)S(1)}, u32[]{:S(2)}, u32[]{:S(2)}) collective-permute-start(bf16[4,2,320,128]{3,2,1,0:T(8,128)(2,1)S(1)} %bitcast.28), channel_id=1, source_target_pairs={{0,1},{1,0},{2,3},{3,2},{4,5},{5,4},{6,7},{7,6},{8,9},{9,8},{10,11... | collective-permute-start | bytes 1966088 | tf_op jit(solution)/shard_map/ppermute | solution.py:188
  89.5 6.8 %collective-permute-start.6 = (bf16[4,2,320,128]{3,2,1,0:T(8,128)(2,1)S(1)}, bf16[4,2,320,128]{3,2,1,0:T(8,128)(2,1)S(1)}, u32[]{:S(2)}, u32[]{:S(2)}) collective-permute-start(bf16[4,2,320,128]{3,2,1,0:T(8,128)(2,1)S(1)} %pad_maximum_fusion.refs_4_), channel_id=1, source_target_pairs={{0,1},{1,0},{2,3},{3,2},{4,5},{5,4},{6,7},{7,6},{8,9},{9,8},{10,11... | collective-permute-start | bytes 1966088 | tf_op jit(solution)/shard_map/ppermute | solution.py:188
  94.4 4.0 %collective-permute-start.2 = (bf16[4,2,320,128]{3,2,1,0:T(8,128)(2,1)S(1)}, bf16[4,2,320,128]{3,2,1,0:T(8,128)(2,1)S(1)}, u32[]{:S(2)}, u32[]{:S(2)}) collective-permute-start(bf16[4,2,320,128]{3,2,1,0:T(8,128)(2,1)S(1)} %collective-permute-done.1.refs_2_), channel_id=1, source_target_pairs={{0,1},{1,0},{2,3},{3,2},{4,5},{5,4},{6,7},{7,6},{8,9},{9,8},{10,11... | collective-permute-start | bytes 1966088 | tf_op jit(solution)/shard_map/ppermute | solution.py:188
  96.3 0.9 copy-start
  98.4 0.9 copy-start.2
  103.0 14.5 %collective-permute-start.8 = (bf16[4,320,128]{2,1,0:T(8,128)(2,1)}, bf16[4,320,128]{2,1,0:T(8,128)(2,1)}, u32[]{:S(2)}, u32[]{:S(2)}) collective-permute-start(bf16[4,320,128]{2,1,0:T(8,128)(2,1)} %get-tuple-element.55), channel_id=1, source_target_pairs={{0,4},{4,8},{8,12},{12,0},{1,5},{5,9},{9,13},{13,1},{2,6},{6,10},{... | collective-permute-start | bytes 983048 | tf_op jit(solution)/shard_map/ppermute | solution.py:188
  106.2 14.2 %copy-start.1 = (bf16[4,2,320,128]{3,2,1,0:T(8,128)(2,1)S(1)}, bf16[4,2,320,128]{3,2,1,0:T(8,128)(2,1)}, u32[]{:S(2)}) copy-start(bf16[4,2,320,128]{3,2,1,0:T(8,128)(2,1)} %copy-done) | copy-start | bytes 1966084
  106.2 14.2 %copy-start.3 = (bf16[4,2,320,128]{3,2,1,0:T(8,128)(2,1)S(1)}, bf16[4,2,320,128]{3,2,1,0:T(8,128)(2,1)}, u32[]{:S(2)}) copy-start(bf16[4,2,320,128]{3,2,1,0:T(8,128)(2,1)} %copy-done.2) | copy-start | bytes 1966084
  106.3 16.3 %collective-permute-start.11 = (bf16[4,2,320,128]{3,2,1,0:T(8,128)(2,1)S(1)}, bf16[4,2,320,128]{3,2,1,0:T(8,128)(2,1)S(1)}, u32[]{:S(2)}, u32[]{:S(2)}) collective-permute-start(bf16[4,2,320,128]{3,2,1,0:T(8,128)(2,1)S(1)} %bitcast.22), channel_id=1, source_target_pairs={{0,1},{1,0},{2,3},{3,2},{4,5},{5,4},{6,7},{7,6},{8,9},{9,8},{10,11... | collective-permute-start | bytes 1966088 | tf_op jit(solution)/shard_map/ppermute | solution.py:188
  112.6 18.2 %collective-permute-start.7 = (bf16[4,2,320,128]{3,2,1,0:T(8,128)(2,1)S(1)}, bf16[4,2,320,128]{3,2,1,0:T(8,128)(2,1)S(1)}, u32[]{:S(2)}, u32[]{:S(2)}) collective-permute-start(bf16[4,2,320,128]{3,2,1,0:T(8,128)(2,1)S(1)} %bitcast.23), channel_id=1, source_target_pairs={{0,12},{4,0},{8,4},{12,8},{1,13},{5,1},{9,5},{13,9},{2,14},{6,2},{... | collective-permute-start | bytes 1966088 | tf_op jit(solution)/shard_map/ppermute | solution.py:188
  116.8 8.2 %collective-permute-start.10 = (bf16[4,320,128]{2,1,0:T(8,128)(2,1)}, bf16[4,320,128]{2,1,0:T(8,128)(2,1)S(1)}, u32[]{:S(2)}, u32[]{:S(2)}) collective-permute-start(bf16[4,320,128]{2,1,0:T(8,128)(2,1)} %get-tuple-element.56), channel_id=1, source_target_pairs={{2,10},{6,14},{10,2},{14,6},{3,11},{7,15},{11,3},{15,7},{18,26},{2... | collective-permute-start | bytes 983048 | tf_op jit(solution)/shard_map/ppermute | solution.py:194
  118.4 12.3 %collective-permute-start.9 = (bf16[4,320,128]{2,1,0:T(8,128)(2,1)}, bf16[4,320,128]{2,1,0:T(8,128)(2,1)S(1)}, u32[]{:S(2)}, u32[]{:S(2)}) collective-permute-start(bf16[4,320,128]{2,1,0:T(8,128)(2,1)} %collective-permute-done.8), channel_id=1, source_target_pairs={{0,4},{4,8},{8,12},{12,0},{1,5},{5,9},{9,13},{13,1},{2,6},{6,10},{... | collective-permute-start | bytes 983048 | tf_op jit(solution)/shard_map/ppermute | solution.py:188
  130.9 4.8 %collective-permute-start.13 = (bf16[4,2,320,128]{3,2,1,0:T(8,128)(2,1)S(1)}, bf16[4,2,320,128]{3,2,1,0:T(8,128)(2,1)S(1)}, u32[]{:S(2)}, u32[]{:S(2)}) collective-permute-start(bf16[4,2,320,128]{3,2,1,0:T(8,128)(2,1)S(1)} %collective-permute-done.7.one), channel_id=1, source_target_pairs={{0,1},{1,0},{2,3},{3,2},{4,5},{5,4},{6,7},{7,6},{8,9},{9,8},{10,11... | collective-permute-start | bytes 1966088 | tf_op jit(solution)/shard_map/ppermute | solution.py:188
  133.8 4.4 %collective-permute-start.12 = (bf16[4,2,320,128]{3,2,1,0:T(8,128)(2,1)S(1)}, bf16[4,2,320,128]{3,2,1,0:T(8,128)(2,1)S(1)}, u32[]{:S(2)}, u32[]{:S(2)}) collective-permute-start(bf16[4,2,320,128]{3,2,1,0:T(8,128)(2,1)S(1)} %pad_maximum_fusion.1.one), channel_id=1, source_target_pairs={{0,1},{1,0},{2,3},{3,2},{4,5},{5,4},{6,7},{7,6},{8,9},{9,8},{10,11... | collective-permute-start | bytes 1966088 | tf_op jit(solution)/shard_map/ppermute | solution.py:188

commit v8 on v7

--- a/solution.py
+++ b/solution.py
@@ -132,7 +132,7 @@
         in_specs=[whole] * 7,
         out_specs=[whole] * 3,
         out_shape=[jax.ShapeDtypeStruct((2, 4 * CH, 2 * CH), jnp.float32)] * 3,
-        cost_estimate=pl.CostEstimate(flops=7 * 10**9, transcendentals=0, bytes_accessed=12 * 10**6),
+        cost_estimate=pl.CostEstimate(flops=20 * 10**9, transcendentals=0, bytes_accessed=12 * 10**6),
         compiler_params=grant(24),
         name="early",
     )(left, *data)
@@ -177,7 +177,7 @@
         out_shape=jax.ShapeDtypeStruct((2, 2, NOFF, CH, CH), jnp.float32),
         input_output_aliases={5: 0} if extra else {},
         scratch_shapes=[pltpu.VMEM((4, 2, 2, CH, CH), jnp.float32), pltpu.SemaphoreType.DMA((4,))],
-        cost_estimate=pl.CostEstimate(flops=2 * 10**9, transcendentals=0, bytes_accessed=4 * 10**6),
+        cost_estimate=pl.CostEstimate(flops=4 * 10**9, transcendentals=0, bytes_accessed=4 * 10**6),
         compiler_params=grant(16),
         name="late",
     )(where, left, begun, one, two, *extra)
@@ -196,8 +196,9 @@
 
 def fetched(here, held):
     ahead1 = shifted(here, "y", -1)
-    low, *held = lax.optimization_barrier((shifted(here[:, 0], "y", 1), *held))
-    return [here, ahead1, jnp.stack([shifted(low, "y", 1), upper(here[:, 1], 2)], axis=1)], held
+    high = upper(here[:, 1], 2)
+    low, here, *held = lax.optimization_barrier((shifted(here[:, 0], "y", 1), here, *held))
+    return [here, ahead1, (shifted(low, "y", 1), high)], held
 
 
 def both(own):
@@ -223,19 +224,18 @@
 
     first, second = spread(made(0, CHUNKS[0])), made(*CHUNKS)
     first, second = lax.optimization_barrier((first, second))
-    head = both(fetched(first, [])[0])
+    (first, ahead1, ahead2), _ = fetched(first, [])
+    head = both([first, ahead1, jnp.stack(ahead2, axis=1)])
     tail = spread(second)
     tail, *head = lax.optimization_barrier((tail, *head))
-    (_, ahead1, ahead2), head = fetched(tail, head)
+    (tail, ahead1, ahead2), head = fetched(tail, head)
     begun = early(left_of(where, head[0]), head)
     left = left_of(where, tail)
     filled = late(where, left, begun[0], tail, shifted(tail, "core", 1), None, 0, scale)
-    ahead1, ahead2, left, filled, *begun = lax.optimization_barrier((ahead1, ahead2, left, filled, *begun))
-    data = both([ahead1, ahead2])
-    for ahead in (1, 2):
-        one, two = data[2 * ahead - 2 : 2 * ahead]
-        filled = late(where, left, begun[ahead], one, two, filled, ahead, scale)
-    return filled
+    filled = late(where, left, begun[1], ahead1, shifted(ahead1, "core", 1), filled, 1, scale)
+    ahead2, filled = lax.optimization_barrier((ahead2, filled))
+    ahead2 = jnp.stack(ahead2, axis=1)
+    return late(where, left, begun[2], ahead2, shifted(ahead2, "core", 1), filled, 2, scale)
 
 
 def solution(mesh):

time: 142 us -> 149 us (1.049)
  the two profiles are of different devices: /device:TPU:1 before, /device:TPU:263 now
where the time goes in v8:
time: 149 us
  starting transfers between devices  70.6 us (47%)
  waiting for transfers between devices  53.2 us (36%)
  Pallas kernels  21.6 us (14%)
  local copies, waits for them, and re-layouts  2.64 us (2%)
    ppermute x12, starting transfers between devices, shifted(): lax.ppermute(value, axis, [(s, (s + steps) % count) for s in range(count)])  34.1 us
    all_to_all x2, starting transfers between devices, spread(): here = lax.all_to_all(sent, ('x', 'z_hi', 'z_lo'), 0, 0, tiled=True)  29.6 us
    ppermute x12, waiting for transfers between devices, shifted(): lax.ppermute(value, axis, [(s, (s + steps) % count) for s in range(count)])  27.2 us
    all_to_all x2, waiting for transfers between devices, spread(): here = lax.all_to_all(sent, ('x', 'z_hi', 'z_lo'), 0, 0, tiled=True)  23.7 us
    pallas_call x2, Pallas kernels, spectra(): pl.pallas_call(functools.partial(spectra_body, first=first, count=count,...  10.1 us
    pallas_call x3, Pallas kernels, late(): pl.pallas_call(functools.partial(late_body, ahead=ahead, scale=scale), in...  7.54 us
    ppermute x2, starting transfers between devices, upper(): return lax.ppermute(value, ('y', 'z_hi'), pairs)  6.87 us
  transfers between devices with their start and end apart: 16, of which 8 were waited for; matrix products, arithmetic and copies ran while one was open for 1% of the time, Pallas kernels for 10%

profile of v8, /device:TPU:263, one launch (start us, length us, event | category | flops | bytes accessed | tf_op | source)
XLA Modules:
  0.0 148.6 jit_solution(2266516646939821178)
XLA Ops:
  0.0 5.1 %spectra.2 = bf16[4,2,320,128]{3,2,1,0:T(8,128)(2,1)} custom-call(bf16[20,128,512]{2,1,0:T(8,128)(2,1)} %bitcast.31, s32[20,128]{1,0:T(8,128)} %bitcast.39, s32[1,128]{1,0:T(1,128)} %order.3, bf16[128,512]{1,0:T(8,128)(2,1)} %constant.8.clone.basis, f32[1,64]{1,0:T(1,128)} %bitcast.41), custom_call_target="tpu_custom_call" | custom-call | tf_op jit(solution)/shard_map/spectra/pallas_call | solution.py:76
  5.1 14.7 %all-to-all-start = ((bf16[64,40,128]{2,1,0:T(8,128)(2,1)}), bf16[64,40,128]{2,1,0:T(8,128)(2,1)S(1)}, u32[]{:S(2)}, u32[]{:S(2)}) async-start(bf16[64,40,128]{2,1,0:T(8,128)(2,1)} %bitcast.34), calls=%async_computation | async-start | bytes 1310720 | tf_op jit(solution)/shard_map/all_to_all | solution.py:222
  19.7 5.0 %spectra.3 = bf16[4,2,320,128]{3,2,1,0:T(8,128)(2,1)} custom-call(bf16[20,128,512]{2,1,0:T(8,128)(2,1)} %bitcast.32, s32[20,128]{1,0:T(8,128)} %bitcast.40, s32[1,128]{1,0:T(1,128)} %order.3, bf16[128,512]{1,0:T(8,128)(2,1)} %constant.8.clone.basis, f32[1,64]{1,0:T(1,128)} %bitcast.42), custom_call_target="tpu_custom_call" | custom-call | tf_op jit(solution)/shard_map/spectra/pallas_call | solution.py:76
  24.8 23.7 %all-to-all-done = bf16[64,40,128]{2,1,0:T(8,128)(2,1)S(1)} async-done(((bf16[64,40,128]{2,1,0:T(8,128)(2,1)}), bf16[64,40,128]{2,1,0:T(8,128)(2,1)S(1)}, u32[]{:S(2)}, u32[]{:S(2)}) %all-to-all-start) | async-done | bytes 655392 | tf_op jit(solution)/shard_map/all_to_all | solution.py:222
  48.4 14.9 %all-to-all-start.1 = ((bf16[64,40,128]{2,1,0:T(8,128)(2,1)}), bf16[64,40,128]{2,1,0:T(8,128)(2,1)S(1)}, u32[]{:S(2)}, u32[]{:S(2)}) async-start(bf16[64,40,128]{2,1,0:T(8,128)(2,1)} %bitcast.33), calls=%async_computation.1 | async-start | bytes 1310720 | tf_op jit(solution)/shard_map/all_to_all | solution.py:222
  63.4 3.2 %collective-permute-start = (bf16[4,320,128]{2,1,0:T(8,128)(2,1)S(1)}, bf16[4,320,128]{2,1,0:T(8,128)(2,1)S(1)}, u32[]{:S(2)}, u32[]{:S(2)}) collective-permute-start(bf16[4,320,128]{2,1,0:T(8,128)(2,1)S(1)} %get-tuple-element.58), channel_id=1, source_target_pairs={{0,4},{4,8},{8,12},{12,0},{1,5},{5,9},{9,13},{13,1},{2,6},{6,10},{... | collective-permute-start | bytes 983048 | tf_op jit(solution)/shard_map/ppermute | solution.py:188
  66.7 3.4 %collective-permute-start.2 = (bf16[4,2,320,128]{3,2,1,0:T(8,128)(2,1)S(1)}, bf16[4,2,320,128]{3,2,1,0:T(8,128)(2,1)S(1)}, u32[]{:S(2)}, u32[]{:S(2)}) collective-permute-start(bf16[4,2,320,128]{3,2,1,0:T(8,128)(2,1)S(1)} %bitcast.22), channel_id=1, source_target_pairs={{0,12},{4,0},{8,4},{12,8},{1,13},{5,1},{9,5},{13,9},{2,14},{6,2},{... | collective-permute-start | bytes 1966088 | tf_op jit(solution)/shard_map/ppermute | solution.py:188
  70.0 3.5 %collective-permute-start.5 = (bf16[4,320,128]{2,1,0:T(8,128)(2,1)S(1)}, bf16[4,320,128]{2,1,0:T(8,128)(2,1)S(1)}, u32[]{:S(2)}, u32[]{:S(2)}) collective-permute-start(bf16[4,320,128]{2,1,0:T(8,128)(2,1)S(1)} %get-tuple-element.57), channel_id=1, source_target_pairs={{2,10},{6,14},{10,2},{14,6},{3,11},{7,15},{11,3},{15,7},{18,26},{2... | collective-permute-start | bytes 983048 | tf_op jit(solution)/shard_map/ppermute | solution.py:194
  73.6 0.8 collective-permute-done
  74.4 1.9 %collective-permute-start.4 = (bf16[4,320,128]{2,1,0:T(8,128)(2,1)S(1)}, bf16[4,320,128]{2,1,0:T(8,128)(2,1)S(1)}, u32[]{:S(2)}, u32[]{:S(2)}) collective-permute-start(bf16[4,320,128]{2,1,0:T(8,128)(2,1)S(1)} %collective-permute-done), channel_id=1, source_target_pairs={{0,4},{4,8},{8,12},{12,0},{1,5},{5,9},{9,13},{13,1},{2,6},{6,10},{... | collective-permute-start | bytes 983048 | tf_op jit(solution)/shard_map/ppermute | solution.py:188
  76.3 4.6 %collective-permute-start.1 = (bf16[4,2,320,128]{3,2,1,0:T(8,128)(2,1)S(1)}, bf16[4,2,320,128]{3,2,1,0:T(8,128)(2,1)S(1)}, u32[]{:S(2)}, u32[]{:S(2)}) collective-permute-start(bf16[4,2,320,128]{3,2,1,0:T(8,128)(2,1)S(1)} %bitcast.23), channel_id=1, source_target_pairs={{0,1},{1,0},{2,3},{3,2},{4,5},{5,4},{6,7},{7,6},{8,9},{9,8},{10,11... | collective-permute-start | bytes 1966088 | tf_op jit(solution)/shard_map/ppermute | solution.py:188
  80.9 2.4 %collective-permute-done.5 = bf16[4,320,128]{2,1,0:T(8,128)(2,1)S(1)} collective-permute-done((bf16[4,320,128]{2,1,0:T(8,128)(2,1)S(1)}, bf16[4,320,128]{2,1,0:T(8,128)(2,1)S(1)}, u32[]{:S(2)}, u32[]{:S(2)}) %collective-permute-start.5) | collective-permute-done | bytes 327712 | tf_op jit(solution)/shard_map/ppermute | solution.py:194
  83.3 8.2 %collective-permute-done.4 = bf16[4,320,128]{2,1,0:T(8,128)(2,1)S(1)} collective-permute-done((bf16[4,320,128]{2,1,0:T(8,128)(2,1)S(1)}, bf16[4,320,128]{2,1,0:T(8,128)(2,1)S(1)}, u32[]{:S(2)}, u32[]{:S(2)}) %collective-permute-start.4) | collective-permute-done | bytes 327712 | tf_op jit(solution)/shard_map/ppermute | solution.py:188
  91.5 0.1 pad_maximum_fusion.refs_4_
  91.5 2.4 %collective-permute-start.6 = (bf16[4,2,320,128]{3,2,1,0:T(8,128)(2,1)S(1)}, bf16[4,2,320,128]{3,2,1,0:T(8,128)(2,1)S(1)}, u32[]{:S(2)}, u32[]{:S(2)}) collective-permute-start(bf16[4,2,320,128]{3,2,1,0:T(8,128)(2,1)S(1)} %pad_maximum_fusion.refs_4_), channel_id=1, source_target_pairs={{0,1},{1,0},{2,3},{3,2},{4,5},{5,4},{6,7},{7,6},{8,9},{9,8},{10,11... | collective-permute-start | bytes 1966088 | tf_op jit(solution)/shard_map/ppermute | solution.py:188
  93.9 0.0 collective-permute-done.2.refs_2_
  93.9 1.9 %collective-permute-start.3 = (bf16[4,2,320,128]{3,2,1,0:T(8,128)(2,1)S(1)}, bf16[4,2,320,128]{3,2,1,0:T(8,128)(2,1)S(1)}, u32[]{:S(2)}, u32[]{:S(2)}) collective-permute-start(bf16[4,2,320,128]{3,2,1,0:T(8,128)(2,1)S(1)} %collective-permute-done.2.refs_2_), channel_id=1, source_target_pairs={{0,1},{1,0},{2,3},{3,2},{4,5},{5,4},{6,7},{7,6},{8,9},{9,8},{10,11... | collective-permute-start | bytes 1966088 | tf_op jit(solution)/shard_map/ppermute | solution.py:188
  95.9 0.0 collective-permute-done.1.refs_1_
  95.9 0.0 collective-permute-done.6.refs_5_
  95.9 0.8 copy-done
  96.8 1.2 collective-permute-done.3.refs_3_
  97.9 0.9 copy-done.2
  98.8 0.0 all-to-all-done.1
  98.8 5.2 %collective-permute-start.10 = (bf16[4,2,320,128]{3,2,1,0:T(8,128)(2,1)S(1)}, bf16[4,2,320,128]{3,2,1,0:T(8,128)(2,1)}, u32[]{:S(2)}, u32[]{:S(2)}) collective-permute-start(bf16[4,2,320,128]{3,2,1,0:T(8,128)(2,1)S(1)} %bitcast.26), channel_id=1, source_target_pairs={{0,12},{4,0},{8,4},{12,8},{1,13},{5,1},{9,5},{13,9},{2,14},{6,2},{... | collective-permute-start | bytes 1966088 | tf_op jit(solution)/shard_map/ppermute | solution.py:188
  104.0 0.9 slice_bitcast_fusion
  104.9 1.9 %collective-permute-start.7 = (bf16[4,320,128]{2,1,0:T(8,128)(2,1)}, bf16[4,320,128]{2,1,0:T(8,128)(2,1)}, u32[]{:S(2)}, u32[]{:S(2)}) collective-permute-start(bf16[4,320,128]{2,1,0:T(8,128)(2,1)} %get-tuple-element.56), channel_id=1, source_target_pairs={{0,4},{4,8},{8,12},{12,0},{1,5},{5,9},{9,13},{13,1},{2,6},{6,10},{... | collective-permute-start | bytes 983048 | tf_op jit(solution)/shard_map/ppermute | solution.py:188
  106.8 0.0 copy-start.1
  106.8 0.0 copy-start.3
  106.8 0.1 pad_add_fusion.where
  106.9 3.3 %collective-permute-start.9 = (bf16[4,320,128]{2,1,0:T(8,128)(2,1)}, bf16[4,320,128]{2,1,0:T(8,128)(2,1)S(1)}, u32[]{:S(2)}, u32[]{:S(2)}) collective-permute-start(bf16[4,320,128]{2,1,0:T(8,128)(2,1)} %get-tuple-element.55), channel_id=1, source_target_pairs={{2,10},{6,14},{10,2},{14,6},{3,11},{7,15},{11,3},{15,7},{18,26},{2... | collective-permute-start | bytes 983048 | tf_op jit(solution)/shard_map/ppermute | solution.py:194
  110.2 13.9 %collective-permute-done.7 = bf16[4,320,128]{2,1,0:T(8,128)(2,1)} collective-permute-done((bf16[4,320,128]{2,1,0:T(8,128)(2,1)}, bf16[4,320,128]{2,1,0:T(8,128)(2,1)}, u32[]{:S(2)}, u32[]{:S(2)}) %collective-permute-start.7) | collective-permute-done | bytes 327712 | tf_op jit(solution)/shard_map/ppermute | solution.py:188
  124.1 3.2 %collective-permute-start.12 = (bf16[4,2,320,128]{3,2,1,0:T(8,128)(2,1)S(1)}, bf16[4,2,320,128]{3,2,1,0:T(8,128)(2,1)S(1)}, u32[]{:S(2)}, u32[]{:S(2)}) collective-permute-start(bf16[4,2,320,128]{3,2,1,0:T(8,128)(2,1)S(1)} %bitcast.28), channel_id=1, source_target_pairs={{0,1},{1,0},{2,3},{3,2},{4,5},{5,4},{6,7},{7,6},{8,9},{9,8},{10,11... | collective-permute-start | bytes 1966088 | tf_op jit(solution)/shard_map/ppermute | solution.py:188
  127.3 0.9 left.2
  128.2 0.9 left.3
  129.1 1.9 %collective-permute-start.8 = (bf16[4,320,128]{2,1,0:T(8,128)(2,1)}, bf16[4,320,128]{2,1,0:T(8,128)(2,1)S(1)}, u32[]{:S(2)}, u32[]{:S(2)}) collective-permute-start(bf16[4,320,128]{2,1,0:T(8,128)(2,1)} %collective-permute-done.7), channel_id=1, source_target_pairs={{0,4},{4,8},{8,12},{12,0},{1,5},{5,9},{9,13},{13,1},{2,6},{6,10},{... | collective-permute-start | bytes 983048 | tf_op jit(solution)/shard_map/ppermute | solution.py:188
  131.0 0.0 collective-permute-done.10.one
  131.0 1.9 %collective-permute-start.11 = (bf16[4,2,320,128]{3,2,1,0:T(8,128)(2,1)}, bf16[4,2,320,128]{3,2,1,0:T(8,128)(2,1)S(1)}, u32[]{:S(2)}, u32[]{:S(2)}) collective-permute-start(bf16[4,2,320,128]{3,2,1,0:T(8,128)(2,1)} %collective-permute-done.10.one), channel_id=1, source_target_pairs={{0,1},{1,0},{2,3},{3,2},{4,5},{5,4},{6,7},{7,6},{8,9},{9,8},{10,11... | collective-permute-start | bytes 1966088 | tf_op jit(solution)/shard_map/ppermute | solution.py:188
  132.9 2.2 %early.1 = (f32[2,512,256]{2,1,0:T(8,128)S(1)}, f32[2,512,256]{2,1,0:T(8,128)S(1)}, f32[2,512,256]{2,1,0:T(8,128)S(1)}) custom-call(bf16[512,1280]{1,0:T(8,128)(2,1)S(1)} %left.3, bf16[4,2,320,128]{3,2,1,0:T(8,128)(2,1)S(1)} %bitcast.25, bf16[4,2,320,128]{3,2,1,0:T(8,128)(2,1)S(1)} %collective-permute-done.1.refs_1_, ...), custom_call_target="tpu_custom_call" | custom-call | flops 20000000000 | bytes 12000000 | tf_op jit(solution)/shard_map/early/pallas_call | solution.py:130
  135.2 0.0 collective-permute-done.12.two
  135.2 2.2 %late.3.refs_0_ = f32[2,2,9,128,128]{4,3,2,1,0:T(8,128)} custom-call(s32[2]{0:T(128)S(1)} %pad_add_fusion.where, bf16[512,1280]{1,0:T(8,128)(2,1)S(1)} %left.2, f32[2,512,256]{2,1,0:T(8,128)S(1)} %get-tuple-element.51.begun, bf16[4,2,320,128]{3,2,1,0:T(8,128)(2,1)S(1)} %bitcast.30, bf16[4,2,320,128]{3,2,1,0:T(8,128)(2,1)S(1)} %collective-permute-done.12.two), custom_call_target="tpu_custom_call" | custom-call | flops 4000000000 | bytes 4000000 | tf_op jit(solution)/shard_map/late/pallas_call | solution.py:166
  137.4 0.0 collective-permute-done.11.two
  137.4 3.0 %late.4.refs_0_ = f32[2,2,9,128,128]{4,3,2,1,0:T(8,128)} custom-call(s32[2]{0:T(128)S(1)} %pad_add_fusion.where, bf16[512,1280]{1,0:T(8,128)(2,1)S(1)} %left.2, f32[2,512,256]{2,1,0:T(8,128)S(1)} %get-tuple-element.50.begun, bf16[4,2,320,128]{3,2,1,0:T(8,128)(2,1)} %collective-permute-done.10.one, ...), custom_call_target="tpu_custom_call", output_to_operand_aliasing={{}: (5, {})} | custom-call | flops 4000000000 | bytes 4000000 | tf_op jit(solution)/shard_map/late/pallas_call | solution.py:166
  140.3 0.0 collective-permute-done.9
  140.3 1.4 collective-permute-done.8
  141.7 0.1 pad_maximum_fusion.1.one
  141.8 2.7 %collective-permute-start.13 = (bf16[4,2,320,128]{3,2,1,0:T(8,128)(2,1)S(1)}, bf16[4,2,320,128]{3,2,1,0:T(8,128)(2,1)S(1)}, u32[]{:S(2)}, u32[]{:S(2)}) collective-permute-start(bf16[4,2,320,128]{3,2,1,0:T(8,128)(2,1)S(1)} %pad_maximum_fusion.1.one), channel_id=1, source_target_pairs={{0,1},{1,0},{2,3},{3,2},{4,5},{5,4},{6,7},{7,6},{8,9},{9,8},{10,11... | collective-permute-start | bytes 1966088 | tf_op jit(solution)/shard_map/ppermute | solution.py:188
  144.5 1.7 %collective-permute-done.13.two = bf16[4,2,320,128]{3,2,1,0:T(8,128)(2,1)S(1)} collective-permute-done((bf16[4,2,320,128]{3,2,1,0:T(8,128)(2,1)S(1)}, bf16[4,2,320,128]{3,2,1,0:T(8,128)(2,1)S(1)}, u32[]{:S(2)}, u32[]{:S(2)}) %collective-permute-start.13) | collective-permute-done | bytes 655392 | tf_op jit(solution)/shard_map/ppermute | solution.py:188
  146.2 2.4 %late.5 = f32[2,2,9,128,128]{4,3,2,1,0:T(8,128)} custom-call(s32[2]{0:T(128)S(1)} %pad_add_fusion.where, bf16[512,1280]{1,0:T(8,128)(2,1)S(1)} %left.2, f32[2,512,256]{2,1,0:T(8,128)S(1)} %get-tuple-element.48.begun, bf16[4,2,320,128]{3,2,1,0:T(8,128)(2,1)S(1)} %pad_maximum_fusion.1.one, ...), custom_call_target="tpu_custom_call", output_to_operand_aliasing={{}: (5, {})} | custom-call | flops 4000000000 | bytes 4000000 | tf_op jit(solution)/shard_map/late/pallas_call | solution.py:166
  (5 shorter events, 0.1 us)
Async XLA Ops:
  5.1 43.4 %all-to-all-start = ((bf16[64,40,128]{2,1,0:T(8,128)(2,1)}), bf16[64,40,128]{2,1,0:T(8,128)(2,1)S(1)}, u32[]{:S(2)}, u32[]{:S(2)}) async-start(bf16[64,40,128]{2,1,0:T(8,128)(2,1)} %bitcast.34), calls=%async_computation | async-start | bytes 1310720 | tf_op jit(solution)/shard_map/all_to_all | solution.py:222
  48.4 50.4 %all-to-all-start.1 = ((bf16[64,40,128]{2,1,0:T(8,128)(2,1)}), bf16[64,40,128]{2,1,0:T(8,128)(2,1)S(1)}, u32[]{:S(2)}, u32[]{:S(2)}) async-start(bf16[64,40,128]{2,1,0:T(8,128)(2,1)} %bitcast.33), calls=%async_computation.1 | async-start | bytes 1310720 | tf_op jit(solution)/shard_map/all_to_all | solution.py:222
  63.4 11.0 %collective-permute-start = (bf16[4,320,128]{2,1,0:T(8,128)(2,1)S(1)}, bf16[4,320,128]{2,1,0:T(8,128)(2,1)S(1)}, u32[]{:S(2)}, u32[]{:S(2)}) collective-permute-start(bf16[4,320,128]{2,1,0:T(8,128)(2,1)S(1)} %get-tuple-element.58), channel_id=1, source_target_pairs={{0,4},{4,8},{8,12},{12,0},{1,5},{5,9},{9,13},{13,1},{2,6},{6,10},{... | collective-permute-start | bytes 983048 | tf_op jit(solution)/shard_map/ppermute | solution.py:188
  66.7 27.3 %collective-permute-start.2 = (bf16[4,2,320,128]{3,2,1,0:T(8,128)(2,1)S(1)}, bf16[4,2,320,128]{3,2,1,0:T(8,128)(2,1)S(1)}, u32[]{:S(2)}, u32[]{:S(2)}) collective-permute-start(bf16[4,2,320,128]{3,2,1,0:T(8,128)(2,1)S(1)} %bitcast.22), channel_id=1, source_target_pairs={{0,12},{4,0},{8,4},{12,8},{1,13},{5,1},{9,5},{13,9},{2,14},{6,2},{... | collective-permute-start | bytes 1966088 | tf_op jit(solution)/shard_map/ppermute | solution.py:188
  70.0 13.2 %collective-permute-start.5 = (bf16[4,320,128]{2,1,0:T(8,128)(2,1)S(1)}, bf16[4,320,128]{2,1,0:T(8,128)(2,1)S(1)}, u32[]{:S(2)}, u32[]{:S(2)}) collective-permute-start(bf16[4,320,128]{2,1,0:T(8,128)(2,1)S(1)} %get-tuple-element.57), channel_id=1, source_target_pairs={{2,10},{6,14},{10,2},{14,6},{3,11},{7,15},{11,3},{15,7},{18,26},{2... | collective-permute-start | bytes 983048 | tf_op jit(solution)/shard_map/ppermute | solution.py:194
  74.4 17.1 %collective-permute-start.4 = (bf16[4,320,128]{2,1,0:T(8,128)(2,1)S(1)}, bf16[4,320,128]{2,1,0:T(8,128)(2,1)S(1)}, u32[]{:S(2)}, u32[]{:S(2)}) collective-permute-start(bf16[4,320,128]{2,1,0:T(8,128)(2,1)S(1)} %collective-permute-done), channel_id=1, source_target_pairs={{0,4},{4,8},{8,12},{12,0},{1,5},{5,9},{9,13},{13,1},{2,6},{6,10},{... | collective-permute-start | bytes 983048 | tf_op jit(solution)/shard_map/ppermute | solution.py:188
  76.3 19.6 %collective-permute-start.1 = (bf16[4,2,320,128]{3,2,1,0:T(8,128)(2,1)S(1)}, bf16[4,2,320,128]{3,2,1,0:T(8,128)(2,1)S(1)}, u32[]{:S(2)}, u32[]{:S(2)}) collective-permute-start(bf16[4,2,320,128]{3,2,1,0:T(8,128)(2,1)S(1)} %bitcast.23), channel_id=1, source_target_pairs={{0,1},{1,0},{2,3},{3,2},{4,5},{5,4},{6,7},{7,6},{8,9},{9,8},{10,11... | collective-permute-start | bytes 1966088 | tf_op jit(solution)/shard_map/ppermute | solution.py:188
  91.5 4.4 %collective-permute-start.6 = (bf16[4,2,320,128]{3,2,1,0:T(8,128)(2,1)S(1)}, bf16[4,2,320,128]{3,2,1,0:T(8,128)(2,1)S(1)}, u32[]{:S(2)}, u32[]{:S(2)}) collective-permute-start(bf16[4,2,320,128]{3,2,1,0:T(8,128)(2,1)S(1)} %pad_maximum_fusion.refs_4_), channel_id=1, source_target_pairs={{0,1},{1,0},{2,3},{3,2},{4,5},{5,4},{6,7},{7,6},{8,9},{9,8},{10,11... | collective-permute-start | bytes 1966088 | tf_op jit(solution)/shard_map/ppermute | solution.py:188
  93.9 4.0 %collective-permute-start.3 = (bf16[4,2,320,128]{3,2,1,0:T(8,128)(2,1)S(1)}, bf16[4,2,320,128]{3,2,1,0:T(8,128)(2,1)S(1)}, u32[]{:S(2)}, u32[]{:S(2)}) collective-permute-start(bf16[4,2,320,128]{3,2,1,0:T(8,128)(2,1)S(1)} %collective-permute-done.2.refs_2_), channel_id=1, source_target_pairs={{0,1},{1,0},{2,3},{3,2},{4,5},{5,4},{6,7},{7,6},{8,9},{9,8},{10,11... | collective-permute-start | bytes 1966088 | tf_op jit(solution)/shard_map/ppermute | solution.py:188
  95.9 0.9 copy-start
  97.9 0.9 copy-start.2
  98.8 32.2 %collective-permute-start.10 = (bf16[4,2,320,128]{3,2,1,0:T(8,128)(2,1)S(1)}, bf16[4,2,320,128]{3,2,1,0:T(8,128)(2,1)}, u32[]{:S(2)}, u32[]{:S(2)}) collective-permute-start(bf16[4,2,320,128]{3,2,1,0:T(8,128)(2,1)S(1)} %bitcast.26), channel_id=1, source_target_pairs={{0,12},{4,0},{8,4},{12,8},{1,13},{5,1},{9,5},{13,9},{2,14},{6,2},{... | collective-permute-start | bytes 1966088 | tf_op jit(solution)/shard_map/ppermute | solution.py:188
  104.9 19.3 %collective-permute-start.7 = (bf16[4,320,128]{2,1,0:T(8,128)(2,1)}, bf16[4,320,128]{2,1,0:T(8,128)(2,1)}, u32[]{:S(2)}, u32[]{:S(2)}) collective-permute-start(bf16[4,320,128]{2,1,0:T(8,128)(2,1)} %get-tuple-element.56), channel_id=1, source_target_pairs={{0,4},{4,8},{8,12},{12,0},{1,5},{5,9},{9,13},{13,1},{2,6},{6,10},{... | collective-permute-start | bytes 983048 | tf_op jit(solution)/shard_map/ppermute | solution.py:188
  106.8 26.1 %copy-start.1 = (bf16[4,2,320,128]{3,2,1,0:T(8,128)(2,1)S(1)}, bf16[4,2,320,128]{3,2,1,0:T(8,128)(2,1)}, u32[]{:S(2)}) copy-start(bf16[4,2,320,128]{3,2,1,0:T(8,128)(2,1)} %copy-done) | copy-start | bytes 1966084
  106.8 26.1 %copy-start.3 = (bf16[4,2,320,128]{3,2,1,0:T(8,128)(2,1)S(1)}, bf16[4,2,320,128]{3,2,1,0:T(8,128)(2,1)}, u32[]{:S(2)}) copy-start(bf16[4,2,320,128]{3,2,1,0:T(8,128)(2,1)} %copy-done.2) | copy-start | bytes 1966084
  106.9 33.5 %collective-permute-start.9 = (bf16[4,320,128]{2,1,0:T(8,128)(2,1)}, bf16[4,320,128]{2,1,0:T(8,128)(2,1)S(1)}, u32[]{:S(2)}, u32[]{:S(2)}) collective-permute-start(bf16[4,320,128]{2,1,0:T(8,128)(2,1)} %get-tuple-element.55), channel_id=1, source_target_pairs={{2,10},{6,14},{10,2},{14,6},{3,11},{7,15},{11,3},{15,7},{18,26},{2... | collective-permute-start | bytes 983048 | tf_op jit(solution)/shard_map/ppermute | solution.py:194
  124.1 11.0 %collective-permute-start.12 = (bf16[4,2,320,128]{3,2,1,0:T(8,128)(2,1)S(1)}, bf16[4,2,320,128]{3,2,1,0:T(8,128)(2,1)S(1)}, u32[]{:S(2)}, u32[]{:S(2)}) collective-permute-start(bf16[4,2,320,128]{3,2,1,0:T(8,128)(2,1)S(1)} %bitcast.28), channel_id=1, source_target_pairs={{0,1},{1,0},{2,3},{3,2},{4,5},{5,4},{6,7},{7,6},{8,9},{9,8},{10,11... | collective-permute-start | bytes 1966088 | tf_op jit(solution)/shard_map/ppermute | solution.py:188
  129.1 12.6 %collective-permute-start.8 = (bf16[4,320,128]{2,1,0:T(8,128)(2,1)}, bf16[4,320,128]{2,1,0:T(8,128)(2,1)S(1)}, u32[]{:S(2)}, u32[]{:S(2)}) collective-permute-start(bf16[4,320,128]{2,1,0:T(8,128)(2,1)} %collective-permute-done.7), channel_id=1, source_target_pairs={{0,4},{4,8},{8,12},{12,0},{1,5},{5,9},{9,13},{13,1},{2,6},{6,10},{... | collective-permute-start | bytes 983048 | tf_op jit(solution)/shard_map/ppermute | solution.py:188
  131.0 6.4 %collective-permute-start.11 = (bf16[4,2,320,128]{3,2,1,0:T(8,128)(2,1)}, bf16[4,2,320,128]{3,2,1,0:T(8,128)(2,1)S(1)}, u32[]{:S(2)}, u32[]{:S(2)}) collective-permute-start(bf16[4,2,320,128]{3,2,1,0:T(8,128)(2,1)} %collective-permute-done.10.one), channel_id=1, source_target_pairs={{0,1},{1,0},{2,3},{3,2},{4,5},{5,4},{6,7},{7,6},{8,9},{9,8},{10,11... | collective-permute-start | bytes 1966088 | tf_op jit(solution)/shard_map/ppermute | solution.py:188
  141.8 4.4 %collective-permute-start.13 = (bf16[4,2,320,128]{3,2,1,0:T(8,128)(2,1)S(1)}, bf16[4,2,320,128]{3,2,1,0:T(8,128)(2,1)S(1)}, u32[]{:S(2)}, u32[]{:S(2)}) collective-permute-start(bf16[4,2,320,128]{3,2,1,0:T(8,128)(2,1)S(1)} %pad_maximum_fusion.1.one), channel_id=1, source_target_pairs={{0,1},{1,0},{2,3},{3,2},{4,5},{5,4},{6,7},{7,6},{8,9},{9,8},{10,11... | collective-permute-start | bytes 1966088 | tf_op jit(solution)/shard_map/ppermute | solution.py:188

commit v9 on v8

--- a/solution.py
+++ b/solution.py
@@ -33,15 +33,22 @@
     return jnp.asarray(table.astype(jnp.bfloat16))
 
 
-def spectra_body(strain, live, order, basis, whiten, out, held, place, loaded, *, first, count, groups):
+def spectra_body(*refs, first, count, groups):
+    (strain, *small), out = refs[:5], refs[5]
+    held, live, order, basis, whiten, place, packed, loaded, ready, gone = refs[6:]
     rows = 4 * count
-
-    def load(i):
+    copies = []
+    for i in range(count // GROUP):
         part = pl.ds(first + i * GROUP, GROUP)
-        return pltpu.make_async_copy(strain.at[part], held.at[pl.ds(i * GROUP, GROUP)], loaded.at[i])
-
-    for i in range(count // GROUP):
-        load(i).start()
+        copies.append(pltpu.make_async_copy(strain.at[part], held.at[pl.ds(i * GROUP, GROUP)], loaded.at[i]))
+    fixed = [
+        pltpu.make_async_copy(source, target, ready.at[i])
+        for i, (source, target) in enumerate(zip(small, (live, order, basis, whiten)))
+    ]
+    for copy in [*fixed, *copies]:
+        copy.start()
+    for copy in fixed:
+        copy.wait()
     channel = lax.broadcasted_iota(jnp.int32, (CH, CH), 0)
     pick = (channel == order[...]).astype(jnp.float32).astype(jnp.bfloat16)
     shape = (4 * groups, 2 * groups)
@@ -50,7 +57,7 @@
     spread = jnp.where(column == 2 * (row % groups) + row // (2 * groups), whiten[...], 0.0)
     gain = jnp.sum(spread, axis=1, keepdims=True) * (2.0 / math.sqrt(NT))
     for i in range(count // GROUP):
-        load(i).wait()
+        copies[i].wait()
         for at in range(i * GROUP, (i + 1) * GROUP):
             value = held[at].astype(jnp.float32)
             centered = value - jnp.sum(value, axis=1, keepdims=True) * (1.0 / NT)
@@ -62,29 +69,38 @@
             spec = jnp.dot(spec, pick, preferred_element_type=jnp.float32)
             for part in range(4):
                 place[pl.ds(at * 4 + part, groups, stride=rows), :] = spec[part * groups : (part + 1) * groups]
+    copies = []
     for x in range(4):
         size = groups * rows // 4
-        packed = place[x * size : (x + 1) * size].astype(jnp.bfloat16)
-        out[x, 0] = packed
-        out[x, 1] = packed
+        packed[x] = place[x * size : (x + 1) * size].astype(jnp.bfloat16)
+        for half in range(2):
+            copies.append(pltpu.make_async_copy(packed.at[x], out.at[x, half], gone.at[x, half]))
+            copies[-1].start()
+    for copy in copies:
+        copy.wait()
 
 
 def spectra(strain, live, order, basis, whiten, first, count):
     groups = basis.shape[0] // 4
     rows = 4 * count
-    whole = pl.BlockSpec(memory_space=pltpu.VMEM)
+    somewhere = pl.BlockSpec(memory_space=pl.ANY)
+    small = (live, order, basis, whiten)
     return pl.pallas_call(
         functools.partial(spectra_body, first=first, count=count, groups=groups),
-        in_specs=[pl.BlockSpec(memory_space=pl.ANY)] + [whole] * 4,
-        out_specs=whole,
+        in_specs=[somewhere] * 5,
+        out_specs=somewhere,
         out_shape=jax.ShapeDtypeStruct((4, 2, groups * rows // 4, CH), jnp.bfloat16),
         scratch_shapes=[
             pltpu.VMEM((count, CH, NT), jnp.bfloat16),
+            *[pltpu.VMEM(v.shape, v.dtype) for v in small],
             pltpu.VMEM((groups * rows, CH), jnp.float32),
+            pltpu.VMEM((4, groups * rows // 4, CH), jnp.bfloat16),
             pltpu.SemaphoreType.DMA((count // GROUP,)),
+            pltpu.SemaphoreType.DMA((4,)),
+            pltpu.SemaphoreType.DMA((4, 2)),
         ],
         name="spectra",
-    )(strain, live, order, basis, whiten)
+    )(strain, *small)
 
 
 def left_body(where, data, out):
@@ -194,11 +210,9 @@
     return lax.ppermute(value, ("y", "z_hi"), pairs)
 
 
-def fetched(here, held):
-    ahead1 = shifted(here, "y", -1)
-    high = upper(here[:, 1], 2)
-    low, here, *held = lax.optimization_barrier((shifted(here[:, 0], "y", 1), here, *held))
-    return [here, ahead1, (shifted(low, "y", 1), high)], held
+def hopped(here):
+    low = shifted(shifted(here[:, 0], "y", 1), "y", 1)
+    return [here, shifted(here, "y", -1), jnp.stack([low, upper(here[:, 1], 2)], axis=1)]
 
 
 def both(own):
@@ -224,17 +238,15 @@
 
     first, second = spread(made(0, CHUNKS[0])), made(*CHUNKS)
     first, second = lax.optimization_barrier((first, second))
-    (first, ahead1, ahead2), _ = fetched(first, [])
-    head = both([first, ahead1, jnp.stack(ahead2, axis=1)])
+    head = both(hopped(first))
     tail = spread(second)
     tail, *head = lax.optimization_barrier((tail, *head))
-    (tail, ahead1, ahead2), head = fetched(tail, head)
+    ahead1, ahead2 = shifted(tail, "y", -1), shifted(tail, "y", 2)
     begun = early(left_of(where, head[0]), head)
     left = left_of(where, tail)
     filled = late(where, left, begun[0], tail, shifted(tail, "core", 1), None, 0, scale)
     filled = late(where, left, begun[1], ahead1, shifted(ahead1, "core", 1), filled, 1, scale)
     ahead2, filled = lax.optimization_barrier((ahead2, filled))
-    ahead2 = jnp.stack(ahead2, axis=1)
     return late(where, left, begun[2], ahead2, shifted(ahead2, "core", 1), filled, 2, scale)
 
 

time: 149 us -> 153 us (1.027)
  the two profiles are of different devices: /device:TPU:263 before, /device:TPU:1 now
where the time goes in v9:
time: 153 us; the launch traced here: 151 us
  starting transfers between devices  84.2 us (55%)
  waiting for transfers between devices  44.2 us (29%)
  Pallas kernels  20 us (13%)
  local copies, waits for them, and re-layouts  1.75 us (1%)
    ppermute x11, starting transfers between devices, shifted(): lax.ppermute(value, axis, [(s, (s + steps) % count) for s in range(count)])  55.2 us
    all_to_all x2, waiting for transfers between devices, spread(): here = lax.all_to_all(sent, ('x', 'z_hi', 'z_lo'), 0, 0, tiled=True)  33 us
    all_to_all x2, starting transfers between devices, spread(): here = lax.all_to_all(sent, ('x', 'z_hi', 'z_lo'), 0, 0, tiled=True)  28.4 us
    ppermute x11, waiting for transfers between devices, shifted(): lax.ppermute(value, axis, [(s, (s + steps) % count) for s in range(count)])  11.2 us
    pallas_call x2, Pallas kernels, spectra(): pl.pallas_call(functools.partial(spectra_body, first=first, count=count,...  8.59 us
    pallas_call x3, Pallas kernels, late(): pl.pallas_call(functools.partial(late_body, ahead=ahead, scale=scale), in...  7.52 us
  transfers between devices with their start and end apart: 14, of which 6 were waited for; matrix products, arithmetic and copies ran while one was open for 0% of the time, Pallas kernels for 9%

profile of v9, /device:TPU:1, one launch (start us, length us, event | category | flops | bytes accessed | tf_op | source)
XLA Modules:
  0.0 150.7 jit_solution(14200169320407264824)
XLA Ops:
  0.0 4.3 %spectra.2 = bf16[4,2,320,128]{3,2,1,0:T(8,128)(2,1)} custom-call(bf16[20,128,512]{2,1,0:T(8,128)(2,1)} %bitcast.25, s32[20,128]{1,0:T(8,128)} %bitcast.31, s32[1,128]{1,0:T(1,128)} %refs_2_.3, bf16[128,512]{1,0:T(8,128)(2,1)} %constant.8.clone.refs_3_, f32[1,64]{1,0:T(1,128)} %bitcast.33), custom_call_target="tpu_custom_call" | custom-call | tf_op jit(solution)/shard_map/spectra/pallas_call | solution.py:88
  4.3 19.1 %all-to-all-start = ((bf16[64,40,128]{2,1,0:T(8,128)(2,1)}), bf16[64,40,128]{2,1,0:T(8,128)(2,1)S(1)}, u32[]{:S(2)}, u32[]{:S(2)}) async-start(bf16[64,40,128]{2,1,0:T(8,128)(2,1)} %bitcast.28), calls=%async_computation | async-start | bytes 1310720 | tf_op jit(solution)/shard_map/all_to_all | solution.py:236
  23.5 4.3 %spectra.3 = bf16[4,2,320,128]{3,2,1,0:T(8,128)(2,1)} custom-call(bf16[20,128,512]{2,1,0:T(8,128)(2,1)} %bitcast.26, s32[20,128]{1,0:T(8,128)} %bitcast.32, s32[1,128]{1,0:T(1,128)} %refs_2_.3, bf16[128,512]{1,0:T(8,128)(2,1)} %constant.8.clone.refs_3_, f32[1,64]{1,0:T(1,128)} %bitcast.34), custom_call_target="tpu_custom_call" | custom-call | tf_op jit(solution)/shard_map/spectra/pallas_call | solution.py:88
  27.7 30.1 %all-to-all-done = bf16[64,40,128]{2,1,0:T(8,128)(2,1)S(1)} async-done(((bf16[64,40,128]{2,1,0:T(8,128)(2,1)}), bf16[64,40,128]{2,1,0:T(8,128)(2,1)S(1)}, u32[]{:S(2)}, u32[]{:S(2)}) %all-to-all-start) | async-done | bytes 655392 | tf_op jit(solution)/shard_map/all_to_all | solution.py:236
  57.8 9.2 %all-to-all-start.1 = ((bf16[64,40,128]{2,1,0:T(8,128)(2,1)}), bf16[64,40,128]{2,1,0:T(8,128)(2,1)S(1)}, u32[]{:S(2)}, u32[]{:S(2)}) async-start(bf16[64,40,128]{2,1,0:T(8,128)(2,1)} %bitcast.27), calls=%async_computation.1 | async-start | bytes 1310720 | tf_op jit(solution)/shard_map/all_to_all | solution.py:236
  67.1 3.2 %collective-permute-start.3 = (bf16[4,320,128]{2,1,0:T(8,128)(2,1)S(1)}, bf16[4,320,128]{2,1,0:T(8,128)(2,1)S(1)}, u32[]{:S(2)}, u32[]{:S(2)}) collective-permute-start(bf16[4,320,128]{2,1,0:T(8,128)(2,1)S(1)} %get-tuple-element.33), channel_id=1, source_target_pairs={{0,4},{4,8},{8,12},{12,0},{1,5},{5,9},{9,13},{13,1},{2,6},{6,10},{... | collective-permute-start | bytes 983048 | tf_op jit(solution)/shard_map/ppermute | solution.py:204
  70.4 3.4 %collective-permute-start.1 = (bf16[4,2,320,128]{3,2,1,0:T(8,128)(2,1)S(1)}, bf16[4,2,320,128]{3,2,1,0:T(8,128)(2,1)S(1)}, u32[]{:S(2)}, u32[]{:S(2)}) collective-permute-start(bf16[4,2,320,128]{3,2,1,0:T(8,128)(2,1)S(1)} %bitcast.16), channel_id=1, source_target_pairs={{0,12},{4,0},{8,4},{12,8},{1,13},{5,1},{9,5},{13,9},{2,14},{6,2},{... | collective-permute-start | bytes 1966088 | tf_op jit(solution)/shard_map/ppermute | solution.py:204
  73.7 0.7 collective-permute-start.5
  74.4 4.0 %collective-permute-done.3 = bf16[4,320,128]{2,1,0:T(8,128)(2,1)S(1)} collective-permute-done((bf16[4,320,128]{2,1,0:T(8,128)(2,1)S(1)}, bf16[4,320,128]{2,1,0:T(8,128)(2,1)S(1)}, u32[]{:S(2)}, u32[]{:S(2)}) %collective-permute-start.3) | collective-permute-done | bytes 327712 | tf_op jit(solution)/shard_map/ppermute | solution.py:204
  78.4 1.9 %collective-permute-start.4 = (bf16[4,320,128]{2,1,0:T(8,128)(2,1)S(1)}, bf16[4,320,128]{2,1,0:T(8,128)(2,1)S(1)}, u32[]{:S(2)}, u32[]{:S(2)}) collective-permute-start(bf16[4,320,128]{2,1,0:T(8,128)(2,1)S(1)} %collective-permute-done.3), channel_id=1, source_target_pairs={{0,4},{4,8},{8,12},{12,0},{1,5},{5,9},{9,13},{13,1},{2,6},{6,10},{... | collective-permute-start | bytes 983048 | tf_op jit(solution)/shard_map/ppermute | solution.py:204
  80.3 4.2 %collective-permute-start = (bf16[4,2,320,128]{3,2,1,0:T(8,128)(2,1)S(1)}, bf16[4,2,320,128]{3,2,1,0:T(8,128)(2,1)S(1)}, u32[]{:S(2)}, u32[]{:S(2)}) collective-permute-start(bf16[4,2,320,128]{3,2,1,0:T(8,128)(2,1)S(1)} %bitcast.17), channel_id=1, source_target_pairs={{0,1},{1,0},{2,3},{3,2},{4,5},{5,4},{6,7},{7,6},{8,9},{9,8},{10,11... | collective-permute-start | bytes 1966088 | tf_op jit(solution)/shard_map/ppermute | solution.py:204
  84.6 0.0 collective-permute-done.5
  84.6 4.1 %collective-permute-done.4 = bf16[4,320,128]{2,1,0:T(8,128)(2,1)S(1)} collective-permute-done((bf16[4,320,128]{2,1,0:T(8,128)(2,1)S(1)}, bf16[4,320,128]{2,1,0:T(8,128)(2,1)S(1)}, u32[]{:S(2)}, u32[]{:S(2)}) %collective-permute-start.4) | collective-permute-done | bytes 327712 | tf_op jit(solution)/shard_map/ppermute | solution.py:204
  88.6 0.1 pad_maximum_fusion.refs_4_
  88.7 4.9 %collective-permute-start.6 = (bf16[4,2,320,128]{3,2,1,0:T(8,128)(2,1)S(1)}, bf16[4,2,320,128]{3,2,1,0:T(8,128)(2,1)S(1)}, u32[]{:S(2)}, u32[]{:S(2)}) collective-permute-start(bf16[4,2,320,128]{3,2,1,0:T(8,128)(2,1)S(1)} %pad_maximum_fusion.refs_4_), channel_id=1, source_target_pairs={{0,1},{1,0},{2,3},{3,2},{4,5},{5,4},{6,7},{7,6},{8,9},{9,8},{10,11... | collective-permute-start | bytes 1966088 | tf_op jit(solution)/shard_map/ppermute | solution.py:204
  93.6 0.0 collective-permute-done.1.refs_2_
  93.6 1.9 %collective-permute-start.2 = (bf16[4,2,320,128]{3,2,1,0:T(8,128)(2,1)S(1)}, bf16[4,2,320,128]{3,2,1,0:T(8,128)(2,1)S(1)}, u32[]{:S(2)}, u32[]{:S(2)}) collective-permute-start(bf16[4,2,320,128]{3,2,1,0:T(8,128)(2,1)S(1)} %collective-permute-done.1.refs_2_), channel_id=1, source_target_pairs={{0,1},{1,0},{2,3},{3,2},{4,5},{5,4},{6,7},{7,6},{8,9},{9,8},{10,11... | collective-permute-start | bytes 1966088 | tf_op jit(solution)/shard_map/ppermute | solution.py:204
  95.5 0.0 collective-permute-done.refs_1_
  95.5 0.0 collective-permute-done.6.refs_5_
  95.6 0.0 copy-start
  95.6 0.8 copy-done
  96.4 1.2 collective-permute-done.2.refs_3_
  97.6 0.0 copy-start.2
  97.6 0.9 copy-done.2
  98.5 2.9 %all-to-all-done.1 = bf16[64,40,128]{2,1,0:T(8,128)(2,1)S(1)} async-done(((bf16[64,40,128]{2,1,0:T(8,128)(2,1)}), bf16[64,40,128]{2,1,0:T(8,128)(2,1)S(1)}, u32[]{:S(2)}, u32[]{:S(2)}) %all-to-all-start.1) | async-done | bytes 655392 | tf_op jit(solution)/shard_map/all_to_all | solution.py:236
  101.3 4.6 %collective-permute-start.8 = (bf16[4,2,320,128]{3,2,1,0:T(8,128)(2,1)S(1)}, bf16[4,2,320,128]{3,2,1,0:T(8,128)(2,1)}, u32[]{:S(2)}, u32[]{:S(2)}) collective-permute-start(bf16[4,2,320,128]{3,2,1,0:T(8,128)(2,1)S(1)} %bitcast.20), channel_id=1, source_target_pairs={{0,12},{4,0},{8,4},{12,8},{1,13},{5,1},{9,5},{13,9},{2,14},{6,2},{... | collective-permute-start | bytes 1966088 | tf_op jit(solution)/shard_map/ppermute | solution.py:204
  106.0 0.0 copy-start.1
  106.0 0.0 copy-start.3
  106.0 0.1 pad_add_fusion.where
  106.1 6.3 %collective-permute-start.10 = (bf16[4,2,320,128]{3,2,1,0:T(8,128)(2,1)S(1)}, bf16[4,2,320,128]{3,2,1,0:T(8,128)(2,1)S(1)}, u32[]{:S(2)}, u32[]{:S(2)}) collective-permute-start(bf16[4,2,320,128]{3,2,1,0:T(8,128)(2,1)S(1)} %bitcast.21), channel_id=1, source_target_pairs={{0,1},{1,0},{2,3},{3,2},{4,5},{5,4},{6,7},{7,6},{8,9},{9,8},{10,11... | collective-permute-start | bytes 1966088 | tf_op jit(solution)/shard_map/ppermute | solution.py:204
  112.4 2.3 %collective-permute-start.7 = (bf16[4,2,320,128]{3,2,1,0:T(8,128)(2,1)S(1)}, bf16[4,2,320,128]{3,2,1,0:T(8,128)(2,1)S(1)}, u32[]{:S(2)}, u32[]{:S(2)}) collective-permute-start(bf16[4,2,320,128]{3,2,1,0:T(8,128)(2,1)S(1)} %bitcast.22), channel_id=1, source_target_pairs={{0,8},{4,12},{8,0},{12,4},{1,9},{5,13},{9,1},{13,5},{2,10},{6,14},... | collective-permute-start | bytes 1966088 | tf_op jit(solution)/shard_map/ppermute | solution.py:204
  114.7 0.9 left.2
  115.6 0.9 left.3
  116.4 0.0 collective-permute-done.8.one
  116.4 20.4 %collective-permute-start.9 = (bf16[4,2,320,128]{3,2,1,0:T(8,128)(2,1)}, bf16[4,2,320,128]{3,2,1,0:T(8,128)(2,1)S(1)}, u32[]{:S(2)}, u32[]{:S(2)}) collective-permute-start(bf16[4,2,320,128]{3,2,1,0:T(8,128)(2,1)} %collective-permute-done.8.one), channel_id=1, source_target_pairs={{0,1},{1,0},{2,3},{3,2},{4,5},{5,4},{6,7},{7,6},{8,9},{9,8},{10,11... | collective-permute-start | bytes 1966088 | tf_op jit(solution)/shard_map/ppermute | solution.py:204
  136.9 0.0 copy-done.1
  136.9 0.0 copy-done.3
  136.9 2.2 %early.1 = (f32[2,512,256]{2,1,0:T(8,128)S(1)}, f32[2,512,256]{2,1,0:T(8,128)S(1)}, f32[2,512,256]{2,1,0:T(8,128)S(1)}) custom-call(bf16[512,1280]{1,0:T(8,128)(2,1)S(1)} %left.3, bf16[4,2,320,128]{3,2,1,0:T(8,128)(2,1)S(1)} %bitcast.19, bf16[4,2,320,128]{3,2,1,0:T(8,128)(2,1)S(1)} %collective-permute-done.refs_1_, ...), custom_call_target="tpu_custom_call" | custom-call | flops 20000000000 | bytes 12000000 | tf_op jit(solution)/shard_map/early/pallas_call | solution.py:146
  139.1 0.0 collective-permute-done.10.two
  139.1 2.3 %late.3.refs_0_ = f32[2,2,9,128,128]{4,3,2,1,0:T(8,128)} custom-call(s32[2]{0:T(128)S(1)} %pad_add_fusion.where, bf16[512,1280]{1,0:T(8,128)(2,1)S(1)} %left.2, f32[2,512,256]{2,1,0:T(8,128)S(1)} %get-tuple-element.30.begun, bf16[4,2,320,128]{3,2,1,0:T(8,128)(2,1)S(1)} %bitcast.24, bf16[4,2,320,128]{3,2,1,0:T(8,128)(2,1)S(1)} %collective-permute-done.10.two), custom_call_target="tpu_custom_call" | custom-call | flops 4000000000 | bytes 4000000 | tf_op jit(solution)/shard_map/late/pallas_call | solution.py:182
  141.4 0.0 collective-permute-done.9.two
  141.5 3.0 %late.4.refs_0_ = f32[2,2,9,128,128]{4,3,2,1,0:T(8,128)} custom-call(s32[2]{0:T(128)S(1)} %pad_add_fusion.where, bf16[512,1280]{1,0:T(8,128)(2,1)S(1)} %left.2, f32[2,512,256]{2,1,0:T(8,128)S(1)} %get-tuple-element.29.begun, bf16[4,2,320,128]{3,2,1,0:T(8,128)(2,1)} %collective-permute-done.8.one, ...), custom_call_target="tpu_custom_call", output_to_operand_aliasing={{}: (5, {})} | custom-call | flops 4000000000 | bytes 4000000 | tf_op jit(solution)/shard_map/late/pallas_call | solution.py:182
  144.4 0.0 collective-permute-done.7.one
  144.4 2.0 %collective-permute-start.11 = (bf16[4,2,320,128]{3,2,1,0:T(8,128)(2,1)S(1)}, bf16[4,2,320,128]{3,2,1,0:T(8,128)(2,1)S(1)}, u32[]{:S(2)}, u32[]{:S(2)}) collective-permute-start(bf16[4,2,320,128]{3,2,1,0:T(8,128)(2,1)S(1)} %collective-permute-done.7.one), channel_id=1, source_target_pairs={{0,1},{1,0},{2,3},{3,2},{4,5},{5,4},{6,7},{7,6},{8,9},{9,8},{10,11... | collective-permute-start | bytes 1966088 | tf_op jit(solution)/shard_map/ppermute | solution.py:204
  146.5 2.0 %collective-permute-done.11.two = bf16[4,2,320,128]{3,2,1,0:T(8,128)(2,1)S(1)} collective-permute-done((bf16[4,2,320,128]{3,2,1,0:T(8,128)(2,1)S(1)}, bf16[4,2,320,128]{3,2,1,0:T(8,128)(2,1)S(1)}, u32[]{:S(2)}, u32[]{:S(2)}) %collective-permute-start.11) | collective-permute-done | bytes 655392 | tf_op jit(solution)/shard_map/ppermute | solution.py:204
  148.4 2.2 %late.5 = f32[2,2,9,128,128]{4,3,2,1,0:T(8,128)} custom-call(s32[2]{0:T(128)S(1)} %pad_add_fusion.where, bf16[512,1280]{1,0:T(8,128)(2,1)S(1)} %left.2, f32[2,512,256]{2,1,0:T(8,128)S(1)} %get-tuple-element.28.begun, bf16[4,2,320,128]{3,2,1,0:T(8,128)(2,1)S(1)} %collective-permute-done.7.one, ...), custom_call_target="tpu_custom_call", output_to_operand_aliasing={{}: (5, {})} | custom-call | flops 4000000000 | bytes 4000000 | tf_op jit(solution)/shard_map/late/pallas_call | solution.py:182
  (1 shorter events, 0.0 us)
Async XLA Ops:
  4.3 53.5 %all-to-all-start = ((bf16[64,40,128]{2,1,0:T(8,128)(2,1)}), bf16[64,40,128]{2,1,0:T(8,128)(2,1)S(1)}, u32[]{:S(2)}, u32[]{:S(2)}) async-start(bf16[64,40,128]{2,1,0:T(8,128)(2,1)} %bitcast.28), calls=%async_computation | async-start | bytes 1310720 | tf_op jit(solution)/shard_map/all_to_all | solution.py:236
  57.8 43.5 %all-to-all-start.1 = ((bf16[64,40,128]{2,1,0:T(8,128)(2,1)}), bf16[64,40,128]{2,1,0:T(8,128)(2,1)S(1)}, u32[]{:S(2)}, u32[]{:S(2)}) async-start(bf16[64,40,128]{2,1,0:T(8,128)(2,1)} %bitcast.27), calls=%async_computation.1 | async-start | bytes 1310720 | tf_op jit(solution)/shard_map/all_to_all | solution.py:236
  67.1 11.2 %collective-permute-start.3 = (bf16[4,320,128]{2,1,0:T(8,128)(2,1)S(1)}, bf16[4,320,128]{2,1,0:T(8,128)(2,1)S(1)}, u32[]{:S(2)}, u32[]{:S(2)}) collective-permute-start(bf16[4,320,128]{2,1,0:T(8,128)(2,1)S(1)} %get-tuple-element.33), channel_id=1, source_target_pairs={{0,4},{4,8},{8,12},{12,0},{1,5},{5,9},{9,13},{13,1},{2,6},{6,10},{... | collective-permute-start | bytes 983048 | tf_op jit(solution)/shard_map/ppermute | solution.py:204
  70.4 23.2 %collective-permute-start.1 = (bf16[4,2,320,128]{3,2,1,0:T(8,128)(2,1)S(1)}, bf16[4,2,320,128]{3,2,1,0:T(8,128)(2,1)S(1)}, u32[]{:S(2)}, u32[]{:S(2)}) collective-permute-start(bf16[4,2,320,128]{3,2,1,0:T(8,128)(2,1)S(1)} %bitcast.16), channel_id=1, source_target_pairs={{0,12},{4,0},{8,4},{12,8},{1,13},{5,1},{9,5},{13,9},{2,14},{6,2},{... | collective-permute-start | bytes 1966088 | tf_op jit(solution)/shard_map/ppermute | solution.py:204
  73.7 10.8 %collective-permute-start.5 = (bf16[4,320,128]{2,1,0:T(8,128)(2,1)S(1)}, bf16[4,320,128]{2,1,0:T(8,128)(2,1)S(1)}, u32[]{:S(2)}, u32[]{:S(2)}) collective-permute-start(bf16[4,320,128]{2,1,0:T(8,128)(2,1)S(1)} %get-tuple-element.34), channel_id=1, source_target_pairs={{2,10},{6,14},{10,2},{14,6},{3,11},{7,15},{11,3},{15,7},{18,26},{2... | collective-permute-start | bytes 983048 | tf_op jit(solution)/shard_map/ppermute | solution.py:210
  78.4 10.2 %collective-permute-start.4 = (bf16[4,320,128]{2,1,0:T(8,128)(2,1)S(1)}, bf16[4,320,128]{2,1,0:T(8,128)(2,1)S(1)}, u32[]{:S(2)}, u32[]{:S(2)}) collective-permute-start(bf16[4,320,128]{2,1,0:T(8,128)(2,1)S(1)} %collective-permute-done.3), channel_id=1, source_target_pairs={{0,4},{4,8},{8,12},{12,0},{1,5},{5,9},{9,13},{13,1},{2,6},{6,10},{... | collective-permute-start | bytes 983048 | tf_op jit(solution)/shard_map/ppermute | solution.py:204
  80.3 15.2 %collective-permute-start = (bf16[4,2,320,128]{3,2,1,0:T(8,128)(2,1)S(1)}, bf16[4,2,320,128]{3,2,1,0:T(8,128)(2,1)S(1)}, u32[]{:S(2)}, u32[]{:S(2)}) collective-permute-start(bf16[4,2,320,128]{3,2,1,0:T(8,128)(2,1)S(1)} %bitcast.17), channel_id=1, source_target_pairs={{0,1},{1,0},{2,3},{3,2},{4,5},{5,4},{6,7},{7,6},{8,9},{9,8},{10,11... | collective-permute-start | bytes 1966088 | tf_op jit(solution)/shard_map/ppermute | solution.py:204
  88.7 6.8 %collective-permute-start.6 = (bf16[4,2,320,128]{3,2,1,0:T(8,128)(2,1)S(1)}, bf16[4,2,320,128]{3,2,1,0:T(8,128)(2,1)S(1)}, u32[]{:S(2)}, u32[]{:S(2)}) collective-permute-start(bf16[4,2,320,128]{3,2,1,0:T(8,128)(2,1)S(1)} %pad_maximum_fusion.refs_4_), channel_id=1, source_target_pairs={{0,1},{1,0},{2,3},{3,2},{4,5},{5,4},{6,7},{7,6},{8,9},{9,8},{10,11... | collective-permute-start | bytes 1966088 | tf_op jit(solution)/shard_map/ppermute | solution.py:204
  93.6 4.0 %collective-permute-start.2 = (bf16[4,2,320,128]{3,2,1,0:T(8,128)(2,1)S(1)}, bf16[4,2,320,128]{3,2,1,0:T(8,128)(2,1)S(1)}, u32[]{:S(2)}, u32[]{:S(2)}) collective-permute-start(bf16[4,2,320,128]{3,2,1,0:T(8,128)(2,1)S(1)} %collective-permute-done.1.refs_2_), channel_id=1, source_target_pairs={{0,1},{1,0},{2,3},{3,2},{4,5},{5,4},{6,7},{7,6},{8,9},{9,8},{10,11... | collective-permute-start | bytes 1966088 | tf_op jit(solution)/shard_map/ppermute | solution.py:204
  95.6 0.9 copy-start
  97.6 0.9 copy-start.2
  101.3 15.1 %collective-permute-start.8 = (bf16[4,2,320,128]{3,2,1,0:T(8,128)(2,1)S(1)}, bf16[4,2,320,128]{3,2,1,0:T(8,128)(2,1)}, u32[]{:S(2)}, u32[]{:S(2)}) collective-permute-start(bf16[4,2,320,128]{3,2,1,0:T(8,128)(2,1)S(1)} %bitcast.20), channel_id=1, source_target_pairs={{0,12},{4,0},{8,4},{12,8},{1,13},{5,1},{9,5},{13,9},{2,14},{6,2},{... | collective-permute-start | bytes 1966088 | tf_op jit(solution)/shard_map/ppermute | solution.py:204
  106.0 30.9 %copy-start.1 = (bf16[4,2,320,128]{3,2,1,0:T(8,128)(2,1)S(1)}, bf16[4,2,320,128]{3,2,1,0:T(8,128)(2,1)}, u32[]{:S(2)}) copy-start(bf16[4,2,320,128]{3,2,1,0:T(8,128)(2,1)} %copy-done) | copy-start | bytes 1966084
  106.0 30.9 %copy-start.3 = (bf16[4,2,320,128]{3,2,1,0:T(8,128)(2,1)S(1)}, bf16[4,2,320,128]{3,2,1,0:T(8,128)(2,1)}, u32[]{:S(2)}) copy-start(bf16[4,2,320,128]{3,2,1,0:T(8,128)(2,1)} %copy-done.2) | copy-start | bytes 1966084
  106.1 33.0 %collective-permute-start.10 = (bf16[4,2,320,128]{3,2,1,0:T(8,128)(2,1)S(1)}, bf16[4,2,320,128]{3,2,1,0:T(8,128)(2,1)S(1)}, u32[]{:S(2)}, u32[]{:S(2)}) collective-permute-start(bf16[4,2,320,128]{3,2,1,0:T(8,128)(2,1)S(1)} %bitcast.21), channel_id=1, source_target_pairs={{0,1},{1,0},{2,3},{3,2},{4,5},{5,4},{6,7},{7,6},{8,9},{9,8},{10,11... | collective-permute-start | bytes 1966088 | tf_op jit(solution)/shard_map/ppermute | solution.py:204
  112.4 32.0 %collective-permute-start.7 = (bf16[4,2,320,128]{3,2,1,0:T(8,128)(2,1)S(1)}, bf16[4,2,320,128]{3,2,1,0:T(8,128)(2,1)S(1)}, u32[]{:S(2)}, u32[]{:S(2)}) collective-permute-start(bf16[4,2,320,128]{3,2,1,0:T(8,128)(2,1)S(1)} %bitcast.22), channel_id=1, source_target_pairs={{0,8},{4,12},{8,0},{12,4},{1,9},{5,13},{9,1},{13,5},{2,10},{6,14},... | collective-permute-start | bytes 1966088 | tf_op jit(solution)/shard_map/ppermute | solution.py:204
  116.4 25.0 %collective-permute-start.9 = (bf16[4,2,320,128]{3,2,1,0:T(8,128)(2,1)}, bf16[4,2,320,128]{3,2,1,0:T(8,128)(2,1)S(1)}, u32[]{:S(2)}, u32[]{:S(2)}) collective-permute-start(bf16[4,2,320,128]{3,2,1,0:T(8,128)(2,1)} %collective-permute-done.8.one), channel_id=1, source_target_pairs={{0,1},{1,0},{2,3},{3,2},{4,5},{5,4},{6,7},{7,6},{8,9},{9,8},{10,11... | collective-permute-start | bytes 1966088 | tf_op jit(solution)/shard_map/ppermute | solution.py:204
  144.4 4.0 %collective-permute-start.11 = (bf16[4,2,320,128]{3,2,1,0:T(8,128)(2,1)S(1)}, bf16[4,2,320,128]{3,2,1,0:T(8,128)(2,1)S(1)}, u32[]{:S(2)}, u32[]{:S(2)}) collective-permute-start(bf16[4,2,320,128]{3,2,1,0:T(8,128)(2,1)S(1)} %collective-permute-done.7.one), channel_id=1, source_target_pairs={{0,1},{1,0},{2,3},{3,2},{4,5},{5,4},{6,7},{7,6},{8,9},{9,8},{10,11... | collective-permute-start | bytes 1966088 | tf_op jit(solution)/shard_map/ppermute | solution.py:204

commit v10 on v9

--- a/solution.py
+++ b/solution.py
@@ -210,9 +210,11 @@
     return lax.ppermute(value, ("y", "z_hi"), pairs)
 
 
-def hopped(here):
-    low = shifted(shifted(here[:, 0], "y", 1), "y", 1)
-    return [here, shifted(here, "y", -1), jnp.stack([low, upper(here[:, 1], 2)], axis=1)]
+def fetched(here, held):
+    ahead1 = shifted(here, "y", -1)
+    high = upper(here[:, 1], 2)
+    low, here, *held = lax.optimization_barrier((shifted(here[:, 0], "y", 1), here, *held))
+    return [here, ahead1, (shifted(low, "y", 1), high)], held
 
 
 def both(own):
@@ -238,16 +240,20 @@
 
     first, second = spread(made(0, CHUNKS[0])), made(*CHUNKS)
     first, second = lax.optimization_barrier((first, second))
-    head = both(hopped(first))
+    (first, ahead1, ahead2), _ = fetched(first, [])
+    head = both([first, ahead1, jnp.stack(ahead2, axis=1)])
     tail = spread(second)
     tail, *head = lax.optimization_barrier((tail, *head))
-    ahead1, ahead2 = shifted(tail, "y", -1), shifted(tail, "y", 2)
+    (tail, ahead1, ahead2), head = fetched(tail, head)
     begun = early(left_of(where, head[0]), head)
     left = left_of(where, tail)
     filled = late(where, left, begun[0], tail, shifted(tail, "core", 1), None, 0, scale)
-    filled = late(where, left, begun[1], ahead1, shifted(ahead1, "core", 1), filled, 1, scale)
-    ahead2, filled = lax.optimization_barrier((ahead2, filled))
-    return late(where, left, begun[2], ahead2, shifted(ahead2, "core", 1), filled, 2, scale)
+    ahead1, ahead2, filled = lax.optimization_barrier((ahead1, ahead2, filled))
+    other1 = shifted(ahead1, "core", 1)
+    ahead2 = jnp.stack(ahead2, axis=1)
+    other2 = shifted(ahead2, "core", 1)
+    filled = late(where, left, begun[1], ahead1, other1, filled, 1, scale)
+    return late(where, left, begun[2], ahead2, other2, filled, 2, scale)
 
 
 def solution(mesh):

time: 153 us -> 143 us (0.935); the launches traced: 151 us -> 142 us
  starting transfers between devices: 84.2 us -> 69.5 us
  waiting for transfers between devices: 44.2 us -> 50.2 us
    ppermute x11 -> x12, starting transfers between devices: 55.2 us -> 39.8 us  [shifted(): lax.ppermute(value, axis, [(s, (s + steps) % count) for s in range(count)])]
    ppermute x11 -> x12, waiting for transfers between devices: 11.2 us -> 17.2 us  [shifted(): lax.ppermute(value, axis, [(s, (s + steps) % count) for s in range(count)])]
  transfers between devices with their start and end apart: 14 -> 16, of which waited for: 6 -> 7; matrix products, arithmetic and copies ran while one was open for 0% -> 0% of each run, Pallas kernels for 9% -> 9%
where the time goes in v10:
time: 143 us; the launch traced here: 142 us
  starting transfers between devices  69.5 us (49%)
  waiting for transfers between devices  50.2 us (35%)
  Pallas kernels  19.5 us (14%)
  local copies, waits for them, and re-layouts  2.64 us (2%)
    ppermute x12, starting transfers between devices, shifted(): lax.ppermute(value, axis, [(s, (s + steps) % count) for s in range(count)])  39.8 us
    all_to_all x2, waiting for transfers between devices, spread(): here = lax.all_to_all(sent, ('x', 'z_hi', 'z_lo'), 0, 0, tiled=True)  33 us
    all_to_all x2, starting transfers between devices, spread(): here = lax.all_to_all(sent, ('x', 'z_hi', 'z_lo'), 0, 0, tiled=True)  28.4 us
    ppermute x12, waiting for transfers between devices, shifted(): lax.ppermute(value, axis, [(s, (s + steps) % count) for s in range(count)])  17.2 us
    pallas_call x2, Pallas kernels, spectra(): pl.pallas_call(functools.partial(spectra_body, first=first, count=count,...  8.6 us
    pallas_call x3, Pallas kernels, late(): pl.pallas_call(functools.partial(late_body, ahead=ahead, scale=scale), in...  6.96 us
  transfers between devices with their start and end apart: 16, of which 7 were waited for; matrix products, arithmetic and copies ran while one was open for 0% of the time, Pallas kernels for 9%

profile of v10, /device:TPU:1, one launch (start us, length us, event | category | flops | bytes accessed | tf_op | source)
XLA Modules:
  0.0 142.4 jit_solution(2893453395692737564)
XLA Ops:
  0.0 4.3 %spectra.2 = bf16[4,2,320,128]{3,2,1,0:T(8,128)(2,1)} custom-call(bf16[20,128,512]{2,1,0:T(8,128)(2,1)} %bitcast.31, s32[20,128]{1,0:T(8,128)} %bitcast.39, s32[1,128]{1,0:T(1,128)} %refs_2_.3, bf16[128,512]{1,0:T(8,128)(2,1)} %constant.8.clone.refs_3_, f32[1,64]{1,0:T(1,128)} %bitcast.41), custom_call_target="tpu_custom_call" | custom-call | tf_op jit(solution)/shard_map/spectra/pallas_call | solution.py:88
  4.3 19.1 %all-to-all-start = ((bf16[64,40,128]{2,1,0:T(8,128)(2,1)}), bf16[64,40,128]{2,1,0:T(8,128)(2,1)S(1)}, u32[]{:S(2)}, u32[]{:S(2)}) async-start(bf16[64,40,128]{2,1,0:T(8,128)(2,1)} %bitcast.34), calls=%async_computation | async-start | bytes 1310720 | tf_op jit(solution)/shard_map/all_to_all | solution.py:238
  23.5 4.3 %spectra.3 = bf16[4,2,320,128]{3,2,1,0:T(8,128)(2,1)} custom-call(bf16[20,128,512]{2,1,0:T(8,128)(2,1)} %bitcast.32, s32[20,128]{1,0:T(8,128)} %bitcast.40, s32[1,128]{1,0:T(1,128)} %refs_2_.3, bf16[128,512]{1,0:T(8,128)(2,1)} %constant.8.clone.refs_3_, f32[1,64]{1,0:T(1,128)} %bitcast.42), custom_call_target="tpu_custom_call" | custom-call | tf_op jit(solution)/shard_map/spectra/pallas_call | solution.py:88
  27.7 30.1 %all-to-all-done = bf16[64,40,128]{2,1,0:T(8,128)(2,1)S(1)} async-done(((bf16[64,40,128]{2,1,0:T(8,128)(2,1)}), bf16[64,40,128]{2,1,0:T(8,128)(2,1)S(1)}, u32[]{:S(2)}, u32[]{:S(2)}) %all-to-all-start) | async-done | bytes 655392 | tf_op jit(solution)/shard_map/all_to_all | solution.py:238
  57.9 9.2 %all-to-all-start.1 = ((bf16[64,40,128]{2,1,0:T(8,128)(2,1)}), bf16[64,40,128]{2,1,0:T(8,128)(2,1)S(1)}, u32[]{:S(2)}, u32[]{:S(2)}) async-start(bf16[64,40,128]{2,1,0:T(8,128)(2,1)} %bitcast.33), calls=%async_computation.1 | async-start | bytes 1310720 | tf_op jit(solution)/shard_map/all_to_all | solution.py:238
  67.2 3.2 %collective-permute-start = (bf16[4,320,128]{2,1,0:T(8,128)(2,1)S(1)}, bf16[4,320,128]{2,1,0:T(8,128)(2,1)S(1)}, u32[]{:S(2)}, u32[]{:S(2)}) collective-permute-start(bf16[4,320,128]{2,1,0:T(8,128)(2,1)S(1)} %get-tuple-element.60), channel_id=1, source_target_pairs={{0,4},{4,8},{8,12},{12,0},{1,5},{5,9},{9,13},{13,1},{2,6},{6,10},{... | collective-permute-start | bytes 983048 | tf_op jit(solution)/shard_map/ppermute | solution.py:204
  70.4 3.4 %collective-permute-start.2 = (bf16[4,2,320,128]{3,2,1,0:T(8,128)(2,1)S(1)}, bf16[4,2,320,128]{3,2,1,0:T(8,128)(2,1)S(1)}, u32[]{:S(2)}, u32[]{:S(2)}) collective-permute-start(bf16[4,2,320,128]{3,2,1,0:T(8,128)(2,1)S(1)} %bitcast.27), channel_id=1, source_target_pairs={{0,12},{4,0},{8,4},{12,8},{1,13},{5,1},{9,5},{13,9},{2,14},{6,2},{... | collective-permute-start | bytes 1966088 | tf_op jit(solution)/shard_map/ppermute | solution.py:204
  73.7 0.7 collective-permute-start.5
  74.4 4.0 %collective-permute-done = bf16[4,320,128]{2,1,0:T(8,128)(2,1)S(1)} collective-permute-done((bf16[4,320,128]{2,1,0:T(8,128)(2,1)S(1)}, bf16[4,320,128]{2,1,0:T(8,128)(2,1)S(1)}, u32[]{:S(2)}, u32[]{:S(2)}) %collective-permute-start) | collective-permute-done | bytes 327712 | tf_op jit(solution)/shard_map/ppermute | solution.py:204
  78.4 1.9 %collective-permute-start.4 = (bf16[4,320,128]{2,1,0:T(8,128)(2,1)S(1)}, bf16[4,320,128]{2,1,0:T(8,128)(2,1)S(1)}, u32[]{:S(2)}, u32[]{:S(2)}) collective-permute-start(bf16[4,320,128]{2,1,0:T(8,128)(2,1)S(1)} %collective-permute-done), channel_id=1, source_target_pairs={{0,4},{4,8},{8,12},{12,0},{1,5},{5,9},{9,13},{13,1},{2,6},{6,10},{... | collective-permute-start | bytes 983048 | tf_op jit(solution)/shard_map/ppermute | solution.py:204
  80.3 4.2 %collective-permute-start.1 = (bf16[4,2,320,128]{3,2,1,0:T(8,128)(2,1)S(1)}, bf16[4,2,320,128]{3,2,1,0:T(8,128)(2,1)S(1)}, u32[]{:S(2)}, u32[]{:S(2)}) collective-permute-start(bf16[4,2,320,128]{3,2,1,0:T(8,128)(2,1)S(1)} %bitcast.28), channel_id=1, source_target_pairs={{0,1},{1,0},{2,3},{3,2},{4,5},{5,4},{6,7},{7,6},{8,9},{9,8},{10,11... | collective-permute-start | bytes 1966088 | tf_op jit(solution)/shard_map/ppermute | solution.py:204
  84.6 0.0 collective-permute-done.5
  84.6 4.1 %collective-permute-done.4 = bf16[4,320,128]{2,1,0:T(8,128)(2,1)S(1)} collective-permute-done((bf16[4,320,128]{2,1,0:T(8,128)(2,1)S(1)}, bf16[4,320,128]{2,1,0:T(8,128)(2,1)S(1)}, u32[]{:S(2)}, u32[]{:S(2)}) %collective-permute-start.4) | collective-permute-done | bytes 327712 | tf_op jit(solution)/shard_map/ppermute | solution.py:204
  88.6 0.1 pad_maximum_fusion.refs_4_
  88.7 4.9 %collective-permute-start.6 = (bf16[4,2,320,128]{3,2,1,0:T(8,128)(2,1)S(1)}, bf16[4,2,320,128]{3,2,1,0:T(8,128)(2,1)S(1)}, u32[]{:S(2)}, u32[]{:S(2)}) collective-permute-start(bf16[4,2,320,128]{3,2,1,0:T(8,128)(2,1)S(1)} %pad_maximum_fusion.refs_4_), channel_id=1, source_target_pairs={{0,1},{1,0},{2,3},{3,2},{4,5},{5,4},{6,7},{7,6},{8,9},{9,8},{10,11... | collective-permute-start | bytes 1966088 | tf_op jit(solution)/shard_map/ppermute | solution.py:204
  93.6 0.0 collective-permute-done.2.refs_2_
  93.6 1.9 %collective-permute-start.3 = (bf16[4,2,320,128]{3,2,1,0:T(8,128)(2,1)S(1)}, bf16[4,2,320,128]{3,2,1,0:T(8,128)(2,1)S(1)}, u32[]{:S(2)}, u32[]{:S(2)}) collective-permute-start(bf16[4,2,320,128]{3,2,1,0:T(8,128)(2,1)S(1)} %collective-permute-done.2.refs_2_), channel_id=1, source_target_pairs={{0,1},{1,0},{2,3},{3,2},{4,5},{5,4},{6,7},{7,6},{8,9},{9,8},{10,11... | collective-permute-start | bytes 1966088 | tf_op jit(solution)/shard_map/ppermute | solution.py:204
  95.5 0.0 collective-permute-done.1.refs_1_
  95.5 0.0 collective-permute-done.6.refs_5_
  95.6 0.0 copy-start
  95.6 0.8 copy-done
  96.4 1.2 collective-permute-done.3.refs_3_
  97.6 0.9 copy-done.2
  98.5 2.9 %all-to-all-done.1 = bf16[64,40,128]{2,1,0:T(8,128)(2,1)S(1)} async-done(((bf16[64,40,128]{2,1,0:T(8,128)(2,1)}), bf16[64,40,128]{2,1,0:T(8,128)(2,1)S(1)}, u32[]{:S(2)}, u32[]{:S(2)}) %all-to-all-start.1) | async-done | bytes 655392 | tf_op jit(solution)/shard_map/all_to_all | solution.py:238
  101.4 0.9 slice_bitcast_fusion
  102.2 3.2 %collective-permute-start.7 = (bf16[4,320,128]{2,1,0:T(8,128)(2,1)}, bf16[4,320,128]{2,1,0:T(8,128)(2,1)}, u32[]{:S(2)}, u32[]{:S(2)}) collective-permute-start(bf16[4,320,128]{2,1,0:T(8,128)(2,1)} %get-tuple-element.58), channel_id=1, source_target_pairs={{0,4},{4,8},{8,12},{12,0},{1,5},{5,9},{9,13},{13,1},{2,6},{6,10},{... | collective-permute-start | bytes 983048 | tf_op jit(solution)/shard_map/ppermute | solution.py:204
  105.4 0.0 copy-start.1
  105.5 0.1 pad_add_fusion.where
  105.5 3.5 %collective-permute-start.8 = (bf16[4,2,320,128]{3,2,1,0:T(8,128)(2,1)S(1)}, bf16[4,2,320,128]{3,2,1,0:T(8,128)(2,1)S(1)}, u32[]{:S(2)}, u32[]{:S(2)}) collective-permute-start(bf16[4,2,320,128]{3,2,1,0:T(8,128)(2,1)S(1)} %bitcast.22), channel_id=1, source_target_pairs={{0,12},{4,0},{8,4},{12,8},{1,13},{5,1},{9,5},{13,9},{2,14},{6,2},{... | collective-permute-start | bytes 1966088 | tf_op jit(solution)/shard_map/ppermute | solution.py:204
  109.0 0.7 collective-permute-start.10
  109.7 1.9 %collective-permute-done.7 = bf16[4,320,128]{2,1,0:T(8,128)(2,1)} collective-permute-done((bf16[4,320,128]{2,1,0:T(8,128)(2,1)}, bf16[4,320,128]{2,1,0:T(8,128)(2,1)}, u32[]{:S(2)}, u32[]{:S(2)}) %collective-permute-start.7) | collective-permute-done | bytes 327712 | tf_op jit(solution)/shard_map/ppermute | solution.py:204
  111.6 7.0 %collective-permute-start.11 = (bf16[4,2,320,128]{3,2,1,0:T(8,128)(2,1)S(1)}, bf16[4,2,320,128]{3,2,1,0:T(8,128)(2,1)S(1)}, u32[]{:S(2)}, u32[]{:S(2)}) collective-permute-start(bf16[4,2,320,128]{3,2,1,0:T(8,128)(2,1)S(1)} %bitcast.23), channel_id=1, source_target_pairs={{0,1},{1,0},{2,3},{3,2},{4,5},{5,4},{6,7},{7,6},{8,9},{9,8},{10,11... | collective-permute-start | bytes 1966088 | tf_op jit(solution)/shard_map/ppermute | solution.py:204
  118.6 0.9 left.2
  119.5 0.9 left.3
  120.4 2.0 %collective-permute-start.9 = (bf16[4,320,128]{2,1,0:T(8,128)(2,1)}, bf16[4,320,128]{2,1,0:T(8,128)(2,1)S(1)}, u32[]{:S(2)}, u32[]{:S(2)}) collective-permute-start(bf16[4,320,128]{2,1,0:T(8,128)(2,1)} %collective-permute-done.7), channel_id=1, source_target_pairs={{0,4},{4,8},{8,12},{12,0},{1,5},{5,9},{9,13},{13,1},{2,6},{6,10},{... | collective-permute-start | bytes 983048 | tf_op jit(solution)/shard_map/ppermute | solution.py:204
  122.4 2.2 %early.1 = (f32[2,512,256]{2,1,0:T(8,128)S(1)}, f32[2,512,256]{2,1,0:T(8,128)S(1)}, f32[2,512,256]{2,1,0:T(8,128)S(1)}) custom-call(bf16[512,1280]{1,0:T(8,128)(2,1)S(1)} %left.3, bf16[4,2,320,128]{3,2,1,0:T(8,128)(2,1)S(1)} %bitcast.30, bf16[4,2,320,128]{3,2,1,0:T(8,128)(2,1)S(1)} %collective-permute-done.1.refs_1_, ...), custom_call_target="tpu_custom_call" | custom-call | flops 20000000000 | bytes 12000000 | tf_op jit(solution)/shard_map/early/pallas_call | solution.py:146
  124.6 0.0 collective-permute-done.11.two
  124.6 2.3 %late.3.refs_0_ = f32[2,2,9,128,128]{4,3,2,1,0:T(8,128)} custom-call(s32[2]{0:T(128)S(1)} %pad_add_fusion.where, bf16[512,1280]{1,0:T(8,128)(2,1)S(1)} %left.2, f32[2,512,256]{2,1,0:T(8,128)S(1)} %get-tuple-element.51.begun, bf16[4,2,320,128]{3,2,1,0:T(8,128)(2,1)S(1)} %bitcast.25, bf16[4,2,320,128]{3,2,1,0:T(8,128)(2,1)S(1)} %collective-permute-done.11.two), custom_call_target="tpu_custom_call" | custom-call | flops 4000000000 | bytes 4000000 | tf_op jit(solution)/shard_map/late/pallas_call | solution.py:182
  127.0 0.0 collective-permute-done.10
  127.0 0.0 collective-permute-done.8.one
  127.0 6.0 %collective-permute-done.9 = bf16[4,320,128]{2,1,0:T(8,128)(2,1)S(1)} collective-permute-done((bf16[4,320,128]{2,1,0:T(8,128)(2,1)}, bf16[4,320,128]{2,1,0:T(8,128)(2,1)S(1)}, u32[]{:S(2)}, u32[]{:S(2)}) %collective-permute-start.9) | collective-permute-done | bytes 327712 | tf_op jit(solution)/shard_map/ppermute | solution.py:204
  133.0 2.7 %collective-permute-start.13 = (bf16[4,2,320,128]{3,2,1,0:T(8,128)(2,1)S(1)}, bf16[4,2,320,128]{3,2,1,0:T(8,128)(2,1)S(1)}, u32[]{:S(2)}, u32[]{:S(2)}) collective-permute-start(bf16[4,2,320,128]{3,2,1,0:T(8,128)(2,1)S(1)} %collective-permute-done.8.one), channel_id=1, source_target_pairs={{0,1},{1,0},{2,3},{3,2},{4,5},{5,4},{6,7},{7,6},{8,9},{9,8},{10,11... | collective-permute-start | bytes 1966088 | tf_op jit(solution)/shard_map/ppermute | solution.py:204
  135.7 0.1 pad_maximum_fusion.1.one
  135.8 1.9 %collective-permute-start.12 = (bf16[4,2,320,128]{3,2,1,0:T(8,128)(2,1)S(1)}, bf16[4,2,320,128]{3,2,1,0:T(8,128)(2,1)S(1)}, u32[]{:S(2)}, u32[]{:S(2)}) collective-permute-start(bf16[4,2,320,128]{3,2,1,0:T(8,128)(2,1)S(1)} %pad_maximum_fusion.1.one), channel_id=1, source_target_pairs={{0,1},{1,0},{2,3},{3,2},{4,5},{5,4},{6,7},{7,6},{8,9},{9,8},{10,11... | collective-permute-start | bytes 1966088 | tf_op jit(solution)/shard_map/ppermute | solution.py:204
  137.7 0.0 collective-permute-done.13.two
  137.7 2.4 %late.4.refs_0_ = f32[2,2,9,128,128]{4,3,2,1,0:T(8,128)} custom-call(s32[2]{0:T(128)S(1)} %pad_add_fusion.where, bf16[512,1280]{1,0:T(8,128)(2,1)S(1)} %left.2, f32[2,512,256]{2,1,0:T(8,128)S(1)} %get-tuple-element.54.begun, bf16[4,2,320,128]{3,2,1,0:T(8,128)(2,1)S(1)} %collective-permute-done.8.one, ...), custom_call_target="tpu_custom_call", output_to_operand_aliasing={{}: (5, {})} | custom-call | flops 4000000000 | bytes 4000000 | tf_op jit(solution)/shard_map/late/pallas_call | solution.py:182
  140.1 0.0 collective-permute-done.12.two
  140.2 2.2 %late.5 = f32[2,2,9,128,128]{4,3,2,1,0:T(8,128)} custom-call(s32[2]{0:T(128)S(1)} %pad_add_fusion.where, bf16[512,1280]{1,0:T(8,128)(2,1)S(1)} %left.2, f32[2,512,256]{2,1,0:T(8,128)S(1)} %get-tuple-element.49.begun, bf16[4,2,320,128]{3,2,1,0:T(8,128)(2,1)S(1)} %pad_maximum_fusion.1.one, ...), custom_call_target="tpu_custom_call", output_to_operand_aliasing={{}: (5, {})} | custom-call | flops 4000000000 | bytes 4000000 | tf_op jit(solution)/shard_map/late/pallas_call | solution.py:182
  (5 shorter events, 0.1 us)
Async XLA Ops:
  4.3 53.5 %all-to-all-start = ((bf16[64,40,128]{2,1,0:T(8,128)(2,1)}), bf16[64,40,128]{2,1,0:T(8,128)(2,1)S(1)}, u32[]{:S(2)}, u32[]{:S(2)}) async-start(bf16[64,40,128]{2,1,0:T(8,128)(2,1)} %bitcast.34), calls=%async_computation | async-start | bytes 1310720 | tf_op jit(solution)/shard_map/all_to_all | solution.py:238
  57.9 43.5 %all-to-all-start.1 = ((bf16[64,40,128]{2,1,0:T(8,128)(2,1)}), bf16[64,40,128]{2,1,0:T(8,128)(2,1)S(1)}, u32[]{:S(2)}, u32[]{:S(2)}) async-start(bf16[64,40,128]{2,1,0:T(8,128)(2,1)} %bitcast.33), calls=%async_computation.1 | async-start | bytes 1310720 | tf_op jit(solution)/shard_map/all_to_all | solution.py:238
  67.2 11.2 %collective-permute-start = (bf16[4,320,128]{2,1,0:T(8,128)(2,1)S(1)}, bf16[4,320,128]{2,1,0:T(8,128)(2,1)S(1)}, u32[]{:S(2)}, u32[]{:S(2)}) collective-permute-start(bf16[4,320,128]{2,1,0:T(8,128)(2,1)S(1)} %get-tuple-element.60), channel_id=1, source_target_pairs={{0,4},{4,8},{8,12},{12,0},{1,5},{5,9},{9,13},{13,1},{2,6},{6,10},{... | collective-permute-start | bytes 983048 | tf_op jit(solution)/shard_map/ppermute | solution.py:204
  70.4 23.2 %collective-permute-start.2 = (bf16[4,2,320,128]{3,2,1,0:T(8,128)(2,1)S(1)}, bf16[4,2,320,128]{3,2,1,0:T(8,128)(2,1)S(1)}, u32[]{:S(2)}, u32[]{:S(2)}) collective-permute-start(bf16[4,2,320,128]{3,2,1,0:T(8,128)(2,1)S(1)} %bitcast.27), channel_id=1, source_target_pairs={{0,12},{4,0},{8,4},{12,8},{1,13},{5,1},{9,5},{13,9},{2,14},{6,2},{... | collective-permute-start | bytes 1966088 | tf_op jit(solution)/shard_map/ppermute | solution.py:204
  73.7 10.8 %collective-permute-start.5 = (bf16[4,320,128]{2,1,0:T(8,128)(2,1)S(1)}, bf16[4,320,128]{2,1,0:T(8,128)(2,1)S(1)}, u32[]{:S(2)}, u32[]{:S(2)}) collective-permute-start(bf16[4,320,128]{2,1,0:T(8,128)(2,1)S(1)} %get-tuple-element.59), channel_id=1, source_target_pairs={{2,10},{6,14},{10,2},{14,6},{3,11},{7,15},{11,3},{15,7},{18,26},{2... | collective-permute-start | bytes 983048 | tf_op jit(solution)/shard_map/ppermute | solution.py:210
  78.4 10.2 %collective-permute-start.4 = (bf16[4,320,128]{2,1,0:T(8,128)(2,1)S(1)}, bf16[4,320,128]{2,1,0:T(8,128)(2,1)S(1)}, u32[]{:S(2)}, u32[]{:S(2)}) collective-permute-start(bf16[4,320,128]{2,1,0:T(8,128)(2,1)S(1)} %collective-permute-done), channel_id=1, source_target_pairs={{0,4},{4,8},{8,12},{12,0},{1,5},{5,9},{9,13},{13,1},{2,6},{6,10},{... | collective-permute-start | bytes 983048 | tf_op jit(solution)/shard_map/ppermute | solution.py:204
  80.3 15.2 %collective-permute-start.1 = (bf16[4,2,320,128]{3,2,1,0:T(8,128)(2,1)S(1)}, bf16[4,2,320,128]{3,2,1,0:T(8,128)(2,1)S(1)}, u32[]{:S(2)}, u32[]{:S(2)}) collective-permute-start(bf16[4,2,320,128]{3,2,1,0:T(8,128)(2,1)S(1)} %bitcast.28), channel_id=1, source_target_pairs={{0,1},{1,0},{2,3},{3,2},{4,5},{5,4},{6,7},{7,6},{8,9},{9,8},{10,11... | collective-permute-start | bytes 1966088 | tf_op jit(solution)/shard_map/ppermute | solution.py:204
  88.7 6.8 %collective-permute-start.6 = (bf16[4,2,320,128]{3,2,1,0:T(8,128)(2,1)S(1)}, bf16[4,2,320,128]{3,2,1,0:T(8,128)(2,1)S(1)}, u32[]{:S(2)}, u32[]{:S(2)}) collective-permute-start(bf16[4,2,320,128]{3,2,1,0:T(8,128)(2,1)S(1)} %pad_maximum_fusion.refs_4_), channel_id=1, source_target_pairs={{0,1},{1,0},{2,3},{3,2},{4,5},{5,4},{6,7},{7,6},{8,9},{9,8},{10,11... | collective-permute-start | bytes 1966088 | tf_op jit(solution)/shard_map/ppermute | solution.py:204
  93.6 4.0 %collective-permute-start.3 = (bf16[4,2,320,128]{3,2,1,0:T(8,128)(2,1)S(1)}, bf16[4,2,320,128]{3,2,1,0:T(8,128)(2,1)S(1)}, u32[]{:S(2)}, u32[]{:S(2)}) collective-permute-start(bf16[4,2,320,128]{3,2,1,0:T(8,128)(2,1)S(1)} %collective-permute-done.2.refs_2_), channel_id=1, source_target_pairs={{0,1},{1,0},{2,3},{3,2},{4,5},{5,4},{6,7},{7,6},{8,9},{9,8},{10,11... | collective-permute-start | bytes 1966088 | tf_op jit(solution)/shard_map/ppermute | solution.py:204
  95.6 0.9 copy-start
  97.6 0.9 copy-start.2
  102.2 9.4 %collective-permute-start.7 = (bf16[4,320,128]{2,1,0:T(8,128)(2,1)}, bf16[4,320,128]{2,1,0:T(8,128)(2,1)}, u32[]{:S(2)}, u32[]{:S(2)}) collective-permute-start(bf16[4,320,128]{2,1,0:T(8,128)(2,1)} %get-tuple-element.58), channel_id=1, source_target_pairs={{0,4},{4,8},{8,12},{12,0},{1,5},{5,9},{9,13},{13,1},{2,6},{6,10},{... | collective-permute-start | bytes 983048 | tf_op jit(solution)/shard_map/ppermute | solution.py:204
  105.4 16.9 %copy-start.1 = (bf16[4,2,320,128]{3,2,1,0:T(8,128)(2,1)S(1)}, bf16[4,2,320,128]{3,2,1,0:T(8,128)(2,1)}, u32[]{:S(2)}) copy-start(bf16[4,2,320,128]{3,2,1,0:T(8,128)(2,1)} %copy-done) | copy-start | bytes 1966084
  105.4 16.9 %copy-start.3 = (bf16[4,2,320,128]{3,2,1,0:T(8,128)(2,1)S(1)}, bf16[4,2,320,128]{3,2,1,0:T(8,128)(2,1)}, u32[]{:S(2)}) copy-start(bf16[4,2,320,128]{3,2,1,0:T(8,128)(2,1)} %copy-done.2) | copy-start | bytes 1966084
  105.5 21.4 %collective-permute-start.8 = (bf16[4,2,320,128]{3,2,1,0:T(8,128)(2,1)S(1)}, bf16[4,2,320,128]{3,2,1,0:T(8,128)(2,1)S(1)}, u32[]{:S(2)}, u32[]{:S(2)}) collective-permute-start(bf16[4,2,320,128]{3,2,1,0:T(8,128)(2,1)S(1)} %bitcast.22), channel_id=1, source_target_pairs={{0,12},{4,0},{8,4},{12,8},{1,13},{5,1},{9,5},{13,9},{2,14},{6,2},{... | collective-permute-start | bytes 1966088 | tf_op jit(solution)/shard_map/ppermute | solution.py:204
  109.0 17.9 %collective-permute-start.10 = (bf16[4,320,128]{2,1,0:T(8,128)(2,1)}, bf16[4,320,128]{2,1,0:T(8,128)(2,1)S(1)}, u32[]{:S(2)}, u32[]{:S(2)}) collective-permute-start(bf16[4,320,128]{2,1,0:T(8,128)(2,1)} %get-tuple-element.57), channel_id=1, source_target_pairs={{2,10},{6,14},{10,2},{14,6},{3,11},{7,15},{11,3},{15,7},{18,26},{2... | collective-permute-start | bytes 983048 | tf_op jit(solution)/shard_map/ppermute | solution.py:210
  111.6 13.0 %collective-permute-start.11 = (bf16[4,2,320,128]{3,2,1,0:T(8,128)(2,1)S(1)}, bf16[4,2,320,128]{3,2,1,0:T(8,128)(2,1)S(1)}, u32[]{:S(2)}, u32[]{:S(2)}) collective-permute-start(bf16[4,2,320,128]{3,2,1,0:T(8,128)(2,1)S(1)} %bitcast.23), channel_id=1, source_target_pairs={{0,1},{1,0},{2,3},{3,2},{4,5},{5,4},{6,7},{7,6},{8,9},{9,8},{10,11... | collective-permute-start | bytes 1966088 | tf_op jit(solution)/shard_map/ppermute | solution.py:204
  120.4 12.6 %collective-permute-start.9 = (bf16[4,320,128]{2,1,0:T(8,128)(2,1)}, bf16[4,320,128]{2,1,0:T(8,128)(2,1)S(1)}, u32[]{:S(2)}, u32[]{:S(2)}) collective-permute-start(bf16[4,320,128]{2,1,0:T(8,128)(2,1)} %collective-permute-done.7), channel_id=1, source_target_pairs={{0,4},{4,8},{8,12},{12,0},{1,5},{5,9},{9,13},{13,1},{2,6},{6,10},{... | collective-permute-start | bytes 983048 | tf_op jit(solution)/shard_map/ppermute | solution.py:204
  133.0 4.7 %collective-permute-start.13 = (bf16[4,2,320,128]{3,2,1,0:T(8,128)(2,1)S(1)}, bf16[4,2,320,128]{3,2,1,0:T(8,128)(2,1)S(1)}, u32[]{:S(2)}, u32[]{:S(2)}) collective-permute-start(bf16[4,2,320,128]{3,2,1,0:T(8,128)(2,1)S(1)} %collective-permute-done.8.one), channel_id=1, source_target_pairs={{0,1},{1,0},{2,3},{3,2},{4,5},{5,4},{6,7},{7,6},{8,9},{9,8},{10,11... | collective-permute-start | bytes 1966088 | tf_op jit(solution)/shard_map/ppermute | solution.py:204
  135.8 4.4 %collective-permute-start.12 = (bf16[4,2,320,128]{3,2,1,0:T(8,128)(2,1)S(1)}, bf16[4,2,320,128]{3,2,1,0:T(8,128)(2,1)S(1)}, u32[]{:S(2)}, u32[]{:S(2)}) collective-permute-start(bf16[4,2,320,128]{3,2,1,0:T(8,128)(2,1)S(1)} %pad_maximum_fusion.1.one), channel_id=1, source_target_pairs={{0,1},{1,0},{2,3},{3,2},{4,5},{5,4},{6,7},{7,6},{8,9},{9,8},{10,11... | collective-permute-start | bytes 1966088 | tf_op jit(solution)/shard_map/ppermute | solution.py:204

commit v11 on v10

--- a/solution.py
+++ b/solution.py
@@ -13,8 +13,8 @@
 CH = 128
 NT = 512
 BIN0 = 8
-GROUP = 5
-CHUNKS = (10, 10)
+GROUP = 4
+CHUNKS = (12, 8)
 NOFF = 9
 
 

time: 143 us -> 146 us (1.021)
  waiting for transfers between devices: 50.2 us -> 55.2 us
  starting transfers between devices: 69.5 us -> 65.3 us
    ppermute x12, starting transfers between devices: 39.8 us -> 35.3 us  [shifted(): lax.ppermute(value, axis, [(s, (s + steps) % count) for s in range(count)])]
    all_to_all x2, waiting for transfers between devices: 33 us -> 35.6 us  [spread(): here = lax.all_to_all(sent, ('x', 'z_hi', 'z_lo'), 0, 0, tiled=True)]
    ppermute x12, waiting for transfers between devices: 17.2 us -> 19.5 us  [shifted(): lax.ppermute(value, axis, [(s, (s + steps) % count) for s in range(count)])]
  transfers between devices with their start and end apart: 16 -> 16, of which waited for: 7 -> 6; matrix products, arithmetic and copies ran while one was open for 0% -> 0% of each run, Pallas kernels for 9% -> 9%
where the time goes in v11:
time: 146 us; the launch traced here: 144 us
  starting transfers between devices  65.3 us (45%)
  waiting for transfers between devices  55.2 us (38%)
  Pallas kernels  20.2 us (14%)
  local copies, waits for them, and re-layouts  2.81 us (2%)
    all_to_all x2, waiting for transfers between devices, spread(): here = lax.all_to_all(sent, ('x', 'z_hi', 'z_lo'), 0, 0, tiled=True)  35.6 us
    ppermute x12, starting transfers between devices, shifted(): lax.ppermute(value, axis, [(s, (s + steps) % count) for s in range(count)])  35.3 us
    all_to_all x2, starting transfers between devices, spread(): here = lax.all_to_all(sent, ('x', 'z_hi', 'z_lo'), 0, 0, tiled=True)  28.6 us
    ppermute x12, waiting for transfers between devices, shifted(): lax.ppermute(value, axis, [(s, (s + steps) % count) for s in range(count)])  19.5 us
    pallas_call x2, Pallas kernels, spectra(): pl.pallas_call(functools.partial(spectra_body, first=first, count=count,...  9.29 us
    pallas_call x3, Pallas kernels, late(): pl.pallas_call(functools.partial(late_body, ahead=ahead, scale=scale), in...  6.53 us
  transfers between devices with their start and end apart: 16, of which 6 were waited for; matrix products, arithmetic and copies ran while one was open for 0% of the time, Pallas kernels for 9%

profile of v11, /device:TPU:1, one launch (start us, length us, event | category | flops | bytes accessed | tf_op | source)
XLA Modules:
  0.0 144.0 jit_solution(8637894307045742809)
XLA Ops:
  0.0 5.2 %spectra.2 = bf16[4,2,384,128]{3,2,1,0:T(8,128)(2,1)} custom-call(bf16[20,128,512]{2,1,0:T(8,128)(2,1)} %bitcast.31, s32[20,128]{1,0:T(8,128)} %bitcast.39, s32[1,128]{1,0:T(1,128)} %refs_2_.3, bf16[128,512]{1,0:T(8,128)(2,1)} %constant.8.clone.refs_3_, f32[1,64]{1,0:T(1,128)} %bitcast.41), custom_call_target="tpu_custom_call" | custom-call | tf_op jit(solution)/shard_map/spectra/pallas_call | solution.py:88
  5.2 19.1 %all-to-all-start = ((bf16[64,48,128]{2,1,0:T(8,128)(2,1)}), bf16[64,48,128]{2,1,0:T(8,128)(2,1)S(1)}, u32[]{:S(2)}, u32[]{:S(2)}) async-start(bf16[64,48,128]{2,1,0:T(8,128)(2,1)} %bitcast.33), calls=%async_computation | async-start | bytes 1572864 | tf_op jit(solution)/shard_map/all_to_all | solution.py:238
  24.3 4.1 %spectra.3 = bf16[4,2,256,128]{3,2,1,0:T(8,128)(2,1)} custom-call(bf16[20,128,512]{2,1,0:T(8,128)(2,1)} %bitcast.32, s32[20,128]{1,0:T(8,128)} %bitcast.40, s32[1,128]{1,0:T(1,128)} %refs_2_.3, bf16[128,512]{1,0:T(8,128)(2,1)} %constant.8.clone.refs_3_, f32[1,64]{1,0:T(1,128)} %bitcast.42), custom_call_target="tpu_custom_call" | custom-call | tf_op jit(solution)/shard_map/spectra/pallas_call | solution.py:88
  28.4 35.6 %all-to-all-done = bf16[64,48,128]{2,1,0:T(8,128)(2,1)S(1)} async-done(((bf16[64,48,128]{2,1,0:T(8,128)(2,1)}), bf16[64,48,128]{2,1,0:T(8,128)(2,1)S(1)}, u32[]{:S(2)}, u32[]{:S(2)}) %all-to-all-start) | async-done | bytes 786464 | tf_op jit(solution)/shard_map/all_to_all | solution.py:238
  64.1 9.4 %all-to-all-start.1 = ((bf16[64,32,128]{2,1,0:T(8,128)(2,1)}), bf16[64,32,128]{2,1,0:T(8,128)(2,1)S(1)}, u32[]{:S(2)}, u32[]{:S(2)}) async-start(bf16[64,32,128]{2,1,0:T(8,128)(2,1)} %bitcast.34), calls=%async_computation.1 | async-start | bytes 1048576 | tf_op jit(solution)/shard_map/all_to_all | solution.py:238
  73.5 0.1 slice_bitcast_fusion
  73.6 3.2 %collective-permute-start = (bf16[4,384,128]{2,1,0:T(8,128)(2,1)S(1)}, bf16[4,384,128]{2,1,0:T(8,128)(2,1)S(1)}, u32[]{:S(2)}, u32[]{:S(2)}) collective-permute-start(bf16[4,384,128]{2,1,0:T(8,128)(2,1)S(1)} %get-tuple-element.58), channel_id=1, source_target_pairs={{0,4},{4,8},{8,12},{12,0},{1,5},{5,9},{9,13},{13,1},{2,6},{6,10},{... | collective-permute-start | bytes 1179656 | tf_op jit(solution)/shard_map/ppermute | solution.py:204
  76.8 3.4 %collective-permute-start.2 = (bf16[4,2,384,128]{3,2,1,0:T(8,128)(2,1)S(1)}, bf16[4,2,384,128]{3,2,1,0:T(8,128)(2,1)S(1)}, u32[]{:S(2)}, u32[]{:S(2)}) collective-permute-start(bf16[4,2,384,128]{3,2,1,0:T(8,128)(2,1)S(1)} %bitcast.22), channel_id=1, source_target_pairs={{0,12},{4,0},{8,4},{12,8},{1,13},{5,1},{9,5},{13,9},{2,14},{6,2},{... | collective-permute-start | bytes 2359304 | tf_op jit(solution)/shard_map/ppermute | solution.py:204
  80.2 0.7 collective-permute-start.5
  80.9 5.5 %collective-permute-done = bf16[4,384,128]{2,1,0:T(8,128)(2,1)S(1)} collective-permute-done((bf16[4,384,128]{2,1,0:T(8,128)(2,1)S(1)}, bf16[4,384,128]{2,1,0:T(8,128)(2,1)S(1)}, u32[]{:S(2)}, u32[]{:S(2)}) %collective-permute-start) | collective-permute-done | bytes 393248 | tf_op jit(solution)/shard_map/ppermute | solution.py:204
  86.3 1.9 %collective-permute-start.4 = (bf16[4,384,128]{2,1,0:T(8,128)(2,1)S(1)}, bf16[4,384,128]{2,1,0:T(8,128)(2,1)S(1)}, u32[]{:S(2)}, u32[]{:S(2)}) collective-permute-start(bf16[4,384,128]{2,1,0:T(8,128)(2,1)S(1)} %collective-permute-done), channel_id=1, source_target_pairs={{0,4},{4,8},{8,12},{12,0},{1,5},{5,9},{9,13},{13,1},{2,6},{6,10},{... | collective-permute-start | bytes 1179656 | tf_op jit(solution)/shard_map/ppermute | solution.py:204
  88.3 4.2 %collective-permute-start.1 = (bf16[4,2,384,128]{3,2,1,0:T(8,128)(2,1)S(1)}, bf16[4,2,384,128]{3,2,1,0:T(8,128)(2,1)S(1)}, u32[]{:S(2)}, u32[]{:S(2)}) collective-permute-start(bf16[4,2,384,128]{3,2,1,0:T(8,128)(2,1)S(1)} %bitcast.23), channel_id=1, source_target_pairs={{0,1},{1,0},{2,3},{3,2},{4,5},{5,4},{6,7},{7,6},{8,9},{9,8},{10,11... | collective-permute-start | bytes 2359304 | tf_op jit(solution)/shard_map/ppermute | solution.py:204
  92.4 5.6 %collective-permute-done.4 = bf16[4,384,128]{2,1,0:T(8,128)(2,1)S(1)} collective-permute-done((bf16[4,384,128]{2,1,0:T(8,128)(2,1)S(1)}, bf16[4,384,128]{2,1,0:T(8,128)(2,1)S(1)}, u32[]{:S(2)}, u32[]{:S(2)}) %collective-permute-start.4) | collective-permute-done | bytes 393248 | tf_op jit(solution)/shard_map/ppermute | solution.py:204
  98.1 0.1 pad_maximum_fusion.refs_4_
  98.2 4.8 %collective-permute-start.6 = (bf16[4,2,384,128]{3,2,1,0:T(8,128)(2,1)S(1)}, bf16[4,2,384,128]{3,2,1,0:T(8,128)(2,1)S(1)}, u32[]{:S(2)}, u32[]{:S(2)}) collective-permute-start(bf16[4,2,384,128]{3,2,1,0:T(8,128)(2,1)S(1)} %pad_maximum_fusion.refs_4_), channel_id=1, source_target_pairs={{0,1},{1,0},{2,3},{3,2},{4,5},{5,4},{6,7},{7,6},{8,9},{9,8},{10,11... | collective-permute-start | bytes 2359304 | tf_op jit(solution)/shard_map/ppermute | solution.py:204
  103.0 0.0 collective-permute-done.2.refs_2_
  103.0 1.9 %collective-permute-start.3 = (bf16[4,2,384,128]{3,2,1,0:T(8,128)(2,1)S(1)}, bf16[4,2,384,128]{3,2,1,0:T(8,128)(2,1)S(1)}, u32[]{:S(2)}, u32[]{:S(2)}) collective-permute-start(bf16[4,2,384,128]{3,2,1,0:T(8,128)(2,1)S(1)} %collective-permute-done.2.refs_2_), channel_id=1, source_target_pairs={{0,1},{1,0},{2,3},{3,2},{4,5},{5,4},{6,7},{7,6},{8,9},{9,8},{10,11... | collective-permute-start | bytes 2359304 | tf_op jit(solution)/shard_map/ppermute | solution.py:204
  104.9 0.0 collective-permute-done.1.refs_1_
  104.9 0.0 copy-start
  104.9 0.9 copy-done
  105.8 0.0 collective-permute-done.6.refs_5_
  105.8 0.9 copy-done.2
  106.7 0.4 collective-permute-done.3.refs_3_
  107.2 0.9 copy-done.4
  108.0 0.0 all-to-all-done.1
  108.1 1.9 %collective-permute-start.7 = (bf16[4,256,128]{2,1,0:T(8,128)(2,1)S(1)}, bf16[4,256,128]{2,1,0:T(8,128)(2,1)}, u32[]{:S(2)}, u32[]{:S(2)}) collective-permute-start(bf16[4,256,128]{2,1,0:T(8,128)(2,1)S(1)} %get-tuple-element.60), channel_id=1, source_target_pairs={{0,4},{4,8},{8,12},{12,0},{1,5},{5,9},{9,13},{13,1},{2,6},{6,10},{... | collective-permute-start | bytes 786440 | tf_op jit(solution)/shard_map/ppermute | solution.py:204
  110.0 0.0 copy-start.1
  110.0 0.1 pad_add_fusion.where
  110.1 4.7 %collective-permute-start.8 = (bf16[4,2,256,128]{3,2,1,0:T(8,128)(2,1)S(1)}, bf16[4,2,256,128]{3,2,1,0:T(8,128)(2,1)S(1)}, u32[]{:S(2)}, u32[]{:S(2)}) collective-permute-start(bf16[4,2,256,128]{3,2,1,0:T(8,128)(2,1)S(1)} %bitcast.27), channel_id=1, source_target_pairs={{0,12},{4,0},{8,4},{12,8},{1,13},{5,1},{9,5},{13,9},{2,14},{6,2},{... | collective-permute-start | bytes 1572872 | tf_op jit(solution)/shard_map/ppermute | solution.py:204
  114.8 0.7 collective-permute-start.10
  115.5 3.5 %collective-permute-done.7 = bf16[4,256,128]{2,1,0:T(8,128)(2,1)} collective-permute-done((bf16[4,256,128]{2,1,0:T(8,128)(2,1)S(1)}, bf16[4,256,128]{2,1,0:T(8,128)(2,1)}, u32[]{:S(2)}, u32[]{:S(2)}) %collective-permute-start.7) | collective-permute-done | bytes 262176 | tf_op jit(solution)/shard_map/ppermute | solution.py:204
  119.1 2.9 %collective-permute-start.11 = (bf16[4,2,256,128]{3,2,1,0:T(8,128)(2,1)S(1)}, bf16[4,2,256,128]{3,2,1,0:T(8,128)(2,1)S(1)}, u32[]{:S(2)}, u32[]{:S(2)}) collective-permute-start(bf16[4,2,256,128]{3,2,1,0:T(8,128)(2,1)S(1)} %bitcast.28), channel_id=1, source_target_pairs={{0,1},{1,0},{2,3},{3,2},{4,5},{5,4},{6,7},{7,6},{8,9},{9,8},{10,11... | collective-permute-start | bytes 1572872 | tf_op jit(solution)/shard_map/ppermute | solution.py:204
  121.9 0.8 left.2
  122.7 0.9 left.3
  123.7 1.9 %collective-permute-start.9 = (bf16[4,256,128]{2,1,0:T(8,128)(2,1)}, bf16[4,256,128]{2,1,0:T(8,128)(2,1)S(1)}, u32[]{:S(2)}, u32[]{:S(2)}) collective-permute-start(bf16[4,256,128]{2,1,0:T(8,128)(2,1)} %collective-permute-done.7), channel_id=1, source_target_pairs={{0,4},{4,8},{8,12},{12,0},{1,5},{5,9},{9,13},{13,1},{2,6},{6,10},{... | collective-permute-start | bytes 786440 | tf_op jit(solution)/shard_map/ppermute | solution.py:204
  125.6 2.6 %early.1 = (f32[2,512,256]{2,1,0:T(8,128)S(1)}, f32[2,512,256]{2,1,0:T(8,128)S(1)}, f32[2,512,256]{2,1,0:T(8,128)S(1)}) custom-call(bf16[512,1536]{1,0:T(8,128)(2,1)S(1)} %left.3, bf16[4,2,384,128]{3,2,1,0:T(8,128)(2,1)S(1)} %bitcast.25, bf16[4,2,384,128]{3,2,1,0:T(8,128)(2,1)S(1)} %copy-done.1, bf16[4,2,384,128]{3,2,1,0:T(8,128)(2,1)S(1)} %collective-permute-done.2.refs_2_, ...), custom_call_target="tpu_custom_call" | custom-call | flops 20000000000 | bytes 12000000 | tf_op jit(solution)/shard_map/early/pallas_call | solution.py:146
  128.3 0.0 collective-permute-done.11.two
  128.3 2.2 %late.3.refs_0_ = f32[2,2,9,128,128]{4,3,2,1,0:T(8,128)} custom-call(s32[2]{0:T(128)S(1)} %pad_add_fusion.where, bf16[512,1024]{1,0:T(8,128)(2,1)S(1)} %left.2, f32[2,512,256]{2,1,0:T(8,128)S(1)} %get-tuple-element.51.begun, bf16[4,2,256,128]{3,2,1,0:T(8,128)(2,1)S(1)} %bitcast.30, bf16[4,2,256,128]{3,2,1,0:T(8,128)(2,1)S(1)} %collective-permute-done.11.two), custom_call_target="tpu_custom_call" | custom-call | flops 4000000000 | bytes 4000000 | tf_op jit(solution)/shard_map/late/pallas_call | solution.py:182
  130.5 0.0 collective-permute-done.10
  130.5 0.0 collective-permute-done.8.one
  130.5 4.4 %collective-permute-done.9 = bf16[4,256,128]{2,1,0:T(8,128)(2,1)S(1)} collective-permute-done((bf16[4,256,128]{2,1,0:T(8,128)(2,1)}, bf16[4,256,128]{2,1,0:T(8,128)(2,1)S(1)}, u32[]{:S(2)}, u32[]{:S(2)}) %collective-permute-start.9) | collective-permute-done | bytes 262176 | tf_op jit(solution)/shard_map/ppermute | solution.py:204
  134.9 2.7 %collective-permute-start.13 = (bf16[4,2,256,128]{3,2,1,0:T(8,128)(2,1)S(1)}, bf16[4,2,256,128]{3,2,1,0:T(8,128)(2,1)S(1)}, u32[]{:S(2)}, u32[]{:S(2)}) collective-permute-start(bf16[4,2,256,128]{3,2,1,0:T(8,128)(2,1)S(1)} %collective-permute-done.8.one), channel_id=1, source_target_pairs={{0,1},{1,0},{2,3},{3,2},{4,5},{5,4},{6,7},{7,6},{8,9},{9,8},{10,11... | collective-permute-start | bytes 1572872 | tf_op jit(solution)/shard_map/ppermute | solution.py:204
  137.6 0.1 pad_maximum_fusion.1.one
  137.7 1.9 %collective-permute-start.12 = (bf16[4,2,256,128]{3,2,1,0:T(8,128)(2,1)S(1)}, bf16[4,2,256,128]{3,2,1,0:T(8,128)(2,1)S(1)}, u32[]{:S(2)}, u32[]{:S(2)}) collective-permute-start(bf16[4,2,256,128]{3,2,1,0:T(8,128)(2,1)S(1)} %pad_maximum_fusion.1.one), channel_id=1, source_target_pairs={{0,1},{1,0},{2,3},{3,2},{4,5},{5,4},{6,7},{7,6},{8,9},{9,8},{10,11... | collective-permute-start | bytes 1572872 | tf_op jit(solution)/shard_map/ppermute | solution.py:204
  139.6 0.0 collective-permute-done.13.two
  139.6 2.3 %late.4.refs_0_ = f32[2,2,9,128,128]{4,3,2,1,0:T(8,128)} custom-call(s32[2]{0:T(128)S(1)} %pad_add_fusion.where, bf16[512,1024]{1,0:T(8,128)(2,1)S(1)} %left.2, f32[2,512,256]{2,1,0:T(8,128)S(1)} %get-tuple-element.54.begun, bf16[4,2,256,128]{3,2,1,0:T(8,128)(2,1)S(1)} %collective-permute-done.8.one, ...), custom_call_target="tpu_custom_call", output_to_operand_aliasing={{}: (5, {})} | custom-call | flops 4000000000 | bytes 4000000 | tf_op jit(solution)/shard_map/late/pallas_call | solution.py:182
  141.9 0.0 collective-permute-done.12.two
  141.9 2.1 %late.5 = f32[2,2,9,128,128]{4,3,2,1,0:T(8,128)} custom-call(s32[2]{0:T(128)S(1)} %pad_add_fusion.where, bf16[512,1024]{1,0:T(8,128)(2,1)S(1)} %left.2, f32[2,512,256]{2,1,0:T(8,128)S(1)} %get-tuple-element.49.begun, bf16[4,2,256,128]{3,2,1,0:T(8,128)(2,1)S(1)} %pad_maximum_fusion.1.one, ...), custom_call_target="tpu_custom_call", output_to_operand_aliasing={{}: (5, {})} | custom-call | flops 4000000000 | bytes 4000000 | tf_op jit(solution)/shard_map/late/pallas_call | solution.py:182
  (9 shorter events, 0.1 us)
Async XLA Ops:
  5.2 58.9 %all-to-all-start = ((bf16[64,48,128]{2,1,0:T(8,128)(2,1)}), bf16[64,48,128]{2,1,0:T(8,128)(2,1)S(1)}, u32[]{:S(2)}, u32[]{:S(2)}) async-start(bf16[64,48,128]{2,1,0:T(8,128)(2,1)} %bitcast.33), calls=%async_computation | async-start | bytes 1572864 | tf_op jit(solution)/shard_map/all_to_all | solution.py:238
  64.1 44.0 %all-to-all-start.1 = ((bf16[64,32,128]{2,1,0:T(8,128)(2,1)}), bf16[64,32,128]{2,1,0:T(8,128)(2,1)S(1)}, u32[]{:S(2)}, u32[]{:S(2)}) async-start(bf16[64,32,128]{2,1,0:T(8,128)(2,1)} %bitcast.34), calls=%async_computation.1 | async-start | bytes 1048576 | tf_op jit(solution)/shard_map/all_to_all | solution.py:238
  73.6 12.7 %collective-permute-start = (bf16[4,384,128]{2,1,0:T(8,128)(2,1)S(1)}, bf16[4,384,128]{2,1,0:T(8,128)(2,1)S(1)}, u32[]{:S(2)}, u32[]{:S(2)}) collective-permute-start(bf16[4,384,128]{2,1,0:T(8,128)(2,1)S(1)} %get-tuple-element.58), channel_id=1, source_target_pairs={{0,4},{4,8},{8,12},{12,0},{1,5},{5,9},{9,13},{13,1},{2,6},{6,10},{... | collective-permute-start | bytes 1179656 | tf_op jit(solution)/shard_map/ppermute | solution.py:204
  76.8 26.1 %collective-permute-start.2 = (bf16[4,2,384,128]{3,2,1,0:T(8,128)(2,1)S(1)}, bf16[4,2,384,128]{3,2,1,0:T(8,128)(2,1)S(1)}, u32[]{:S(2)}, u32[]{:S(2)}) collective-permute-start(bf16[4,2,384,128]{3,2,1,0:T(8,128)(2,1)S(1)} %bitcast.22), channel_id=1, source_target_pairs={{0,12},{4,0},{8,4},{12,8},{1,13},{5,1},{9,5},{13,9},{2,14},{6,2},{... | collective-permute-start | bytes 2359304 | tf_op jit(solution)/shard_map/ppermute | solution.py:204
  80.2 12.2 %collective-permute-start.5 = (bf16[4,384,128]{2,1,0:T(8,128)(2,1)S(1)}, bf16[4,384,128]{2,1,0:T(8,128)(2,1)S(1)}, u32[]{:S(2)}, u32[]{:S(2)}) collective-permute-start(bf16[4,384,128]{2,1,0:T(8,128)(2,1)S(1)} %get-tuple-element.57), channel_id=1, source_target_pairs={{2,10},{6,14},{10,2},{14,6},{3,11},{7,15},{11,3},{15,7},{18,26},{2... | collective-permute-start | bytes 1179656 | tf_op jit(solution)/shard_map/ppermute | solution.py:210
  86.3 11.7 %collective-permute-start.4 = (bf16[4,384,128]{2,1,0:T(8,128)(2,1)S(1)}, bf16[4,384,128]{2,1,0:T(8,128)(2,1)S(1)}, u32[]{:S(2)}, u32[]{:S(2)}) collective-permute-start(bf16[4,384,128]{2,1,0:T(8,128)(2,1)S(1)} %collective-permute-done), channel_id=1, source_target_pairs={{0,4},{4,8},{8,12},{12,0},{1,5},{5,9},{9,13},{13,1},{2,6},{6,10},{... | collective-permute-start | bytes 1179656 | tf_op jit(solution)/shard_map/ppermute | solution.py:204
  88.3 16.6 %collective-permute-start.1 = (bf16[4,2,384,128]{3,2,1,0:T(8,128)(2,1)S(1)}, bf16[4,2,384,128]{3,2,1,0:T(8,128)(2,1)S(1)}, u32[]{:S(2)}, u32[]{:S(2)}) collective-permute-start(bf16[4,2,384,128]{3,2,1,0:T(8,128)(2,1)S(1)} %bitcast.23), channel_id=1, source_target_pairs={{0,1},{1,0},{2,3},{3,2},{4,5},{5,4},{6,7},{7,6},{8,9},{9,8},{10,11... | collective-permute-start | bytes 2359304 | tf_op jit(solution)/shard_map/ppermute | solution.py:204
  98.2 7.6 %collective-permute-start.6 = (bf16[4,2,384,128]{3,2,1,0:T(8,128)(2,1)S(1)}, bf16[4,2,384,128]{3,2,1,0:T(8,128)(2,1)S(1)}, u32[]{:S(2)}, u32[]{:S(2)}) collective-permute-start(bf16[4,2,384,128]{3,2,1,0:T(8,128)(2,1)S(1)} %pad_maximum_fusion.refs_4_), channel_id=1, source_target_pairs={{0,1},{1,0},{2,3},{3,2},{4,5},{5,4},{6,7},{7,6},{8,9},{9,8},{10,11... | collective-permute-start | bytes 2359304 | tf_op jit(solution)/shard_map/ppermute | solution.py:204
  103.0 4.2 %collective-permute-start.3 = (bf16[4,2,384,128]{3,2,1,0:T(8,128)(2,1)S(1)}, bf16[4,2,384,128]{3,2,1,0:T(8,128)(2,1)S(1)}, u32[]{:S(2)}, u32[]{:S(2)}) collective-permute-start(bf16[4,2,384,128]{3,2,1,0:T(8,128)(2,1)S(1)} %collective-permute-done.2.refs_2_), channel_id=1, source_target_pairs={{0,1},{1,0},{2,3},{3,2},{4,5},{5,4},{6,7},{7,6},{8,9},{9,8},{10,11... | collective-permute-start | bytes 2359304 | tf_op jit(solution)/shard_map/ppermute | solution.py:204
  104.9 0.9 copy-start
  105.8 0.9 copy-start.2
  107.2 0.9 copy-start.4
  108.1 11.0 %collective-permute-start.7 = (bf16[4,256,128]{2,1,0:T(8,128)(2,1)S(1)}, bf16[4,256,128]{2,1,0:T(8,128)(2,1)}, u32[]{:S(2)}, u32[]{:S(2)}) collective-permute-start(bf16[4,256,128]{2,1,0:T(8,128)(2,1)S(1)} %get-tuple-element.60), channel_id=1, source_target_pairs={{0,4},{4,8},{8,12},{12,0},{1,5},{5,9},{9,13},{13,1},{2,6},{6,10},{... | collective-permute-start | bytes 786440 | tf_op jit(solution)/shard_map/ppermute | solution.py:204
  110.0 15.6 %copy-start.1 = (bf16[4,2,384,128]{3,2,1,0:T(8,128)(2,1)S(1)}, bf16[4,2,384,128]{3,2,1,0:T(8,128)(2,1)}, u32[]{:S(2)}) copy-start(bf16[4,2,384,128]{3,2,1,0:T(8,128)(2,1)} %copy-done) | copy-start | bytes 2359300
  110.0 15.6 %copy-start.3 = (bf16[4,2,384,128]{3,2,1,0:T(8,128)(2,1)S(1)}, bf16[4,2,384,128]{3,2,1,0:T(8,128)(2,1)}, u32[]{:S(2)}) copy-start(bf16[4,2,384,128]{3,2,1,0:T(8,128)(2,1)} %copy-done.2) | copy-start | bytes 2359300
  110.0 15.6 %copy-start.5 = (bf16[4,2,384,128]{3,2,1,0:T(8,128)(2,1)S(1)}, bf16[4,2,384,128]{3,2,1,0:T(8,128)(2,1)}, u32[]{:S(2)}) copy-start(bf16[4,2,384,128]{3,2,1,0:T(8,128)(2,1)} %copy-done.4) | copy-start | bytes 2359300
  110.1 20.4 %collective-permute-start.8 = (bf16[4,2,256,128]{3,2,1,0:T(8,128)(2,1)S(1)}, bf16[4,2,256,128]{3,2,1,0:T(8,128)(2,1)S(1)}, u32[]{:S(2)}, u32[]{:S(2)}) collective-permute-start(bf16[4,2,256,128]{3,2,1,0:T(8,128)(2,1)S(1)} %bitcast.27), channel_id=1, source_target_pairs={{0,12},{4,0},{8,4},{12,8},{1,13},{5,1},{9,5},{13,9},{2,14},{6,2},{... | collective-permute-start | bytes 1572872 | tf_op jit(solution)/shard_map/ppermute | solution.py:204
  114.8 15.6 %collective-permute-start.10 = (bf16[4,256,128]{2,1,0:T(8,128)(2,1)S(1)}, bf16[4,256,128]{2,1,0:T(8,128)(2,1)S(1)}, u32[]{:S(2)}, u32[]{:S(2)}) collective-permute-start(bf16[4,256,128]{2,1,0:T(8,128)(2,1)S(1)} %get-tuple-element.59), channel_id=1, source_target_pairs={{2,10},{6,14},{10,2},{14,6},{3,11},{7,15},{11,3},{15,7},{18,26},{2... | collective-permute-start | bytes 786440 | tf_op jit(solution)/shard_map/ppermute | solution.py:210
  119.1 9.2 %collective-permute-start.11 = (bf16[4,2,256,128]{3,2,1,0:T(8,128)(2,1)S(1)}, bf16[4,2,256,128]{3,2,1,0:T(8,128)(2,1)S(1)}, u32[]{:S(2)}, u32[]{:S(2)}) collective-permute-start(bf16[4,2,256,128]{3,2,1,0:T(8,128)(2,1)S(1)} %bitcast.28), channel_id=1, source_target_pairs={{0,1},{1,0},{2,3},{3,2},{4,5},{5,4},{6,7},{7,6},{8,9},{9,8},{10,11... | collective-permute-start | bytes 1572872 | tf_op jit(solution)/shard_map/ppermute | solution.py:204
  123.7 11.2 %collective-permute-start.9 = (bf16[4,256,128]{2,1,0:T(8,128)(2,1)}, bf16[4,256,128]{2,1,0:T(8,128)(2,1)S(1)}, u32[]{:S(2)}, u32[]{:S(2)}) collective-permute-start(bf16[4,256,128]{2,1,0:T(8,128)(2,1)} %collective-permute-done.7), channel_id=1, source_target_pairs={{0,4},{4,8},{8,12},{12,0},{1,5},{5,9},{9,13},{13,1},{2,6},{6,10},{... | collective-permute-start | bytes 786440 | tf_op jit(solution)/shard_map/ppermute | solution.py:204
  134.9 4.7 %collective-permute-start.13 = (bf16[4,2,256,128]{3,2,1,0:T(8,128)(2,1)S(1)}, bf16[4,2,256,128]{3,2,1,0:T(8,128)(2,1)S(1)}, u32[]{:S(2)}, u32[]{:S(2)}) collective-permute-start(bf16[4,2,256,128]{3,2,1,0:T(8,128)(2,1)S(1)} %collective-permute-done.8.one), channel_id=1, source_target_pairs={{0,1},{1,0},{2,3},{3,2},{4,5},{5,4},{6,7},{7,6},{8,9},{9,8},{10,11... | collective-permute-start | bytes 1572872 | tf_op jit(solution)/shard_map/ppermute | solution.py:204
  137.7 4.2 %collective-permute-start.12 = (bf16[4,2,256,128]{3,2,1,0:T(8,128)(2,1)S(1)}, bf16[4,2,256,128]{3,2,1,0:T(8,128)(2,1)S(1)}, u32[]{:S(2)}, u32[]{:S(2)}) collective-permute-start(bf16[4,2,256,128]{3,2,1,0:T(8,128)(2,1)S(1)} %pad_maximum_fusion.1.one), channel_id=1, source_target_pairs={{0,1},{1,0},{2,3},{3,2},{4,5},{5,4},{6,7},{7,6},{8,9},{9,8},{10,11... | collective-permute-start | bytes 1572872 | tf_op jit(solution)/shard_map/ppermute | solution.py:204

commit v12 on v10

--- a/solution.py
+++ b/solution.py
@@ -148,7 +148,7 @@
         in_specs=[whole] * 7,
         out_specs=[whole] * 3,
         out_shape=[jax.ShapeDtypeStruct((2, 4 * CH, 2 * CH), jnp.float32)] * 3,
-        cost_estimate=pl.CostEstimate(flops=20 * 10**9, transcendentals=0, bytes_accessed=12 * 10**6),
+        cost_estimate=pl.CostEstimate(flops=1 * 10**8, transcendentals=0, bytes_accessed=10**5),
         compiler_params=grant(24),
         name="early",
     )(left, *data)
@@ -193,7 +193,7 @@
         out_shape=jax.ShapeDtypeStruct((2, 2, NOFF, CH, CH), jnp.float32),
         input_output_aliases={5: 0} if extra else {},
         scratch_shapes=[pltpu.VMEM((4, 2, 2, CH, CH), jnp.float32), pltpu.SemaphoreType.DMA((4,))],
-        cost_estimate=pl.CostEstimate(flops=4 * 10**9, transcendentals=0, bytes_accessed=4 * 10**6),
+        cost_estimate=pl.CostEstimate(flops=1 * 10**8, transcendentals=0, bytes_accessed=10**5),
         compiler_params=grant(16),
         name="late",
     )(where, left, begun, one, two, *extra)
@@ -244,7 +244,7 @@
     head = both([first, ahead1, jnp.stack(ahead2, axis=1)])
     tail = spread(second)
     tail, *head = lax.optimization_barrier((tail, *head))
-    (tail, ahead1, ahead2), head = fetched(tail, head)
+    (own, ahead1, ahead2), _ = fetched(tail, [])
     begun = early(left_of(where, head[0]), head)
     left = left_of(where, tail)
     filled = late(where, left, begun[0], tail, shifted(tail, "core", 1), None, 0, scale)

time: 143 us -> 145 us (1.014)
  transfers between devices with their start and end apart: 16 -> 16, of which waited for: 7 -> 7; matrix products, arithmetic and copies ran while one was open for 0% -> 1% of each run, Pallas kernels for 9% -> 9%
where the time goes in v12:
time: 145 us; the launch traced here: 144 us
  starting transfers between devices  69.8 us (48%)
  waiting for transfers between devices  49.9 us (34%)
  Pallas kernels  20 us (14%)
  local copies, waits for them, and re-layouts  2.6 us (2%)
    ppermute x12, starting transfers between devices, shifted(): lax.ppermute(value, axis, [(s, (s + steps) % count) for s in range(count)])  39.3 us
    all_to_all x2, waiting for transfers between devices, spread(): here = lax.all_to_all(sent, ('x', 'z_hi', 'z_lo'), 0, 0, tiled=True)  33 us
    all_to_all x2, starting transfers between devices, spread(): here = lax.all_to_all(sent, ('x', 'z_hi', 'z_lo'), 0, 0, tiled=True)  28.4 us
    ppermute x12, waiting for transfers between devices, shifted(): lax.ppermute(value, axis, [(s, (s + steps) % count) for s in range(count)])  16.9 us
    pallas_call x2, Pallas kernels, spectra(): pl.pallas_call(functools.partial(spectra_body, first=first, count=count,...  8.59 us
    pallas_call x3, Pallas kernels, late(): pl.pallas_call(functools.partial(late_body, ahead=ahead, scale=scale), in...  7.51 us
  transfers between devices with their start and end apart: 16, of which 7 were waited for; matrix products, arithmetic and copies ran while one was open for 1% of the time, Pallas kernels for 9%

profile of v12, /device:TPU:1, one launch (start us, length us, event | category | flops | bytes accessed | tf_op | source)
XLA Modules:
  0.0 143.9 jit_solution(3761409222933040691)
XLA Ops:
  0.0 4.3 %spectra.2 = bf16[4,2,320,128]{3,2,1,0:T(8,128)(2,1)} custom-call(bf16[20,128,512]{2,1,0:T(8,128)(2,1)} %bitcast.31, s32[20,128]{1,0:T(8,128)} %bitcast.37, s32[1,128]{1,0:T(1,128)} %refs_2_.3, bf16[128,512]{1,0:T(8,128)(2,1)} %constant.8.clone.refs_3_, f32[1,64]{1,0:T(1,128)} %bitcast.39), custom_call_target="tpu_custom_call" | custom-call | tf_op jit(solution)/shard_map/spectra/pallas_call | solution.py:88
  4.3 19.1 %all-to-all-start = ((bf16[64,40,128]{2,1,0:T(8,128)(2,1)}), bf16[64,40,128]{2,1,0:T(8,128)(2,1)S(1)}, u32[]{:S(2)}, u32[]{:S(2)}) async-start(bf16[64,40,128]{2,1,0:T(8,128)(2,1)} %bitcast.34), calls=%async_computation | async-start | bytes 1310720 | tf_op jit(solution)/shard_map/all_to_all | solution.py:238
  23.4 4.3 %spectra.3 = bf16[4,2,320,128]{3,2,1,0:T(8,128)(2,1)} custom-call(bf16[20,128,512]{2,1,0:T(8,128)(2,1)} %bitcast.32, s32[20,128]{1,0:T(8,128)} %bitcast.38, s32[1,128]{1,0:T(1,128)} %refs_2_.3, bf16[128,512]{1,0:T(8,128)(2,1)} %constant.8.clone.refs_3_, f32[1,64]{1,0:T(1,128)} %bitcast.40), custom_call_target="tpu_custom_call" | custom-call | tf_op jit(solution)/shard_map/spectra/pallas_call | solution.py:88
  27.7 30.1 %all-to-all-done = bf16[64,40,128]{2,1,0:T(8,128)(2,1)S(1)} async-done(((bf16[64,40,128]{2,1,0:T(8,128)(2,1)}), bf16[64,40,128]{2,1,0:T(8,128)(2,1)S(1)}, u32[]{:S(2)}, u32[]{:S(2)}) %all-to-all-start) | async-done | bytes 655392 | tf_op jit(solution)/shard_map/all_to_all | solution.py:238
  57.8 9.2 %all-to-all-start.1 = ((bf16[64,40,128]{2,1,0:T(8,128)(2,1)}), bf16[64,40,128]{2,1,0:T(8,128)(2,1)S(1)}, u32[]{:S(2)}, u32[]{:S(2)}) async-start(bf16[64,40,128]{2,1,0:T(8,128)(2,1)} %bitcast.33), calls=%async_computation.1 | async-start | bytes 1310720 | tf_op jit(solution)/shard_map/all_to_all | solution.py:238
  67.1 3.2 %collective-permute-start = (bf16[4,320,128]{2,1,0:T(8,128)(2,1)S(1)}, bf16[4,320,128]{2,1,0:T(8,128)(2,1)S(1)}, u32[]{:S(2)}, u32[]{:S(2)}) collective-permute-start(bf16[4,320,128]{2,1,0:T(8,128)(2,1)S(1)} %get-tuple-element.46), channel_id=1, source_target_pairs={{0,4},{4,8},{8,12},{12,0},{1,5},{5,9},{9,13},{13,1},{2,6},{6,10},{... | collective-permute-start | bytes 983048 | tf_op jit(solution)/shard_map/ppermute | solution.py:204
  70.4 3.4 %collective-permute-start.2 = (bf16[4,2,320,128]{3,2,1,0:T(8,128)(2,1)S(1)}, bf16[4,2,320,128]{3,2,1,0:T(8,128)(2,1)S(1)}, u32[]{:S(2)}, u32[]{:S(2)}) collective-permute-start(bf16[4,2,320,128]{3,2,1,0:T(8,128)(2,1)S(1)} %bitcast.27), channel_id=1, source_target_pairs={{0,12},{4,0},{8,4},{12,8},{1,13},{5,1},{9,5},{13,9},{2,14},{6,2},{... | collective-permute-start | bytes 1966088 | tf_op jit(solution)/shard_map/ppermute | solution.py:204
  73.7 0.7 collective-permute-start.5
  74.4 4.0 %collective-permute-done = bf16[4,320,128]{2,1,0:T(8,128)(2,1)S(1)} collective-permute-done((bf16[4,320,128]{2,1,0:T(8,128)(2,1)S(1)}, bf16[4,320,128]{2,1,0:T(8,128)(2,1)S(1)}, u32[]{:S(2)}, u32[]{:S(2)}) %collective-permute-start) | collective-permute-done | bytes 327712 | tf_op jit(solution)/shard_map/ppermute | solution.py:204
  78.4 1.9 %collective-permute-start.4 = (bf16[4,320,128]{2,1,0:T(8,128)(2,1)S(1)}, bf16[4,320,128]{2,1,0:T(8,128)(2,1)S(1)}, u32[]{:S(2)}, u32[]{:S(2)}) collective-permute-start(bf16[4,320,128]{2,1,0:T(8,128)(2,1)S(1)} %collective-permute-done), channel_id=1, source_target_pairs={{0,4},{4,8},{8,12},{12,0},{1,5},{5,9},{9,13},{13,1},{2,6},{6,10},{... | collective-permute-start | bytes 983048 | tf_op jit(solution)/shard_map/ppermute | solution.py:204
  80.3 4.2 %collective-permute-start.1 = (bf16[4,2,320,128]{3,2,1,0:T(8,128)(2,1)S(1)}, bf16[4,2,320,128]{3,2,1,0:T(8,128)(2,1)S(1)}, u32[]{:S(2)}, u32[]{:S(2)}) collective-permute-start(bf16[4,2,320,128]{3,2,1,0:T(8,128)(2,1)S(1)} %bitcast.28), channel_id=1, source_target_pairs={{0,1},{1,0},{2,3},{3,2},{4,5},{5,4},{6,7},{7,6},{8,9},{9,8},{10,11... | collective-permute-start | bytes 1966088 | tf_op jit(solution)/shard_map/ppermute | solution.py:204
  84.6 0.0 collective-permute-done.5
  84.6 4.1 %collective-permute-done.4 = bf16[4,320,128]{2,1,0:T(8,128)(2,1)S(1)} collective-permute-done((bf16[4,320,128]{2,1,0:T(8,128)(2,1)S(1)}, bf16[4,320,128]{2,1,0:T(8,128)(2,1)S(1)}, u32[]{:S(2)}, u32[]{:S(2)}) %collective-permute-start.4) | collective-permute-done | bytes 327712 | tf_op jit(solution)/shard_map/ppermute | solution.py:204
  88.6 0.1 pad_maximum_fusion.refs_4_
  88.7 4.9 %collective-permute-start.6 = (bf16[4,2,320,128]{3,2,1,0:T(8,128)(2,1)S(1)}, bf16[4,2,320,128]{3,2,1,0:T(8,128)(2,1)S(1)}, u32[]{:S(2)}, u32[]{:S(2)}) collective-permute-start(bf16[4,2,320,128]{3,2,1,0:T(8,128)(2,1)S(1)} %pad_maximum_fusion.refs_4_), channel_id=1, source_target_pairs={{0,1},{1,0},{2,3},{3,2},{4,5},{5,4},{6,7},{7,6},{8,9},{9,8},{10,11... | collective-permute-start | bytes 1966088 | tf_op jit(solution)/shard_map/ppermute | solution.py:204
  93.6 0.0 collective-permute-done.2.refs_2_
  93.6 1.9 %collective-permute-start.3 = (bf16[4,2,320,128]{3,2,1,0:T(8,128)(2,1)S(1)}, bf16[4,2,320,128]{3,2,1,0:T(8,128)(2,1)S(1)}, u32[]{:S(2)}, u32[]{:S(2)}) collective-permute-start(bf16[4,2,320,128]{3,2,1,0:T(8,128)(2,1)S(1)} %collective-permute-done.2.refs_2_), channel_id=1, source_target_pairs={{0,1},{1,0},{2,3},{3,2},{4,5},{5,4},{6,7},{7,6},{8,9},{9,8},{10,11... | collective-permute-start | bytes 1966088 | tf_op jit(solution)/shard_map/ppermute | solution.py:204
  95.5 0.0 collective-permute-done.1.refs_1_
  95.5 0.0 copy-start
  95.5 0.0 collective-permute-done.6.refs_5_
  95.6 0.0 copy-start.2
  95.6 0.9 copy-done.2
  96.4 1.1 collective-permute-done.3.refs_3_
  97.6 0.9 copy-done.4
  98.5 2.9 %all-to-all-done.1 = bf16[64,40,128]{2,1,0:T(8,128)(2,1)S(1)} async-done(((bf16[64,40,128]{2,1,0:T(8,128)(2,1)}), bf16[64,40,128]{2,1,0:T(8,128)(2,1)S(1)}, u32[]{:S(2)}, u32[]{:S(2)}) %all-to-all-start.1) | async-done | bytes 655392 | tf_op jit(solution)/shard_map/all_to_all | solution.py:238
  101.3 5.9 %collective-permute-start.11 = (bf16[4,2,320,128]{3,2,1,0:T(8,128)(2,1)S(1)}, bf16[4,2,320,128]{3,2,1,0:T(8,128)(2,1)}, u32[]{:S(2)}, u32[]{:S(2)}) collective-permute-start(bf16[4,2,320,128]{3,2,1,0:T(8,128)(2,1)S(1)} %bitcast.21), channel_id=1, source_target_pairs={{0,1},{1,0},{2,3},{3,2},{4,5},{5,4},{6,7},{7,6},{8,9},{9,8},{10,11... | collective-permute-start | bytes 1966088 | tf_op jit(solution)/shard_map/ppermute | solution.py:204
  107.3 0.8 slice_bitcast_fusion
  108.1 3.2 %collective-permute-start.8 = (bf16[4,320,128]{2,1,0:T(8,128)(2,1)S(1)}, bf16[4,320,128]{2,1,0:T(8,128)(2,1)}, u32[]{:S(2)}, u32[]{:S(2)}) collective-permute-start(bf16[4,320,128]{2,1,0:T(8,128)(2,1)S(1)} %get-tuple-element.44), channel_id=1, source_target_pairs={{0,4},{4,8},{8,12},{12,0},{1,5},{5,9},{9,13},{13,1},{2,6},{6,10},{... | collective-permute-start | bytes 983048 | tf_op jit(solution)/shard_map/ppermute | solution.py:204
  111.3 3.4 %collective-permute-start.7 = (bf16[4,2,320,128]{3,2,1,0:T(8,128)(2,1)S(1)}, bf16[4,2,320,128]{3,2,1,0:T(8,128)(2,1)S(1)}, u32[]{:S(2)}, u32[]{:S(2)}) collective-permute-start(bf16[4,2,320,128]{3,2,1,0:T(8,128)(2,1)S(1)} %bitcast.23), channel_id=1, source_target_pairs={{0,12},{4,0},{8,4},{12,8},{1,13},{5,1},{9,5},{13,9},{2,14},{6,2},{... | collective-permute-start | bytes 1966088 | tf_op jit(solution)/shard_map/ppermute | solution.py:204
  114.6 1.4 collective-permute-start.10
  116.0 4.7 %collective-permute-done.8 = bf16[4,320,128]{2,1,0:T(8,128)(2,1)} collective-permute-done((bf16[4,320,128]{2,1,0:T(8,128)(2,1)S(1)}, bf16[4,320,128]{2,1,0:T(8,128)(2,1)}, u32[]{:S(2)}, u32[]{:S(2)}) %collective-permute-start.8) | collective-permute-done | bytes 327712 | tf_op jit(solution)/shard_map/ppermute | solution.py:204
  120.7 1.9 %collective-permute-start.9 = (bf16[4,320,128]{2,1,0:T(8,128)(2,1)}, bf16[4,320,128]{2,1,0:T(8,128)(2,1)}, u32[]{:S(2)}, u32[]{:S(2)}) collective-permute-start(bf16[4,320,128]{2,1,0:T(8,128)(2,1)} %collective-permute-done.8), channel_id=1, source_target_pairs={{0,4},{4,8},{8,12},{12,0},{1,5},{5,9},{9,13},{13,1},{2,6},{6,10},{... | collective-permute-start | bytes 983048 | tf_op jit(solution)/shard_map/ppermute | solution.py:204
  122.7 0.1 pad_add_fusion.where
  122.8 0.9 left.2
  123.6 0.9 left.3
  124.5 2.2 %early.1 = (f32[2,512,256]{2,1,0:T(8,128)S(1)}, f32[2,512,256]{2,1,0:T(8,128)S(1)}, f32[2,512,256]{2,1,0:T(8,128)S(1)}) custom-call(bf16[512,1280]{1,0:T(8,128)(2,1)S(1)} %left.3, bf16[4,2,320,128]{3,2,1,0:T(8,128)(2,1)S(1)} %bitcast.30, bf16[4,2,320,128]{3,2,1,0:T(8,128)(2,1)S(1)} %copy-done.1, bf16[4,2,320,128]{3,2,1,0:T(8,128)(2,1)S(1)} %collective-permute-done.2.refs_2_, ...), custom_call_target="tpu_custom_call" | custom-call | flops 100000000 | bytes 100000 | tf_op jit(solution)/shard_map/early/pallas_call | solution.py:146
  126.8 0.0 collective-permute-done.11.two
  126.8 2.9 %late.3.refs_0_ = f32[2,2,9,128,128]{4,3,2,1,0:T(8,128)} custom-call(s32[2]{0:T(128)S(1)} %pad_add_fusion.where, bf16[512,1280]{1,0:T(8,128)(2,1)S(1)} %left.2, f32[2,512,256]{2,1,0:T(8,128)S(1)} %get-tuple-element.37.begun, bf16[4,2,320,128]{3,2,1,0:T(8,128)(2,1)S(1)} %bitcast.25, bf16[4,2,320,128]{3,2,1,0:T(8,128)(2,1)} %collective-permute-done.11.two), custom_call_target="tpu_custom_call" | custom-call | flops 100000000 | bytes 100000 | tf_op jit(solution)/shard_map/late/pallas_call | solution.py:182
  129.7 0.0 collective-permute-done.10
  129.7 0.0 collective-permute-done.7.one
  129.7 3.0 %collective-permute-done.9 = bf16[4,320,128]{2,1,0:T(8,128)(2,1)} collective-permute-done((bf16[4,320,128]{2,1,0:T(8,128)(2,1)}, bf16[4,320,128]{2,1,0:T(8,128)(2,1)}, u32[]{:S(2)}, u32[]{:S(2)}) %collective-permute-start.9) | collective-permute-done | bytes 327712 | tf_op jit(solution)/shard_map/ppermute | solution.py:204
  132.7 3.5 %collective-permute-start.13 = (bf16[4,2,320,128]{3,2,1,0:T(8,128)(2,1)S(1)}, bf16[4,2,320,128]{3,2,1,0:T(8,128)(2,1)S(1)}, u32[]{:S(2)}, u32[]{:S(2)}) collective-permute-start(bf16[4,2,320,128]{3,2,1,0:T(8,128)(2,1)S(1)} %collective-permute-done.7.one), channel_id=1, source_target_pairs={{0,1},{1,0},{2,3},{3,2},{4,5},{5,4},{6,7},{7,6},{8,9},{9,8},{10,11... | collective-permute-start | bytes 1966088 | tf_op jit(solution)/shard_map/ppermute | solution.py:204
  136.2 1.1 pad_maximum_fusion.1.one
  137.3 1.9 %collective-permute-start.12 = (bf16[4,2,320,128]{3,2,1,0:T(8,128)(2,1)S(1)}, bf16[4,2,320,128]{3,2,1,0:T(8,128)(2,1)S(1)}, u32[]{:S(2)}, u32[]{:S(2)}) collective-permute-start(bf16[4,2,320,128]{3,2,1,0:T(8,128)(2,1)S(1)} %pad_maximum_fusion.1.one), channel_id=1, source_target_pairs={{0,1},{1,0},{2,3},{3,2},{4,5},{5,4},{6,7},{7,6},{8,9},{9,8},{10,11... | collective-permute-start | bytes 1966088 | tf_op jit(solution)/shard_map/ppermute | solution.py:204
  139.3 0.0 collective-permute-done.13.two
  139.3 2.4 %late.4.refs_0_ = f32[2,2,9,128,128]{4,3,2,1,0:T(8,128)} custom-call(s32[2]{0:T(128)S(1)} %pad_add_fusion.where, bf16[512,1280]{1,0:T(8,128)(2,1)S(1)} %left.2, f32[2,512,256]{2,1,0:T(8,128)S(1)} %get-tuple-element.40.begun, bf16[4,2,320,128]{3,2,1,0:T(8,128)(2,1)S(1)} %collective-permute-done.7.one, ...), custom_call_target="tpu_custom_call", output_to_operand_aliasing={{}: (5, {})} | custom-call | flops 100000000 | bytes 100000 | tf_op jit(solution)/shard_map/late/pallas_call | solution.py:182
  141.7 0.0 collective-permute-done.12.two
  141.7 2.2 %late.5 = f32[2,2,9,128,128]{4,3,2,1,0:T(8,128)} custom-call(s32[2]{0:T(128)S(1)} %pad_add_fusion.where, bf16[512,1280]{1,0:T(8,128)(2,1)S(1)} %left.2, f32[2,512,256]{2,1,0:T(8,128)S(1)} %get-tuple-element.35.begun, bf16[4,2,320,128]{3,2,1,0:T(8,128)(2,1)S(1)} %pad_maximum_fusion.1.one, ...), custom_call_target="tpu_custom_call", output_to_operand_aliasing={{}: (5, {})} | custom-call | flops 100000000 | bytes 100000 | tf_op jit(solution)/shard_map/late/pallas_call | solution.py:182
  (9 shorter events, 0.1 us)
Async XLA Ops:
  4.3 53.5 %all-to-all-start = ((bf16[64,40,128]{2,1,0:T(8,128)(2,1)}), bf16[64,40,128]{2,1,0:T(8,128)(2,1)S(1)}, u32[]{:S(2)}, u32[]{:S(2)}) async-start(bf16[64,40,128]{2,1,0:T(8,128)(2,1)} %bitcast.34), calls=%async_computation | async-start | bytes 1310720 | tf_op jit(solution)/shard_map/all_to_all | solution.py:238
  57.8 43.5 %all-to-all-start.1 = ((bf16[64,40,128]{2,1,0:T(8,128)(2,1)}), bf16[64,40,128]{2,1,0:T(8,128)(2,1)S(1)}, u32[]{:S(2)}, u32[]{:S(2)}) async-start(bf16[64,40,128]{2,1,0:T(8,128)(2,1)} %bitcast.33), calls=%async_computation.1 | async-start | bytes 1310720 | tf_op jit(solution)/shard_map/all_to_all | solution.py:238
  67.1 11.2 %collective-permute-start = (bf16[4,320,128]{2,1,0:T(8,128)(2,1)S(1)}, bf16[4,320,128]{2,1,0:T(8,128)(2,1)S(1)}, u32[]{:S(2)}, u32[]{:S(2)}) collective-permute-start(bf16[4,320,128]{2,1,0:T(8,128)(2,1)S(1)} %get-tuple-element.46), channel_id=1, source_target_pairs={{0,4},{4,8},{8,12},{12,0},{1,5},{5,9},{9,13},{13,1},{2,6},{6,10},{... | collective-permute-start | bytes 983048 | tf_op jit(solution)/shard_map/ppermute | solution.py:204
  70.4 23.2 %collective-permute-start.2 = (bf16[4,2,320,128]{3,2,1,0:T(8,128)(2,1)S(1)}, bf16[4,2,320,128]{3,2,1,0:T(8,128)(2,1)S(1)}, u32[]{:S(2)}, u32[]{:S(2)}) collective-permute-start(bf16[4,2,320,128]{3,2,1,0:T(8,128)(2,1)S(1)} %bitcast.27), channel_id=1, source_target_pairs={{0,12},{4,0},{8,4},{12,8},{1,13},{5,1},{9,5},{13,9},{2,14},{6,2},{... | collective-permute-start | bytes 1966088 | tf_op jit(solution)/shard_map/ppermute | solution.py:204
  73.7 10.8 %collective-permute-start.5 = (bf16[4,320,128]{2,1,0:T(8,128)(2,1)S(1)}, bf16[4,320,128]{2,1,0:T(8,128)(2,1)S(1)}, u32[]{:S(2)}, u32[]{:S(2)}) collective-permute-start(bf16[4,320,128]{2,1,0:T(8,128)(2,1)S(1)} %get-tuple-element.45), channel_id=1, source_target_pairs={{2,10},{6,14},{10,2},{14,6},{3,11},{7,15},{11,3},{15,7},{18,26},{2... | collective-permute-start | bytes 983048 | tf_op jit(solution)/shard_map/ppermute | solution.py:210
  78.4 10.2 %collective-permute-start.4 = (bf16[4,320,128]{2,1,0:T(8,128)(2,1)S(1)}, bf16[4,320,128]{2,1,0:T(8,128)(2,1)S(1)}, u32[]{:S(2)}, u32[]{:S(2)}) collective-permute-start(bf16[4,320,128]{2,1,0:T(8,128)(2,1)S(1)} %collective-permute-done), channel_id=1, source_target_pairs={{0,4},{4,8},{8,12},{12,0},{1,5},{5,9},{9,13},{13,1},{2,6},{6,10},{... | collective-permute-start | bytes 983048 | tf_op jit(solution)/shard_map/ppermute | solution.py:204
  80.3 15.2 %collective-permute-start.1 = (bf16[4,2,320,128]{3,2,1,0:T(8,128)(2,1)S(1)}, bf16[4,2,320,128]{3,2,1,0:T(8,128)(2,1)S(1)}, u32[]{:S(2)}, u32[]{:S(2)}) collective-permute-start(bf16[4,2,320,128]{3,2,1,0:T(8,128)(2,1)S(1)} %bitcast.28), channel_id=1, source_target_pairs={{0,1},{1,0},{2,3},{3,2},{4,5},{5,4},{6,7},{7,6},{8,9},{9,8},{10,11... | collective-permute-start | bytes 1966088 | tf_op jit(solution)/shard_map/ppermute | solution.py:204
  88.7 6.9 %collective-permute-start.6 = (bf16[4,2,320,128]{3,2,1,0:T(8,128)(2,1)S(1)}, bf16[4,2,320,128]{3,2,1,0:T(8,128)(2,1)S(1)}, u32[]{:S(2)}, u32[]{:S(2)}) collective-permute-start(bf16[4,2,320,128]{3,2,1,0:T(8,128)(2,1)S(1)} %pad_maximum_fusion.refs_4_), channel_id=1, source_target_pairs={{0,1},{1,0},{2,3},{3,2},{4,5},{5,4},{6,7},{7,6},{8,9},{9,8},{10,11... | collective-permute-start | bytes 1966088 | tf_op jit(solution)/shard_map/ppermute | solution.py:204
  93.6 4.0 %collective-permute-start.3 = (bf16[4,2,320,128]{3,2,1,0:T(8,128)(2,1)S(1)}, bf16[4,2,320,128]{3,2,1,0:T(8,128)(2,1)S(1)}, u32[]{:S(2)}, u32[]{:S(2)}) collective-permute-start(bf16[4,2,320,128]{3,2,1,0:T(8,128)(2,1)S(1)} %collective-permute-done.2.refs_2_), channel_id=1, source_target_pairs={{0,1},{1,0},{2,3},{3,2},{4,5},{5,4},{6,7},{7,6},{8,9},{9,8},{10,11... | collective-permute-start | bytes 1966088 | tf_op jit(solution)/shard_map/ppermute | solution.py:204
  95.5 12.5 %copy-start = (bf16[4,2,320,128]{3,2,1,0:T(8,128)(2,1)}, bf16[4,2,320,128]{3,2,1,0:T(8,128)(2,1)S(1)}, u32[]{:S(2)}) copy-start(bf16[4,2,320,128]{3,2,1,0:T(8,128)(2,1)S(1)} %collective-permute-done.1.refs_1_) | copy-start | bytes 1966084
  95.6 0.9 copy-start.2
  97.6 0.9 copy-start.4
  101.3 25.4 %collective-permute-start.11 = (bf16[4,2,320,128]{3,2,1,0:T(8,128)(2,1)S(1)}, bf16[4,2,320,128]{3,2,1,0:T(8,128)(2,1)}, u32[]{:S(2)}, u32[]{:S(2)}) collective-permute-start(bf16[4,2,320,128]{3,2,1,0:T(8,128)(2,1)S(1)} %bitcast.21), channel_id=1, source_target_pairs={{0,1},{1,0},{2,3},{3,2},{4,5},{5,4},{6,7},{7,6},{8,9},{9,8},{10,11... | collective-permute-start | bytes 1966088 | tf_op jit(solution)/shard_map/ppermute | solution.py:204
  108.1 12.7 %collective-permute-start.8 = (bf16[4,320,128]{2,1,0:T(8,128)(2,1)S(1)}, bf16[4,320,128]{2,1,0:T(8,128)(2,1)}, u32[]{:S(2)}, u32[]{:S(2)}) collective-permute-start(bf16[4,320,128]{2,1,0:T(8,128)(2,1)S(1)} %get-tuple-element.44), channel_id=1, source_target_pairs={{0,4},{4,8},{8,12},{12,0},{1,5},{5,9},{9,13},{13,1},{2,6},{6,10},{... | collective-permute-start | bytes 983048 | tf_op jit(solution)/shard_map/ppermute | solution.py:204
  111.3 18.4 %collective-permute-start.7 = (bf16[4,2,320,128]{3,2,1,0:T(8,128)(2,1)S(1)}, bf16[4,2,320,128]{3,2,1,0:T(8,128)(2,1)S(1)}, u32[]{:S(2)}, u32[]{:S(2)}) collective-permute-start(bf16[4,2,320,128]{3,2,1,0:T(8,128)(2,1)S(1)} %bitcast.23), channel_id=1, source_target_pairs={{0,12},{4,0},{8,4},{12,8},{1,13},{5,1},{9,5},{13,9},{2,14},{6,2},{... | collective-permute-start | bytes 1966088 | tf_op jit(solution)/shard_map/ppermute | solution.py:204
  114.6 15.0 %collective-permute-start.10 = (bf16[4,320,128]{2,1,0:T(8,128)(2,1)}, bf16[4,320,128]{2,1,0:T(8,128)(2,1)}, u32[]{:S(2)}, u32[]{:S(2)}) collective-permute-start(bf16[4,320,128]{2,1,0:T(8,128)(2,1)} %get-tuple-element.43), channel_id=1, source_target_pairs={{2,10},{6,14},{10,2},{14,6},{3,11},{7,15},{11,3},{15,7},{18,26},{2... | collective-permute-start | bytes 983048 | tf_op jit(solution)/shard_map/ppermute | solution.py:210
  120.7 11.9 %collective-permute-start.9 = (bf16[4,320,128]{2,1,0:T(8,128)(2,1)}, bf16[4,320,128]{2,1,0:T(8,128)(2,1)}, u32[]{:S(2)}, u32[]{:S(2)}) collective-permute-start(bf16[4,320,128]{2,1,0:T(8,128)(2,1)} %collective-permute-done.8), channel_id=1, source_target_pairs={{0,4},{4,8},{8,12},{12,0},{1,5},{5,9},{9,13},{13,1},{2,6},{6,10},{... | collective-permute-start | bytes 983048 | tf_op jit(solution)/shard_map/ppermute | solution.py:204
  122.7 1.8 %copy-start.1 = (bf16[4,2,320,128]{3,2,1,0:T(8,128)(2,1)S(1)}, bf16[4,2,320,128]{3,2,1,0:T(8,128)(2,1)}, u32[]{:S(2)}) copy-start(bf16[4,2,320,128]{3,2,1,0:T(8,128)(2,1)} %copy-done) | copy-start | bytes 1966084
  122.7 1.8 %copy-start.3 = (bf16[4,2,320,128]{3,2,1,0:T(8,128)(2,1)S(1)}, bf16[4,2,320,128]{3,2,1,0:T(8,128)(2,1)}, u32[]{:S(2)}) copy-start(bf16[4,2,320,128]{3,2,1,0:T(8,128)(2,1)} %copy-done.2) | copy-start | bytes 1966084
  122.7 1.8 %copy-start.5 = (bf16[4,2,320,128]{3,2,1,0:T(8,128)(2,1)S(1)}, bf16[4,2,320,128]{3,2,1,0:T(8,128)(2,1)}, u32[]{:S(2)}) copy-start(bf16[4,2,320,128]{3,2,1,0:T(8,128)(2,1)} %copy-done.4) | copy-start | bytes 1966084
  132.7 6.6 %collective-permute-start.13 = (bf16[4,2,320,128]{3,2,1,0:T(8,128)(2,1)S(1)}, bf16[4,2,320,128]{3,2,1,0:T(8,128)(2,1)S(1)}, u32[]{:S(2)}, u32[]{:S(2)}) collective-permute-start(bf16[4,2,320,128]{3,2,1,0:T(8,128)(2,1)S(1)} %collective-permute-done.7.one), channel_id=1, source_target_pairs={{0,1},{1,0},{2,3},{3,2},{4,5},{5,4},{6,7},{7,6},{8,9},{9,8},{10,11... | collective-permute-start | bytes 1966088 | tf_op jit(solution)/shard_map/ppermute | solution.py:204
  137.3 4.4 %collective-permute-start.12 = (bf16[4,2,320,128]{3,2,1,0:T(8,128)(2,1)S(1)}, bf16[4,2,320,128]{3,2,1,0:T(8,128)(2,1)S(1)}, u32[]{:S(2)}, u32[]{:S(2)}) collective-permute-start(bf16[4,2,320,128]{3,2,1,0:T(8,128)(2,1)S(1)} %pad_maximum_fusion.1.one), channel_id=1, source_target_pairs={{0,1},{1,0},{2,3},{3,2},{4,5},{5,4},{6,7},{7,6},{8,9},{9,8},{10,11... | collective-permute-start | bytes 1966088 | tf_op jit(solution)/shard_map/ppermute | solution.py:204

commit v13 on v9

--- a/solution.py
+++ b/solution.py
@@ -148,7 +148,7 @@
         in_specs=[whole] * 7,
         out_specs=[whole] * 3,
         out_shape=[jax.ShapeDtypeStruct((2, 4 * CH, 2 * CH), jnp.float32)] * 3,
-        cost_estimate=pl.CostEstimate(flops=20 * 10**9, transcendentals=0, bytes_accessed=12 * 10**6),
+        cost_estimate=pl.CostEstimate(flops=7 * 10**9, transcendentals=0, bytes_accessed=12 * 10**6),
         compiler_params=grant(24),
         name="early",
     )(left, *data)
@@ -193,7 +193,7 @@
         out_shape=jax.ShapeDtypeStruct((2, 2, NOFF, CH, CH), jnp.float32),
         input_output_aliases={5: 0} if extra else {},
         scratch_shapes=[pltpu.VMEM((4, 2, 2, CH, CH), jnp.float32), pltpu.SemaphoreType.DMA((4,))],
-        cost_estimate=pl.CostEstimate(flops=4 * 10**9, transcendentals=0, bytes_accessed=4 * 10**6),
+        cost_estimate=pl.CostEstimate(flops=2 * 10**9, transcendentals=0, bytes_accessed=4 * 10**6),
         compiler_params=grant(16),
         name="late",
     )(where, left, begun, one, two, *extra)
@@ -210,9 +210,10 @@
     return lax.ppermute(value, ("y", "z_hi"), pairs)
 
 
-def hopped(here):
-    low = shifted(shifted(here[:, 0], "y", 1), "y", 1)
-    return [here, shifted(here, "y", -1), jnp.stack([low, upper(here[:, 1], 2)], axis=1)]
+def fetched(here, held):
+    ahead1 = shifted(here, "y", -1)
+    low, *held = lax.optimization_barrier((shifted(here[:, 0], "y", 1), *held))
+    return [here, ahead1, jnp.stack([shifted(low, "y", 1), upper(here[:, 1], 2)], axis=1)], held
 
 
 def both(own):
@@ -238,16 +239,19 @@
 
     first, second = spread(made(0, CHUNKS[0])), made(*CHUNKS)
     first, second = lax.optimization_barrier((first, second))
-    head = both(hopped(first))
+    head = both(fetched(first, [])[0])
     tail = spread(second)
     tail, *head = lax.optimization_barrier((tail, *head))
-    ahead1, ahead2 = shifted(tail, "y", -1), shifted(tail, "y", 2)
+    (_, ahead1, ahead2), head = fetched(tail, head)
     begun = early(left_of(where, head[0]), head)
     left = left_of(where, tail)
     filled = late(where, left, begun[0], tail, shifted(tail, "core", 1), None, 0, scale)
-    filled = late(where, left, begun[1], ahead1, shifted(ahead1, "core", 1), filled, 1, scale)
-    ahead2, filled = lax.optimization_barrier((ahead2, filled))
-    return late(where, left, begun[2], ahead2, shifted(ahead2, "core", 1), filled, 2, scale)
+    ahead1, ahead2, left, filled, *begun = lax.optimization_barrier((ahead1, ahead2, left, filled, *begun))
+    data = both([ahead1, ahead2])
+    for ahead in (1, 2):
+        one, two = data[2 * ahead - 2 : 2 * ahead]
+        filled = late(where, left, begun[ahead], one, two, filled, ahead, scale)
+    return filled
 
 
 def solution(mesh):

time: 153 us -> 142 us (0.928)
  starting transfers between devices: 84.2 us -> 68.9 us
  waiting for transfers between devices: 44.2 us -> 48.1 us
    ppermute x11 -> x12, starting transfers between devices: 55.2 us -> 39.2 us  [shifted(): lax.ppermute(value, axis, [(s, (s + steps) % count) for s in range(count)])]
    ppermute x11 -> x12, waiting for transfers between devices: 11.2 us -> 15.1 us  [shifted(): lax.ppermute(value, axis, [(s, (s + steps) % count) for s in range(count)])]
  transfers between devices with their start and end apart: 14 -> 16, of which waited for: 6 -> 7; matrix products, arithmetic and copies ran while one was open for 0% -> 0% of each run, Pallas kernels for 9% -> 9%
where the time goes in v13:
time: 142 us; the launch traced here: 140 us
  starting transfers between devices  68.9 us (49%)
  waiting for transfers between devices  48.1 us (34%)
  Pallas kernels  19.5 us (14%)
  local copies, waits for them, and re-layouts  2.64 us (2%)
    ppermute x12, starting transfers between devices, shifted(): lax.ppermute(value, axis, [(s, (s + steps) % count) for s in range(count)])  39.2 us
    all_to_all x2, waiting for transfers between devices, spread(): here = lax.all_to_all(sent, ('x', 'z_hi', 'z_lo'), 0, 0, tiled=True)  33 us
    all_to_all x2, starting transfers between devices, spread(): here = lax.all_to_all(sent, ('x', 'z_hi', 'z_lo'), 0, 0, tiled=True)  28.4 us
    ppermute x12, waiting for transfers between devices, shifted(): lax.ppermute(value, axis, [(s, (s + steps) % count) for s in range(count)])  15.1 us
    pallas_call x2, Pallas kernels, spectra(): pl.pallas_call(functools.partial(spectra_body, first=first, count=count,...  8.6 us
    pallas_call x3, Pallas kernels, late(): pl.pallas_call(functools.partial(late_body, ahead=ahead, scale=scale), in...  6.96 us
  transfers between devices with their start and end apart: 16, of which 7 were waited for; matrix products, arithmetic and copies ran while one was open for 0% of the time, Pallas kernels for 9%

profile of v13, /device:TPU:1, one launch (start us, length us, event | category | flops | bytes accessed | tf_op | source)
XLA Modules:
  0.0 139.6 jit_solution(16360742598198868129)
XLA Ops:
  0.0 4.3 %spectra.2 = bf16[4,2,320,128]{3,2,1,0:T(8,128)(2,1)} custom-call(bf16[20,128,512]{2,1,0:T(8,128)(2,1)} %bitcast.31, s32[20,128]{1,0:T(8,128)} %bitcast.39, s32[1,128]{1,0:T(1,128)} %refs_2_.3, bf16[128,512]{1,0:T(8,128)(2,1)} %constant.8.clone.refs_3_, f32[1,64]{1,0:T(1,128)} %bitcast.41), custom_call_target="tpu_custom_call" | custom-call | tf_op jit(solution)/shard_map/spectra/pallas_call | solution.py:88
  4.3 19.1 %all-to-all-start = ((bf16[64,40,128]{2,1,0:T(8,128)(2,1)}), bf16[64,40,128]{2,1,0:T(8,128)(2,1)S(1)}, u32[]{:S(2)}, u32[]{:S(2)}) async-start(bf16[64,40,128]{2,1,0:T(8,128)(2,1)} %bitcast.34), calls=%async_computation | async-start | bytes 1310720 | tf_op jit(solution)/shard_map/all_to_all | solution.py:237
  23.5 4.3 %spectra.3 = bf16[4,2,320,128]{3,2,1,0:T(8,128)(2,1)} custom-call(bf16[20,128,512]{2,1,0:T(8,128)(2,1)} %bitcast.32, s32[20,128]{1,0:T(8,128)} %bitcast.40, s32[1,128]{1,0:T(1,128)} %refs_2_.3, bf16[128,512]{1,0:T(8,128)(2,1)} %constant.8.clone.refs_3_, f32[1,64]{1,0:T(1,128)} %bitcast.42), custom_call_target="tpu_custom_call" | custom-call | tf_op jit(solution)/shard_map/spectra/pallas_call | solution.py:88
  27.7 30.1 %all-to-all-done = bf16[64,40,128]{2,1,0:T(8,128)(2,1)S(1)} async-done(((bf16[64,40,128]{2,1,0:T(8,128)(2,1)}), bf16[64,40,128]{2,1,0:T(8,128)(2,1)S(1)}, u32[]{:S(2)}, u32[]{:S(2)}) %all-to-all-start) | async-done | bytes 655392 | tf_op jit(solution)/shard_map/all_to_all | solution.py:237
  57.9 9.2 %all-to-all-start.1 = ((bf16[64,40,128]{2,1,0:T(8,128)(2,1)}), bf16[64,40,128]{2,1,0:T(8,128)(2,1)S(1)}, u32[]{:S(2)}, u32[]{:S(2)}) async-start(bf16[64,40,128]{2,1,0:T(8,128)(2,1)} %bitcast.33), calls=%async_computation.1 | async-start | bytes 1310720 | tf_op jit(solution)/shard_map/all_to_all | solution.py:237
  67.2 3.2 %collective-permute-start.3 = (bf16[4,320,128]{2,1,0:T(8,128)(2,1)S(1)}, bf16[4,320,128]{2,1,0:T(8,128)(2,1)S(1)}, u32[]{:S(2)}, u32[]{:S(2)}) collective-permute-start(bf16[4,320,128]{2,1,0:T(8,128)(2,1)S(1)} %get-tuple-element.57), channel_id=1, source_target_pairs={{0,4},{4,8},{8,12},{12,0},{1,5},{5,9},{9,13},{13,1},{2,6},{6,10},{... | collective-permute-start | bytes 983048 | tf_op jit(solution)/shard_map/ppermute | solution.py:204
  70.4 3.4 %collective-permute-start.1 = (bf16[4,2,320,128]{3,2,1,0:T(8,128)(2,1)S(1)}, bf16[4,2,320,128]{3,2,1,0:T(8,128)(2,1)S(1)}, u32[]{:S(2)}, u32[]{:S(2)}) collective-permute-start(bf16[4,2,320,128]{3,2,1,0:T(8,128)(2,1)S(1)} %bitcast.27), channel_id=1, source_target_pairs={{0,12},{4,0},{8,4},{12,8},{1,13},{5,1},{9,5},{13,9},{2,14},{6,2},{... | collective-permute-start | bytes 1966088 | tf_op jit(solution)/shard_map/ppermute | solution.py:204
  73.7 0.7 collective-permute-start.5
  74.4 4.0 %collective-permute-done.3 = bf16[4,320,128]{2,1,0:T(8,128)(2,1)S(1)} collective-permute-done((bf16[4,320,128]{2,1,0:T(8,128)(2,1)S(1)}, bf16[4,320,128]{2,1,0:T(8,128)(2,1)S(1)}, u32[]{:S(2)}, u32[]{:S(2)}) %collective-permute-start.3) | collective-permute-done | bytes 327712 | tf_op jit(solution)/shard_map/ppermute | solution.py:204
  78.4 1.9 %collective-permute-start.4 = (bf16[4,320,128]{2,1,0:T(8,128)(2,1)S(1)}, bf16[4,320,128]{2,1,0:T(8,128)(2,1)S(1)}, u32[]{:S(2)}, u32[]{:S(2)}) collective-permute-start(bf16[4,320,128]{2,1,0:T(8,128)(2,1)S(1)} %collective-permute-done.3), channel_id=1, source_target_pairs={{0,4},{4,8},{8,12},{12,0},{1,5},{5,9},{9,13},{13,1},{2,6},{6,10},{... | collective-permute-start | bytes 983048 | tf_op jit(solution)/shard_map/ppermute | solution.py:204
  80.3 4.2 %collective-permute-start = (bf16[4,2,320,128]{3,2,1,0:T(8,128)(2,1)S(1)}, bf16[4,2,320,128]{3,2,1,0:T(8,128)(2,1)S(1)}, u32[]{:S(2)}, u32[]{:S(2)}) collective-permute-start(bf16[4,2,320,128]{3,2,1,0:T(8,128)(2,1)S(1)} %bitcast.28), channel_id=1, source_target_pairs={{0,1},{1,0},{2,3},{3,2},{4,5},{5,4},{6,7},{7,6},{8,9},{9,8},{10,11... | collective-permute-start | bytes 1966088 | tf_op jit(solution)/shard_map/ppermute | solution.py:204
  84.6 0.0 collective-permute-done.5
  84.6 4.1 %collective-permute-done.4 = bf16[4,320,128]{2,1,0:T(8,128)(2,1)S(1)} collective-permute-done((bf16[4,320,128]{2,1,0:T(8,128)(2,1)S(1)}, bf16[4,320,128]{2,1,0:T(8,128)(2,1)S(1)}, u32[]{:S(2)}, u32[]{:S(2)}) %collective-permute-start.4) | collective-permute-done | bytes 327712 | tf_op jit(solution)/shard_map/ppermute | solution.py:204
  88.6 0.1 pad_maximum_fusion.refs_4_
  88.7 4.9 %collective-permute-start.6 = (bf16[4,2,320,128]{3,2,1,0:T(8,128)(2,1)S(1)}, bf16[4,2,320,128]{3,2,1,0:T(8,128)(2,1)S(1)}, u32[]{:S(2)}, u32[]{:S(2)}) collective-permute-start(bf16[4,2,320,128]{3,2,1,0:T(8,128)(2,1)S(1)} %pad_maximum_fusion.refs_4_), channel_id=1, source_target_pairs={{0,1},{1,0},{2,3},{3,2},{4,5},{5,4},{6,7},{7,6},{8,9},{9,8},{10,11... | collective-permute-start | bytes 1966088 | tf_op jit(solution)/shard_map/ppermute | solution.py:204
  93.6 0.0 collective-permute-done.1.refs_2_
  93.6 1.9 %collective-permute-start.2 = (bf16[4,2,320,128]{3,2,1,0:T(8,128)(2,1)S(1)}, bf16[4,2,320,128]{3,2,1,0:T(8,128)(2,1)S(1)}, u32[]{:S(2)}, u32[]{:S(2)}) collective-permute-start(bf16[4,2,320,128]{3,2,1,0:T(8,128)(2,1)S(1)} %collective-permute-done.1.refs_2_), channel_id=1, source_target_pairs={{0,1},{1,0},{2,3},{3,2},{4,5},{5,4},{6,7},{7,6},{8,9},{9,8},{10,11... | collective-permute-start | bytes 1966088 | tf_op jit(solution)/shard_map/ppermute | solution.py:204
  95.5 0.0 collective-permute-done.refs_1_
  95.5 0.0 collective-permute-done.6.refs_5_
  95.6 0.0 copy-start
  95.6 0.8 copy-done
  96.4 1.2 collective-permute-done.2.refs_3_
  97.6 0.9 copy-done.2
  98.5 2.9 %all-to-all-done.1 = bf16[64,40,128]{2,1,0:T(8,128)(2,1)S(1)} async-done(((bf16[64,40,128]{2,1,0:T(8,128)(2,1)}), bf16[64,40,128]{2,1,0:T(8,128)(2,1)S(1)}, u32[]{:S(2)}, u32[]{:S(2)}) %all-to-all-start.1) | async-done | bytes 655392 | tf_op jit(solution)/shard_map/all_to_all | solution.py:237
  101.4 0.9 slice_bitcast_fusion.1
  102.2 3.2 %collective-permute-start.8 = (bf16[4,320,128]{2,1,0:T(8,128)(2,1)}, bf16[4,320,128]{2,1,0:T(8,128)(2,1)}, u32[]{:S(2)}, u32[]{:S(2)}) collective-permute-start(bf16[4,320,128]{2,1,0:T(8,128)(2,1)} %get-tuple-element.55), channel_id=1, source_target_pairs={{0,4},{4,8},{8,12},{12,0},{1,5},{5,9},{9,13},{13,1},{2,6},{6,10},{... | collective-permute-start | bytes 983048 | tf_op jit(solution)/shard_map/ppermute | solution.py:204
  105.4 0.0 copy-start.1
  105.5 0.1 pad_add_fusion.where
  105.5 6.3 %collective-permute-start.11 = (bf16[4,2,320,128]{3,2,1,0:T(8,128)(2,1)S(1)}, bf16[4,2,320,128]{3,2,1,0:T(8,128)(2,1)S(1)}, u32[]{:S(2)}, u32[]{:S(2)}) collective-permute-start(bf16[4,2,320,128]{3,2,1,0:T(8,128)(2,1)S(1)} %bitcast.22), channel_id=1, source_target_pairs={{0,1},{1,0},{2,3},{3,2},{4,5},{5,4},{6,7},{7,6},{8,9},{9,8},{10,11... | collective-permute-start | bytes 1966088 | tf_op jit(solution)/shard_map/ppermute | solution.py:204
  111.9 3.3 %collective-permute-start.7 = (bf16[4,2,320,128]{3,2,1,0:T(8,128)(2,1)S(1)}, bf16[4,2,320,128]{3,2,1,0:T(8,128)(2,1)S(1)}, u32[]{:S(2)}, u32[]{:S(2)}) collective-permute-start(bf16[4,2,320,128]{3,2,1,0:T(8,128)(2,1)S(1)} %bitcast.23), channel_id=1, source_target_pairs={{0,12},{4,0},{8,4},{12,8},{1,13},{5,1},{9,5},{13,9},{2,14},{6,2},{... | collective-permute-start | bytes 1966088 | tf_op jit(solution)/shard_map/ppermute | solution.py:204
  115.2 0.9 left.2
  116.0 0.7 collective-permute-start.10
  116.7 0.0 collective-permute-done.8
  116.7 0.9 left.3
  117.6 2.0 %collective-permute-start.9 = (bf16[4,320,128]{2,1,0:T(8,128)(2,1)}, bf16[4,320,128]{2,1,0:T(8,128)(2,1)S(1)}, u32[]{:S(2)}, u32[]{:S(2)}) collective-permute-start(bf16[4,320,128]{2,1,0:T(8,128)(2,1)} %collective-permute-done.8), channel_id=1, source_target_pairs={{0,4},{4,8},{8,12},{12,0},{1,5},{5,9},{9,13},{13,1},{2,6},{6,10},{... | collective-permute-start | bytes 983048 | tf_op jit(solution)/shard_map/ppermute | solution.py:204
  119.6 2.2 %early.1 = (f32[2,512,256]{2,1,0:T(8,128)S(1)}, f32[2,512,256]{2,1,0:T(8,128)S(1)}, f32[2,512,256]{2,1,0:T(8,128)S(1)}) custom-call(bf16[512,1280]{1,0:T(8,128)(2,1)S(1)} %left.3, bf16[4,2,320,128]{3,2,1,0:T(8,128)(2,1)S(1)} %bitcast.30, bf16[4,2,320,128]{3,2,1,0:T(8,128)(2,1)S(1)} %collective-permute-done.refs_1_, ...), custom_call_target="tpu_custom_call" | custom-call | flops 7000000000 | bytes 12000000 | tf_op jit(solution)/shard_map/early/pallas_call | solution.py:146
  121.8 0.0 collective-permute-done.11.two
  121.9 2.3 %late.3.refs_0_ = f32[2,2,9,128,128]{4,3,2,1,0:T(8,128)} custom-call(s32[2]{0:T(128)S(1)} %pad_add_fusion.where, bf16[512,1280]{1,0:T(8,128)(2,1)S(1)} %left.2, f32[2,512,256]{2,1,0:T(8,128)S(1)} %get-tuple-element.46.begun, bf16[4,2,320,128]{3,2,1,0:T(8,128)(2,1)S(1)} %bitcast.25, bf16[4,2,320,128]{3,2,1,0:T(8,128)(2,1)S(1)} %collective-permute-done.11.two), custom_call_target="tpu_custom_call" | custom-call | flops 2000000000 | bytes 4000000 | tf_op jit(solution)/shard_map/late/pallas_call | solution.py:182
  124.2 0.0 collective-permute-done.10
  124.2 5.7 %collective-permute-done.9 = bf16[4,320,128]{2,1,0:T(8,128)(2,1)S(1)} collective-permute-done((bf16[4,320,128]{2,1,0:T(8,128)(2,1)}, bf16[4,320,128]{2,1,0:T(8,128)(2,1)S(1)}, u32[]{:S(2)}, u32[]{:S(2)}) %collective-permute-start.9) | collective-permute-done | bytes 327712 | tf_op jit(solution)/shard_map/ppermute | solution.py:204
  129.9 0.1 pad_maximum_fusion.1.one
  130.0 0.1 collective-permute-done.7.one
  130.1 2.9 %collective-permute-start.13 = (bf16[4,2,320,128]{3,2,1,0:T(8,128)(2,1)S(1)}, bf16[4,2,320,128]{3,2,1,0:T(8,128)(2,1)S(1)}, u32[]{:S(2)}, u32[]{:S(2)}) collective-permute-start(bf16[4,2,320,128]{3,2,1,0:T(8,128)(2,1)S(1)} %collective-permute-done.7.one), channel_id=1, source_target_pairs={{0,1},{1,0},{2,3},{3,2},{4,5},{5,4},{6,7},{7,6},{8,9},{9,8},{10,11... | collective-permute-start | bytes 1966088 | tf_op jit(solution)/shard_map/ppermute | solution.py:204
  133.0 1.9 %collective-permute-start.12 = (bf16[4,2,320,128]{3,2,1,0:T(8,128)(2,1)S(1)}, bf16[4,2,320,128]{3,2,1,0:T(8,128)(2,1)S(1)}, u32[]{:S(2)}, u32[]{:S(2)}) collective-permute-start(bf16[4,2,320,128]{3,2,1,0:T(8,128)(2,1)S(1)} %pad_maximum_fusion.1.one), channel_id=1, source_target_pairs={{0,1},{1,0},{2,3},{3,2},{4,5},{5,4},{6,7},{7,6},{8,9},{9,8},{10,11... | collective-permute-start | bytes 1966088 | tf_op jit(solution)/shard_map/ppermute | solution.py:204
  135.0 0.0 collective-permute-done.13.two
  135.0 2.4 %late.4.refs_0_ = f32[2,2,9,128,128]{4,3,2,1,0:T(8,128)} custom-call(s32[2]{0:T(128)S(1)} %pad_add_fusion.where, bf16[512,1280]{1,0:T(8,128)(2,1)S(1)} %left.2, f32[2,512,256]{2,1,0:T(8,128)S(1)} %get-tuple-element.52.begun, bf16[4,2,320,128]{3,2,1,0:T(8,128)(2,1)S(1)} %collective-permute-done.7.one, ...), custom_call_target="tpu_custom_call", output_to_operand_aliasing={{}: (5, {})} | custom-call | flops 2000000000 | bytes 4000000 | tf_op jit(solution)/shard_map/late/pallas_call | solution.py:182
  137.4 0.0 collective-permute-done.12.two
  137.4 2.2 %late.5 = f32[2,2,9,128,128]{4,3,2,1,0:T(8,128)} custom-call(s32[2]{0:T(128)S(1)} %pad_add_fusion.where, bf16[512,1280]{1,0:T(8,128)(2,1)S(1)} %left.2, f32[2,512,256]{2,1,0:T(8,128)S(1)} %get-tuple-element.50.begun, bf16[4,2,320,128]{3,2,1,0:T(8,128)(2,1)S(1)} %pad_maximum_fusion.1.one, ...), custom_call_target="tpu_custom_call", output_to_operand_aliasing={{}: (5, {})} | custom-call | flops 2000000000 | bytes 4000000 | tf_op jit(solution)/shard_map/late/pallas_call | solution.py:182
  (5 shorter events, 0.1 us)
Async XLA Ops:
  4.3 53.5 %all-to-all-start = ((bf16[64,40,128]{2,1,0:T(8,128)(2,1)}), bf16[64,40,128]{2,1,0:T(8,128)(2,1)S(1)}, u32[]{:S(2)}, u32[]{:S(2)}) async-start(bf16[64,40,128]{2,1,0:T(8,128)(2,1)} %bitcast.34), calls=%async_computation | async-start | bytes 1310720 | tf_op jit(solution)/shard_map/all_to_all | solution.py:237
  57.9 43.5 %all-to-all-start.1 = ((bf16[64,40,128]{2,1,0:T(8,128)(2,1)}), bf16[64,40,128]{2,1,0:T(8,128)(2,1)S(1)}, u32[]{:S(2)}, u32[]{:S(2)}) async-start(bf16[64,40,128]{2,1,0:T(8,128)(2,1)} %bitcast.33), calls=%async_computation.1 | async-start | bytes 1310720 | tf_op jit(solution)/shard_map/all_to_all | solution.py:237
  67.2 11.2 %collective-permute-start.3 = (bf16[4,320,128]{2,1,0:T(8,128)(2,1)S(1)}, bf16[4,320,128]{2,1,0:T(8,128)(2,1)S(1)}, u32[]{:S(2)}, u32[]{:S(2)}) collective-permute-start(bf16[4,320,128]{2,1,0:T(8,128)(2,1)S(1)} %get-tuple-element.57), channel_id=1, source_target_pairs={{0,4},{4,8},{8,12},{12,0},{1,5},{5,9},{9,13},{13,1},{2,6},{6,10},{... | collective-permute-start | bytes 983048 | tf_op jit(solution)/shard_map/ppermute | solution.py:204
  70.4 23.2 %collective-permute-start.1 = (bf16[4,2,320,128]{3,2,1,0:T(8,128)(2,1)S(1)}, bf16[4,2,320,128]{3,2,1,0:T(8,128)(2,1)S(1)}, u32[]{:S(2)}, u32[]{:S(2)}) collective-permute-start(bf16[4,2,320,128]{3,2,1,0:T(8,128)(2,1)S(1)} %bitcast.27), channel_id=1, source_target_pairs={{0,12},{4,0},{8,4},{12,8},{1,13},{5,1},{9,5},{13,9},{2,14},{6,2},{... | collective-permute-start | bytes 1966088 | tf_op jit(solution)/shard_map/ppermute | solution.py:204
  73.7 10.8 %collective-permute-start.5 = (bf16[4,320,128]{2,1,0:T(8,128)(2,1)S(1)}, bf16[4,320,128]{2,1,0:T(8,128)(2,1)S(1)}, u32[]{:S(2)}, u32[]{:S(2)}) collective-permute-start(bf16[4,320,128]{2,1,0:T(8,128)(2,1)S(1)} %get-tuple-element.58), channel_id=1, source_target_pairs={{2,10},{6,14},{10,2},{14,6},{3,11},{7,15},{11,3},{15,7},{18,26},{2... | collective-permute-start | bytes 983048 | tf_op jit(solution)/shard_map/ppermute | solution.py:210
  78.4 10.2 %collective-permute-start.4 = (bf16[4,320,128]{2,1,0:T(8,128)(2,1)S(1)}, bf16[4,320,128]{2,1,0:T(8,128)(2,1)S(1)}, u32[]{:S(2)}, u32[]{:S(2)}) collective-permute-start(bf16[4,320,128]{2,1,0:T(8,128)(2,1)S(1)} %collective-permute-done.3), channel_id=1, source_target_pairs={{0,4},{4,8},{8,12},{12,0},{1,5},{5,9},{9,13},{13,1},{2,6},{6,10},{... | collective-permute-start | bytes 983048 | tf_op jit(solution)/shard_map/ppermute | solution.py:204
  80.3 15.2 %collective-permute-start = (bf16[4,2,320,128]{3,2,1,0:T(8,128)(2,1)S(1)}, bf16[4,2,320,128]{3,2,1,0:T(8,128)(2,1)S(1)}, u32[]{:S(2)}, u32[]{:S(2)}) collective-permute-start(bf16[4,2,320,128]{3,2,1,0:T(8,128)(2,1)S(1)} %bitcast.28), channel_id=1, source_target_pairs={{0,1},{1,0},{2,3},{3,2},{4,5},{5,4},{6,7},{7,6},{8,9},{9,8},{10,11... | collective-permute-start | bytes 1966088 | tf_op jit(solution)/shard_map/ppermute | solution.py:204
  88.7 6.8 %collective-permute-start.6 = (bf16[4,2,320,128]{3,2,1,0:T(8,128)(2,1)S(1)}, bf16[4,2,320,128]{3,2,1,0:T(8,128)(2,1)S(1)}, u32[]{:S(2)}, u32[]{:S(2)}) collective-permute-start(bf16[4,2,320,128]{3,2,1,0:T(8,128)(2,1)S(1)} %pad_maximum_fusion.refs_4_), channel_id=1, source_target_pairs={{0,1},{1,0},{2,3},{3,2},{4,5},{5,4},{6,7},{7,6},{8,9},{9,8},{10,11... | collective-permute-start | bytes 1966088 | tf_op jit(solution)/shard_map/ppermute | solution.py:204
  93.6 4.0 %collective-permute-start.2 = (bf16[4,2,320,128]{3,2,1,0:T(8,128)(2,1)S(1)}, bf16[4,2,320,128]{3,2,1,0:T(8,128)(2,1)S(1)}, u32[]{:S(2)}, u32[]{:S(2)}) collective-permute-start(bf16[4,2,320,128]{3,2,1,0:T(8,128)(2,1)S(1)} %collective-permute-done.1.refs_2_), channel_id=1, source_target_pairs={{0,1},{1,0},{2,3},{3,2},{4,5},{5,4},{6,7},{7,6},{8,9},{9,8},{10,11... | collective-permute-start | bytes 1966088 | tf_op jit(solution)/shard_map/ppermute | solution.py:204
  95.6 0.9 copy-start
  97.6 0.9 copy-start.2
  102.2 14.5 %collective-permute-start.8 = (bf16[4,320,128]{2,1,0:T(8,128)(2,1)}, bf16[4,320,128]{2,1,0:T(8,128)(2,1)}, u32[]{:S(2)}, u32[]{:S(2)}) collective-permute-start(bf16[4,320,128]{2,1,0:T(8,128)(2,1)} %get-tuple-element.55), channel_id=1, source_target_pairs={{0,4},{4,8},{8,12},{12,0},{1,5},{5,9},{9,13},{13,1},{2,6},{6,10},{... | collective-permute-start | bytes 983048 | tf_op jit(solution)/shard_map/ppermute | solution.py:204
  105.4 14.2 %copy-start.1 = (bf16[4,2,320,128]{3,2,1,0:T(8,128)(2,1)S(1)}, bf16[4,2,320,128]{3,2,1,0:T(8,128)(2,1)}, u32[]{:S(2)}) copy-start(bf16[4,2,320,128]{3,2,1,0:T(8,128)(2,1)} %copy-done) | copy-start | bytes 1966084
  105.5 14.2 %copy-start.3 = (bf16[4,2,320,128]{3,2,1,0:T(8,128)(2,1)S(1)}, bf16[4,2,320,128]{3,2,1,0:T(8,128)(2,1)}, u32[]{:S(2)}) copy-start(bf16[4,2,320,128]{3,2,1,0:T(8,128)(2,1)} %copy-done.2) | copy-start | bytes 1966084
  105.5 16.3 %collective-permute-start.11 = (bf16[4,2,320,128]{3,2,1,0:T(8,128)(2,1)S(1)}, bf16[4,2,320,128]{3,2,1,0:T(8,128)(2,1)S(1)}, u32[]{:S(2)}, u32[]{:S(2)}) collective-permute-start(bf16[4,2,320,128]{3,2,1,0:T(8,128)(2,1)S(1)} %bitcast.22), channel_id=1, source_target_pairs={{0,1},{1,0},{2,3},{3,2},{4,5},{5,4},{6,7},{7,6},{8,9},{9,8},{10,11... | collective-permute-start | bytes 1966088 | tf_op jit(solution)/shard_map/ppermute | solution.py:204
  111.9 18.2 %collective-permute-start.7 = (bf16[4,2,320,128]{3,2,1,0:T(8,128)(2,1)S(1)}, bf16[4,2,320,128]{3,2,1,0:T(8,128)(2,1)S(1)}, u32[]{:S(2)}, u32[]{:S(2)}) collective-permute-start(bf16[4,2,320,128]{3,2,1,0:T(8,128)(2,1)S(1)} %bitcast.23), channel_id=1, source_target_pairs={{0,12},{4,0},{8,4},{12,8},{1,13},{5,1},{9,5},{13,9},{2,14},{6,2},{... | collective-permute-start | bytes 1966088 | tf_op jit(solution)/shard_map/ppermute | solution.py:204
  116.0 8.2 %collective-permute-start.10 = (bf16[4,320,128]{2,1,0:T(8,128)(2,1)}, bf16[4,320,128]{2,1,0:T(8,128)(2,1)S(1)}, u32[]{:S(2)}, u32[]{:S(2)}) collective-permute-start(bf16[4,320,128]{2,1,0:T(8,128)(2,1)} %get-tuple-element.56), channel_id=1, source_target_pairs={{2,10},{6,14},{10,2},{14,6},{3,11},{7,15},{11,3},{15,7},{18,26},{2... | collective-permute-start | bytes 983048 | tf_op jit(solution)/shard_map/ppermute | solution.py:210
  117.6 12.3 %collective-permute-start.9 = (bf16[4,320,128]{2,1,0:T(8,128)(2,1)}, bf16[4,320,128]{2,1,0:T(8,128)(2,1)S(1)}, u32[]{:S(2)}, u32[]{:S(2)}) collective-permute-start(bf16[4,320,128]{2,1,0:T(8,128)(2,1)} %collective-permute-done.8), channel_id=1, source_target_pairs={{0,4},{4,8},{8,12},{12,0},{1,5},{5,9},{9,13},{13,1},{2,6},{6,10},{... | collective-permute-start | bytes 983048 | tf_op jit(solution)/shard_map/ppermute | solution.py:204
  130.1 4.8 %collective-permute-start.13 = (bf16[4,2,320,128]{3,2,1,0:T(8,128)(2,1)S(1)}, bf16[4,2,320,128]{3,2,1,0:T(8,128)(2,1)S(1)}, u32[]{:S(2)}, u32[]{:S(2)}) collective-permute-start(bf16[4,2,320,128]{3,2,1,0:T(8,128)(2,1)S(1)} %collective-permute-done.7.one), channel_id=1, source_target_pairs={{0,1},{1,0},{2,3},{3,2},{4,5},{5,4},{6,7},{7,6},{8,9},{9,8},{10,11... | collective-permute-start | bytes 1966088 | tf_op jit(solution)/shard_map/ppermute | solution.py:204
  133.0 4.4 %collective-permute-start.12 = (bf16[4,2,320,128]{3,2,1,0:T(8,128)(2,1)S(1)}, bf16[4,2,320,128]{3,2,1,0:T(8,128)(2,1)S(1)}, u32[]{:S(2)}, u32[]{:S(2)}) collective-permute-start(bf16[4,2,320,128]{3,2,1,0:T(8,128)(2,1)S(1)} %pad_maximum_fusion.1.one), channel_id=1, source_target_pairs={{0,1},{1,0},{2,3},{3,2},{4,5},{5,4},{6,7},{7,6},{8,9},{9,8},{10,11... | collective-permute-start | bytes 1966088 | tf_op jit(solution)/shard_map/ppermute | solution.py:204
